TPU v7x, 512 devices: a whole 4x8x8 slice. The times are simulated.
512 devices in a mesh: grp: 16 (over x, z_lo, core), mem: 32 (over y, z_hi).
Axes of the slice: x: 4, y: 8, z: 8 (z_hi: 4, z_lo: 2; z = z_hi * 2 + z_lo), core: 2. Of those that a mesh axis runs over, the one named last changes fastest.
Arguments:
- images: bfloat16 [16, 2, 768, 16384], P('grp', None, None, 'mem'), may hold values from -6 to 6
- phantom: bfloat16 [16, 16384], P('grp', 'mem'), may hold values from -12 to 12
- inject_rows: int32 [16, 2, 64], P('grp'), may hold values from 0 to 767
- prior_blocks: int32 [16, 2, 768], P('grp'), may hold values from 0 to 127
- basis: bfloat16 [16384, 512], P('mem'), may hold values from -0.046875 to 0.046875
- refs: bfloat16 [512, 32768], P(None, 'mem'), may hold values from -24 to 24
Outputs:
- new_refs: float32 [512, 32768], P('grp', 'mem')
Inputs may be any that keep to these rules, and one draw needn't show every extreme that they name: `inject_rows`: row numbers within a batch; repeats may occur. `prior_blocks`: orientation block numbers; block b holds orientations b * 256 to (b + 1) * 256 - 1.
All inputs are finite; a program needn't handle non-finite values.
Results may differ from a plain program's by a relative error of at most 0.0051.
Values sent between devices are 32-bit elements; how exact they have to be, the bound alone decides.
No kernel may reach another device: no remote copies, remote signals or barrier semaphores. Data moves between devices by JAX's collectives and lax.ppermute only.
A program may use at most 64 MiB of HBM per device.

v0:
```python
import jax
import jax.numpy as jnp
from jax import lax
from jax.sharding import PartitionSpec as P

OBLOCK = 256


PRIOR_INCREMENT = 3.0


def rows_for(lines, length):
    spare = -len(lines) % length
    return jnp.pad(lines, [(0, spare)] + [(0, 0)] * (lines.ndim - 1))


def in_order(parts, dim):
    parts = jnp.moveaxis(parts, 0, dim)
    shape = parts.shape
    return parts.reshape(*shape[:dim], shape[dim] * shape[dim + 1], *shape[dim + 2 :])


def copy_for_each(x, axis):
    length = lax.axis_size(axis)
    return lax.all_to_all(jnp.broadcast_to(x[None], (length, *x.shape)), axis, 0, 0, tiled=True)


def gather_directly(x, axis, dim):
    return in_order(copy_for_each(x, axis), dim)


def split_up(x, dim, length):
    shape = x.shape
    parts = x.reshape(*shape[:dim], length, shape[dim] // length, *shape[dim + 1 :])
    return jnp.moveaxis(parts, dim, 0)


def sum_at_owner(x, axis, dim):
    parts = split_up(x, dim, lax.axis_size(axis))
    arrived = lax.all_to_all(parts, axis, split_axis=0, concat_axis=0, tiled=True)
    return arrived.sum(axis=0)


def total_of(x, axes):
    padded = rows_for(x, lax.axis_size(axes))
    whole = gather_directly(sum_at_owner(padded, axes, 0), axes, 0)
    return lax.slice_in_dim(whole, 0, len(x)).reshape(x.shape)


def packed_total(arrays, axis):
    ends = [0]
    for a in arrays:
        ends.append(ends[-1] + a.size)
    subtotal = total_of(jnp.concatenate([a.ravel() for a in arrays]), axis)
    return tuple((subtotal[b:e].reshape(a.shape) for a, b, e in zip(arrays, ends, ends[1:])))


def gathered_once(x, axis):
    leaves = jax.tree.leaves(x)
    order = sorted(range(len(leaves)), key=lambda k: -leaves[k].size)
    width = (1, *leaves[order[0]].shape)[-1]
    lines = [
        jnp.pad(leaves[k].reshape(-1), (0, -leaves[k].size % width)).reshape(-1, width)
        for k in order
    ]
    both, at, found = (copy_for_each(jnp.concatenate(lines), axis), 0, {})
    for k, line in zip(order, lines):
        section = both[:, at : at + len(line)].reshape(len(both), -1)
        found[k] = section[:, : leaves[k].size].reshape(-1, *leaves[k].shape)
        at += len(line)
    numbers = iter(range(len(leaves)))
    return jax.tree.map(lambda _: found[next(numbers)], x)


def folded_in_pairs(pieces, combine):
    while len(jax.tree.leaves(pieces)[0]) > 1:
        pieces = jax.vmap(combine)(
            *(jax.tree.map(lambda part: part[side::2], pieces) for side in (0, 1))
        )
    return jax.tree.map(lambda part: part[0], pieces)


def combined_all(x, axis, combine):
    pieces = gathered_once(x, axis)
    return folded_in_pairs(pieces, combine)


def taken_together(x, axis):
    return copy_for_each(x, axis).sum(axis=0)


def combine_rows(former, latter):
    row_top = jnp.maximum(former[0], latter[0])
    return (
        row_top,
        former[1] * jnp.exp(former[0] - row_top) + latter[1] * jnp.exp(latter[0] - row_top),
    )


def make_term(pairs):
    final_output = None
    for basis_coefficients, weights in pairs:
        product = lax.dot_general(
            basis_coefficients,
            weights,
            (((0,), (0,)), ((), ())),
            preferred_element_type=jnp.float32,
        )
        final_output = product
    return final_output


def shards(images, phantom, inject_rows, prior_blocks, basis, refs):
    particles = images.shape[2]
    batch_groups = images.shape[1]
    local_orientation = refs.shape[1]
    positions = jnp.arange(particles, dtype=jnp.int32)
    orient_start = lax.axis_index("mem") * local_orientation
    orient_block = (orient_start + jnp.arange(local_orientation, dtype=jnp.int32)) // OBLOCK
    phantom_partial = jnp.dot(phantom[0], basis, preferred_element_type=jnp.float32)
    share_rows = basis.shape[1] // lax.axis_size("grp")
    shares = jnp.zeros((share_rows, local_orientation), jnp.float32)
    masses = jnp.zeros((local_orientation,), jnp.float32)
    for batch_index in range(batch_groups):
        chosen = jnp.any(inject_rows[0, batch_index][:, None] == positions[None, :], axis=0).astype(
            jnp.float32
        )
        partial_output = jnp.dot(images[0, batch_index], basis, preferred_element_type=jnp.float32)
        summed_plain, phantom_coef = packed_total((partial_output, phantom_partial), "mem")
        basis_coefficients = (summed_plain + chosen[:, None] * phantom_coef[None, :]).astype(
            jnp.bfloat16
        )
        match_score = (prior_blocks[0, batch_index][:, None] == orient_block[None, :]).astype(
            jnp.float32
        )
        score_rows = (
            jnp.dot(basis_coefficients, refs, preferred_element_type=jnp.float32)
            + PRIOR_INCREMENT * match_score
        )
        local_top = jnp.max(score_rows, axis=1)
        local_powers = jnp.exp(score_rows - local_top[:, None])
        row_top, row_total = combined_all(
            (local_top, jnp.sum(local_powers, axis=1)), "mem", combine_rows
        )
        powers = local_powers * jnp.exp(local_top - row_top)[:, None]
        weights = (powers / row_total[:, None]).astype(jnp.bfloat16)
        basis_coefficients, weights, local_mass = (
            basis_coefficients,
            weights,
            jnp.sum(weights.astype(jnp.float32), axis=0),
        )
        shares = shares + sum_at_owner(make_term(((basis_coefficients, weights),)), "grp", 0)
        masses = masses + taken_together(local_mass, "grp")
    grp_start = lax.axis_index("grp") * share_rows
    ref_slice = lax.dynamic_slice_in_dim(refs, grp_start, share_rows, 0).astype(jnp.float32)
    return (shares + ref_slice) / (masses[None, :] + 1.0)


def solution(mesh):
    placed = (
        P("grp", None, None, "mem"),
        P("grp", "mem"),
        P("grp", None, None),
        P("grp", None, None),
        P("mem", None),
        P(None, "mem"),
    )
    return jax.shard_map(
        shards, mesh=mesh, in_specs=placed, out_specs=P("grp", "mem"), check_vma=False
    )
```

profile of v0, /device:TPU:1, one launch (start us, length us, event | category | flops | bytes accessed | tf_op | source)
XLA Modules:
  0.0 368.7 jit_solution(4312805109485085000)
XLA Ops:
  0.0 1.0 copy-done
  1.0 1.7 convolution_bitcast_fusion
  4.4 1.4 pad_maximum_fusion
  5.8 3.2 all_to_all.45
  9.0 16.5 %all-to-all-start.4 = ((f32[32,1,12304]{2,1,0:T(1,128)}), f32[32,1,12304]{2,1,0:T(1,128)S(1)}, u32[]{:S(2)}, u32[]{:S(2)}) async-start(f32[32,1,12304]{2,1,0:T(1,128)} %all_to_all.45), calls=%async_computation.4 | async-start | bytes 3178496 | tf_op jit(solution)/shard_map/all_to_all | solution.py:40
  25.5 4.6 %all_to_all.40 = f32[32,1,12304]{2,1,0:T(1,128)} reshape(f32[393728]{0:T(1024)} %get-tuple-element.42) | data formatting | bytes 3149824 | tf_op jit(solution)/shard_map/all_to_all | solution.py:40
  30.1 33.6 %all-to-all-done.4 = f32[32,1,12304]{2,1,0:T(1,128)S(1)} async-done(((f32[32,1,12304]{2,1,0:T(1,128)}), f32[32,1,12304]{2,1,0:T(1,128)S(1)}, u32[]{:S(2)}, u32[]{:S(2)}) %all-to-all-start.4) | async-done | bytes 1574944 | tf_op jit(solution)/shard_map/all_to_all | solution.py:40
  63.7 1.2 copy-done.6
  64.9 11.4 %all-to-all-start = ((f32[32,1,12304]{2,1,0:T(1,128)}), f32[32,1,12304]{2,1,0:T(1,128)S(1)}, u32[]{:S(2)}, u32[]{:S(2)}) async-start(f32[32,1,12304]{2,1,0:T(1,128)} %all_to_all.40), calls=%async_computation | async-start | bytes 3178496 | tf_op jit(solution)/shard_map/all_to_all | solution.py:40
  76.3 2.3 reduce_sum.93
  78.6 34.3 %all-to-all-done = f32[32,1,12304]{2,1,0:T(1,128)S(1)} async-done(((f32[32,1,12304]{2,1,0:T(1,128)}), f32[32,1,12304]{2,1,0:T(1,128)S(1)}, u32[]{:S(2)}, u32[]{:S(2)}) %all-to-all-start) | async-done | bytes 1574944 | tf_op jit(solution)/shard_map/all_to_all | solution.py:40
  112.9 2.0 broadcast_in_dim.14
  114.9 11.0 %all-to-all-start.5 = ((f32[32,1,12304]{2,1,0:T(1,128)}), f32[32,1,12304]{2,1,0:T(1,128)S(1)}, u32[]{:S(2)}, u32[]{:S(2)}) async-start(f32[32,1,12304]{2,1,0:T(1,128)} %broadcast_in_dim.14), calls=%async_computation.5 | async-start | bytes 3178496 | tf_op jit(solution)/shard_map/all_to_all | solution.py:25
  125.9 2.3 reduce_sum.90
  128.3 35.3 %all-to-all-done.5 = f32[32,1,12304]{2,1,0:T(1,128)S(1)} async-done(((f32[32,1,12304]{2,1,0:T(1,128)}), f32[32,1,12304]{2,1,0:T(1,128)S(1)}, u32[]{:S(2)}, u32[]{:S(2)}) %all-to-all-start.5) | async-done | bytes 1574944 | tf_op jit(solution)/shard_map/all_to_all | solution.py:25
  163.6 2.0 broadcast_in_dim.12
  165.6 9.5 %all-to-all-start.1 = ((f32[32,1,12304]{2,1,0:T(1,128)}), f32[32,1,12304]{2,1,0:T(1,128)}, u32[]{:S(2)}, u32[]{:S(2)}) async-start(f32[32,1,12304]{2,1,0:T(1,128)} %broadcast_in_dim.12), calls=%async_computation.1 | async-start | bytes 3178496 | tf_op jit(solution)/shard_map/all_to_all | solution.py:25
  175.4 5.2 %reduce.9 = f32[32,12304]{1,0:T(8,128)S(1)} reduce(f32[32,1,12304]{2,1,0:T(1,128)} %copy-done.4, f32[]{:T(128)} %constant.48), dimensions={1}, to_apply=%all_to_all.47.reduce_sub_computation | reduce | bytes 3149828 | tf_op jit(solution)/shard_map/all_to_all | solution.py:25
  180.6 2.0 reshape.147
  182.6 2.3 slice.205
  185.0 25.6 %all-to-all-done.1 = f32[32,1,12304]{2,1,0:T(1,128)} async-done(((f32[32,1,12304]{2,1,0:T(1,128)}), f32[32,1,12304]{2,1,0:T(1,128)}, u32[]{:S(2)}, u32[]{:S(2)}) %all-to-all-start.1) | async-done | bytes 1574944 | tf_op jit(solution)/shard_map/all_to_all | solution.py:25
  210.5 5.2 %reduce.4 = f32[32,12304]{1,0:T(8,128)S(1)} reduce(f32[32,1,12304]{2,1,0:T(1,128)} %all-to-all-done.1, f32[]{:T(128)} %constant.48), dimensions={1}, to_apply=%all_to_all.42.reduce_sub_computation | reduce | bytes 3149828 | tf_op jit(solution)/shard_map/all_to_all | solution.py:25
  215.7 1.9 reshape.141
  217.6 2.5 slice.177
  220.2 0.7 slice.241
  221.5 2.6 fusion.25
  224.1 1.6 fusion.3
  225.8 1.9 fusion.1
  227.7 0.7 broadcast_in_dim.13
  228.5 12.8 %all-to-all-start.2 = ((f32[32,2,768]{2,1,0:T(2,128)}), f32[32,2,768]{2,1,0:T(2,128)S(1)}, u32[]{:S(2)}, u32[]{:S(2)}) async-start(f32[32,2,768]{2,1,0:T(2,128)} %broadcast_in_dim.13), calls=%async_computation.2 | async-start | bytes 393216 | tf_op jit(solution)/shard_map/all_to_all | solution.py:25
  241.3 11.4 %all-to-all-done.2 = f32[32,2,768]{2,1,0:T(2,128)S(1)} async-done(((f32[32,2,768]{2,1,0:T(2,128)}), f32[32,2,768]{2,1,0:T(2,128)S(1)}, u32[]{:S(2)}, u32[]{:S(2)}) %all-to-all-start.2) | async-done | bytes 196640 | tf_op jit(solution)/shard_map/all_to_all | solution.py:25
  252.7 0.7 broadcast_in_dim.15
  253.5 3.9 %all-to-all-start.6 = ((f32[32,2,768]{2,1,0:T(2,128)}), f32[32,2,768]{2,1,0:T(2,128)S(1)}, u32[]{:S(2)}, u32[]{:S(2)}) async-start(f32[32,2,768]{2,1,0:T(2,128)} %broadcast_in_dim.15), calls=%async_computation.6 | async-start | bytes 393216 | tf_op jit(solution)/shard_map/all_to_all | solution.py:25
  258.1 10.8 %all-to-all-done.6 = f32[32,2,768]{2,1,0:T(2,128)S(1)} async-done(((f32[32,2,768]{2,1,0:T(2,128)}), f32[32,2,768]{2,1,0:T(2,128)S(1)}, u32[]{:S(2)}, u32[]{:S(2)}) %all-to-all-start.6) | async-done | bytes 196640 | tf_op jit(solution)/shard_map/all_to_all | solution.py:25
  269.6 6.4 %convert_reduce_fusion = (f32[1024]{0:T(1024)S(1)}, bf16[768,1024]{1,0:T(8,128)(2,1)}, f32[1024]{0:T(1024)S(1)}, bf16[768,1024]{1,0:T(8,128)(2,1)}) fusion(f32[768]{0:T(1024)S(1)} %get-tuple-element.6, f32[768]{0:T(1024)S(1)} %get-tuple-element.46, f32[768]{0:T(1024)S(1)} %get-tuple-element.13, f32[768,1024]{1,0:T(8,128)} %copy-done.3, ...), kind=kLoop, calls=%fused_computation | loop fusion | flops 14153728 | bytes 9474048 | tf_op jit(solution)/shard_map/reduce_sum | solution.py:150
  276.7 10.8 %all-to-all-start.9 = ((f32[16,1,1024]{2,1,0:T(1,128)}), f32[16,1,1024]{2,1,0:T(1,128)S(1)}, u32[]{:S(2)}, u32[]{:S(2)}) async-start(f32[16,1,1024]{2,1,0:T(1,128)} %broadcast_in_dim.17), calls=%async_computation.9 | async-start | bytes 131072 | tf_op jit(solution)/shard_map/all_to_all | solution.py:25
  287.7 1.2 copy.29
  288.8 4.4 %all-to-all-done.9 = f32[16,1,1024]{2,1,0:T(1,128)S(1)} async-done(((f32[16,1,1024]{2,1,0:T(1,128)}), f32[16,1,1024]{2,1,0:T(1,128)S(1)}, u32[]{:S(2)}, u32[]{:S(2)}) %all-to-all-start.9) | async-done | bytes 65568 | tf_op jit(solution)/shard_map/all_to_all | solution.py:25
  293.9 3.7 %all-to-all-start.8 = ((f32[16,1,1024]{2,1,0:T(1,128)}), f32[16,1,1024]{2,1,0:T(1,128)S(1)}, u32[]{:S(2)}, u32[]{:S(2)}) async-start(f32[16,1,1024]{2,1,0:T(1,128)} %broadcast_in_dim.16), calls=%async_computation.8 | async-start | bytes 131072 | tf_op jit(solution)/shard_map/all_to_all | solution.py:25
  297.7 3.5 fusion.6
  301.1 2.4 all-to-all-done.8
  303.5 4.6 %all-to-all-start.7 = ((f32[16,32,1024]{2,1,0:T(8,128)}), f32[16,32,1024]{2,1,0:T(8,128)}, u32[]{:S(2)}, u32[]{:S(2)}) async-start(f32[16,32,1024]{2,1,0:T(8,128)} %fusion.6), calls=%async_computation.7 | async-start | bytes 4194304 | tf_op jit(solution)/shard_map/all_to_all | solution.py:40
  308.6 3.7 %fusion.8 = f32[16,32,1024]{2,1,0:T(8,128)} fusion(bf16[16,32,768]{2,1,0:T(8,128)(2,1)S(1)} %bitcast.54, bf16[768,1024]{1,0:T(8,128)(2,1)} %get-tuple-element.40), kind=kOutput, calls=%fused_computation.20 | convolution fusion | flops 805306368 | bytes 4456448 | tf_op jit(solution)/shard_map/dot_general | solution.py:103
  312.4 23.1 %all-to-all-done.7 = f32[16,32,1024]{2,1,0:T(8,128)} async-done(((f32[16,32,1024]{2,1,0:T(8,128)}), f32[16,32,1024]{2,1,0:T(8,128)}, u32[]{:S(2)}, u32[]{:S(2)}) %all-to-all-start.7) | async-done | bytes 2097184 | tf_op jit(solution)/shard_map/all_to_all | solution.py:40
  335.5 4.4 %all-to-all-start.3 = ((f32[16,32,1024]{2,1,0:T(8,128)}), f32[16,32,1024]{2,1,0:T(8,128)S(1)}, u32[]{:S(2)}, u32[]{:S(2)}) async-start(f32[16,32,1024]{2,1,0:T(8,128)} %fusion.8), calls=%async_computation.3 | async-start | bytes 4194304 | tf_op jit(solution)/shard_map/all_to_all | solution.py:40
  340.0 1.7 reduce_sum.95
  341.7 25.4 %all-to-all-done.3 = f32[16,32,1024]{2,1,0:T(8,128)S(1)} async-done(((f32[16,32,1024]{2,1,0:T(8,128)}), f32[16,32,1024]{2,1,0:T(8,128)S(1)}, u32[]{:S(2)}, u32[]{:S(2)}) %all-to-all-start.3) | async-done | bytes 2097184 | tf_op jit(solution)/shard_map/all_to_all | solution.py:40
  367.2 1.5 add_divide_fusion
  (102 shorter events, 6.3 us)
Async XLA Ops:
  0.0 1.0 copy-start
  0.0 2.7 copy-start.9
  2.8 0.7 copy-start.12
  9.0 54.7 %all-to-all-start.4 = ((f32[32,1,12304]{2,1,0:T(1,128)}), f32[32,1,12304]{2,1,0:T(1,128)S(1)}, u32[]{:S(2)}, u32[]{:S(2)}) async-start(f32[32,1,12304]{2,1,0:T(1,128)} %all_to_all.45), calls=%async_computation.4 | async-start | bytes 3178496 | tf_op jit(solution)/shard_map/all_to_all | solution.py:40
  63.7 1.2 copy-start.6
  64.9 48.1 %all-to-all-start = ((f32[32,1,12304]{2,1,0:T(1,128)}), f32[32,1,12304]{2,1,0:T(1,128)S(1)}, u32[]{:S(2)}, u32[]{:S(2)}) async-start(f32[32,1,12304]{2,1,0:T(1,128)} %all_to_all.40), calls=%async_computation | async-start | bytes 3178496 | tf_op jit(solution)/shard_map/all_to_all | solution.py:40
  112.9 2.0 copy-start.5
  114.9 48.7 %all-to-all-start.5 = ((f32[32,1,12304]{2,1,0:T(1,128)}), f32[32,1,12304]{2,1,0:T(1,128)S(1)}, u32[]{:S(2)}, u32[]{:S(2)}) async-start(f32[32,1,12304]{2,1,0:T(1,128)} %broadcast_in_dim.14), calls=%async_computation.5 | async-start | bytes 3178496 | tf_op jit(solution)/shard_map/all_to_all | solution.py:25
  163.6 2.0 copy-start.4
  165.6 9.5 %copy-start.13 = (s32[1,2,64]{2,1,0:T(2,128)S(1)}, s32[1,2,64]{2,1,0:T(2,128)}, u32[]{:S(2)}) copy-start(s32[1,2,64]{2,1,0:T(2,128)} %param.8) | copy-start | bytes 1540
  165.6 9.8 %copy-start.11 = (s32[1,2,768]{2,1,0:T(2,128)S(1)}, s32[1,2,768]{2,1,0:T(2,128)}, u32[]{:S(2)}) copy-start(s32[1,2,768]{2,1,0:T(2,128)} %param.9) | copy-start | bytes 18436
  165.6 44.9 %all-to-all-start.1 = ((f32[32,1,12304]{2,1,0:T(1,128)}), f32[32,1,12304]{2,1,0:T(1,128)}, u32[]{:S(2)}, u32[]{:S(2)}) async-start(f32[32,1,12304]{2,1,0:T(1,128)} %broadcast_in_dim.12), calls=%async_computation.1 | async-start | bytes 3178496 | tf_op jit(solution)/shard_map/all_to_all | solution.py:25
  217.6 3.9 %copy-start.10 = (bf16[512,1024]{1,0:T(8,128)(2,1)S(1)}, bf16[512,1024]{1,0:T(8,128)(2,1)}, u32[]{:S(2)}) copy-start(bf16[512,1024]{1,0:T(8,128)(2,1)} %param.11) | copy-start | bytes 3145732
  221.5 2.6 copy-start.7
  224.1 1.7 copy-start.1
  225.7 2.0 copy-start.3
  228.5 24.3 %all-to-all-start.2 = ((f32[32,2,768]{2,1,0:T(2,128)}), f32[32,2,768]{2,1,0:T(2,128)S(1)}, u32[]{:S(2)}, u32[]{:S(2)}) async-start(f32[32,2,768]{2,1,0:T(2,128)} %broadcast_in_dim.13), calls=%async_computation.2 | async-start | bytes 393216 | tf_op jit(solution)/shard_map/all_to_all | solution.py:25
  253.5 15.4 %all-to-all-start.6 = ((f32[32,2,768]{2,1,0:T(2,128)}), f32[32,2,768]{2,1,0:T(2,128)S(1)}, u32[]{:S(2)}, u32[]{:S(2)}) async-start(f32[32,2,768]{2,1,0:T(2,128)} %broadcast_in_dim.15), calls=%async_computation.6 | async-start | bytes 393216 | tf_op jit(solution)/shard_map/all_to_all | solution.py:25
  276.7 16.6 %all-to-all-start.9 = ((f32[16,1,1024]{2,1,0:T(1,128)}), f32[16,1,1024]{2,1,0:T(1,128)S(1)}, u32[]{:S(2)}, u32[]{:S(2)}) async-start(f32[16,1,1024]{2,1,0:T(1,128)} %broadcast_in_dim.17), calls=%async_computation.9 | async-start | bytes 131072 | tf_op jit(solution)/shard_map/all_to_all | solution.py:25
  287.6 10.0 %copy-start.8 = (bf16[768,1024]{1,0:T(8,128)(2,1)S(1)}, bf16[768,1024]{1,0:T(8,128)(2,1)}, u32[]{:S(2)}) copy-start(bf16[768,1024]{1,0:T(8,128)(2,1)} %get-tuple-element.16) | copy-start | bytes 4718596
  293.9 9.6 %all-to-all-start.8 = ((f32[16,1,1024]{2,1,0:T(1,128)}), f32[16,1,1024]{2,1,0:T(1,128)S(1)}, u32[]{:S(2)}, u32[]{:S(2)}) async-start(f32[16,1,1024]{2,1,0:T(1,128)} %broadcast_in_dim.16), calls=%async_computation.8 | async-start | bytes 131072 | tf_op jit(solution)/shard_map/all_to_all | solution.py:25
  301.1 7.0 %copy-start.2 = (f32[769,512]{1,0:T(8,128)S(1)}, f32[769,512]{1,0:T(8,128)}, u32[]{:S(2)}) copy-start(f32[769,512]{1,0:T(8,128)} %slice.177) | copy-start | bytes 4724740
  303.5 31.9 %all-to-all-start.7 = ((f32[16,32,1024]{2,1,0:T(8,128)}), f32[16,32,1024]{2,1,0:T(8,128)}, u32[]{:S(2)}, u32[]{:S(2)}) async-start(f32[16,32,1024]{2,1,0:T(8,128)} %fusion.6), calls=%async_computation.7 | async-start | bytes 4194304 | tf_op jit(solution)/shard_map/all_to_all | solution.py:40
  335.5 31.6 %all-to-all-start.3 = ((f32[16,32,1024]{2,1,0:T(8,128)}), f32[16,32,1024]{2,1,0:T(8,128)S(1)}, u32[]{:S(2)}, u32[]{:S(2)}) async-start(f32[16,32,1024]{2,1,0:T(8,128)} %fusion.8), calls=%async_computation.3 | async-start | bytes 4194304 | tf_op jit(solution)/shard_map/all_to_all | solution.py:40
where the time goes:
time: 370 us; the launch traced here: 369 us
  waiting for transfers between devices  206 us (56%)
  starting transfers between devices  88.6 us (24%)
  local copies, waits for them, and re-layouts  30.4 us (8%)
  other arithmetic  29.1 us (8%)
  matrix products  13.8 us (4%)
    all_to_all x4, waiting for transfers between devices, sum_at_owner(): lax.all_to_all(parts, axis, split_axis=0, concat_axis=0, tiled=True)  116 us
    all_to_all x6, waiting for transfers between devices, copy_for_each(): lax.all_to_all(jnp.broadcast_to(x[None], (length, *x.shape)), axis, 0, 0,...  90 us
    all_to_all x6, starting transfers between devices, copy_for_each(): lax.all_to_all(jnp.broadcast_to(x[None], (length, *x.shape)), axis, 0, 0,...  51.7 us
    all_to_all x4, starting transfers between devices, sum_at_owner(): lax.all_to_all(parts, axis, split_axis=0, concat_axis=0, tiled=True)  36.9 us
    all_to_all x2, other arithmetic, copy_for_each(): lax.all_to_all(jnp.broadcast_to(x[None], (length, *x.shape)), axis, 0, 0,...  10.4 us
    all_to_all x2, local copies, waits for them, and re-layouts, sum_at_owner(): lax.all_to_all(parts, axis, split_axis=0, concat_axis=0, tiled=True)  7.8 us
  transfers between devices with their start and end apart: 10, of which 10 were waited for; matrix products, arithmetic and copies ran while one was open for 7% of the time, Pallas kernels for 0%

commit v1 on v0

v1 whole, which is shorter than its diff:
```python
import jax
import jax.numpy as jnp
from jax import lax
from jax.experimental import pallas as pl
from jax.experimental.pallas import tpu as pltpu
from jax.sharding import Mesh, PartitionSpec as P

OBLOCK = 256
PRIOR_INCREMENT = 3.0
GRP = ("x", "zl", "core")
MEM = ("y", "zh")
LANES = 128


def score_kernel(at, coefs, prior, refs_t, powers, rounded, stats):
    step = pl.program_id(0)
    rows = coefs.shape[1]
    orient = refs_t.shape[0]
    lines = stats.shape[1] // 2
    mine = coefs[...].astype(jnp.bfloat16)
    rounded[...] = mine
    scores = jnp.dot(refs_t[...], mine, preferred_element_type=jnp.float32)
    block = prior[...] - at[0] * (orient // OBLOCK)
    parts = [
        scores[k * OBLOCK : (k + 1) * OBLOCK] + jnp.where(block == k, PRIOR_INCREMENT, 0.0)
        for k in range(orient // OBLOCK)
    ]
    tops = [jnp.max(part, axis=0, keepdims=True) for part in parts]
    top = tops[0]
    for other in tops[1:]:
        top = jnp.maximum(top, other)
    total = jnp.zeros_like(top)
    for k, part in enumerate(parts):
        power = jnp.exp(part - top)
        powers[k * OBLOCK : (k + 1) * OBLOCK, :] = power
        total = total + jnp.sum(power, axis=0, keepdims=True)
    for h in range(rows // LANES):
        line = step * (rows // LANES) + h
        cut = slice(h * LANES, (h + 1) * LANES)
        shape = (stats.shape[0], 1, LANES)
        stats[:, pl.ds(line, 1), :] = jnp.broadcast_to(top[None, :, cut], shape)
        stats[:, pl.ds(lines + line, 1), :] = jnp.broadcast_to(total[None, :, cut], shape)


def scores_of(at, coefs, prior, refs_t, members):
    eigen, rows = coefs.shape
    orient = refs_t.shape[0]
    width = 256
    lines = 2 * rows // LANES
    return pl.pallas_call(
        score_kernel,
        grid_spec=pltpu.PrefetchScalarGridSpec(
            num_scalar_prefetch=1,
            grid=(rows // width,),
            in_specs=[
                pl.BlockSpec((eigen, width), lambda j, at: (0, j)),
                pl.BlockSpec((1, width), lambda j, at: (0, j)),
                pl.BlockSpec((orient, eigen), lambda j, at: (0, 0)),
            ],
            out_specs=[
                pl.BlockSpec((orient, width), lambda j, at: (0, j)),
                pl.BlockSpec((eigen, width), lambda j, at: (0, j)),
                pl.BlockSpec((members, lines, LANES), lambda j, at: (0, 0, 0)),
            ],
        ),
        out_shape=[
            jax.ShapeDtypeStruct((orient, rows), jnp.float32),
            jax.ShapeDtypeStruct((eigen, rows), jnp.bfloat16),
            jax.ShapeDtypeStruct((members, lines, LANES), jnp.float32),
        ],
        compiler_params=pltpu.CompilerParams(vmem_limit_bytes=40 << 20),
        name="scores",
    )(at, coefs, prior, refs_t)


def total_kernel(stats, own, powers, rounded, out, factor):
    step = pl.program_id(0)
    eigen, rows = rounded.shape
    width = powers.shape[0]
    owners = out.shape[0]
    share = eigen // owners
    lines = rows // LANES
    body = out.shape[1] - out.shape[1] % share

    @pl.when(step == 0)
    def _():
        tops = stats[:, :lines, :]
        top = jnp.max(tops, axis=0)
        total = jnp.sum(stats[:, lines:, :] * jnp.exp(tops - top[None]), axis=0)
        scale = jnp.exp(own[0, :lines, :] - top) / total
        for k in range(lines):
            factor[:, k * LANES : (k + 1) * LANES] = scale[k : k + 1, :]

    weights = (powers[...] * factor[...]).astype(jnp.bfloat16)
    contract = (((1,), (1,)), ((), ()))
    totals = lax.dot_general(rounded[...], weights, contract, preferred_element_type=jnp.float32)
    ones = jnp.ones((16, rows), jnp.bfloat16)
    masses = lax.dot_general(ones, weights, contract, preferred_element_type=jnp.float32)
    for h in range(width // LANES):
        column = step * (width // LANES) + h
        cut = slice(h * LANES, (h + 1) * LANES)
        for d in range(owners):
            out[d, pl.ds(pl.multiple_of(column * share, share), share), :] = totals[
                d * share : (d + 1) * share, cut
            ]
        out[:, pl.ds(body + column, 1), :] = jnp.broadcast_to(
            masses[None, 0:1, cut], (owners, 1, LANES)
        )


def totals_of(stats, sent, powers, rounded, owners):
    eigen, rows = rounded.shape
    orient = powers.shape[0]
    width = 256
    deep = (eigen // owners + 1) * (orient // LANES)
    return pl.pallas_call(
        total_kernel,
        grid=(orient // width,),
        in_specs=[
            pl.BlockSpec(stats.shape, lambda j: (0, 0, 0)),
            pl.BlockSpec((1, *sent.shape[1:]), lambda j: (0, 0, 0)),
            pl.BlockSpec((width, rows), lambda j: (j, 0)),
            pl.BlockSpec((eigen, rows), lambda j: (0, 0)),
        ],
        out_specs=pl.BlockSpec((owners, deep, LANES), lambda j: (0, 0, 0)),
        out_shape=jax.ShapeDtypeStruct((owners, deep, LANES), jnp.float32),
        scratch_shapes=[pltpu.VMEM((1, rows), jnp.float32)],
        compiler_params=pltpu.CompilerParams(vmem_limit_bytes=40 << 20),
        name="totals",
    )(stats, sent, powers, rounded)


def final_kernel(at, parts, refs, out):
    share, orient = out.shape
    both = parts[0]
    for d in range(1, parts.shape[0]):
        both = both + parts[d]
    body = share * (orient // LANES)
    for k in range(orient // LANES):
        cut = slice(k * LANES, (k + 1) * LANES)
        above = both[k * share : (k + 1) * share] + refs[:, cut].astype(jnp.float32)
        out[:, cut] = above / (both[body + k : body + k + 1] + 1.0)


def final_of(at, parts, refs):
    owners = parts.shape[0]
    eigen, orient = refs.shape
    share = eigen // owners
    return pl.pallas_call(
        final_kernel,
        grid_spec=pltpu.PrefetchScalarGridSpec(
            num_scalar_prefetch=1,
            grid=(1,),
            in_specs=[
                pl.BlockSpec(parts.shape, lambda j, at: (0, 0, 0)),
                pl.BlockSpec((share, orient), lambda j, at: (at[0], 0)),
            ],
            out_specs=pl.BlockSpec((share, orient), lambda j, at: (0, 0)),
        ),
        out_shape=jax.ShapeDtypeStruct((share, orient), jnp.float32),
        compiler_params=pltpu.CompilerParams(vmem_limit_bytes=40 << 20),
        name="final",
    )(at, parts, refs)


def shifted(x, axis, by):
    size = lax.axis_size(axis)
    return lax.ppermute(x, axis, [(i, (i + by) % size) for i in range(size)])


def sum_at_owner(x, axis):
    size, me = lax.axis_size(axis), lax.axis_index(axis)
    share = x.shape[0] // size
    total = lax.dynamic_slice_in_dim(x, me * share, share, 0)
    for by in range(1, size):
        block = lax.dynamic_slice_in_dim(x, ((me + by) % size) * share, share, 0)
        total = total + shifted(block, axis, by)
    return total


def gathered(x, axis):
    size, me = lax.axis_size(axis), lax.axis_index(axis)
    blocks = [x] + [shifted(x, axis, -by) for by in range(1, size)]
    around = jnp.concatenate(blocks + blocks[:-1])
    return lax.dynamic_slice_in_dim(around, ((size - me) % size) * x.shape[0], size * x.shape[0], 0)


def shards(images, phantom, inject_rows, prior_blocks, basis, refs):
    batches, particles = images.shape[1:3]
    rows = batches * particles
    positions = jnp.arange(particles, dtype=jnp.int32)
    chosen = jnp.any(inject_rows[0][:, :, None] == positions, axis=1)
    contract = (((0,), (1,)), ((), ()))
    plain = lax.dot_general(
        basis, images[0].reshape(rows, -1), contract, preferred_element_type=jnp.float32
    )
    extra = lax.dot_general(basis, phantom, contract, preferred_element_type=jnp.float32)
    partial = plain + extra * chosen.reshape(1, rows).astype(jnp.float32)
    owned = lax.psum_scatter(partial, "y", scatter_dimension=0, tiled=True)
    owned = gathered(sum_at_owner(owned, "zh"), "zh")
    coefs = lax.all_gather(owned, "y", axis=0, tiled=True)
    mem = lax.axis_index(MEM).astype(jnp.int32).reshape(1)
    grp = lax.axis_index(GRP).astype(jnp.int32).reshape(1)
    powers, rounded, sent = scores_of(
        mem, coefs, prior_blocks[0].reshape(1, rows), refs.T, lax.axis_size(MEM)
    )
    stats = lax.all_to_all(sent, MEM, 0, 0, tiled=True)
    parts = totals_of(stats, sent, powers, rounded, lax.axis_size(GRP))
    parts = lax.all_to_all(parts, GRP, 0, 0, tiled=True)
    return final_of(grp, parts, refs)


def solution(mesh):
    fine = Mesh(mesh.devices.reshape(4, 2, 2, 8, 4), GRP + MEM)
    placed = (
        P(GRP, None, None, MEM),
        P(GRP, MEM),
        P(GRP, None, None),
        P(GRP, None, None),
        P(MEM, None),
        P(None, MEM),
    )
    return jax.shard_map(
        shards, mesh=fine, in_specs=placed, out_specs=P(GRP, MEM), check_vma=False
    )
```

time: 370 us -> 235 us (0.64)
  waiting for transfers between devices: 206 us -> 135 us
  starting transfers between devices: 88.6 us -> 35.7 us
  other arithmetic: 29.1 us -> 1.85 us
  blocking collectives: 0 us -> 25 us
  local copies, waits for them, and re-layouts: 30.4 us -> 6.59 us
  between operations: 0.48 us -> 13.7 us
  Pallas kernels: 0 us -> 10.4 us
  matrix products: 13.8 us -> 5.12 us
    all_to_all x10 -> x1, waiting for transfers between devices: 206 us -> 27.9 us  [shards(): parts = lax.all_to_all(parts, GRP, 0, 0, tiled=True)]
    all_to_all x10 -> x1, starting transfers between devices: 88.6 us -> 7.18 us  [shards(): parts = lax.all_to_all(parts, GRP, 0, 0, tiled=True)]
    reduce_scatter x0 -> x1, waiting for transfers between devices: none -> 51.8 us  [shards(): owned = lax.psum_scatter(partial, 'y', scatter_dimension=0, tiled=True)]
    all_gather x0 -> x1, waiting for transfers between devices: none -> 50.4 us  [shards(): coefs = lax.all_gather(owned, 'y', axis=0, tiled=True)]
    ppermute x0 -> x6, starting transfers between devices: none -> 28.5 us  [shifted(): return lax.ppermute(x, axis, [(i, (i + by) % size) for i in range(size)])]
    all_to_all x0 -> x1, blocking collectives: none -> 25 us  [shards(): stats = lax.all_to_all(sent, MEM, 0, 0, tiled=True)]
    reduce_sum x8 -> x0, other arithmetic: 14.9 us -> none  [the longest x4 6.48 us: sum_at_owner(): return arrived.sum(axis=0)]
    all_to_all x2 -> x0, other arithmetic: 10.4 us -> none  [copy_for_each(): lax.all_to_all(jnp.broadcast_to(x[None], (length, *x.shape)), axis, 0, 0,...]
  transfers between devices with their start and end apart: 10 -> 9, of which waited for: 10 -> 5; matrix products, arithmetic and copies ran while one was open for 7% -> 1% of each run, Pallas kernels for 0% -> 0%
where the time goes in v1:
time: 235 us; the launch traced here: 234 us
  waiting for transfers between devices  135 us (57%)
  starting transfers between devices  35.7 us (15%)
  blocking collectives  25 us (11%)
  between operations  13.7 us (6%)
  Pallas kernels  10.4 us (4%)
  local copies, waits for them, and re-layouts  6.59 us (3%)
  matrix products  5.12 us (2%)
    reduce_scatter x1, waiting for transfers between devices, shards(): owned = lax.psum_scatter(partial, 'y', scatter_dimension=0, tiled=True)  51.8 us
    all_gather x1, waiting for transfers between devices, shards(): coefs = lax.all_gather(owned, 'y', axis=0, tiled=True)  50.4 us
    ppermute x6, starting transfers between devices, shifted(): return lax.ppermute(x, axis, [(i, (i + by) % size) for i in range(size)])  28.5 us
    all_to_all x1, waiting for transfers between devices, shards(): parts = lax.all_to_all(parts, GRP, 0, 0, tiled=True)  27.9 us
    all_to_all x1, blocking collectives, shards(): stats = lax.all_to_all(sent, MEM, 0, 0, tiled=True)  25 us
    all_to_all x1, starting transfers between devices, shards(): parts = lax.all_to_all(parts, GRP, 0, 0, tiled=True)  7.18 us
    ppermute x6, waiting for transfers between devices, shifted(): return lax.ppermute(x, axis, [(i, (i + by) % size) for i in range(size)])  5.25 us
    unnamed x17, local copies, waits for them, and re-layouts  4.77 us
  transfers between devices with their start and end apart: 9, of which 5 were waited for; matrix products, arithmetic and copies ran while one was open for 1% of the time, Pallas kernels for 0%

profile of v1, /device:TPU:1, one launch (start us, length us, event | category | flops | bytes accessed | tf_op | source)
XLA Modules:
  0.0 233.8 jit_solution(6163572319730573122)
XLA Ops:
  6.5 0.0 copy-start
  6.5 0.0 reduce-scatter.2.cloned.1.call-start
  6.5 0.9 fusion
  7.5 1.2 fusion.1
  8.7 0.0 copy-done
  8.7 3.9 %convolution_add_fusion = f32[512,1536]{1,0:T(8,128)} fusion(bf16[512,512]{1,0:T(8,128)(2,1)} %param.10, bf16[1536,512]{1,0:T(8,128)(2,1)S(1)} %bitcast.14, f32[1536]{0:T(1024)S(1)} %reshape.25, f32[512]{0:T(512)S(1)} %bitcast.18), kind=kOutput, calls=%fused_computation | convolution fusion | flops 806879232 | bytes 5251072 | tf_op jit(solution)/shard_map/dot_general | solution.py:194
  12.6 0.0 copy-start.4
  12.6 0.0 reduce-scatter.2.cloned.1.call-update
  12.7 0.0 all-gather.2.cloned.1.call-start
  12.7 51.8 %reduce-scatter.2.cloned.1.call-done = f32[64,1536]{1,0:T(8,128)} async-done(((f32[512,1536]{1,0:T(8,128)}), f32[64,1536]{1,0:T(8,128)}) %reduce-scatter.2.cloned.1.call-update) | async-done | bytes 393232 | tf_op jit(solution)/shard_map/reduce_scatter | solution.py:199
  64.6 1.0 constant_dynamic-slice_fusion.3
  65.6 4.3 %collective-permute-start = (f32[16,1536]{1,0:T(8,128)S(1)}, f32[16,1536]{1,0:T(8,128)S(1)}, u32[]{:S(2)}, u32[]{:S(2)}) collective-permute-start(f32[16,1536]{1,0:T(8,128)S(1)} %get-tuple-element.13), channel_id=1, source_target_pairs={{0,1},{1,2},{2,3},{3,0},{4,5},{5,6},{6,7},{7,4},{8,9},{9,10},{10,1... | collective-permute-start | bytes 294920 | tf_op jit(solution)/shard_map/ppermute | solution.py:168
  69.9 4.0 %collective-permute-start.2 = (f32[16,1536]{1,0:T(8,128)S(1)}, f32[16,1536]{1,0:T(8,128)S(1)}, u32[]{:S(2)}, u32[]{:S(2)}) collective-permute-start(f32[16,1536]{1,0:T(8,128)S(1)} %get-tuple-element.14), channel_id=1, source_target_pairs={{0,3},{1,0},{2,1},{3,2},{4,7},{5,4},{6,5},{7,6},{8,11},{9,8},{10,9... | collective-permute-start | bytes 294920 | tf_op jit(solution)/shard_map/ppermute | solution.py:168
  73.9 7.0 %collective-permute-start.1 = (f32[16,1536]{1,0:T(8,128)S(1)}, f32[16,1536]{1,0:T(8,128)S(1)}, u32[]{:S(2)}, u32[]{:S(2)}) collective-permute-start(f32[16,1536]{1,0:T(8,128)S(1)} %get-tuple-element.15), channel_id=1, source_target_pairs={{0,2},{1,3},{2,0},{3,1},{4,6},{5,7},{6,4},{7,5},{8,10},{9,11},{10,... | collective-permute-start | bytes 294920 | tf_op jit(solution)/shard_map/ppermute | solution.py:168
  80.9 0.0 collective-permute-done
  80.9 0.0 collective-permute-done.2
  80.9 2.4 %collective-permute-done.1 = f32[16,1536]{1,0:T(8,128)S(1)} collective-permute-done((f32[16,1536]{1,0:T(8,128)S(1)}, f32[16,1536]{1,0:T(8,128)S(1)}, u32[]{:S(2)}, u32[]{:S(2)}) %collective-permute-start.1) | collective-permute-done | bytes 98336 | tf_op jit(solution)/shard_map/ppermute | solution.py:168
  83.3 0.9 constant_dynamic-update-slice_fusion.6
  84.2 4.2 %collective-permute-start.3 = (f32[16,1536]{1,0:T(8,128)S(1)}, f32[16,1536]{1,0:T(8,128)S(1)}, u32[]{:S(2)}, u32[]{:S(2)}) collective-permute-start(f32[16,1536]{1,0:T(8,128)S(1)} %get-tuple-element.12), channel_id=1, source_target_pairs={{0,3},{1,0},{2,1},{3,2},{4,7},{5,4},{6,5},{7,6},{8,11},{9,8},{10,9... | collective-permute-start | bytes 294920 | tf_op jit(solution)/shard_map/ppermute | solution.py:168
  88.4 2.4 %collective-permute-start.5 = (f32[16,1536]{1,0:T(8,128)S(1)}, f32[16,1536]{1,0:T(8,128)S(1)}, u32[]{:S(2)}, u32[]{:S(2)}) collective-permute-start(f32[16,1536]{1,0:T(8,128)S(1)} %get-tuple-element.12), channel_id=1, source_target_pairs={{0,1},{1,2},{2,3},{3,0},{4,5},{5,6},{6,7},{7,4},{8,9},{9,10},{10,1... | collective-permute-start | bytes 294920 | tf_op jit(solution)/shard_map/ppermute | solution.py:168
  90.8 6.6 %collective-permute-start.4 = (f32[16,1536]{1,0:T(8,128)S(1)}, f32[16,1536]{1,0:T(8,128)S(1)}, u32[]{:S(2)}, u32[]{:S(2)}) collective-permute-start(f32[16,1536]{1,0:T(8,128)S(1)} %get-tuple-element.12), channel_id=1, source_target_pairs={{0,2},{1,3},{2,0},{3,1},{4,6},{5,7},{6,4},{7,5},{8,10},{9,11},{10,... | collective-permute-start | bytes 294920 | tf_op jit(solution)/shard_map/ppermute | solution.py:168
  97.4 0.0 collective-permute-done.3
  97.5 2.9 %collective-permute-done.4 = f32[16,1536]{1,0:T(8,128)S(1)} collective-permute-done((f32[16,1536]{1,0:T(8,128)S(1)}, f32[16,1536]{1,0:T(8,128)S(1)}, u32[]{:S(2)}, u32[]{:S(2)}) %collective-permute-start.4) | collective-permute-done | bytes 98336 | tf_op jit(solution)/shard_map/ppermute | solution.py:168
  100.3 0.0 collective-permute-done.5
  100.4 0.8 constant_dynamic-slice_fusion
  101.2 0.0 all-gather.2.cloned.1.call-update
  101.3 0.0 copy-done.4
  101.3 1.5 copy.8
  102.8 50.4 %all-gather.2.cloned.1.call-done.coefs = f32[512,1536]{1,0:T(8,128)} async-done(((f32[64,1536]{1,0:T(8,128)}), f32[512,1536]{1,0:T(8,128)}) %all-gather.2.cloned.1.call-update) | async-done | bytes 3145744 | tf_op jit(solution)/shard_map/all_gather | solution.py:201
  153.2 0.0 copy-start.3
  153.2 1.9 copy-done.3
  155.1 4.6 %scores.1 = (f32[1024,1536]{1,0:T(8,128)S(1)}, bf16[512,1536]{1,0:T(8,128)(2,1)S(1)}, f32[32,24,128]{2,1,0:T(8,128)S(1)}) custom-call(s32[1]{0:T(128)} %bitcast.1.at, f32[512,1536]{1,0:T(8,128)S(1)} %copy-done.3, s32[1,1536]{1,0:T(1,128)S(1)} %bitcast.16, bf16[1024,512]{1,0:T(8,128)(2,1)S(1)} %bitcast.15), custom_call_target="tpu_custom_call" | custom-call | tf_op jit(solution)/shard_map/scores/pallas_call | solution.py:50
  159.7 25.0 %all_to_all.10.stats = f32[32,24,128]{2,1,0:T(8,128)S(1)} all-to-all(f32[32,24,128]{2,1,0:T(8,128)S(1)} %get-tuple-element.8.own), channel_id=1, replica_groups=mesh['x'=4,'zl'=2,'core'=2,'y'=8,'zh'=4] {'y','zh'}, dimensions={0} | all-to-all | bytes 786432 | tf_op jit(solution)/shard_map/all_to_all | solution.py:207
  184.7 3.4 %totals.1 = f32[16,264,128]{2,1,0:T(8,128)S(1)} custom-call(f32[32,24,128]{2,1,0:T(8,128)S(1)} %all_to_all.10.stats, f32[32,24,128]{2,1,0:T(8,128)S(1)} %get-tuple-element.8.own, f32[1024,1536]{1,0:T(8,128)S(1)} %get-tuple-element.9.powers, bf16[512,1536]{1,0:T(8,128)(2,1)S(1)} %get-tuple-element.10.rounded), custom_call_target="tpu_custom_call" | custom-call | tf_op jit(solution)/shard_map/totals/pallas_call | solution.py:116
  188.1 0.0 copy-start.1
  188.1 1.3 copy-done.1
  189.4 0.0 copy-start.2
  189.4 7.2 %all-to-all-start.1 = ((f32[16,264,128]{2,1,0:T(8,128)}), f32[16,264,128]{2,1,0:T(8,128)}, u32[]{:S(2)}, u32[]{:S(2)}) async-start(f32[16,264,128]{2,1,0:T(8,128)} %copy-done.1), calls=%async_computation.2 | async-start | bytes 4325376 | tf_op jit(solution)/shard_map/all_to_all | solution.py:209
  196.6 27.9 %all-to-all-done.1.parts = f32[16,264,128]{2,1,0:T(8,128)} async-done(((f32[16,264,128]{2,1,0:T(8,128)}), f32[16,264,128]{2,1,0:T(8,128)}, u32[]{:S(2)}, u32[]{:S(2)}) %all-to-all-start.1) | async-done | bytes 2162720 | tf_op jit(solution)/shard_map/all_to_all | solution.py:209
  224.5 0.0 copy-done.2
  224.5 2.4 %final.1 = f32[32,1024]{1,0:T(8,128)} custom-call(s32[1]{0:T(128)} %bitcast.at, f32[16,264,128]{2,1,0:T(8,128)} %all-to-all-done.1.parts, bf16[512,1024]{1,0:T(8,128)(2,1)S(1)} %copy-done.2), custom_call_target="tpu_custom_call" | custom-call | tf_op jit(solution)/shard_map/final/pallas_call | solution.py:149
  (9 shorter events, 0.1 us)
Async XLA Ops:
  6.5 2.2 copy-start
  6.5 58.1 %reduce-scatter.2.cloned.1.call-start = ((), (), s32[]{:S(2)}) async-start(), calls=%async_computation.3 | async-start | bytes 3538944 | tf_op jit(solution)/shard_map/reduce_scatter | solution.py:199
  12.6 88.6 %copy-start.4 = (s32[1,2,768]{2,1,0:T(2,128)S(1)}, s32[1,2,768]{2,1,0:T(2,128)}, u32[]{:S(2)}) copy-start(s32[1,2,768]{2,1,0:T(2,128)} %param.9) | copy-start | bytes 18436
  12.7 140.6 %all-gather.2.cloned.1.call-start = ((), (), s32[]{:S(2)}) async-start(), calls=%async_computation.4 | async-start | bytes 3538944 | tf_op jit(solution)/shard_map/all_gather | solution.py:201
  65.6 15.3 %collective-permute-start = (f32[16,1536]{1,0:T(8,128)S(1)}, f32[16,1536]{1,0:T(8,128)S(1)}, u32[]{:S(2)}, u32[]{:S(2)}) collective-permute-start(f32[16,1536]{1,0:T(8,128)S(1)} %get-tuple-element.13), channel_id=1, source_target_pairs={{0,1},{1,2},{2,3},{3,0},{4,5},{5,6},{6,7},{7,4},{8,9},{9,10},{10,1... | collective-permute-start | bytes 294920 | tf_op jit(solution)/shard_map/ppermute | solution.py:168
  69.9 11.0 %collective-permute-start.2 = (f32[16,1536]{1,0:T(8,128)S(1)}, f32[16,1536]{1,0:T(8,128)S(1)}, u32[]{:S(2)}, u32[]{:S(2)}) collective-permute-start(f32[16,1536]{1,0:T(8,128)S(1)} %get-tuple-element.14), channel_id=1, source_target_pairs={{0,3},{1,0},{2,1},{3,2},{4,7},{5,4},{6,5},{7,6},{8,11},{9,8},{10,9... | collective-permute-start | bytes 294920 | tf_op jit(solution)/shard_map/ppermute | solution.py:168
  73.9 9.4 %collective-permute-start.1 = (f32[16,1536]{1,0:T(8,128)S(1)}, f32[16,1536]{1,0:T(8,128)S(1)}, u32[]{:S(2)}, u32[]{:S(2)}) collective-permute-start(f32[16,1536]{1,0:T(8,128)S(1)} %get-tuple-element.15), channel_id=1, source_target_pairs={{0,2},{1,3},{2,0},{3,1},{4,6},{5,7},{6,4},{7,5},{8,10},{9,11},{10,... | collective-permute-start | bytes 294920 | tf_op jit(solution)/shard_map/ppermute | solution.py:168
  84.2 13.2 %collective-permute-start.3 = (f32[16,1536]{1,0:T(8,128)S(1)}, f32[16,1536]{1,0:T(8,128)S(1)}, u32[]{:S(2)}, u32[]{:S(2)}) collective-permute-start(f32[16,1536]{1,0:T(8,128)S(1)} %get-tuple-element.12), channel_id=1, source_target_pairs={{0,3},{1,0},{2,1},{3,2},{4,7},{5,4},{6,5},{7,6},{8,11},{9,8},{10,9... | collective-permute-start | bytes 294920 | tf_op jit(solution)/shard_map/ppermute | solution.py:168
  88.4 11.9 %collective-permute-start.5 = (f32[16,1536]{1,0:T(8,128)S(1)}, f32[16,1536]{1,0:T(8,128)S(1)}, u32[]{:S(2)}, u32[]{:S(2)}) collective-permute-start(f32[16,1536]{1,0:T(8,128)S(1)} %get-tuple-element.12), channel_id=1, source_target_pairs={{0,1},{1,2},{2,3},{3,0},{4,5},{5,6},{6,7},{7,4},{8,9},{9,10},{10,1... | collective-permute-start | bytes 294920 | tf_op jit(solution)/shard_map/ppermute | solution.py:168
  90.8 9.5 %collective-permute-start.4 = (f32[16,1536]{1,0:T(8,128)S(1)}, f32[16,1536]{1,0:T(8,128)S(1)}, u32[]{:S(2)}, u32[]{:S(2)}) collective-permute-start(f32[16,1536]{1,0:T(8,128)S(1)} %get-tuple-element.12), channel_id=1, source_target_pairs={{0,2},{1,3},{2,0},{3,1},{4,6},{5,7},{6,4},{7,5},{8,10},{9,11},{10,... | collective-permute-start | bytes 294920 | tf_op jit(solution)/shard_map/ppermute | solution.py:168
  153.2 1.9 copy-start.3
  188.1 1.3 copy-start.1
  189.4 35.1 %copy-start.2 = (bf16[512,1024]{1,0:T(8,128)(2,1)S(1)}, bf16[512,1024]{1,0:T(8,128)(2,1)}, u32[]{:S(2)}) copy-start(bf16[512,1024]{1,0:T(8,128)(2,1)} %refs.1) | copy-start | bytes 3145732
  189.4 35.1 %all-to-all-start.1 = ((f32[16,264,128]{2,1,0:T(8,128)}), f32[16,264,128]{2,1,0:T(8,128)}, u32[]{:S(2)}, u32[]{:S(2)}) async-start(f32[16,264,128]{2,1,0:T(8,128)} %copy-done.1), calls=%async_computation.2 | async-start | bytes 4325376 | tf_op jit(solution)/shard_map/all_to_all | solution.py:209
Sparse Core Ops, SparseCore 0:
  12.8 51.7 reduce-scatter.1
  101.4 51.8 all-gather.1

commit v2 on v1

v2 whole, which is shorter than its diff:
```python
import jax
import jax.numpy as jnp
from jax import lax
from jax.experimental import pallas as pl
from jax.experimental.pallas import tpu as pltpu
from jax.sharding import Mesh, PartitionSpec as P

OBLOCK = 256
PRIOR_INCREMENT = 3.0
GRP = ("x", "zl", "core")
MEM = ("yh", "yl", "zh")
RING = ("yh", "yl")
ALIKE = ("yh", "zh")
PEERS = ("x", "zl")
LANES = 128
BIG = pltpu.CompilerParams(vmem_limit_bytes=40 << 20)
LAST = (((1,), (1,)), ((), ()))


def project_kernel(inject, images, half, phantom, out_a, out_b):
    step = pl.program_id(0)
    width = images.shape[0]
    per_batch = 2
    injected = inject.shape[1]
    batch, part = step // per_batch, step % per_batch
    position = part * width + lax.broadcasted_iota(jnp.int32, (1, width), 1)
    hit = jnp.zeros((1, width), jnp.float32)
    for i in range(injected):
        hit = jnp.where(position == inject[batch, i], 1.0, hit)
    mine = half[...]
    plain = lax.dot_general(mine, images[...], LAST, preferred_element_type=jnp.float32)
    spread = jnp.broadcast_to(phantom[...], (LANES, phantom.shape[1]))
    extra = lax.dot_general(mine, spread, LAST, preferred_element_type=jnp.float32)
    middle = out_a.shape[0]
    for k in range(width // LANES):
        cut = slice(k * LANES, (k + 1) * LANES)
        value = plain[:, cut] + extra * hit[:, cut]
        out_a[:, cut] = value[:middle]
        out_b[:, cut] = value[middle:]


def projected(inject, images, half, phantom):
    rows, pixels = images.shape
    batches = inject.shape[0]
    width = rows // (2 * batches)
    count = half.shape[0]
    out = jax.ShapeDtypeStruct((count // 2, rows), jnp.float32)
    return pl.pallas_call(
        project_kernel,
        grid_spec=pltpu.PrefetchScalarGridSpec(
            num_scalar_prefetch=1,
            grid=(2 * batches,),
            in_specs=[
                pl.BlockSpec((width, pixels), lambda j, s: (j, 0)),
                pl.BlockSpec((count, pixels), lambda j, s: (0, 0)),
                pl.BlockSpec((1, pixels), lambda j, s: (0, 0)),
            ],
            out_specs=[pl.BlockSpec((count // 2, width), lambda j, s: (0, j))] * 2,
        ),
        out_shape=[out, out],
        compiler_params=BIG,
        name="project",
    )(inject, images, half, phantom)


def join_kernel(keep_a, keep_b, came_a, came_b, out):
    for q in range(out.shape[0]):
        cut = slice(q * 8, (q + 1) * 8)
        out[q, :8, :] = keep_a[cut, :] + came_a[cut, :]
        out[q, 8:, :] = keep_b[cut, :] + came_b[cut, :]


def joined(keep, came):
    high, rows = keep[0].shape
    steps = 4
    members = high // 8
    return pl.pallas_call(
        join_kernel,
        grid=(steps,),
        in_specs=[pl.BlockSpec((high // steps, rows), lambda j: (j, 0))] * 4,
        out_specs=pl.BlockSpec((members // steps, 16, rows), lambda j: (j, 0, 0)),
        out_shape=jax.ShapeDtypeStruct((members, 16, rows), jnp.float32),
        compiler_params=BIG,
        name="join",
    )(*keep, *came)


def spread_kernel(parts, out):
    total = parts[0]
    for k in range(1, parts.shape[0]):
        total = total + parts[k]
    for k in range(out.shape[0]):
        out[k] = total


def summed_copies(parts):
    members, high, rows = parts.shape
    steps = 4
    block = pl.BlockSpec((members, high, rows // steps), lambda j: (0, 0, j))
    return pl.pallas_call(
        spread_kernel,
        grid=(steps,),
        in_specs=[block],
        out_specs=block,
        out_shape=jax.ShapeDtypeStruct(parts.shape, jnp.float32),
        compiler_params=BIG,
        name="spread",
    )(parts)


def score_kernel(at, own_a, own_b, came_a, came_b, prior, refs_t, powers, rounded, stats):
    step = pl.program_id(0)
    rows = prior.shape[1]
    orient, eigen = refs_t.shape
    lines = stats.shape[1] // 2
    high = eigen // 4
    for base, held in ((0, (own_a, came_a)), (2 * high, (own_b, came_b))):
        for side, source in enumerate(held):
            place = base + high * (at[1] if side == 0 else 1 - at[1])
            rounded[pl.ds(pl.multiple_of(place, high), high), :] = (
                source[...].reshape(high, rows).astype(jnp.bfloat16)
            )
    scores = jnp.dot(refs_t[...], rounded[...], preferred_element_type=jnp.float32)
    block = prior[...] - at[0] * (orient // OBLOCK)
    parts = [
        scores[k * OBLOCK : (k + 1) * OBLOCK] + jnp.where(block == k, PRIOR_INCREMENT, 0.0)
        for k in range(orient // OBLOCK)
    ]
    tops = [jnp.max(part, axis=0, keepdims=True) for part in parts]
    top = tops[0]
    for other in tops[1:]:
        top = jnp.maximum(top, other)
    total = jnp.zeros_like(top)
    for k, part in enumerate(parts):
        power = jnp.exp(part - top)
        powers[k * OBLOCK : (k + 1) * OBLOCK, :] = power
        total = total + jnp.sum(power, axis=0, keepdims=True)
    for h in range(rows // LANES):
        line = step * (rows // LANES) + h
        cut = slice(h * LANES, (h + 1) * LANES)
        shape = (stats.shape[0], 1, LANES)
        stats[:, pl.ds(line, 1), :] = jnp.broadcast_to(top[None, :, cut], shape)
        stats[:, pl.ds(lines + line, 1), :] = jnp.broadcast_to(total[None, :, cut], shape)


def scores_of(at, own, came, prior, refs_t, members):
    rows = prior.shape[1]
    orient, eigen = refs_t.shape
    width = 256
    lines = 2 * rows // LANES
    group = own.shape[0]
    return pl.pallas_call(
        score_kernel,
        grid_spec=pltpu.PrefetchScalarGridSpec(
            num_scalar_prefetch=1,
            grid=(rows // width,),
            in_specs=[
                pl.BlockSpec((group, 8, width), lambda j, at: (0, 0, j)),
                pl.BlockSpec((group, 8, width), lambda j, at: (0, 1, j)),
                pl.BlockSpec((group, 8, width), lambda j, at: (0, 0, j)),
                pl.BlockSpec((group, 8, width), lambda j, at: (0, 0, j)),
                pl.BlockSpec((1, width), lambda j, at: (0, j)),
                pl.BlockSpec((orient, eigen), lambda j, at: (0, 0)),
            ],
            out_specs=[
                pl.BlockSpec((orient, width), lambda j, at: (0, j)),
                pl.BlockSpec((eigen, width), lambda j, at: (0, j)),
                pl.BlockSpec((members, lines, LANES), lambda j, at: (0, 0, 0)),
            ],
        ),
        out_shape=[
            jax.ShapeDtypeStruct((orient, rows), jnp.float32),
            jax.ShapeDtypeStruct((eigen, rows), jnp.bfloat16),
            jax.ShapeDtypeStruct((members, lines, LANES), jnp.float32),
        ],
        compiler_params=BIG,
        name="scores",
    )(at, own, own, *came, prior, refs_t)


def total_kernel(at, stats, own, powers, rounded, keep, send, factor):
    step = pl.program_id(0)
    eigen, rows = rounded.shape
    width = powers.shape[0]
    peers = keep.shape[0]
    share = eigen // (2 * peers)
    lines = rows // LANES
    body = keep.shape[1] - keep.shape[1] % share

    @pl.when(step == 0)
    def _():
        tops = stats[:, :lines, :]
        top = jnp.max(tops, axis=0)
        total = jnp.sum(stats[:, lines:, :] * jnp.exp(tops - top[None]), axis=0)
        scale = jnp.exp(own[0, :lines, :] - top) / total
        for k in range(lines):
            factor[:, k * LANES : (k + 1) * LANES] = scale[k : k + 1, :]

    weights = (powers[...] * factor[...]).astype(jnp.bfloat16)
    totals = lax.dot_general(rounded[...], weights, LAST, preferred_element_type=jnp.float32)
    ones = jnp.ones((16, rows), jnp.bfloat16)
    masses = lax.dot_general(ones, weights, LAST, preferred_element_type=jnp.float32)
    first = at[2] == 0
    for h in range(width // LANES):
        column = step * (width // LANES) + h
        cut = slice(h * LANES, (h + 1) * LANES)
        place = pl.ds(pl.multiple_of(column * share, share), share)
        for q in range(peers):
            even = totals[2 * q * share : (2 * q + 1) * share, cut]
            odd = totals[(2 * q + 1) * share : (2 * q + 2) * share, cut]
            keep[q, place, :] = jnp.where(first, even, odd)
            send[q, place, :] = jnp.where(first, odd, even)
        mass = jnp.broadcast_to(masses[None, 0:1, cut], (peers, 1, LANES))
        keep[:, pl.ds(body + column, 1), :] = mass
        send[:, pl.ds(body + column, 1), :] = mass


def totals_of(at, stats, sent, powers, rounded, peers):
    eigen, rows = rounded.shape
    orient = powers.shape[0]
    width = 256
    deep = (eigen // (2 * peers) + 1) * (orient // LANES)
    out = jax.ShapeDtypeStruct((peers, deep, LANES), jnp.float32)
    return pl.pallas_call(
        total_kernel,
        grid_spec=pltpu.PrefetchScalarGridSpec(
            num_scalar_prefetch=1,
            grid=(orient // width,),
            in_specs=[
                pl.BlockSpec(stats.shape, lambda j, at: (0, 0, 0)),
                pl.BlockSpec((1, *sent.shape[1:]), lambda j, at: (0, 0, 0)),
                pl.BlockSpec((width, rows), lambda j, at: (j, 0)),
                pl.BlockSpec((eigen, rows), lambda j, at: (0, 0)),
            ],
            out_specs=[pl.BlockSpec((peers, deep, LANES), lambda j, at: (0, 0, 0))] * 2,
            scratch_shapes=[pltpu.VMEM((1, rows), jnp.float32)],
        ),
        out_shape=[out, out],
        compiler_params=BIG,
        name="totals",
    )(at, stats, sent, powers, rounded)


def final_kernel(at, parts, refs, out):
    share, orient = out.shape
    both = parts[0]
    for d in range(1, parts.shape[0]):
        both = both + parts[d]
    body = share * (orient // LANES)
    for k in range(orient // LANES):
        cut = slice(k * LANES, (k + 1) * LANES)
        above = both[k * share : (k + 1) * share] + refs[:, cut].astype(jnp.float32)
        out[:, cut] = above / (both[body + k : body + k + 1] + 1.0)


def final_of(at, parts, refs):
    eigen, orient = refs.shape
    share = eigen // (2 * parts.shape[0])
    return pl.pallas_call(
        final_kernel,
        grid_spec=pltpu.PrefetchScalarGridSpec(
            num_scalar_prefetch=1,
            grid=(1,),
            in_specs=[
                pl.BlockSpec(parts.shape, lambda j, at: (0, 0, 0)),
                pl.BlockSpec((share, orient), lambda j, at: (at[3], 0)),
            ],
            out_specs=pl.BlockSpec((share, orient), lambda j, at: (0, 0)),
        ),
        out_shape=jax.ShapeDtypeStruct((share, orient), jnp.float32),
        compiler_params=BIG,
        name="final",
    )(at, parts, refs)


def swapped(pair):
    size = lax.axis_size(RING)
    with_a = [(i, i ^ 1) for i in range(size)]
    with_b = [(i, (i + (1 if i % 2 else -1)) % size) for i in range(size)]
    return tuple(lax.ppermute(x, RING, p) for x, p in zip(pair, (with_a, with_b)))


def shards(images, phantom, inject_rows, prior_blocks, basis, refs):
    rows = images.shape[1] * images.shape[2]
    pixels, eigen = basis.shape
    flat = images[0].reshape(rows, pixels)
    parity = lax.axis_index("yl").astype(jnp.int32)
    at = jnp.stack(
        [
            lax.axis_index(MEM).astype(jnp.int32),
            parity,
            lax.axis_index("core").astype(jnp.int32),
            lax.axis_index(GRP).astype(jnp.int32),
        ]
    )
    halves = basis.T.reshape(2, 2, eigen // 4, pixels)

    def half(side):
        chosen = lax.dynamic_index_in_dim(halves, side, 1, keepdims=False)
        return projected(inject_rows[0], flat, chosen.reshape(eigen // 2, pixels), phantom)

    came = swapped(half(1 - parity))
    parts = joined(half(parity), came)
    parts = lax.all_to_all(parts, ALIKE, 0, 0, tiled=True)
    own = lax.all_to_all(summed_copies(parts), ALIKE, 0, 0, tiled=True)
    came = swapped((own[:, :8], own[:, 8:]))
    powers, rounded, sent = scores_of(
        at, own, came, prior_blocks[0].reshape(1, rows), refs.T, lax.axis_size(MEM)
    )
    stats = lax.all_to_all(sent, MEM, 0, 0, tiled=True)
    keep, send = totals_of(at, stats, sent, powers, rounded, lax.axis_size(PEERS))
    parts = keep + lax.ppermute(send, "core", [(0, 1), (1, 0)])
    parts = lax.all_to_all(parts, PEERS, 0, 0, tiled=True)
    return final_of(at, parts, refs)


def solution(mesh):
    fine = Mesh(mesh.devices.reshape(4, 2, 2, 4, 2, 4), GRP + MEM)
    placed = (
        P(GRP, None, None, MEM),
        P(GRP, MEM),
        P(GRP, None, None),
        P(GRP, None, None),
        P(MEM, None),
        P(None, MEM),
    )
    return jax.shard_map(
        shards, mesh=fine, in_specs=placed, out_specs=P(GRP, MEM), check_vma=False
    )
```

time: 235 us -> 228 us (0.970)
  blocking collectives: 25 us -> 148 us
  waiting for transfers between devices: 135 us -> 30.2 us
  between operations: 13.7 us -> 0.22 us
  starting transfers between devices: 35.7 us -> 23 us
  Pallas kernels: 10.4 us -> 17.9 us
  matrix products: 5.12 us -> 0 us
    all_to_all x0 -> x3, blocking collectives: none -> 130 us  [the longest x1 57.2 us: shards(): parts = lax.all_to_all(parts, ALIKE, 0, 0, tiled=True)]
    reduce_scatter x1 -> x0, waiting for transfers between devices: 51.8 us -> none  [shards(): owned = lax.psum_scatter(partial, 'y', scatter_dimension=0, tiled=True)]
    all_gather x1 -> x0, waiting for transfers between devices: 50.4 us -> none  [shards(): coefs = lax.all_gather(owned, 'y', axis=0, tiled=True)]
    all_to_all x1 -> x0, waiting for transfers between devices: 27.9 us -> none  [shards(): parts = lax.all_to_all(parts, GRP, 0, 0, tiled=True)]
    ppermute x6 -> x5, waiting for transfers between devices: 5.25 us -> 30.2 us  [the longest x4 27.9 us: swapped(): lax.ppermute(x, RING, p)]
    all_to_all x1 -> x0, starting transfers between devices: 7.18 us -> none  [shards(): parts = lax.all_to_all(parts, GRP, 0, 0, tiled=True)]
    all_to_all x1, blocking collectives: 25 us -> 18.2 us  [shards(): stats = lax.all_to_all(sent, MEM, 0, 0, tiled=True)]
    pallas_call x1 -> x5, Pallas kernels: 3.41 us -> 10.2 us  [the longest x2 5.47 us: projected(): pl.pallas_call(project_kernel, grid_spec=pltpu.PrefetchScalarGridSpec(num...]
  transfers between devices with their start and end apart: 9 -> 5, of which waited for: 5 -> 5; matrix products, arithmetic and copies ran while one was open for 1% -> 1% of each run, Pallas kernels for 0% -> 1%
where the time goes in v2:
time: 228 us; the launch traced here: 227 us
  blocking collectives  148 us (65%)
  waiting for transfers between devices  30.2 us (13%)
  starting transfers between devices  23 us (10%)
  Pallas kernels  17.9 us (8%)
  local copies, waits for them, and re-layouts  7.79 us (3%)
    all_to_all x1, blocking collectives, shards(): parts = lax.all_to_all(parts, ALIKE, 0, 0, tiled=True)  57.2 us
    all_to_all x1, blocking collectives, shards(): own = lax.all_to_all(summed_copies(parts), ALIKE, 0, 0, tiled=True)  50.6 us
    ppermute x4, waiting for transfers between devices, swapped(): lax.ppermute(x, RING, p)  27.9 us
    all_to_all x1, blocking collectives, shards(): parts = lax.all_to_all(parts, PEERS, 0, 0, tiled=True)  22 us
    all_to_all x1, blocking collectives, shards(): stats = lax.all_to_all(sent, MEM, 0, 0, tiled=True)  18.2 us
    ppermute x4, starting transfers between devices, swapped(): lax.ppermute(x, RING, p)  17.3 us
    pallas_call x1, Pallas kernels, scores_of(): pl.pallas_call(score_kernel, grid_spec=pltpu.PrefetchScalarGridSpec(num_s...  6.42 us
    ppermute x1, starting transfers between devices, shards(): parts = keep + lax.ppermute(send, 'core', [(0, 1), (1, 0)])  5.68 us
  transfers between devices with their start and end apart: 5, of which 5 were waited for; matrix products, arithmetic and copies ran while one was open for 1% of the time, Pallas kernels for 1%

profile of v2, /device:TPU:1, one launch (start us, length us, event | category | flops | bytes accessed | tf_op | source)
XLA Modules:
  0.0 227.2 jit_solution(12872821342615165067)
XLA Ops:
  0.0 1.2 reshape.11
  1.2 0.0 copy-start
  1.2 0.0 copy-start.2
  1.2 0.0 copy-start.3
  1.2 1.9 constant_dynamic-slice_fusion
  3.1 0.7 copy.11
  3.8 0.0 copy-done
  3.8 0.0 copy-done.2
  3.8 0.0 copy-done.3
  3.8 3.2 %project.3 = (f32[128,1536]{1,0:T(8,128)}, f32[128,1536]{1,0:T(8,128)}) custom-call(s32[2,64]{1,0:T(2,128)S(1)} %bitcast.20, bf16[1536,512]{1,0:T(8,128)(2,1)S(1)} %bitcast.14, bf16[256,512]{1,0:T(8,128)(2,1)S(1)} %bitcast.17, bf16[1,512]{1,0:T(2,128)(2,1)S(1)} %copy-done.2), custom_call_target="tpu_custom_call" | custom-call | tf_op jit(solution)/shard_map/project/pallas_call | solution.py:48
  7.1 4.0 %collective-permute-start = (f32[128,1536]{1,0:T(8,128)}, f32[128,1536]{1,0:T(8,128)S(1)}, u32[]{:S(2)}, u32[]{:S(2)}) collective-permute-start(f32[128,1536]{1,0:T(8,128)} %get-tuple-element.16), channel_id=1, source_target_pairs={{0,4},{4,0},{8,12},{12,8},{16,20},{20,16},{24,28},{28,24},{1,5},{5... | collective-permute-start | bytes 2359304 | tf_op jit(solution)/shard_map/ppermute | solution.py:280
  11.1 4.9 %collective-permute-start.1 = (f32[128,1536]{1,0:T(8,128)}, f32[128,1536]{1,0:T(8,128)S(1)}, u32[]{:S(2)}, u32[]{:S(2)}) collective-permute-start(f32[128,1536]{1,0:T(8,128)} %get-tuple-element.17), channel_id=1, source_target_pairs={{0,28},{4,8},{8,4},{12,16},{16,12},{20,24},{24,20},{28,0},{1,29},{... | collective-permute-start | bytes 2359304 | tf_op jit(solution)/shard_map/ppermute | solution.py:280
  16.0 1.2 copy.10
  17.2 2.2 project.2
  19.5 4.3 %collective-permute-done.came_a = f32[128,1536]{1,0:T(8,128)S(1)} collective-permute-done((f32[128,1536]{1,0:T(8,128)}, f32[128,1536]{1,0:T(8,128)S(1)}, u32[]{:S(2)}, u32[]{:S(2)}) %collective-permute-start) | collective-permute-done | bytes 786464 | tf_op jit(solution)/shard_map/ppermute | solution.py:280
  23.7 7.8 %collective-permute-done.1.came_b = f32[128,1536]{1,0:T(8,128)S(1)} collective-permute-done((f32[128,1536]{1,0:T(8,128)}, f32[128,1536]{1,0:T(8,128)S(1)}, u32[]{:S(2)}, u32[]{:S(2)}) %collective-permute-start.1) | collective-permute-done | bytes 786464 | tf_op jit(solution)/shard_map/ppermute | solution.py:280
  31.6 0.2 join.1
  31.8 57.2 %all_to_all.20.parts = f32[16,16,1536]{2,1,0:T(8,128)S(1)} all-to-all(f32[16,16,1536]{2,1,0:T(8,128)S(1)} %join.1), channel_id=1, replica_groups=mesh['x'=4,'zl'=2,'core'=2,'yh'=4,'yl'=2,'zh'=4] {'yh','zh'}, dimensions={0} | all-to-all | bytes 3145728 | tf_op jit(solution)/shard_map/all_to_all | solution.py:304
  89.0 0.5 spread.1
  89.4 50.6 %all_to_all.21.own_a.own_b = f32[16,16,1536]{2,1,0:T(8,128)S(1)} all-to-all(f32[16,16,1536]{2,1,0:T(8,128)S(1)} %spread.1), channel_id=1, replica_groups=mesh['x'=4,'zl'=2,'core'=2,'yh'=4,'yl'=2,'zh'=4] {'yh','zh'}, dimensions={0} | all-to-all | bytes 3145728 | tf_op jit(solution)/shard_map/all_to_all | solution.py:305
  140.0 0.0 copy-start.4
  140.0 1.3 fusion
  141.3 1.9 collective-permute-start.3
  143.2 6.5 %collective-permute-start.2 = (f32[16,8,1536]{2,1,0:T(8,128)}, f32[16,8,1536]{2,1,0:T(8,128)}, u32[]{:S(2)}, u32[]{:S(2)}) collective-permute-start(f32[16,8,1536]{2,1,0:T(8,128)} %get-tuple-element.24), channel_id=1, source_target_pairs={{0,4},{4,0},{8,12},{12,8},{16,20},{20,16},{24,28},{28,24},{1,5},{5... | collective-permute-start | bytes 2359304 | tf_op jit(solution)/shard_map/ppermute | solution.py:280
  149.7 0.0 copy-done.4
  149.8 1.5 copy.9
  151.3 0.1 pad_add_fusion.at
  151.4 11.0 %collective-permute-done.3.came_b = f32[16,8,1536]{2,1,0:T(8,128)S(1)} collective-permute-done((f32[16,8,1536]{2,1,0:T(8,128)}, f32[16,8,1536]{2,1,0:T(8,128)S(1)}, u32[]{:S(2)}, u32[]{:S(2)}) %collective-permute-start.3) | collective-permute-done | bytes 786464 | tf_op jit(solution)/shard_map/ppermute | solution.py:280
  162.4 4.8 %collective-permute-done.2.came_a = f32[16,8,1536]{2,1,0:T(8,128)} collective-permute-done((f32[16,8,1536]{2,1,0:T(8,128)}, f32[16,8,1536]{2,1,0:T(8,128)}, u32[]{:S(2)}, u32[]{:S(2)}) %collective-permute-start.2) | collective-permute-done | bytes 786464 | tf_op jit(solution)/shard_map/ppermute | solution.py:280
  167.2 6.4 %scores.1 = (f32[1024,1536]{1,0:T(8,128)S(1)}, bf16[512,1536]{1,0:T(8,128)(2,1)S(1)}, f32[32,24,128]{2,1,0:T(8,128)S(1)}) custom-call(s32[4]{0:T(128)S(1)} %pad_add_fusion.at, f32[16,16,1536]{2,1,0:T(8,128)S(1)} %all_to_all.21.own_a.own_b, f32[16,16,1536]{2,1,0:T(8,128)S(1)} %all_to_all.21.own_a.own_b, f32[16,8,1536]{2,1,0:T(8,128)} %collective-permute-done.2.came_a, ...), custom_call_target="tpu_custom_call" | custom-call | tf_op jit(solution)/shard_map/scores/pallas_call | solution.py:152
  173.6 18.2 %all_to_all.22.stats = f32[32,24,128]{2,1,0:T(8,128)S(1)} all-to-all(f32[32,24,128]{2,1,0:T(8,128)S(1)} %get-tuple-element.18.own), channel_id=1, replica_groups=mesh['x'=4,'zl'=2,'core'=2,'yh'=4,'yl'=2,'zh'=4] {'yh','yl','zh'}, dimensions={0} | all-to-all | bytes 786432 | tf_op jit(solution)/shard_map/all_to_all | solution.py:310
  191.8 4.0 %totals.1 = (f32[8,264,128]{2,1,0:T(8,128)S(1)}, f32[8,264,128]{2,1,0:T(8,128)S(1)}) custom-call(s32[4]{0:T(128)S(1)} %pad_add_fusion.at, f32[32,24,128]{2,1,0:T(8,128)S(1)} %all_to_all.22.stats, f32[32,24,128]{2,1,0:T(8,128)S(1)} %get-tuple-element.18.own, f32[1024,1536]{1,0:T(8,128)S(1)} %get-tuple-element.19.powers, ...), custom_call_target="tpu_custom_call" | custom-call | tf_op jit(solution)/shard_map/totals/pallas_call | solution.py:224
  195.8 5.7 %collective-permute-start.4 = (f32[8,264,128]{2,1,0:T(8,128)S(1)}, f32[8,264,128]{2,1,0:T(8,128)S(1)}, u32[]{:S(2)}, u32[]{:S(2)}) collective-permute-start(f32[8,264,128]{2,1,0:T(8,128)S(1)} %get-tuple-element.22), channel_id=1, source_target_pairs={{0,32},{32,0},{1,33},{33,1},{2,34},{34,2},{3,35},{35,3},{4,36},{36... | collective-permute-start | bytes 3244040 | tf_op jit(solution)/shard_map/ppermute | solution.py:312
  201.5 2.3 %collective-permute-done.4 = f32[8,264,128]{2,1,0:T(8,128)S(1)} collective-permute-done((f32[8,264,128]{2,1,0:T(8,128)S(1)}, f32[8,264,128]{2,1,0:T(8,128)S(1)}, u32[]{:S(2)}, u32[]{:S(2)}) %collective-permute-start.4) | collective-permute-done | bytes 1081376 | tf_op jit(solution)/shard_map/ppermute | solution.py:312
  203.8 0.1 add.29
  203.9 0.0 copy-start.1
  203.9 22.0 %all_to_all.23.parts = f32[8,264,128]{2,1,0:T(8,128)S(1)} all-to-all(f32[8,264,128]{2,1,0:T(8,128)S(1)} %add.29), channel_id=1, replica_groups=mesh['x'=4,'zl'=2,'core'=2,'yh'=4,'yl'=2,'zh'=4] {'x','zl'}, dimensions={0} | all-to-all | bytes 2162688 | tf_op jit(solution)/shard_map/all_to_all | solution.py:313
  225.9 0.0 copy-done.1
  225.9 1.3 final.1
  (1 shorter events, 0.0 us)
Async XLA Ops:
  1.2 2.6 %copy-start = (bf16[1,2,768,512]{3,2,1,0:T(8,128)(2,1)S(1)}, bf16[1,2,768,512]{3,2,1,0:T(8,128)(2,1)}, u32[]{:S(2)}) copy-start(bf16[1,2,768,512]{3,2,1,0:T(8,128)(2,1)} %param.6) | copy-start | bytes 4718596
  1.2 2.6 %copy-start.2 = (bf16[1,512]{1,0:T(2,128)(2,1)S(1)}, bf16[1,512]{1,0:T(2,128)(2,1)}, u32[]{:S(2)}) copy-start(bf16[1,512]{1,0:T(2,128)(2,1)} %phantom.3) | copy-start | bytes 3076
  1.2 2.6 %copy-start.3 = (s32[1,2,64]{2,1,0:T(2,128)S(1)}, s32[1,2,64]{2,1,0:T(2,128)}, u32[]{:S(2)}) copy-start(s32[1,2,64]{2,1,0:T(2,128)} %param.8) | copy-start | bytes 1540
  7.1 16.6 %collective-permute-start = (f32[128,1536]{1,0:T(8,128)}, f32[128,1536]{1,0:T(8,128)S(1)}, u32[]{:S(2)}, u32[]{:S(2)}) collective-permute-start(f32[128,1536]{1,0:T(8,128)} %get-tuple-element.16), channel_id=1, source_target_pairs={{0,4},{4,0},{8,12},{12,8},{16,20},{20,16},{24,28},{28,24},{1,5},{5... | collective-permute-start | bytes 2359304 | tf_op jit(solution)/shard_map/ppermute | solution.py:280
  11.1 20.5 %collective-permute-start.1 = (f32[128,1536]{1,0:T(8,128)}, f32[128,1536]{1,0:T(8,128)S(1)}, u32[]{:S(2)}, u32[]{:S(2)}) collective-permute-start(f32[128,1536]{1,0:T(8,128)} %get-tuple-element.17), channel_id=1, source_target_pairs={{0,28},{4,8},{8,4},{12,16},{16,12},{20,24},{24,20},{28,0},{1,29},{... | collective-permute-start | bytes 2359304 | tf_op jit(solution)/shard_map/ppermute | solution.py:280
  140.0 9.7 %copy-start.4 = (s32[1,2,768]{2,1,0:T(2,128)S(1)}, s32[1,2,768]{2,1,0:T(2,128)}, u32[]{:S(2)}) copy-start(s32[1,2,768]{2,1,0:T(2,128)} %param.9) | copy-start | bytes 18436
  141.3 21.0 %collective-permute-start.3 = (f32[16,8,1536]{2,1,0:T(8,128)}, f32[16,8,1536]{2,1,0:T(8,128)S(1)}, u32[]{:S(2)}, u32[]{:S(2)}) collective-permute-start(f32[16,8,1536]{2,1,0:T(8,128)} %get-tuple-element.23), channel_id=1, source_target_pairs={{0,28},{4,8},{8,4},{12,16},{16,12},{20,24},{24,20},{28,0},{1,29},{... | collective-permute-start | bytes 2359304 | tf_op jit(solution)/shard_map/ppermute | solution.py:280
  143.2 24.0 %collective-permute-start.2 = (f32[16,8,1536]{2,1,0:T(8,128)}, f32[16,8,1536]{2,1,0:T(8,128)}, u32[]{:S(2)}, u32[]{:S(2)}) collective-permute-start(f32[16,8,1536]{2,1,0:T(8,128)} %get-tuple-element.24), channel_id=1, source_target_pairs={{0,4},{4,0},{8,12},{12,8},{16,20},{20,16},{24,28},{28,24},{1,5},{5... | collective-permute-start | bytes 2359304 | tf_op jit(solution)/shard_map/ppermute | solution.py:280
  195.8 8.0 %collective-permute-start.4 = (f32[8,264,128]{2,1,0:T(8,128)S(1)}, f32[8,264,128]{2,1,0:T(8,128)S(1)}, u32[]{:S(2)}, u32[]{:S(2)}) collective-permute-start(f32[8,264,128]{2,1,0:T(8,128)S(1)} %get-tuple-element.22), channel_id=1, source_target_pairs={{0,32},{32,0},{1,33},{33,1},{2,34},{34,2},{3,35},{35,3},{4,36},{36... | collective-permute-start | bytes 3244040 | tf_op jit(solution)/shard_map/ppermute | solution.py:312
  203.9 22.0 %copy-start.1 = (bf16[512,1024]{1,0:T(8,128)(2,1)S(1)}, bf16[512,1024]{1,0:T(8,128)(2,1)}, u32[]{:S(2)}) copy-start(bf16[512,1024]{1,0:T(8,128)(2,1)} %refs.1) | copy-start | bytes 3145732

commit v3 on v2

--- a/solution.py
+++ b/solution.py
@@ -8,26 +8,26 @@
 OBLOCK = 256
 PRIOR_INCREMENT = 3.0
 GRP = ("x", "zl", "core")
-MEM = ("yh", "yl", "zh")
 RING = ("yh", "yl")
-ALIKE = ("yh", "zh")
+TALL = ("zhh", "zhl")
+MEM = RING + TALL
+ALIKE = ("yh", "zhh")
 PEERS = ("x", "zl")
 LANES = 128
 BIG = pltpu.CompilerParams(vmem_limit_bytes=40 << 20)
 LAST = (((1,), (1,)), ((), ()))
 
 
-def project_kernel(inject, images, half, phantom, out_a, out_b):
+def project_kernel(at, inject, images, basis, phantom, out_a, out_b):
     step = pl.program_id(0)
     width = images.shape[0]
-    per_batch = 2
-    injected = inject.shape[1]
+    per_batch = pl.num_programs(0) // inject.shape[0]
     batch, part = step // per_batch, step % per_batch
     position = part * width + lax.broadcasted_iota(jnp.int32, (1, width), 1)
     hit = jnp.zeros((1, width), jnp.float32)
-    for i in range(injected):
+    for i in range(inject.shape[1]):
         hit = jnp.where(position == inject[batch, i], 1.0, hit)
-    mine = half[...]
+    mine = basis[...].T
     plain = lax.dot_general(mine, images[...], LAST, preferred_element_type=jnp.float32)
     spread = jnp.broadcast_to(phantom[...], (LANES, phantom.shape[1]))
     extra = lax.dot_general(mine, spread, LAST, preferred_element_type=jnp.float32)
@@ -39,50 +39,79 @@
         out_b[:, cut] = value[middle:]
 
 
-def projected(inject, images, half, phantom):
+def projected(at, which, inject, images, basis, phantom):
     rows, pixels = images.shape
     batches = inject.shape[0]
     width = rows // (2 * batches)
-    count = half.shape[0]
+    count = basis.shape[1] // 4
     out = jax.ShapeDtypeStruct((count // 2, rows), jnp.float32)
     return pl.pallas_call(
         project_kernel,
         grid_spec=pltpu.PrefetchScalarGridSpec(
-            num_scalar_prefetch=1,
+            num_scalar_prefetch=2,
             grid=(2 * batches,),
             in_specs=[
-                pl.BlockSpec((width, pixels), lambda j, s: (j, 0)),
-                pl.BlockSpec((count, pixels), lambda j, s: (0, 0)),
-                pl.BlockSpec((1, pixels), lambda j, s: (0, 0)),
-            ],
-            out_specs=[pl.BlockSpec((count // 2, width), lambda j, s: (0, j))] * 2,
+                pl.BlockSpec((width, pixels), lambda j, at, s: (j, 0)),
+                pl.BlockSpec((pixels, count), lambda j, at, s: (0, at[which])),
+                pl.BlockSpec((1, pixels), lambda j, at, s: (0, 0)),
+            ],
+            out_specs=[pl.BlockSpec((count // 2, width), lambda j, at, s: (0, j))] * 2,
         ),
         out_shape=[out, out],
         compiler_params=BIG,
         name="project",
-    )(inject, images, half, phantom)
-
-
-def join_kernel(keep_a, keep_b, came_a, came_b, out):
-    for q in range(out.shape[0]):
-        cut = slice(q * 8, (q + 1) * 8)
-        out[q, :8, :] = keep_a[cut, :] + came_a[cut, :]
-        out[q, 8:, :] = keep_b[cut, :] + came_b[cut, :]
-
-
-def joined(keep, came):
-    high, rows = keep[0].shape
-    steps = 4
-    members = high // 8
+    )(at, inject, images, basis, phantom)
+
+
+def relay_kernel(here_a, here_b, came_a, came_b, low, high):
+    members = low.shape[0]
+    for side, out in enumerate((low, high)):
+        for q in range(members):
+            cut = slice((side * members + q) * 8, (side * members + q + 1) * 8)
+            out[q, :8, :] = here_a[cut, :] + came_a[cut, :]
+            out[q, 8:, :] = here_b[cut, :] + came_b[cut, :]
+
+
+def relayed(here, came):
+    count, rows = here[0].shape
+    width = rows // 3
+    members = count // 8
+    out = jax.ShapeDtypeStruct((members // 2, 16, rows), jnp.float32)
+    return pl.pallas_call(
+        relay_kernel,
+        grid=(rows // width,),
+        in_specs=[pl.BlockSpec((count, width), lambda j: (0, j))] * 4,
+        out_specs=[pl.BlockSpec((members // 2, 16, width), lambda j: (0, 0, j))] * 2,
+        out_shape=[out, out],
+        compiler_params=BIG,
+        name="relay",
+    )(*here, *came)
+
+
+def join_kernel(here_a, here_b, came_a, came_b, low, high, out):
+    members = low.shape[0]
+    for side, other in enumerate((low, high)):
+        for q in range(members):
+            m = side * members + q
+            cut = slice(m * 8, (m + 1) * 8)
+            out[m, :8, :] = here_a[cut, :] + came_a[cut, :] + other[q, :8, :]
+            out[m, 8:, :] = here_b[cut, :] + came_b[cut, :] + other[q, 8:, :]
+
+
+def joined(here, came, others):
+    count, rows = here[0].shape
+    width = rows // 3
+    members = count // 8
     return pl.pallas_call(
         join_kernel,
-        grid=(steps,),
-        in_specs=[pl.BlockSpec((high // steps, rows), lambda j: (j, 0))] * 4,
-        out_specs=pl.BlockSpec((members // steps, 16, rows), lambda j: (j, 0, 0)),
+        grid=(rows // width,),
+        in_specs=[pl.BlockSpec((count, width), lambda j: (0, j))] * 4
+        + [pl.BlockSpec((members // 2, 16, width), lambda j: (0, 0, j))] * 2,
+        out_specs=pl.BlockSpec((members, 16, width), lambda j: (0, 0, j)),
         out_shape=jax.ShapeDtypeStruct((members, 16, rows), jnp.float32),
         compiler_params=BIG,
         name="join",
-    )(*keep, *came)
+    )(*here, *came, *others)
 
 
 def spread_kernel(parts, out):
@@ -95,7 +124,7 @@
 
 def summed_copies(parts):
     members, high, rows = parts.shape
-    steps = 4
+    steps = 3
     block = pl.BlockSpec((members, high, rows // steps), lambda j: (0, 0, j))
     return pl.pallas_call(
         spread_kernel,
@@ -108,20 +137,54 @@
     )(parts)
 
 
-def score_kernel(at, own_a, own_b, came_a, came_b, prior, refs_t, powers, rounded, stats):
+def peel_kernel(low, high, out_a, out_b):
+    middle = low.shape[0]
+    for offset, source in ((0, low), (middle, high)):
+        out_a[offset : offset + middle] = source[:, :8, :]
+        out_b[offset : offset + middle] = source[:, 8:, :]
+
+
+def peeled(low, high):
+    members, _, rows = low.shape
+    width = rows // 3
+    out = jax.ShapeDtypeStruct((2 * members, 8, rows), jnp.float32)
+    return pl.pallas_call(
+        peel_kernel,
+        grid=(rows // width,),
+        in_specs=[pl.BlockSpec((members, 16, width), lambda j: (0, 0, j))] * 2,
+        out_specs=[pl.BlockSpec((2 * members, 8, width), lambda j: (0, 0, j))] * 2,
+        out_shape=[out, out],
+        compiler_params=BIG,
+        name="peel",
+    )(low, high)
+
+
+def score_kernel(
+    at, own, low, high, near_a, near_b, far_a, far_b, prior, refs_t, powers, rounded, stats
+):
     step = pl.program_id(0)
     rows = prior.shape[1]
     orient, eigen = refs_t.shape
     lines = stats.shape[1] // 2
-    high = eigen // 4
-    for base, held in ((0, (own_a, came_a)), (2 * high, (own_b, came_b))):
-        for side, source in enumerate(held):
-            place = base + high * (at[1] if side == 0 else 1 - at[1])
-            rounded[pl.ds(pl.multiple_of(place, high), high), :] = (
-                source[...].reshape(high, rows).astype(jnp.bfloat16)
-            )
+    half = eigen // 8
+    quarter = half // 2
+
+    def put(which, offset, block):
+        count = block.shape[0] * block.shape[1]
+        place = pl.multiple_of(at[which] * 2 * half + offset, quarter)
+        rounded[pl.ds(place, count), :] = block.reshape(count, rows).astype(jnp.bfloat16)
+
+    put(0, 0, far_a[...])
+    put(0, half, far_b[...])
+    put(1, 0, near_a[...])
+    put(1, half, near_b[...])
+    for offset, source in ((0, low), (quarter, high)):
+        put(2, offset, source[:, :8, :])
+        put(2, half + offset, source[:, 8:, :])
+    put(3, 0, own[:, :8, :])
+    put(3, half, own[:, 8:, :])
     scores = jnp.dot(refs_t[...], rounded[...], preferred_element_type=jnp.float32)
-    block = prior[...] - at[0] * (orient // OBLOCK)
+    block = prior[...] - at[4] * (orient // OBLOCK)
     parts = [
         scores[k * OBLOCK : (k + 1) * OBLOCK] + jnp.where(block == k, PRIOR_INCREMENT, 0.0)
         for k in range(orient // OBLOCK)
@@ -143,22 +206,18 @@
         stats[:, pl.ds(lines + line, 1), :] = jnp.broadcast_to(total[None, :, cut], shape)
 
 
-def scores_of(at, own, came, prior, refs_t, members):
+def scores_of(at, held, prior, refs_t, members):
     rows = prior.shape[1]
     orient, eigen = refs_t.shape
     width = 256
     lines = 2 * rows // LANES
-    group = own.shape[0]
     return pl.pallas_call(
         score_kernel,
         grid_spec=pltpu.PrefetchScalarGridSpec(
             num_scalar_prefetch=1,
             grid=(rows // width,),
-            in_specs=[
-                pl.BlockSpec((group, 8, width), lambda j, at: (0, 0, j)),
-                pl.BlockSpec((group, 8, width), lambda j, at: (0, 1, j)),
-                pl.BlockSpec((group, 8, width), lambda j, at: (0, 0, j)),
-                pl.BlockSpec((group, 8, width), lambda j, at: (0, 0, j)),
+            in_specs=[pl.BlockSpec((*x.shape[:2], width), lambda j, at: (0, 0, j)) for x in held]
+            + [
                 pl.BlockSpec((1, width), lambda j, at: (0, j)),
                 pl.BlockSpec((orient, eigen), lambda j, at: (0, 0)),
             ],
@@ -175,7 +234,7 @@
         ],
         compiler_params=BIG,
         name="scores",
-    )(at, own, own, *came, prior, refs_t)
+    )(at, *held, prior, refs_t)
 
 
 def total_kernel(at, stats, own, powers, rounded, keep, send, factor):
@@ -200,7 +259,7 @@
     totals = lax.dot_general(rounded[...], weights, LAST, preferred_element_type=jnp.float32)
     ones = jnp.ones((16, rows), jnp.bfloat16)
     masses = lax.dot_general(ones, weights, LAST, preferred_element_type=jnp.float32)
-    first = at[2] == 0
+    first = at[5] == 0
     for h in range(width // LANES):
         column = step * (width // LANES) + h
         cut = slice(h * LANES, (h + 1) * LANES)
@@ -263,7 +322,7 @@
             grid=(1,),
             in_specs=[
                 pl.BlockSpec(parts.shape, lambda j, at: (0, 0, 0)),
-                pl.BlockSpec((share, orient), lambda j, at: (at[3], 0)),
+                pl.BlockSpec((share, orient), lambda j, at: (at[6], 0)),
             ],
             out_specs=pl.BlockSpec((share, orient), lambda j, at: (0, 0)),
         ),
@@ -273,39 +332,46 @@
     )(at, parts, refs)
 
 
-def swapped(pair):
-    size = lax.axis_size(RING)
+def swapped(pair, axis):
+    size = lax.axis_size(axis)
     with_a = [(i, i ^ 1) for i in range(size)]
     with_b = [(i, (i + (1 if i % 2 else -1)) % size) for i in range(size)]
-    return tuple(lax.ppermute(x, RING, p) for x, p in zip(pair, (with_a, with_b)))
+    return tuple(lax.ppermute(x, axis, p) for x, p in zip(pair, (with_a, with_b)))
 
 
 def shards(images, phantom, inject_rows, prior_blocks, basis, refs):
     rows = images.shape[1] * images.shape[2]
-    pixels, eigen = basis.shape
-    flat = images[0].reshape(rows, pixels)
-    parity = lax.axis_index("yl").astype(jnp.int32)
+    flat = images[0].reshape(rows, basis.shape[0])
+    p, q = lax.axis_index("yl"), lax.axis_index("zhl")
     at = jnp.stack(
         [
-            lax.axis_index(MEM).astype(jnp.int32),
-            parity,
-            lax.axis_index("core").astype(jnp.int32),
-            lax.axis_index(GRP).astype(jnp.int32),
+            (1 - p) * 2 + 1 - q,
+            (1 - p) * 2 + q,
+            p * 2 + 1 - q,
+            p * 2 + q,
+            lax.axis_index(MEM),
+            lax.axis_index("core"),
+            lax.axis_index(GRP),
         ]
-    )
-    halves = basis.T.reshape(2, 2, eigen // 4, pixels)
-
-    def half(side):
-        chosen = lax.dynamic_index_in_dim(halves, side, 1, keepdims=False)
-        return projected(inject_rows[0], flat, chosen.reshape(eigen // 2, pixels), phantom)
-
-    came = swapped(half(1 - parity))
-    parts = joined(half(parity), came)
+    ).astype(jnp.int32)
+    blocks = [projected(at, k, inject_rows[0], flat, basis, phantom) for k in range(4)]
+
+    through = swapped(blocks[0], RING)
+    came = swapped(blocks[1], RING)
+    others = swapped(relayed(blocks[2], through), TALL)
+    parts = joined(blocks[3], came, others)
     parts = lax.all_to_all(parts, ALIKE, 0, 0, tiled=True)
     own = lax.all_to_all(summed_copies(parts), ALIKE, 0, 0, tiled=True)
-    came = swapped((own[:, :8], own[:, 8:]))
+    middle = own.shape[0] // 2
+    low, high = swapped((own[:middle], own[middle:]), TALL)
+    near = swapped((own[:, :8], own[:, 8:]), RING)
+    far = swapped(peeled(low, high), RING)
     powers, rounded, sent = scores_of(
-        at, own, came, prior_blocks[0].reshape(1, rows), refs.T, lax.axis_size(MEM)
+        at,
+        (own, low, high, *near, *far),
+        prior_blocks[0].reshape(1, rows),
+        refs.T,
+        lax.axis_size(MEM),
     )
     stats = lax.all_to_all(sent, MEM, 0, 0, tiled=True)
     keep, send = totals_of(at, stats, sent, powers, rounded, lax.axis_size(PEERS))
@@ -315,7 +381,7 @@
 
 
 def solution(mesh):
-    fine = Mesh(mesh.devices.reshape(4, 2, 2, 4, 2, 4), GRP + MEM)
+    fine = Mesh(mesh.devices.reshape(4, 2, 2, 4, 2, 2, 2), GRP + MEM)
     placed = (
         P(GRP, None, None, MEM),
         P(GRP, MEM),

time: 228 us -> 218 us (0.956)
  blocking collectives: 148 us -> 109 us
  starting transfers between devices: 23 us -> 49.8 us
  Pallas kernels: 17.9 us -> 22.4 us
    ppermute x4 -> x12, starting transfers between devices: 17.3 us -> 44.6 us  [swapped(): lax.ppermute(x, axis, p)]
    all_to_all x1, blocking collectives: 50.6 us -> 27.3 us  [shards(): own = lax.all_to_all(summed_copies(parts), ALIKE, 0, 0, tiled=True)]
    all_to_all x1, blocking collectives: 57.2 us -> 40.4 us  [shards(): parts = lax.all_to_all(parts, ALIKE, 0, 0, tiled=True)]
    pallas_call x2 -> x4, Pallas kernels: 5.47 us -> 7.8 us  [projected(): pl.pallas_call(project_kernel, grid_spec=pltpu.PrefetchScalarGridSpec(num...]
    unnamed x14 -> x24, local copies, waits for them, and re-layouts: 3.45 us -> 5.39 us
    ppermute x4 -> x12, waiting for transfers between devices: 27.9 us -> 26.5 us  [swapped(): lax.ppermute(x, axis, p)]
  transfers between devices with their start and end apart: 5 -> 13, of which waited for: 5 -> 7; matrix products, arithmetic and copies ran while one was open for 1% -> 1% of each run, Pallas kernels for 1% -> 4%
where the time goes in v3:
time: 218 us; the launch traced here: 216 us
  blocking collectives  109 us (50%)
  starting transfers between devices  49.8 us (23%)
  waiting for transfers between devices  28.8 us (13%)
  Pallas kernels  22.4 us (10%)
  local copies, waits for them, and re-layouts  6.46 us (3%)
    ppermute x12, starting transfers between devices, swapped(): lax.ppermute(x, axis, p)  44.6 us
    all_to_all x1, blocking collectives, shards(): parts = lax.all_to_all(parts, ALIKE, 0, 0, tiled=True)  40.4 us
    all_to_all x1, blocking collectives, shards(): own = lax.all_to_all(summed_copies(parts), ALIKE, 0, 0, tiled=True)  27.3 us
    ppermute x12, waiting for transfers between devices, swapped(): lax.ppermute(x, axis, p)  26.5 us
    all_to_all x1, blocking collectives, shards(): parts = lax.all_to_all(parts, PEERS, 0, 0, tiled=True)  21 us
    all_to_all x1, blocking collectives, shards(): stats = lax.all_to_all(sent, MEM, 0, 0, tiled=True)  19.8 us
    pallas_call x4, Pallas kernels, projected(): pl.pallas_call(project_kernel, grid_spec=pltpu.PrefetchScalarGridSpec(num...  7.8 us
    pallas_call x1, Pallas kernels, scores_of(): pl.pallas_call(score_kernel, grid_spec=pltpu.PrefetchScalarGridSpec(num_s...  6.61 us
  transfers between devices with their start and end apart: 13, of which 7 were waited for; matrix products, arithmetic and copies ran while one was open for 1% of the time, Pallas kernels for 4%

profile of v3, /device:TPU:1, one launch (start us, length us, event | category | flops | bytes accessed | tf_op | source)
XLA Modules:
  0.0 216.4 jit_solution(215684491149237859)
XLA Ops:
  0.0 0.1 stack.31.at
  0.1 1.4 copy-done
  1.5 1.0 copy-done.2
  2.5 0.7 copy-done.7
  3.2 0.7 copy-done.9
  3.9 1.9 project.7
  5.9 4.0 %collective-permute-start.2 = (f32[64,1536]{1,0:T(8,128)S(1)}, f32[64,1536]{1,0:T(8,128)S(1)}, u32[]{:S(2)}, u32[]{:S(2)}) collective-permute-start(f32[64,1536]{1,0:T(8,128)S(1)} %get-tuple-element.28), channel_id=1, source_target_pairs={{0,4},{4,0},{8,12},{12,8},{16,20},{20,16},{24,28},{28,24},{1,5},{5... | collective-permute-start | bytes 1179656 | tf_op jit(solution)/shard_map/ppermute | solution.py:339
  9.9 4.9 %collective-permute-start.3 = (f32[64,1536]{1,0:T(8,128)S(1)}, f32[64,1536]{1,0:T(8,128)S(1)}, u32[]{:S(2)}, u32[]{:S(2)}) collective-permute-start(f32[64,1536]{1,0:T(8,128)S(1)} %get-tuple-element.29), channel_id=1, source_target_pairs={{0,28},{4,8},{8,4},{12,16},{16,12},{20,24},{24,20},{28,0},{1,29},{... | collective-permute-start | bytes 1179656 | tf_op jit(solution)/shard_map/ppermute | solution.py:339
  14.8 2.0 project.5
  16.7 1.9 collective-permute-start
  18.7 4.0 %collective-permute-start.1 = (f32[64,1536]{1,0:T(8,128)S(1)}, f32[64,1536]{1,0:T(8,128)S(1)}, u32[]{:S(2)}, u32[]{:S(2)}) collective-permute-start(f32[64,1536]{1,0:T(8,128)S(1)} %get-tuple-element.25), channel_id=1, source_target_pairs={{0,28},{4,8},{8,4},{12,16},{16,12},{20,24},{24,20},{28,0},{1,29},{... | collective-permute-start | bytes 1179656 | tf_op jit(solution)/shard_map/ppermute | solution.py:339
  22.7 0.0 copy-start.3
  22.7 1.9 project.6
  24.7 0.0 copy-start.1
  24.7 0.3 relay.1
  25.1 5.9 %collective-permute-start.4 = (f32[4,16,1536]{2,1,0:T(8,128)S(1)}, f32[4,16,1536]{2,1,0:T(8,128)S(1)}, u32[]{:S(2)}, u32[]{:S(2)}) collective-permute-start(f32[4,16,1536]{2,1,0:T(8,128)S(1)} %get-tuple-element.30), channel_id=1, source_target_pairs={{0,1},{1,0},{2,3},{3,2},{4,5},{5,4},{6,7},{7,6},{8,9},{9,8},{10,11... | collective-permute-start | bytes 1179656 | tf_op jit(solution)/shard_map/ppermute | solution.py:339
  31.0 7.0 %collective-permute-start.5 = (f32[4,16,1536]{2,1,0:T(8,128)S(1)}, f32[4,16,1536]{2,1,0:T(8,128)S(1)}, u32[]{:S(2)}, u32[]{:S(2)}) collective-permute-start(f32[4,16,1536]{2,1,0:T(8,128)S(1)} %get-tuple-element.31), channel_id=1, source_target_pairs={{0,3},{1,2},{2,1},{3,0},{4,7},{5,6},{6,5},{7,4},{8,11},{9,10},{10,... | collective-permute-start | bytes 1179656 | tf_op jit(solution)/shard_map/ppermute | solution.py:339
  38.1 2.0 project.4
  40.1 7.1 %collective-permute-done.4.low = f32[4,16,1536]{2,1,0:T(8,128)S(1)} collective-permute-done((f32[4,16,1536]{2,1,0:T(8,128)S(1)}, f32[4,16,1536]{2,1,0:T(8,128)S(1)}, u32[]{:S(2)}, u32[]{:S(2)}) %collective-permute-start.4) | collective-permute-done | bytes 393248 | tf_op jit(solution)/shard_map/ppermute | solution.py:339
  47.2 0.3 collective-permute-done.5.high
  47.5 0.4 join.1
  47.9 40.4 %all_to_all.20.parts = f32[8,16,1536]{2,1,0:T(8,128)S(1)} all-to-all(f32[8,16,1536]{2,1,0:T(8,128)S(1)} %join.1), channel_id=1, replica_groups=mesh['x'=4,'zl'=2,'core'=2,'yh'=4,'yl'=2,'zhh'=2,'zhl'=2] {'yh','zhh'}, dimensions={0} | all-to-all | bytes 1572864 | tf_op jit(solution)/shard_map/all_to_all | solution.py:363
  88.3 0.3 spread.1
  88.6 27.3 %all_to_all.21.own = f32[8,16,1536]{2,1,0:T(8,128)S(1)} all-to-all(f32[8,16,1536]{2,1,0:T(8,128)S(1)} %spread.1), channel_id=1, replica_groups=mesh['x'=4,'zl'=2,'core'=2,'yh'=4,'yl'=2,'zhh'=2,'zhl'=2] {'yh','zhh'}, dimensions={0} | all-to-all | bytes 1572864 | tf_op jit(solution)/shard_map/all_to_all | solution.py:364
  115.9 0.1 fusion.1
  116.0 1.9 collective-permute-start.7
  117.9 0.0 copy-start.4
  117.9 5.5 %collective-permute-start.6 = (f32[4,16,1536]{2,1,0:T(8,128)S(1)}, f32[4,16,1536]{2,1,0:T(8,128)S(1)}, u32[]{:S(2)}, u32[]{:S(2)}) collective-permute-start(f32[4,16,1536]{2,1,0:T(8,128)S(1)} %get-tuple-element.42), channel_id=1, source_target_pairs={{0,1},{1,0},{2,3},{3,2},{4,5},{5,4},{6,7},{7,6},{8,9},{9,8},{10,11... | collective-permute-start | bytes 1179656 | tf_op jit(solution)/shard_map/ppermute | solution.py:339
  123.5 0.9 fusion
  124.4 1.9 collective-permute-start.9
  126.3 2.0 collective-permute-start.8
  128.3 8.2 %collective-permute-done.7.high = f32[4,16,1536]{2,1,0:T(8,128)S(1)} collective-permute-done((f32[4,16,1536]{2,1,0:T(8,128)S(1)}, f32[4,16,1536]{2,1,0:T(8,128)S(1)}, u32[]{:S(2)}, u32[]{:S(2)}) %collective-permute-start.7) | collective-permute-done | bytes 393248 | tf_op jit(solution)/shard_map/ppermute | solution.py:339
  136.5 1.3 collective-permute-done.6.low
  137.8 1.6 peel.1
  139.4 1.9 collective-permute-start.10
  141.3 3.5 %collective-permute-start.11 = (f32[8,8,1536]{2,1,0:T(8,128)}, f32[8,8,1536]{2,1,0:T(8,128)}, u32[]{:S(2)}, u32[]{:S(2)}) collective-permute-start(f32[8,8,1536]{2,1,0:T(8,128)} %get-tuple-element.33), channel_id=1, source_target_pairs={{0,28},{4,8},{8,4},{12,16},{16,12},{20,24},{24,20},{28,0},{1,29},{... | collective-permute-start | bytes 1179656 | tf_op jit(solution)/shard_map/ppermute | solution.py:339
  144.9 0.5 copy.7
  145.5 6.4 %collective-permute-done.10.far_a = f32[8,8,1536]{2,1,0:T(8,128)} collective-permute-done((f32[8,8,1536]{2,1,0:T(8,128)}, f32[8,8,1536]{2,1,0:T(8,128)}, u32[]{:S(2)}, u32[]{:S(2)}) %collective-permute-start.10) | collective-permute-done | bytes 393248 | tf_op jit(solution)/shard_map/ppermute | solution.py:339
  151.9 3.1 %collective-permute-done.11.far_b = f32[8,8,1536]{2,1,0:T(8,128)} collective-permute-done((f32[8,8,1536]{2,1,0:T(8,128)}, f32[8,8,1536]{2,1,0:T(8,128)}, u32[]{:S(2)}, u32[]{:S(2)}) %collective-permute-start.11) | collective-permute-done | bytes 393248 | tf_op jit(solution)/shard_map/ppermute | solution.py:339
  155.1 1.0 copy-done.6
  156.0 6.6 %scores.1 = (f32[1024,1536]{1,0:T(8,128)S(1)}, bf16[512,1536]{1,0:T(8,128)(2,1)S(1)}, f32[32,24,128]{2,1,0:T(8,128)S(1)}) custom-call(s32[7]{0:T(128)S(1)} %stack.31.at, f32[8,16,1536]{2,1,0:T(8,128)S(1)} %all_to_all.21.own, f32[4,16,1536]{2,1,0:T(8,128)S(1)} %copy-done.6, f32[4,16,1536]{2,1,0:T(8,128)S(1)} %collective-permute-done.7.high, ...), custom_call_target="tpu_custom_call" | custom-call | tf_op jit(solution)/shard_map/scores/pallas_call | solution.py:214
  162.7 19.8 %all_to_all.22.stats = f32[32,24,128]{2,1,0:T(8,128)S(1)} all-to-all(f32[32,24,128]{2,1,0:T(8,128)S(1)} %get-tuple-element.34.own), channel_id=1, replica_groups=mesh['x'=4,'zl'=2,'core'=2,'yh'=4,'yl'=2,'zhh'=2,'zhl'=2] {'yh','yl','zh..., dimensions={0} | all-to-all | bytes 786432 | tf_op jit(solution)/shard_map/all_to_all | solution.py:376
  182.5 4.1 %totals.1 = (f32[8,264,128]{2,1,0:T(8,128)S(1)}, f32[8,264,128]{2,1,0:T(8,128)S(1)}) custom-call(s32[7]{0:T(128)S(1)} %stack.31.at, f32[32,24,128]{2,1,0:T(8,128)S(1)} %all_to_all.22.stats, f32[32,24,128]{2,1,0:T(8,128)S(1)} %get-tuple-element.34.own, f32[1024,1536]{1,0:T(8,128)S(1)} %get-tuple-element.35.powers, bf16[512,1536]{1,0:T(8,128)(2,1)S(1)} %get-tuple-element.36.rounded), custom_call_target="tpu_custom_call" | custom-call | tf_op jit(solution)/shard_map/totals/pallas_call | solution.py:283
  186.5 5.2 %collective-permute-start.12 = (f32[8,264,128]{2,1,0:T(8,128)S(1)}, f32[8,264,128]{2,1,0:T(8,128)S(1)}, u32[]{:S(2)}, u32[]{:S(2)}) collective-permute-start(f32[8,264,128]{2,1,0:T(8,128)S(1)} %get-tuple-element.38), channel_id=1, source_target_pairs={{0,32},{32,0},{1,33},{33,1},{2,34},{34,2},{3,35},{35,3},{4,36},{36... | collective-permute-start | bytes 3244040 | tf_op jit(solution)/shard_map/ppermute | solution.py:378
  191.8 2.3 %collective-permute-done.12 = f32[8,264,128]{2,1,0:T(8,128)S(1)} collective-permute-done((f32[8,264,128]{2,1,0:T(8,128)S(1)}, f32[8,264,128]{2,1,0:T(8,128)S(1)}, u32[]{:S(2)}, u32[]{:S(2)}) %collective-permute-start.12) | collective-permute-done | bytes 1081376 | tf_op jit(solution)/shard_map/ppermute | solution.py:378
  194.1 0.1 add.39
  194.2 21.0 %all_to_all.23.parts = f32[8,264,128]{2,1,0:T(8,128)S(1)} all-to-all(f32[8,264,128]{2,1,0:T(8,128)S(1)} %add.39), channel_id=1, replica_groups=mesh['x'=4,'zl'=2,'core'=2,'yh'=4,'yl'=2,'zhh'=2,'zhl'=2] {'x','zl'}, dimensions={0} | all-to-all | bytes 2162688 | tf_op jit(solution)/shard_map/all_to_all | solution.py:379
  215.2 1.3 final.1
  (21 shorter events, 0.1 us)
Async XLA Ops:
  0.1 1.4 copy-start
  1.5 1.0 copy-start.2
  2.5 0.7 copy-start.7
  3.2 0.7 copy-start.9
  5.9 18.8 %collective-permute-start.2 = (f32[64,1536]{1,0:T(8,128)S(1)}, f32[64,1536]{1,0:T(8,128)S(1)}, u32[]{:S(2)}, u32[]{:S(2)}) collective-permute-start(f32[64,1536]{1,0:T(8,128)S(1)} %get-tuple-element.28), channel_id=1, source_target_pairs={{0,4},{4,0},{8,12},{12,8},{16,20},{20,16},{24,28},{28,24},{1,5},{5... | collective-permute-start | bytes 1179656 | tf_op jit(solution)/shard_map/ppermute | solution.py:339
  9.9 14.8 %collective-permute-start.3 = (f32[64,1536]{1,0:T(8,128)S(1)}, f32[64,1536]{1,0:T(8,128)S(1)}, u32[]{:S(2)}, u32[]{:S(2)}) collective-permute-start(f32[64,1536]{1,0:T(8,128)S(1)} %get-tuple-element.29), channel_id=1, source_target_pairs={{0,28},{4,8},{8,4},{12,16},{16,12},{20,24},{24,20},{28,0},{1,29},{... | collective-permute-start | bytes 1179656 | tf_op jit(solution)/shard_map/ppermute | solution.py:339
  16.7 23.3 %collective-permute-start = (f32[64,1536]{1,0:T(8,128)S(1)}, f32[64,1536]{1,0:T(8,128)S(1)}, u32[]{:S(2)}, u32[]{:S(2)}) collective-permute-start(f32[64,1536]{1,0:T(8,128)S(1)} %get-tuple-element.24), channel_id=1, source_target_pairs={{0,4},{4,0},{8,12},{12,8},{16,20},{20,16},{24,28},{28,24},{1,5},{5... | collective-permute-start | bytes 1179656 | tf_op jit(solution)/shard_map/ppermute | solution.py:339
  18.7 21.4 %collective-permute-start.1 = (f32[64,1536]{1,0:T(8,128)S(1)}, f32[64,1536]{1,0:T(8,128)S(1)}, u32[]{:S(2)}, u32[]{:S(2)}) collective-permute-start(f32[64,1536]{1,0:T(8,128)S(1)} %get-tuple-element.25), channel_id=1, source_target_pairs={{0,28},{4,8},{8,4},{12,16},{16,12},{20,24},{24,20},{28,0},{1,29},{... | collective-permute-start | bytes 1179656 | tf_op jit(solution)/shard_map/ppermute | solution.py:339
  22.7 15.3 %copy-start.3 = (bf16[512,512]{1,0:T(8,128)(2,1)S(1)}, bf16[512,512]{1,0:T(8,128)(2,1)}, u32[]{:S(2)}) copy-start(bf16[512,512]{1,0:T(8,128)(2,1)} %basis.7) | copy-start | bytes 1572868
  24.7 13.4 %copy-start.1 = (bf16[1,2,768,512]{3,2,1,0:T(8,128)(2,1)S(1)}, bf16[1,2,768,512]{3,2,1,0:T(8,128)(2,1)}, u32[]{:S(2)}) copy-start(bf16[1,2,768,512]{3,2,1,0:T(8,128)(2,1)} %param.6) | copy-start | bytes 4718596
  24.7 13.4 %copy-start.8 = (bf16[1,512]{1,0:T(2,128)(2,1)S(1)}, bf16[1,512]{1,0:T(2,128)(2,1)}, u32[]{:S(2)}) copy-start(bf16[1,512]{1,0:T(2,128)(2,1)} %phantom.7) | copy-start | bytes 3076
  25.1 22.1 %collective-permute-start.4 = (f32[4,16,1536]{2,1,0:T(8,128)S(1)}, f32[4,16,1536]{2,1,0:T(8,128)S(1)}, u32[]{:S(2)}, u32[]{:S(2)}) collective-permute-start(f32[4,16,1536]{2,1,0:T(8,128)S(1)} %get-tuple-element.30), channel_id=1, source_target_pairs={{0,1},{1,0},{2,3},{3,2},{4,5},{5,4},{6,7},{7,6},{8,9},{9,8},{10,11... | collective-permute-start | bytes 1179656 | tf_op jit(solution)/shard_map/ppermute | solution.py:339
  31.0 16.5 %collective-permute-start.5 = (f32[4,16,1536]{2,1,0:T(8,128)S(1)}, f32[4,16,1536]{2,1,0:T(8,128)S(1)}, u32[]{:S(2)}, u32[]{:S(2)}) collective-permute-start(f32[4,16,1536]{2,1,0:T(8,128)S(1)} %get-tuple-element.31), channel_id=1, source_target_pairs={{0,3},{1,2},{2,1},{3,0},{4,7},{5,6},{6,5},{7,4},{8,11},{9,10},{10,... | collective-permute-start | bytes 1179656 | tf_op jit(solution)/shard_map/ppermute | solution.py:339
  116.0 20.5 %collective-permute-start.7 = (f32[4,16,1536]{2,1,0:T(8,128)S(1)}, f32[4,16,1536]{2,1,0:T(8,128)S(1)}, u32[]{:S(2)}, u32[]{:S(2)}) collective-permute-start(f32[4,16,1536]{2,1,0:T(8,128)S(1)} %get-tuple-element.41), channel_id=1, source_target_pairs={{0,3},{1,2},{2,1},{3,0},{4,7},{5,6},{6,5},{7,4},{8,11},{9,10},{10,... | collective-permute-start | bytes 1179656 | tf_op jit(solution)/shard_map/ppermute | solution.py:339
  117.9 26.9 %copy-start.10 = (s32[1,2,768]{2,1,0:T(2,128)S(1)}, s32[1,2,768]{2,1,0:T(2,128)}, u32[]{:S(2)}) copy-start(s32[1,2,768]{2,1,0:T(2,128)} %param.9) | copy-start | bytes 18436
  117.9 27.0 %copy-start.4 = (bf16[512,1024]{1,0:T(8,128)(2,1)S(1)}, bf16[512,1024]{1,0:T(8,128)(2,1)}, u32[]{:S(2)}) copy-start(bf16[512,1024]{1,0:T(8,128)(2,1)} %refs.1) | copy-start | bytes 3145732
  117.9 19.9 %collective-permute-start.6 = (f32[4,16,1536]{2,1,0:T(8,128)S(1)}, f32[4,16,1536]{2,1,0:T(8,128)S(1)}, u32[]{:S(2)}, u32[]{:S(2)}) collective-permute-start(f32[4,16,1536]{2,1,0:T(8,128)S(1)} %get-tuple-element.42), channel_id=1, source_target_pairs={{0,1},{1,0},{2,3},{3,2},{4,5},{5,4},{6,7},{7,6},{8,9},{9,8},{10,11... | collective-permute-start | bytes 1179656 | tf_op jit(solution)/shard_map/ppermute | solution.py:339
  124.4 21.1 %collective-permute-start.9 = (f32[8,8,1536]{2,1,0:T(8,128)}, f32[8,8,1536]{2,1,0:T(8,128)}, u32[]{:S(2)}, u32[]{:S(2)}) collective-permute-start(f32[8,8,1536]{2,1,0:T(8,128)} %get-tuple-element.39), channel_id=1, source_target_pairs={{0,28},{4,8},{8,4},{12,16},{16,12},{20,24},{24,20},{28,0},{1,29},{... | collective-permute-start | bytes 1179656 | tf_op jit(solution)/shard_map/ppermute | solution.py:339
  126.3 19.2 %collective-permute-start.8 = (f32[8,8,1536]{2,1,0:T(8,128)}, f32[8,8,1536]{2,1,0:T(8,128)}, u32[]{:S(2)}, u32[]{:S(2)}) collective-permute-start(f32[8,8,1536]{2,1,0:T(8,128)} %get-tuple-element.40), channel_id=1, source_target_pairs={{0,4},{4,0},{8,12},{12,8},{16,20},{20,16},{24,28},{28,24},{1,5},{5... | collective-permute-start | bytes 1179656 | tf_op jit(solution)/shard_map/ppermute | solution.py:339
  137.8 7.0 %copy-start.5 = (f32[4,16,1536]{2,1,0:T(8,128)}, f32[4,16,1536]{2,1,0:T(8,128)S(1)}, u32[]{:S(2)}) copy-start(f32[4,16,1536]{2,1,0:T(8,128)S(1)} %collective-permute-done.6.low) | copy-start | bytes 1179652
  139.4 12.5 %collective-permute-start.10 = (f32[8,8,1536]{2,1,0:T(8,128)}, f32[8,8,1536]{2,1,0:T(8,128)}, u32[]{:S(2)}, u32[]{:S(2)}) collective-permute-start(f32[8,8,1536]{2,1,0:T(8,128)} %get-tuple-element.32), channel_id=1, source_target_pairs={{0,4},{4,0},{8,12},{12,8},{16,20},{20,16},{24,28},{28,24},{1,5},{5... | collective-permute-start | bytes 1179656 | tf_op jit(solution)/shard_map/ppermute | solution.py:339
  141.3 13.7 %collective-permute-start.11 = (f32[8,8,1536]{2,1,0:T(8,128)}, f32[8,8,1536]{2,1,0:T(8,128)}, u32[]{:S(2)}, u32[]{:S(2)}) collective-permute-start(f32[8,8,1536]{2,1,0:T(8,128)} %get-tuple-element.33), channel_id=1, source_target_pairs={{0,28},{4,8},{8,4},{12,16},{16,12},{20,24},{24,20},{28,0},{1,29},{... | collective-permute-start | bytes 1179656 | tf_op jit(solution)/shard_map/ppermute | solution.py:339
  155.0 1.0 copy-start.6
  186.5 7.6 %collective-permute-start.12 = (f32[8,264,128]{2,1,0:T(8,128)S(1)}, f32[8,264,128]{2,1,0:T(8,128)S(1)}, u32[]{:S(2)}, u32[]{:S(2)}) collective-permute-start(f32[8,264,128]{2,1,0:T(8,128)S(1)} %get-tuple-element.38), channel_id=1, source_target_pairs={{0,32},{32,0},{1,33},{33,1},{2,34},{34,2},{3,35},{35,3},{4,36},{36... | collective-permute-start | bytes 3244040 | tf_op jit(solution)/shard_map/ppermute | solution.py:378

commit v4 on v3

v4 whole, which is shorter than its diff:
```python
import jax
import jax.numpy as jnp
from jax import lax
from jax.experimental import pallas as pl
from jax.experimental.pallas import tpu as pltpu
from jax.sharding import Mesh, PartitionSpec as P

OBLOCK = 256
PRIOR_INCREMENT = 3.0
GRP = ("x", "zl", "core")
RING = ("yh", "yl")
TALL = ("zhh", "zhl")
MEM = RING + TALL
ALIKE = ("yh", "zhh")
PEERS = ("x", "zl")
LANES = 128
BIG = pltpu.CompilerParams(vmem_limit_bytes=28 << 20)
SMALL = pltpu.CompilerParams(vmem_limit_bytes=14 << 20)
LAST = (((1,), (1,)), ((), ()))


def project_kernel(at, inject, images, basis, phantom, *rest):
    outs, (pixels_in, columns, ghost, sems) = rest[:-4], rest[-4:]
    which = pixels_in.shape[0]
    width = pixels_in.shape[1]
    count = columns.shape[1]
    first = pl.multiple_of(at[0] * count, count)
    loads = [
        pltpu.make_async_copy(basis.at[:, pl.ds(first, count)], columns, sems.at[which]),
        pltpu.make_async_copy(phantom, ghost, sems.at[which + 1]),
    ] + [
        pltpu.make_async_copy(images.at[pl.ds(k * width, width), :], pixels_in.at[k], sems.at[k])
        for k in range(which)
    ]
    for load in loads:
        load.start()
    per_batch = which // inject.shape[0]
    hits = []
    for k in range(which):
        position = (k % per_batch) * width + lax.broadcasted_iota(jnp.int32, (1, width), 1)
        hit = jnp.zeros((1, width), jnp.float32)
        for i in range(inject.shape[1]):
            hit = jnp.where(position == inject[k // per_batch, i], 1.0, hit)
        hits.append(hit)
    loads[0].wait()
    loads[1].wait()
    mine = columns[...].T
    spread = jnp.broadcast_to(ghost[...], (LANES, ghost.shape[1]))
    extra = lax.dot_general(mine, spread, LAST, preferred_element_type=jnp.float32)
    share = count // len(outs)
    for k in range(which):
        loads[2 + k].wait()
        plain = lax.dot_general(mine, pixels_in[k], LAST, preferred_element_type=jnp.float32)
        for c in range(width // LANES):
            cut = slice(c * LANES, (c + 1) * LANES)
            value = plain[:, cut] + extra * hits[k][:, cut]
            for j, out in enumerate(outs):
                out[:, k * width + c * LANES : k * width + (c + 1) * LANES] = value[
                    j * share : (j + 1) * share
                ]


def projected(block, inject, images, basis, phantom, pieces):
    rows, pixels = images.shape
    steps = 2 * inject.shape[0]
    count = basis.shape[1] // 4
    out = jax.ShapeDtypeStruct((count // pieces, rows), jnp.float32)
    images, basis, phantom = (
        pltpu.with_memory_space_constraint(x, pltpu.HBM) for x in (images, basis, phantom)
    )
    found = pl.pallas_call(
        project_kernel,
        grid_spec=pltpu.PrefetchScalarGridSpec(
            num_scalar_prefetch=2,
            grid=(1,),
            in_specs=[pl.BlockSpec(memory_space=pltpu.HBM)] * 3,
            out_specs=[pl.BlockSpec(out.shape, lambda j, at, s: (0, 0))] * pieces,
            scratch_shapes=[
                pltpu.VMEM((steps, rows // steps, pixels), images.dtype),
                pltpu.VMEM((pixels, count), basis.dtype),
                pltpu.VMEM((1, pixels), phantom.dtype),
                pltpu.SemaphoreType.DMA((steps + 2,)),
            ],
        ),
        out_shape=[out] * pieces,
        compiler_params=SMALL,
        name="project",
    )(block, inject, images, basis, phantom)
    return tuple(found)


def relay_kernel(at, tall, wide, came_y, came_a, came_b, to_a, to_b, to_y, left, right):
    p, q = at[0], at[1]
    piece = to_a.shape[0]
    for s, (out, came) in enumerate(((to_a, came_a), (to_b, came_b))):
        base = 2 * s * piece
        here = pl.ds(pl.multiple_of(base + q * piece, piece), piece)
        there = pl.ds(pl.multiple_of(base + (1 - q) * piece, piece), piece)
        out[...] = tall[there, :] + came_y[there, :]
        left[s * piece : (s + 1) * piece, :] = tall[here, :] + came_y[here, :]
        for spot, side in ((right, p), (to_y, 1 - p)):
            inner = pl.multiple_of(side * piece, piece)
            spot[s * piece : (s + 1) * piece, :] = (
                wide[pl.ds(pl.multiple_of(base + side * piece, piece), piece), :]
                + came[pl.ds(inner, piece), :]
            )


def relayed(at, tall, wide, came_y, came_z):
    count, rows = tall.shape
    width = rows // 3

    def spec(high):
        return pl.BlockSpec((high, width), lambda j, at: (0, j))

    highs = (count // 4, count // 4, count // 2, count // 2, count // 2)
    return pl.pallas_call(
        relay_kernel,
        grid_spec=pltpu.PrefetchScalarGridSpec(
            num_scalar_prefetch=1,
            grid=(rows // width,),
            in_specs=[spec(x.shape[0]) for x in (tall, wide, came_y, *came_z)],
            out_specs=[spec(high) for high in highs],
        ),
        out_shape=[jax.ShapeDtypeStruct((high, rows), jnp.float32) for high in highs],
        compiler_params=SMALL,
        name="relay",
    )(at, tall, wide, came_y, *came_z)


def join_kernel(left, right, came_a, came_b, came_y, out):
    members = out.shape[0]
    for m in range(members):
        cut = slice(m * 8, (m + 1) * 8)
        source = (came_a, came_b)[m // (members // 2)]
        inner = (m % (members // 2)) * 8
        out[m, :8, :] = left[cut, :] + source[inner : inner + 8, :]
        out[m, 8:, :] = right[cut, :] + came_y[cut, :]


def joined(left, right, came_z, came_y):
    count, rows = left.shape
    width = rows // 3
    operands = (left, right, *came_z, came_y)
    return pl.pallas_call(
        join_kernel,
        grid=(rows // width,),
        in_specs=[pl.BlockSpec((x.shape[0], width), lambda j: (0, j)) for x in operands],
        out_specs=pl.BlockSpec((count // 8, 16, width), lambda j: (0, 0, j)),
        out_shape=jax.ShapeDtypeStruct((count // 8, 16, rows), jnp.float32),
        compiler_params=SMALL,
        name="join",
    )(*operands)


def spread_kernel(parts, out):
    total = parts[0]
    for k in range(1, parts.shape[0]):
        total = total + parts[k]
    for k in range(out.shape[0]):
        out[k] = total


def summed_copies(parts):
    members, high, rows = parts.shape
    steps = 3
    block = pl.BlockSpec((members, high, rows // steps), lambda j: (0, 0, j))
    return pl.pallas_call(
        spread_kernel,
        grid=(steps,),
        in_specs=[block],
        out_specs=block,
        out_shape=jax.ShapeDtypeStruct(parts.shape, jnp.float32),
        compiler_params=SMALL,
        name="spread",
    )(parts)


def part_kernel(own, to_a, to_b, to_y):
    middle = to_a.shape[0]
    to_a[...] = own[:middle, :8, :]
    to_b[...] = own[middle:, :8, :]
    to_y[...] = own[:, 8:, :]


def peel_kernel(own, came_a, came_b, came_y, to_y, to_a, to_b):
    members = own.shape[0]
    middle = members // 2
    to_y[:members] = own[:, :8, :]
    to_y[members : members + middle] = came_a[...]
    to_y[members + middle :] = came_b[...]
    for out, cut in ((to_a, slice(0, middle)), (to_b, slice(middle, members))):
        out[:middle] = own[cut, 8:, :]
        out[middle:] = came_y[cut]


def copied(kernel, name, operands, lengths):
    rows = operands[0].shape[2]
    width = rows // 3

    def spec(length, high):
        return pl.BlockSpec((length, high, width), lambda j: (0, 0, j))

    return pl.pallas_call(
        kernel,
        grid=(rows // width,),
        in_specs=[spec(*x.shape[:2]) for x in operands],
        out_specs=[spec(length, 8) for length in lengths],
        out_shape=[jax.ShapeDtypeStruct((length, 8, rows), jnp.float32) for length in lengths],
        compiler_params=SMALL,
        name=name,
    )(*operands)


def score_kernel(
    at, own, za0, zb0, yb1, ya0, za1, zb1, prior, refs_t, powers, rounded, stats
):
    step = pl.program_id(0)
    p, q = at[0], at[1]
    rows = prior.shape[1]
    orient, eigen = refs_t.shape
    lines = stats.shape[1] // 2
    piece = eigen // 16
    middle = own.shape[0] // 2

    def put(base, major, s, minor, block):
        place = base + major * (4 * piece) + s * (2 * piece) + minor * piece
        rounded[pl.ds(pl.multiple_of(place, piece), piece), :] = block.reshape(piece, rows).astype(
            jnp.bfloat16
        )

    wide = eigen // 2
    for s, (z0, z1) in enumerate(((za0, za1), (zb0, zb1))):
        cut = slice(s * middle, (s + 1) * middle)
        after = slice((2 + s) * middle, (3 + s) * middle)
        put(0, p, s, q, own[cut, :8, :])
        put(0, p, s, 1 - q, z0[...])
        put(0, 1 - p, s, q, ya0[cut])
        put(0, 1 - p, s, 1 - q, ya0[after])
        put(wide, q, s, p, own[cut, 8:, :])
        put(wide, q, s, 1 - p, yb1[cut])
        put(wide, 1 - q, s, p, z1[:middle])
        put(wide, 1 - q, s, 1 - p, z1[middle:])
    scores = jnp.dot(refs_t[...], rounded[...], preferred_element_type=jnp.float32)
    block = prior[...] - at[2] * (orient // OBLOCK)
    parts = [
        scores[k * OBLOCK : (k + 1) * OBLOCK] + jnp.where(block == k, PRIOR_INCREMENT, 0.0)
        for k in range(orient // OBLOCK)
    ]
    tops = [jnp.max(part, axis=0, keepdims=True) for part in parts]
    top = tops[0]
    for other in tops[1:]:
        top = jnp.maximum(top, other)
    total = jnp.zeros_like(top)
    for k, part in enumerate(parts):
        power = jnp.exp(part - top)
        powers[k * OBLOCK : (k + 1) * OBLOCK, :] = power
        total = total + jnp.sum(power, axis=0, keepdims=True)
    for h in range(rows // LANES):
        line = step * (rows // LANES) + h
        cut = slice(h * LANES, (h + 1) * LANES)
        shape = (stats.shape[0], 1, LANES)
        stats[:, pl.ds(line, 1), :] = jnp.broadcast_to(top[None, :, cut], shape)
        stats[:, pl.ds(lines + line, 1), :] = jnp.broadcast_to(total[None, :, cut], shape)


def scores_of(at, held, prior, refs_t, members):
    rows = prior.shape[1]
    orient, eigen = refs_t.shape
    width = 256
    lines = 2 * rows // LANES
    return pl.pallas_call(
        score_kernel,
        grid_spec=pltpu.PrefetchScalarGridSpec(
            num_scalar_prefetch=1,
            grid=(rows // width,),
            in_specs=[pl.BlockSpec((*x.shape[:2], width), lambda j, at: (0, 0, j)) for x in held]
            + [
                pl.BlockSpec((1, width), lambda j, at: (0, j)),
                pl.BlockSpec((orient, eigen), lambda j, at: (0, 0)),
            ],
            out_specs=[
                pl.BlockSpec((orient, width), lambda j, at: (0, j)),
                pl.BlockSpec((eigen, width), lambda j, at: (0, j)),
                pl.BlockSpec((members, lines, LANES), lambda j, at: (0, 0, 0)),
            ],
        ),
        out_shape=[
            jax.ShapeDtypeStruct((orient, rows), jnp.float32),
            jax.ShapeDtypeStruct((eigen, rows), jnp.bfloat16),
            jax.ShapeDtypeStruct((members, lines, LANES), jnp.float32),
        ],
        compiler_params=BIG,
        name="scores",
    )(at, *held, prior, refs_t)


def total_kernel(at, stats, own, powers, rounded, keep, send, factor):
    step = pl.program_id(0)
    eigen, rows = rounded.shape
    width = powers.shape[0]
    peers = keep.shape[0]
    share = eigen // (2 * peers)
    lines = rows // LANES
    body = keep.shape[1] - keep.shape[1] % share

    @pl.when(step == 0)
    def _():
        tops = stats[:, :lines, :]
        top = jnp.max(tops, axis=0)
        total = jnp.sum(stats[:, lines:, :] * jnp.exp(tops - top[None]), axis=0)
        scale = jnp.exp(own[0, :lines, :] - top) / total
        for k in range(lines):
            factor[:, k * LANES : (k + 1) * LANES] = scale[k : k + 1, :]

    weights = (powers[...] * factor[...]).astype(jnp.bfloat16)
    totals = lax.dot_general(rounded[...], weights, LAST, preferred_element_type=jnp.float32)
    ones = jnp.ones((16, rows), jnp.bfloat16)
    masses = lax.dot_general(ones, weights, LAST, preferred_element_type=jnp.float32)
    first = at[3] == 0
    for h in range(width // LANES):
        column = step * (width // LANES) + h
        cut = slice(h * LANES, (h + 1) * LANES)
        place = pl.ds(pl.multiple_of(column * share, share), share)
        for q in range(peers):
            even = totals[2 * q * share : (2 * q + 1) * share, cut]
            odd = totals[(2 * q + 1) * share : (2 * q + 2) * share, cut]
            keep[q, place, :] = jnp.where(first, even, odd)
            send[q, place, :] = jnp.where(first, odd, even)
        mass = jnp.broadcast_to(masses[None, 0:1, cut], (peers, 1, LANES))
        keep[:, pl.ds(body + column, 1), :] = mass
        send[:, pl.ds(body + column, 1), :] = mass


def totals_of(at, stats, sent, powers, rounded, peers):
    eigen, rows = rounded.shape
    orient = powers.shape[0]
    width = 256
    deep = (eigen // (2 * peers) + 1) * (orient // LANES)
    out = jax.ShapeDtypeStruct((peers, deep, LANES), jnp.float32)
    return pl.pallas_call(
        total_kernel,
        grid_spec=pltpu.PrefetchScalarGridSpec(
            num_scalar_prefetch=1,
            grid=(orient // width,),
            in_specs=[
                pl.BlockSpec(stats.shape, lambda j, at: (0, 0, 0)),
                pl.BlockSpec((1, *sent.shape[1:]), lambda j, at: (0, 0, 0)),
                pl.BlockSpec((width, rows), lambda j, at: (j, 0)),
                pl.BlockSpec((eigen, rows), lambda j, at: (0, 0)),
            ],
            out_specs=[pl.BlockSpec((peers, deep, LANES), lambda j, at: (0, 0, 0))] * 2,
            scratch_shapes=[pltpu.VMEM((1, rows), jnp.float32)],
        ),
        out_shape=[out, out],
        compiler_params=BIG,
        name="totals",
    )(at, stats, sent, powers, rounded)


def final_kernel(at, parts, refs, out):
    share, orient = out.shape
    both = parts[0]
    for d in range(1, parts.shape[0]):
        both = both + parts[d]
    body = share * (orient // LANES)
    for k in range(orient // LANES):
        cut = slice(k * LANES, (k + 1) * LANES)
        above = both[k * share : (k + 1) * share] + refs[:, cut].astype(jnp.float32)
        out[:, cut] = above / (both[body + k : body + k + 1] + 1.0)


def final_of(at, parts, refs):
    eigen, orient = refs.shape
    share = eigen // (2 * parts.shape[0])
    return pl.pallas_call(
        final_kernel,
        grid_spec=pltpu.PrefetchScalarGridSpec(
            num_scalar_prefetch=1,
            grid=(1,),
            in_specs=[
                pl.BlockSpec(parts.shape, lambda j, at: (0, 0, 0)),
                pl.BlockSpec((share, orient), lambda j, at: (at[4], 0)),
            ],
            out_specs=pl.BlockSpec((share, orient), lambda j, at: (0, 0)),
        ),
        out_shape=jax.ShapeDtypeStruct((share, orient), jnp.float32),
        compiler_params=SMALL,
        name="final",
    )(at, parts, refs)


def with_a(x, axis):
    return lax.ppermute(x, axis, [(i, i ^ 1) for i in range(lax.axis_size(axis))])


def with_b(x, axis):
    size = lax.axis_size(axis)
    return lax.ppermute(x, axis, [(i, (i + (1 if i % 2 else -1)) % size) for i in range(size)])


def shards(images, phantom, inject_rows, prior_blocks, basis, refs):
    rows = images.shape[1] * images.shape[2]
    flat = images[0].reshape(rows, basis.shape[0])
    p, q = lax.axis_index("yl"), lax.axis_index("zhl")
    at = jnp.stack(
        [p, q, lax.axis_index(MEM), lax.axis_index("core"), lax.axis_index(GRP)]
    ).astype(jnp.int32)

    def block(which, pieces):
        column = jnp.int32(which).reshape(1)
        return projected(column, inject_rows[0], flat, basis, phantom, pieces)

    to_a, to_b = block(3 - q, 2)
    (to_y,) = block(1 - p, 1)
    came_z = with_a(to_a, TALL), with_b(to_b, TALL)
    came_y = with_a(to_y, RING)
    to_a, to_b, to_y, left, right = relayed(at, *block(p, 1), *block(2 + q, 1), came_y, came_z)
    came_z = with_a(to_a, TALL), with_b(to_b, TALL)
    parts = joined(left, right, came_z, with_b(to_y, RING))
    parts = lax.all_to_all(parts, ALIKE, 0, 0, tiled=True)
    own = lax.all_to_all(summed_copies(parts), ALIKE, 0, 0, tiled=True)
    members = own.shape[0]
    to_a, to_b, to_y = copied(
        part_kernel, "part", (own,), (members // 2, members // 2, members)
    )
    first = with_a(to_a, TALL), with_b(to_b, TALL), with_b(to_y, RING)
    to_y, to_a, to_b = copied(
        peel_kernel, "peel", (own, *first), (2 * members, members, members)
    )
    second = with_a(to_y, RING), with_a(to_a, TALL), with_b(to_b, TALL)
    powers, rounded, sent = scores_of(
        at,
        (own, *first, *second),
        prior_blocks[0].reshape(1, rows),
        refs.T,
        lax.axis_size(MEM),
    )
    stats = lax.all_to_all(sent, MEM, 0, 0, tiled=True)
    keep, send = totals_of(at, stats, sent, powers, rounded, lax.axis_size(PEERS))
    parts = keep + lax.ppermute(send, "core", [(0, 1), (1, 0)])
    parts = lax.all_to_all(parts, PEERS, 0, 0, tiled=True)
    return final_of(at, parts, refs)


def solution(mesh):
    fine = Mesh(mesh.devices.reshape(4, 2, 2, 4, 2, 2, 2), GRP + MEM)
    placed = (
        P(GRP, None, None, MEM),
        P(GRP, MEM),
        P(GRP, None, None),
        P(GRP, None, None),
        P(MEM, None),
        P(None, MEM),
    )
    return jax.shard_map(
        shards, mesh=fine, in_specs=placed, out_specs=P(GRP, MEM), check_vma=False
    )
```

time: 218 us -> 232 us (1.064)
  blocking collectives: 109 us -> 94.9 us
  starting transfers between devices: 49.8 us -> 62.1 us
  waiting for transfers between devices: 28.8 us -> 40.3 us
  Pallas kernels: 22.4 us -> 30 us
  local copies, waits for them, and re-layouts: 6.46 us -> 2.26 us
    all_to_all x1, blocking collectives: 40.4 us -> 25 us  [shards(): parts = lax.all_to_all(parts, ALIKE, 0, 0, tiled=True)]
    ppermute x12, starting transfers between devices: 44.6 us -> 56.4 us  [the longest x6 33 us: with_b(): lax.ppermute(x, axis, [(i, (i + (1 if i % 2 else -1)) % size) for i in ra...]
    ppermute x12, waiting for transfers between devices: 26.5 us -> 38 us  [the longest x6 26 us: with_a(): lax.ppermute(x, axis, [(i, i ^ 1) for i in range(lax.axis_size(axis))])]
    pallas_call x4, Pallas kernels: 7.8 us -> 12.5 us  [projected(): pl.pallas_call(project_kernel, grid_spec=pltpu.PrefetchScalarGridSpec(num...]
    all_to_all x1, blocking collectives: 27.3 us -> 30.8 us  [shards(): own = lax.all_to_all(summed_copies(parts), ALIKE, 0, 0, tiled=True)]
    unnamed x24 -> x14, local copies, waits for them, and re-layouts: 5.39 us -> 2.17 us
    pallas_call x2 -> x3, Pallas kernels: 1.94 us -> 4.81 us  [the longest x1 2.73 us: relayed(): pl.pallas_call(relay_kernel, grid_spec=pltpu.PrefetchScalarGridSpec(num_s...]
  transfers between devices with their start and end apart: 13 -> 13, of which waited for: 7 -> 8; matrix products, arithmetic and copies ran while one was open for 1% -> 0% of each run, Pallas kernels for 4% -> 4%
where the time goes in v4:
time: 232 us; the launch traced here: 230 us
  blocking collectives  94.9 us (41%)
  starting transfers between devices  62.1 us (27%)
  waiting for transfers between devices  40.3 us (17%)
  Pallas kernels  30 us (13%)
    ppermute x6, starting transfers between devices, with_b(): lax.ppermute(x, axis, [(i, (i + (1 if i % 2 else -1)) % size) for i in ra...  33 us
    all_to_all x1, blocking collectives, shards(): own = lax.all_to_all(summed_copies(parts), ALIKE, 0, 0, tiled=True)  30.8 us
    ppermute x6, waiting for transfers between devices, with_a(): lax.ppermute(x, axis, [(i, i ^ 1) for i in range(lax.axis_size(axis))])  26 us
    all_to_all x1, blocking collectives, shards(): parts = lax.all_to_all(parts, ALIKE, 0, 0, tiled=True)  25 us
    ppermute x6, starting transfers between devices, with_a(): lax.ppermute(x, axis, [(i, i ^ 1) for i in range(lax.axis_size(axis))])  23.4 us
    all_to_all x1, blocking collectives, shards(): stats = lax.all_to_all(sent, MEM, 0, 0, tiled=True)  19.8 us
    all_to_all x1, blocking collectives, shards(): parts = lax.all_to_all(parts, PEERS, 0, 0, tiled=True)  19.2 us
    pallas_call x4, Pallas kernels, projected(): pl.pallas_call(project_kernel, grid_spec=pltpu.PrefetchScalarGridSpec(num...  12.5 us
  transfers between devices with their start and end apart: 13, of which 8 were waited for; matrix products, arithmetic and copies ran while one was open for 0% of the time, Pallas kernels for 4%

profile of v4, /device:TPU:1, one launch (start us, length us, event | category | flops | bytes accessed | tf_op | source)
XLA Modules:
  0.0 230.0 jit_solution(4969660284877889480)
XLA Ops:
  0.0 0.7 copy-done.3
  0.7 2.9 %project.6 = f32[128,1536]{1,0:T(8,128)S(1)} custom-call(s32[1]{0:T(128)} %bitcast.8.at, s32[2,64]{1,0:T(2,128)S(1)} %bitcast.15, bf16[1536,512]{1,0:T(8,128)(2,1)} %bitcast.19, bf16[512,512]{1,0:T(8,128)(2,1)} %basis.7, bf16[1,512]{1,0:T(2,128)(2,1)} %phantom.7), custom_call_target="tpu_custom_call" | custom-call | tf_op jit(solution)/shard_map/project/pallas_call | solution.py:71
  3.6 4.0 %collective-permute-start = (f32[128,1536]{1,0:T(8,128)S(1)}, f32[128,1536]{1,0:T(8,128)S(1)}, u32[]{:S(2)}, u32[]{:S(2)}) collective-permute-start(f32[128,1536]{1,0:T(8,128)S(1)} %project.6), channel_id=1, source_target_pairs={{0,4},{4,0},{8,12},{12,8},{16,20},{20,16},{24,28},{28,24},{1,5},{5... | collective-permute-start | bytes 2359304 | tf_op jit(solution)/shard_map/ppermute | solution.py:394
  7.7 3.8 %project.7 = (f32[64,1536]{1,0:T(8,128)}, f32[64,1536]{1,0:T(8,128)}) custom-call(s32[1]{0:T(128)} %bitcast.9.at, s32[2,64]{1,0:T(2,128)S(1)} %bitcast.16, bf16[1536,512]{1,0:T(8,128)(2,1)} %bitcast.20, bf16[512,512]{1,0:T(8,128)(2,1)} %basis.7, bf16[1,512]{1,0:T(2,128)(2,1)} %phantom.7), custom_call_target="tpu_custom_call" | custom-call | tf_op jit(solution)/shard_map/project/pallas_call | solution.py:71
  11.4 5.8 %collective-permute-start.1 = (f32[64,1536]{1,0:T(8,128)}, f32[64,1536]{1,0:T(8,128)S(1)}, u32[]{:S(2)}, u32[]{:S(2)}) collective-permute-start(f32[64,1536]{1,0:T(8,128)} %get-tuple-element.23), channel_id=1, source_target_pairs={{0,1},{1,0},{2,3},{3,2},{4,5},{5,4},{6,7},{7,6},{8,9},{9,8},{10,11... | collective-permute-start | bytes 1179656 | tf_op jit(solution)/shard_map/ppermute | solution.py:394
  17.3 7.0 %collective-permute-start.2 = (f32[64,1536]{1,0:T(8,128)}, f32[64,1536]{1,0:T(8,128)}, u32[]{:S(2)}, u32[]{:S(2)}) collective-permute-start(f32[64,1536]{1,0:T(8,128)} %get-tuple-element.24), channel_id=1, source_target_pairs={{0,3},{1,2},{2,1},{3,0},{4,7},{5,6},{6,5},{7,4},{8,11},{9,10},{10,... | collective-permute-start | bytes 1179656 | tf_op jit(solution)/shard_map/ppermute | solution.py:399
  24.3 2.9 %project.5.wide = f32[128,1536]{1,0:T(8,128)S(1)} custom-call(s32[1]{0:T(128)} %bitcast.7.at, s32[2,64]{1,0:T(2,128)S(1)} %bitcast.17, bf16[1536,512]{1,0:T(8,128)(2,1)} %bitcast.21, bf16[512,512]{1,0:T(8,128)(2,1)} %basis.7, bf16[1,512]{1,0:T(2,128)(2,1)} %phantom.7), custom_call_target="tpu_custom_call" | custom-call | tf_op jit(solution)/shard_map/project/pallas_call | solution.py:71
  27.2 2.9 %project.4.tall = f32[128,1536]{1,0:T(8,128)S(1)} custom-call(s32[1]{0:T(128)} %bitcast.at, s32[2,64]{1,0:T(2,128)S(1)} %bitcast.18, bf16[1536,512]{1,0:T(8,128)(2,1)} %bitcast.22, bf16[512,512]{1,0:T(8,128)(2,1)} %basis.7, bf16[1,512]{1,0:T(2,128)(2,1)} %phantom.7), custom_call_target="tpu_custom_call" | custom-call | tf_op jit(solution)/shard_map/project/pallas_call | solution.py:71
  30.2 0.1 stack.23.at
  30.2 3.5 %collective-permute-done.1.came_a = f32[64,1536]{1,0:T(8,128)S(1)} collective-permute-done((f32[64,1536]{1,0:T(8,128)}, f32[64,1536]{1,0:T(8,128)S(1)}, u32[]{:S(2)}, u32[]{:S(2)}) %collective-permute-start.1) | collective-permute-done | bytes 393248 | tf_op jit(solution)/shard_map/ppermute | solution.py:394
  33.7 7.6 %collective-permute-done.2.came_b = f32[64,1536]{1,0:T(8,128)} collective-permute-done((f32[64,1536]{1,0:T(8,128)}, f32[64,1536]{1,0:T(8,128)}, u32[]{:S(2)}, u32[]{:S(2)}) %collective-permute-start.2) | collective-permute-done | bytes 393248 | tf_op jit(solution)/shard_map/ppermute | solution.py:399
  41.3 0.0 collective-permute-done.came_y
  41.3 2.7 %relay.1 = (f32[32,1536]{1,0:T(8,128)S(1)}, f32[32,1536]{1,0:T(8,128)S(1)}, f32[64,1536]{1,0:T(8,128)S(1)}, f32[64,1536]{1,0:T(8,128)S(1)}, f32[64,1536]{1,0:T(8,128)S(1)}) custom-call(s32[5]{0:T(128)S(1)} %stack.23.at, f32[128,1536]{1,0:T(8,128)S(1)} %project.4.tall, f32[128,1536]{1,0:T(8,128)S(1)} %project.5.wide, ...), custom_call_target="tpu_custom_call" | custom-call | tf_op jit(solution)/shard_map/relay/pallas_call | solution.py:117
  44.0 4.9 %collective-permute-start.5 = (f32[64,1536]{1,0:T(8,128)S(1)}, f32[64,1536]{1,0:T(8,128)S(1)}, u32[]{:S(2)}, u32[]{:S(2)}) collective-permute-start(f32[64,1536]{1,0:T(8,128)S(1)} %get-tuple-element.29), channel_id=1, source_target_pairs={{0,28},{4,8},{8,4},{12,16},{16,12},{20,24},{24,20},{28,0},{1,29},{... | collective-permute-start | bytes 1179656 | tf_op jit(solution)/shard_map/ppermute | solution.py:399
  48.9 2.9 %collective-permute-start.3 = (f32[32,1536]{1,0:T(8,128)S(1)}, f32[32,1536]{1,0:T(8,128)S(1)}, u32[]{:S(2)}, u32[]{:S(2)}) collective-permute-start(f32[32,1536]{1,0:T(8,128)S(1)} %get-tuple-element.27), channel_id=1, source_target_pairs={{0,1},{1,0},{2,3},{3,2},{4,5},{5,4},{6,7},{7,6},{8,9},{9,8},{10,11... | collective-permute-start | bytes 589832 | tf_op jit(solution)/shard_map/ppermute | solution.py:394
  51.8 6.2 %collective-permute-start.4 = (f32[32,1536]{1,0:T(8,128)S(1)}, f32[32,1536]{1,0:T(8,128)S(1)}, u32[]{:S(2)}, u32[]{:S(2)}) collective-permute-start(f32[32,1536]{1,0:T(8,128)S(1)} %get-tuple-element.28), channel_id=1, source_target_pairs={{0,3},{1,2},{2,1},{3,0},{4,7},{5,6},{6,5},{7,4},{8,11},{9,10},{10,... | collective-permute-start | bytes 589832 | tf_op jit(solution)/shard_map/ppermute | solution.py:399
  58.0 4.2 %collective-permute-done.3.came_a = f32[32,1536]{1,0:T(8,128)S(1)} collective-permute-done((f32[32,1536]{1,0:T(8,128)S(1)}, f32[32,1536]{1,0:T(8,128)S(1)}, u32[]{:S(2)}, u32[]{:S(2)}) %collective-permute-start.3) | collective-permute-done | bytes 196640 | tf_op jit(solution)/shard_map/ppermute | solution.py:394
  62.2 3.1 %collective-permute-done.4.came_b = f32[32,1536]{1,0:T(8,128)S(1)} collective-permute-done((f32[32,1536]{1,0:T(8,128)S(1)}, f32[32,1536]{1,0:T(8,128)S(1)}, u32[]{:S(2)}, u32[]{:S(2)}) %collective-permute-start.4) | collective-permute-done | bytes 196640 | tf_op jit(solution)/shard_map/ppermute | solution.py:399
  65.3 0.0 collective-permute-done.5.came_y
  65.3 0.3 join.1
  65.7 25.0 %all_to_all.20.parts = f32[8,16,1536]{2,1,0:T(8,128)S(1)} all-to-all(f32[8,16,1536]{2,1,0:T(8,128)S(1)} %join.1), channel_id=1, replica_groups=mesh['x'=4,'zl'=2,'core'=2,'yh'=4,'yl'=2,'zhh'=2,'zhl'=2] {'yh','zhh'}, dimensions={0} | all-to-all | bytes 1572864 | tf_op jit(solution)/shard_map/all_to_all | solution.py:421
  90.7 0.3 spread.1
  91.0 30.8 %all_to_all.21.own = f32[8,16,1536]{2,1,0:T(8,128)S(1)} all-to-all(f32[8,16,1536]{2,1,0:T(8,128)S(1)} %spread.1), channel_id=1, replica_groups=mesh['x'=4,'zl'=2,'core'=2,'yh'=4,'yl'=2,'zhh'=2,'zhl'=2] {'yh','zhh'}, dimensions={0} | all-to-all | bytes 1572864 | tf_op jit(solution)/shard_map/all_to_all | solution.py:422
  121.8 0.2 part.1
  122.0 11.0 %collective-permute-start.8 = (f32[8,8,1536]{2,1,0:T(8,128)S(1)}, f32[8,8,1536]{2,1,0:T(8,128)S(1)}, u32[]{:S(2)}, u32[]{:S(2)}) collective-permute-start(f32[8,8,1536]{2,1,0:T(8,128)S(1)} %get-tuple-element.32), channel_id=1, source_target_pairs={{0,28},{4,8},{8,4},{12,16},{16,12},{20,24},{24,20},{28,0},{1,29},{... | collective-permute-start | bytes 1179656 | tf_op jit(solution)/shard_map/ppermute | solution.py:399
  133.1 1.9 collective-permute-start.6
  135.0 1.9 collective-permute-start.7
  136.9 6.5 %collective-permute-done.6.came_a.za0 = f32[4,8,1536]{2,1,0:T(8,128)S(1)} collective-permute-done((f32[4,8,1536]{2,1,0:T(8,128)S(1)}, f32[4,8,1536]{2,1,0:T(8,128)S(1)}, u32[]{:S(2)}, u32[]{:S(2)}) %collective-permute-start.6) | collective-permute-done | bytes 196640 | tf_op jit(solution)/shard_map/ppermute | solution.py:394
  143.5 1.2 collective-permute-done.7.came_b.zb0
  144.7 0.0 collective-permute-done.8.came_y.yb1
  144.7 1.8 peel.1
  146.5 1.9 collective-permute-start.9
  148.4 6.8 %collective-permute-start.10 = (f32[8,8,1536]{2,1,0:T(8,128)}, f32[8,8,1536]{2,1,0:T(8,128)}, u32[]{:S(2)}, u32[]{:S(2)}) collective-permute-start(f32[8,8,1536]{2,1,0:T(8,128)} %get-tuple-element.34), channel_id=1, source_target_pairs={{0,1},{1,0},{2,3},{3,2},{4,5},{5,4},{6,7},{7,6},{8,9},{9,8},{10,11... | collective-permute-start | bytes 1179656 | tf_op jit(solution)/shard_map/ppermute | solution.py:394
  155.3 1.9 collective-permute-start.11
  157.3 0.0 copy-done
  157.3 0.5 copy.7
  157.8 11.9 %collective-permute-done.10.za1 = f32[8,8,1536]{2,1,0:T(8,128)} collective-permute-done((f32[8,8,1536]{2,1,0:T(8,128)}, f32[8,8,1536]{2,1,0:T(8,128)}, u32[]{:S(2)}, u32[]{:S(2)}) %collective-permute-start.10) | collective-permute-done | bytes 393248 | tf_op jit(solution)/shard_map/ppermute | solution.py:394
  169.7 0.0 collective-permute-done.11.zb1
  169.7 0.0 collective-permute-done.9.ya0
  169.7 0.9 copy-done.2
  170.6 6.7 %scores.1 = (f32[1024,1536]{1,0:T(8,128)S(1)}, bf16[512,1536]{1,0:T(8,128)(2,1)S(1)}, f32[32,24,128]{2,1,0:T(8,128)S(1)}) custom-call(s32[5]{0:T(128)S(1)} %stack.23.at, f32[8,16,1536]{2,1,0:T(8,128)S(1)} %all_to_all.21.own, f32[4,8,1536]{2,1,0:T(8,128)S(1)} %collective-permute-done.6.came_a.za0, f32[4,8,1536]{2,1,0:T(8,128)S(1)} %copy-done.2, ...), custom_call_target="tpu_custom_call" | custom-call | tf_op jit(solution)/shard_map/scores/pallas_call | solution.py:272
  177.4 19.8 %all_to_all.22.stats = f32[32,24,128]{2,1,0:T(8,128)S(1)} all-to-all(f32[32,24,128]{2,1,0:T(8,128)S(1)} %get-tuple-element.36.own), channel_id=1, replica_groups=mesh['x'=4,'zl'=2,'core'=2,'yh'=4,'yl'=2,'zhh'=2,'zhl'=2] {'yh','yl','zh..., dimensions={0} | all-to-all | bytes 786432 | tf_op jit(solution)/shard_map/all_to_all | solution.py:439
  197.2 4.1 %totals.1 = (f32[8,264,128]{2,1,0:T(8,128)S(1)}, f32[8,264,128]{2,1,0:T(8,128)S(1)}) custom-call(s32[5]{0:T(128)S(1)} %stack.23.at, f32[32,24,128]{2,1,0:T(8,128)S(1)} %all_to_all.22.stats, f32[32,24,128]{2,1,0:T(8,128)S(1)} %get-tuple-element.36.own, f32[1024,1536]{1,0:T(8,128)S(1)} %get-tuple-element.37.powers, bf16[512,1536]{1,0:T(8,128)(2,1)S(1)} %get-tuple-element.38.rounded), custom_call_target="tpu_custom_call" | custom-call | tf_op jit(solution)/shard_map/totals/pallas_call | solution.py:341
  201.3 5.8 %collective-permute-start.12 = (f32[8,264,128]{2,1,0:T(8,128)S(1)}, f32[8,264,128]{2,1,0:T(8,128)S(1)}, u32[]{:S(2)}, u32[]{:S(2)}) collective-permute-start(f32[8,264,128]{2,1,0:T(8,128)S(1)} %get-tuple-element.40), channel_id=1, source_target_pairs={{0,32},{32,0},{1,33},{33,1},{2,34},{34,2},{3,35},{35,3},{4,36},{36... | collective-permute-start | bytes 3244040 | tf_op jit(solution)/shard_map/ppermute | solution.py:441
  207.1 2.3 %collective-permute-done.12 = f32[8,264,128]{2,1,0:T(8,128)S(1)} collective-permute-done((f32[8,264,128]{2,1,0:T(8,128)S(1)}, f32[8,264,128]{2,1,0:T(8,128)S(1)}, u32[]{:S(2)}, u32[]{:S(2)}) %collective-permute-start.12) | collective-permute-done | bytes 1081376 | tf_op jit(solution)/shard_map/ppermute | solution.py:441
  209.4 0.1 add.27
  209.5 19.2 %all_to_all.23.parts = f32[8,264,128]{2,1,0:T(8,128)S(1)} all-to-all(f32[8,264,128]{2,1,0:T(8,128)S(1)} %add.27), channel_id=1, replica_groups=mesh['x'=4,'zl'=2,'core'=2,'yh'=4,'yl'=2,'zhh'=2,'zhl'=2] {'x','zl'}, dimensions={0} | all-to-all | bytes 2162688 | tf_op jit(solution)/shard_map/all_to_all | solution.py:442
  228.7 1.3 final.1
  (10 shorter events, 0.0 us)
Async XLA Ops:
  0.0 0.7 copy-start.3
  0.7 7.0 %copy-start.4 = (s32[1,2,64]{2,1,0:T(2,128)S(1)}, s32[1,2,64]{2,1,0:T(2,128)}, u32[]{:S(2)}) copy-start(s32[1,2,64]{2,1,0:T(2,128)} %param.8) | copy-start | bytes 1540
  3.6 37.7 %collective-permute-start = (f32[128,1536]{1,0:T(8,128)S(1)}, f32[128,1536]{1,0:T(8,128)S(1)}, u32[]{:S(2)}, u32[]{:S(2)}) collective-permute-start(f32[128,1536]{1,0:T(8,128)S(1)} %project.6), channel_id=1, source_target_pairs={{0,4},{4,0},{8,12},{12,8},{16,20},{20,16},{24,28},{28,24},{1,5},{5... | collective-permute-start | bytes 2359304 | tf_op jit(solution)/shard_map/ppermute | solution.py:394
  11.4 22.3 %collective-permute-start.1 = (f32[64,1536]{1,0:T(8,128)}, f32[64,1536]{1,0:T(8,128)S(1)}, u32[]{:S(2)}, u32[]{:S(2)}) collective-permute-start(f32[64,1536]{1,0:T(8,128)} %get-tuple-element.23), channel_id=1, source_target_pairs={{0,1},{1,0},{2,3},{3,2},{4,5},{5,4},{6,7},{7,6},{8,9},{9,8},{10,11... | collective-permute-start | bytes 1179656 | tf_op jit(solution)/shard_map/ppermute | solution.py:394
  17.3 24.0 %collective-permute-start.2 = (f32[64,1536]{1,0:T(8,128)}, f32[64,1536]{1,0:T(8,128)}, u32[]{:S(2)}, u32[]{:S(2)}) collective-permute-start(f32[64,1536]{1,0:T(8,128)} %get-tuple-element.24), channel_id=1, source_target_pairs={{0,3},{1,2},{2,1},{3,0},{4,7},{5,6},{6,5},{7,4},{8,11},{9,10},{10,... | collective-permute-start | bytes 1179656 | tf_op jit(solution)/shard_map/ppermute | solution.py:399
  44.0 21.3 %collective-permute-start.5 = (f32[64,1536]{1,0:T(8,128)S(1)}, f32[64,1536]{1,0:T(8,128)S(1)}, u32[]{:S(2)}, u32[]{:S(2)}) collective-permute-start(f32[64,1536]{1,0:T(8,128)S(1)} %get-tuple-element.29), channel_id=1, source_target_pairs={{0,28},{4,8},{8,4},{12,16},{16,12},{20,24},{24,20},{28,0},{1,29},{... | collective-permute-start | bytes 1179656 | tf_op jit(solution)/shard_map/ppermute | solution.py:399
  48.9 13.3 %collective-permute-start.3 = (f32[32,1536]{1,0:T(8,128)S(1)}, f32[32,1536]{1,0:T(8,128)S(1)}, u32[]{:S(2)}, u32[]{:S(2)}) collective-permute-start(f32[32,1536]{1,0:T(8,128)S(1)} %get-tuple-element.27), channel_id=1, source_target_pairs={{0,1},{1,0},{2,3},{3,2},{4,5},{5,4},{6,7},{7,6},{8,9},{9,8},{10,11... | collective-permute-start | bytes 589832 | tf_op jit(solution)/shard_map/ppermute | solution.py:394
  51.8 13.5 %collective-permute-start.4 = (f32[32,1536]{1,0:T(8,128)S(1)}, f32[32,1536]{1,0:T(8,128)S(1)}, u32[]{:S(2)}, u32[]{:S(2)}) collective-permute-start(f32[32,1536]{1,0:T(8,128)S(1)} %get-tuple-element.28), channel_id=1, source_target_pairs={{0,3},{1,2},{2,1},{3,0},{4,7},{5,6},{6,5},{7,4},{8,11},{9,10},{10,... | collective-permute-start | bytes 589832 | tf_op jit(solution)/shard_map/ppermute | solution.py:399
  121.8 35.4 %copy-start.5 = (s32[1,2,768]{2,1,0:T(2,128)S(1)}, s32[1,2,768]{2,1,0:T(2,128)}, u32[]{:S(2)}) copy-start(s32[1,2,768]{2,1,0:T(2,128)} %param.9) | copy-start | bytes 18436
  121.8 35.5 %copy-start = (bf16[512,1024]{1,0:T(8,128)(2,1)S(1)}, bf16[512,1024]{1,0:T(8,128)(2,1)}, u32[]{:S(2)}) copy-start(bf16[512,1024]{1,0:T(8,128)(2,1)} %refs.1) | copy-start | bytes 3145732
  122.0 22.6 %collective-permute-start.8 = (f32[8,8,1536]{2,1,0:T(8,128)S(1)}, f32[8,8,1536]{2,1,0:T(8,128)S(1)}, u32[]{:S(2)}, u32[]{:S(2)}) collective-permute-start(f32[8,8,1536]{2,1,0:T(8,128)S(1)} %get-tuple-element.32), channel_id=1, source_target_pairs={{0,28},{4,8},{8,4},{12,16},{16,12},{20,24},{24,20},{28,0},{1,29},{... | collective-permute-start | bytes 1179656 | tf_op jit(solution)/shard_map/ppermute | solution.py:399
  133.1 10.4 %collective-permute-start.6 = (f32[4,8,1536]{2,1,0:T(8,128)S(1)}, f32[4,8,1536]{2,1,0:T(8,128)S(1)}, u32[]{:S(2)}, u32[]{:S(2)}) collective-permute-start(f32[4,8,1536]{2,1,0:T(8,128)S(1)} %get-tuple-element.30), channel_id=1, source_target_pairs={{0,1},{1,0},{2,3},{3,2},{4,5},{5,4},{6,7},{7,6},{8,9},{9,8},{10,11... | collective-permute-start | bytes 589832 | tf_op jit(solution)/shard_map/ppermute | solution.py:394
  135.0 9.7 %collective-permute-start.7 = (f32[4,8,1536]{2,1,0:T(8,128)S(1)}, f32[4,8,1536]{2,1,0:T(8,128)S(1)}, u32[]{:S(2)}, u32[]{:S(2)}) collective-permute-start(f32[4,8,1536]{2,1,0:T(8,128)S(1)} %get-tuple-element.31), channel_id=1, source_target_pairs={{0,3},{1,2},{2,1},{3,0},{4,7},{5,6},{6,5},{7,4},{8,11},{9,10},{10,... | collective-permute-start | bytes 589832 | tf_op jit(solution)/shard_map/ppermute | solution.py:399
  144.7 12.5 %copy-start.1 = (f32[4,8,1536]{2,1,0:T(8,128)}, f32[4,8,1536]{2,1,0:T(8,128)S(1)}, u32[]{:S(2)}) copy-start(f32[4,8,1536]{2,1,0:T(8,128)S(1)} %collective-permute-done.7.came_b.zb0) | copy-start | bytes 589828
  146.5 23.2 %collective-permute-start.9 = (f32[16,8,1536]{2,1,0:T(8,128)}, f32[16,8,1536]{2,1,0:T(8,128)}, u32[]{:S(2)}, u32[]{:S(2)}) collective-permute-start(f32[16,8,1536]{2,1,0:T(8,128)} %get-tuple-element.33), channel_id=1, source_target_pairs={{0,4},{4,0},{8,12},{12,8},{16,20},{20,16},{24,28},{28,24},{1,5},{5... | collective-permute-start | bytes 2359304 | tf_op jit(solution)/shard_map/ppermute | solution.py:394
  148.4 21.2 %collective-permute-start.10 = (f32[8,8,1536]{2,1,0:T(8,128)}, f32[8,8,1536]{2,1,0:T(8,128)}, u32[]{:S(2)}, u32[]{:S(2)}) collective-permute-start(f32[8,8,1536]{2,1,0:T(8,128)} %get-tuple-element.34), channel_id=1, source_target_pairs={{0,1},{1,0},{2,3},{3,2},{4,5},{5,4},{6,7},{7,6},{8,9},{9,8},{10,11... | collective-permute-start | bytes 1179656 | tf_op jit(solution)/shard_map/ppermute | solution.py:394
  155.3 14.4 %collective-permute-start.11 = (f32[8,8,1536]{2,1,0:T(8,128)}, f32[8,8,1536]{2,1,0:T(8,128)}, u32[]{:S(2)}, u32[]{:S(2)}) collective-permute-start(f32[8,8,1536]{2,1,0:T(8,128)} %get-tuple-element.35), channel_id=1, source_target_pairs={{0,3},{1,2},{2,1},{3,0},{4,7},{5,6},{6,5},{7,4},{8,11},{9,10},{10,... | collective-permute-start | bytes 1179656 | tf_op jit(solution)/shard_map/ppermute | solution.py:399
  169.7 0.9 copy-start.2
  201.3 8.1 %collective-permute-start.12 = (f32[8,264,128]{2,1,0:T(8,128)S(1)}, f32[8,264,128]{2,1,0:T(8,128)S(1)}, u32[]{:S(2)}, u32[]{:S(2)}) collective-permute-start(f32[8,264,128]{2,1,0:T(8,128)S(1)} %get-tuple-element.40), channel_id=1, source_target_pairs={{0,32},{32,0},{1,33},{33,1},{2,34},{34,2},{3,35},{35,3},{4,36},{36... | collective-permute-start | bytes 3244040 | tf_op jit(solution)/shard_map/ppermute | solution.py:441

commit v5 on v2

v5 whole, which is shorter than its diff:
```python
import functools

import jax
import jax.numpy as jnp
from jax import lax
from jax.experimental import pallas as pl
from jax.experimental.pallas import tpu as pltpu
from jax.sharding import Mesh, PartitionSpec as P

OBLOCK = 256
PRIOR_INCREMENT = 3.0
GRP = ("x", "zl", "core")
RING = ("yh", "yl")
MEM = RING + ("zh",)
ALIKE = ("yh", "zh")
PEERS = ("x", "zl")
LANES = 128
BIG = pltpu.CompilerParams(vmem_limit_bytes=28 << 20)
SMALL = pltpu.CompilerParams(vmem_limit_bytes=14 << 20)
LAST = (((1,), (1,)), ((), ()))


def project_kernel(batch, at, inject, images, basis, phantom, *rest):
    outs, (pixels_in, columns, ghost, sems) = rest[:-4], rest[-4:]
    steps, width = pixels_in.shape[:2]
    count = columns.shape[2]
    start = batch * steps * width
    loads = [
        pltpu.make_async_copy(
            basis.at[:, pl.ds(pl.multiple_of(at[j] * count, count), count)],
            columns.at[j],
            sems.at[j],
        )
        for j in range(2)
    ]
    loads.append(pltpu.make_async_copy(phantom, ghost, sems.at[2]))
    for k in range(steps):
        source = images.at[pl.ds(start + k * width, width), :]
        loads.append(pltpu.make_async_copy(source, pixels_in.at[k], sems.at[3 + k]))
    for load in loads:
        load.start()
    hits = []
    for k in range(steps):
        position = k * width + lax.broadcasted_iota(jnp.int32, (1, width), 1)
        hit = jnp.zeros((1, width), jnp.float32)
        for i in range(inject.shape[1]):
            hit = jnp.where(position == inject[batch, i], 1.0, hit)
        hits.append(hit)
    for load in loads[:3]:
        load.wait()
    spread = jnp.broadcast_to(ghost[...], (LANES, ghost.shape[1]))
    mine = [columns[j].T for j in range(2)]
    extra = [
        lax.dot_general(m, spread, LAST, preferred_element_type=jnp.float32) for m in mine
    ]
    for k in range(steps):
        loads[3 + k].wait()
        for j, out in enumerate(outs):
            plain = lax.dot_general(
                mine[j], pixels_in[k], LAST, preferred_element_type=jnp.float32
            )
            for c in range(width // LANES):
                cut = slice(c * LANES, (c + 1) * LANES)
                out[:, k * width + c * LANES : k * width + (c + 1) * LANES] = (
                    plain[:, cut] + extra[j] * hits[k][:, cut]
                )


def projected(at, batch, inject, images, basis, phantom):
    pixels = images.shape[1]
    rows = images.shape[0] // inject.shape[0]
    steps = 2
    count = basis.shape[1] // 4
    out = jax.ShapeDtypeStruct((count, rows), jnp.float32)
    images, basis, phantom = (
        pltpu.with_memory_space_constraint(x, pltpu.HBM) for x in (images, basis, phantom)
    )
    found = pl.pallas_call(
        functools.partial(project_kernel, batch),
        grid_spec=pltpu.PrefetchScalarGridSpec(
            num_scalar_prefetch=2,
            grid=(1,),
            in_specs=[pl.BlockSpec(memory_space=pltpu.HBM)] * 3,
            out_specs=[pl.BlockSpec(out.shape, lambda j, at, s: (0, 0))] * 2,
            scratch_shapes=[
                pltpu.VMEM((steps, rows // steps, pixels), images.dtype),
                pltpu.VMEM((2, pixels, count), basis.dtype),
                pltpu.VMEM((1, pixels), phantom.dtype),
                pltpu.SemaphoreType.DMA((steps + 3,)),
            ],
        ),
        out_shape=[out, out],
        compiler_params=SMALL,
        name="project",
    )(at, inject, images, basis, phantom)
    return tuple(found)


def by_columns(kernel, name, operands, shapes):
    rows = operands[0].shape[-1]
    width = rows // 3

    def spec(shape):
        head = tuple(shape[:-1])
        zeros = (0,) * len(head)
        return pl.BlockSpec((*head, width), lambda j: (*zeros, j))

    shapes = [(*shape, rows) for shape in shapes]
    return pl.pallas_call(
        kernel,
        grid=(rows // width,),
        in_specs=[spec(x.shape) for x in operands],
        out_specs=[spec(shape) for shape in shapes],
        out_shape=[jax.ShapeDtypeStruct(shape, jnp.float32) for shape in shapes],
        compiler_params=SMALL,
        name=name,
    )(*operands)


def join_kernel(keep_a, keep_b, came_a, came_b, out):
    for m in range(out.shape[0]):
        cut = slice(m * 8, (m + 1) * 8)
        out[m, :8, :] = keep_a[cut, :] + came_a[cut, :]
        out[m, 8:, :] = keep_b[cut, :] + came_b[cut, :]


def total_of(parts):
    total = parts[0]
    for part in parts[1:]:
        total = total + part
    return total


def middle_kernel(parts, keep_a, keep_b, came_a, came_b, out):
    total = total_of([parts[m] for m in range(parts.shape[0])])
    for m in range(out.shape[0]):
        cut = slice(m * 8, (m + 1) * 8)
        out[m, 0] = total
        out[m, 1, :8, :] = keep_a[cut, :] + came_a[cut, :]
        out[m, 1, 8:, :] = keep_b[cut, :] + came_b[cut, :]


def turn_kernel(both, copies, out_a, out_b):
    total = total_of([both[m, 1] for m in range(both.shape[0])])
    for m in range(both.shape[0]):
        copies[m] = total
        out_a[m] = both[m, 0, :8, :]
        out_b[m] = both[m, 0, 8:, :]


def part_kernel(own, out_a, out_b):
    for m in range(own.shape[0]):
        out_a[m] = own[m, :8, :]
        out_b[m] = own[m, 8:, :]


def score_kernel(at, own_a, own_b, came_a, came_b, prior, refs_t, past, powers, rounded, stats):
    step = pl.program_id(0)
    rows = prior.shape[1]
    orient, eigen = refs_t.shape
    high = eigen // 4
    before = stats.shape[1] - 2 * pl.num_programs(0) * (rows // LANES)
    lines = (stats.shape[1] - before) // 2

    if before:

        @pl.when(step == 0)
        def _():
            stats[:, :before, :] = past[:, :before, :]

    for base, held in ((0, (own_a, came_a)), (2 * high, (own_b, came_b))):
        for side, source in zip((at[0], 1 - at[0]), held):
            place = pl.multiple_of(base + high * side, high)
            rounded[pl.ds(place, high), :] = source[...].reshape(high, rows).astype(jnp.bfloat16)
    scores = jnp.dot(refs_t[...], rounded[...], preferred_element_type=jnp.float32)
    block = prior[...] - at[1] * (orient // OBLOCK)
    parts = [
        scores[k * OBLOCK : (k + 1) * OBLOCK] + jnp.where(block == k, PRIOR_INCREMENT, 0.0)
        for k in range(orient // OBLOCK)
    ]
    tops = [jnp.max(part, axis=0, keepdims=True) for part in parts]
    top = tops[0]
    for other in tops[1:]:
        top = jnp.maximum(top, other)
    total = jnp.zeros_like(top)
    for k, part in enumerate(parts):
        power = jnp.exp(part - top)
        powers[k * OBLOCK : (k + 1) * OBLOCK, :] = power
        total = total + jnp.sum(power, axis=0, keepdims=True)
    for h in range(rows // LANES):
        line = before + step * (rows // LANES) + h
        cut = slice(h * LANES, (h + 1) * LANES)
        shape = (stats.shape[0], 1, LANES)
        stats[:, pl.ds(line, 1), :] = jnp.broadcast_to(top[None, :, cut], shape)
        stats[:, pl.ds(lines + line, 1), :] = jnp.broadcast_to(total[None, :, cut], shape)


def scores_of(at, own, came, prior, refs_t, past, members):
    rows = prior.shape[1]
    orient, eigen = refs_t.shape
    width = 256
    group = own[0].shape[0]
    lines = 2 * rows // LANES
    if past is None:
        past = jnp.zeros((1, 1, LANES), jnp.float32)
    else:
        lines += past.shape[1]
    piece = pl.BlockSpec((group, 8, width), lambda j, at: (0, 0, j))
    return pl.pallas_call(
        score_kernel,
        grid_spec=pltpu.PrefetchScalarGridSpec(
            num_scalar_prefetch=1,
            grid=(rows // width,),
            in_specs=[piece] * 4
            + [
                pl.BlockSpec((1, width), lambda j, at: (0, j)),
                pl.BlockSpec((orient, eigen), lambda j, at: (0, 0)),
                pl.BlockSpec(past.shape, lambda j, at: (0, 0, 0)),
            ],
            out_specs=[
                pl.BlockSpec((orient, width), lambda j, at: (0, j)),
                pl.BlockSpec((eigen, width), lambda j, at: (0, j)),
                pl.BlockSpec((members, lines, LANES), lambda j, at: (0, 0, 0)),
            ],
        ),
        out_shape=[
            jax.ShapeDtypeStruct((orient, rows), jnp.float32),
            jax.ShapeDtypeStruct((eigen, rows), jnp.bfloat16),
            jax.ShapeDtypeStruct((members, lines, LANES), jnp.float32),
        ],
        compiler_params=BIG,
        name="scores",
    )(at, *own, *came, prior, refs_t, past)


def total_kernel(at, stats, own, powers_0, powers_1, rounded_0, rounded_1, keep, send, factor):
    step = pl.program_id(0)
    eigen, rows = rounded_0.shape
    width = powers_0.shape[0]
    peers = keep.shape[0]
    share = eigen // (2 * peers)
    lines = rows // LANES
    body = keep.shape[1] - keep.shape[1] % share

    @pl.when(step == 0)
    def _():
        for b in range(2):
            low, high = 2 * b * lines, (2 * b + 1) * lines
            tops = stats[:, low:high, :]
            top = jnp.max(tops, axis=0)
            total = jnp.sum(stats[:, high : high + lines, :] * jnp.exp(tops - top[None]), axis=0)
            scale = jnp.exp(own[0, low:high, :] - top) / total
            for k in range(lines):
                factor[b : b + 1, k * LANES : (k + 1) * LANES] = scale[k : k + 1, :]

    totals, masses = 0.0, 0.0
    ones = jnp.ones((16, rows), jnp.bfloat16)
    for b, (powers, rounded) in enumerate(((powers_0, rounded_0), (powers_1, rounded_1))):
        weights = (powers[...] * factor[b : b + 1, :]).astype(jnp.bfloat16)
        totals += lax.dot_general(rounded[...], weights, LAST, preferred_element_type=jnp.float32)
        masses += lax.dot_general(ones, weights, LAST, preferred_element_type=jnp.float32)
    first = at[2] == 0
    for h in range(width // LANES):
        column = step * (width // LANES) + h
        cut = slice(h * LANES, (h + 1) * LANES)
        place = pl.ds(pl.multiple_of(column * share, share), share)
        for q in range(peers):
            even = totals[2 * q * share : (2 * q + 1) * share, cut]
            odd = totals[(2 * q + 1) * share : (2 * q + 2) * share, cut]
            keep[q, place, :] = jnp.where(first, even, odd)
            send[q, place, :] = jnp.where(first, odd, even)
        mass = jnp.broadcast_to(masses[None, 0:1, cut], (peers, 1, LANES))
        keep[:, pl.ds(body + column, 1), :] = mass
        send[:, pl.ds(body + column, 1), :] = mass


def totals_of(at, stats, sent, powers, rounded, peers):
    eigen, rows = rounded[0].shape
    orient = powers[0].shape[0]
    width = 256
    deep = (eigen // (2 * peers) + 1) * (orient // LANES)
    out = jax.ShapeDtypeStruct((peers, deep, LANES), jnp.float32)
    return pl.pallas_call(
        total_kernel,
        grid_spec=pltpu.PrefetchScalarGridSpec(
            num_scalar_prefetch=1,
            grid=(orient // width,),
            in_specs=[
                pl.BlockSpec(stats.shape, lambda j, at: (0, 0, 0)),
                pl.BlockSpec((1, *sent.shape[1:]), lambda j, at: (0, 0, 0)),
            ]
            + [pl.BlockSpec((width, rows), lambda j, at: (j, 0))] * 2
            + [pl.BlockSpec((eigen, rows), lambda j, at: (0, 0))] * 2,
            out_specs=[pl.BlockSpec((peers, deep, LANES), lambda j, at: (0, 0, 0))] * 2,
            scratch_shapes=[pltpu.VMEM((2, rows), jnp.float32)],
        ),
        out_shape=[out, out],
        compiler_params=BIG,
        name="totals",
    )(at, stats, sent, *powers, *rounded)


def final_kernel(at, parts, refs, out):
    share, orient = out.shape
    both = parts[0]
    for d in range(1, parts.shape[0]):
        both = both + parts[d]
    body = share * (orient // LANES)
    for k in range(orient // LANES):
        cut = slice(k * LANES, (k + 1) * LANES)
        above = both[k * share : (k + 1) * share] + refs[:, cut].astype(jnp.float32)
        out[:, cut] = above / (both[body + k : body + k + 1] + 1.0)


def final_of(at, parts, refs):
    eigen, orient = refs.shape
    share = eigen // (2 * parts.shape[0])
    return pl.pallas_call(
        final_kernel,
        grid_spec=pltpu.PrefetchScalarGridSpec(
            num_scalar_prefetch=1,
            grid=(1,),
            in_specs=[
                pl.BlockSpec(parts.shape, lambda j, at: (0, 0, 0)),
                pl.BlockSpec((share, orient), lambda j, at: (at[3], 0)),
            ],
            out_specs=pl.BlockSpec((share, orient), lambda j, at: (0, 0)),
        ),
        out_shape=jax.ShapeDtypeStruct((share, orient), jnp.float32),
        compiler_params=SMALL,
        name="final",
    )(at, parts, refs)


def swapped(pair, axis):
    size = lax.axis_size(axis)
    with_a = [(i, i ^ 1) for i in range(size)]
    with_b = [(i, (i + (1 if i % 2 else -1)) % size) for i in range(size)]
    return tuple(lax.ppermute(x, axis, p) for x, p in zip(pair, (with_a, with_b)))


def shards(images, phantom, inject_rows, prior_blocks, basis, refs):
    batches, particles = images.shape[1:3]
    flat = images[0].reshape(batches * particles, basis.shape[0])
    p = lax.axis_index("yl").astype(jnp.int32)
    at = jnp.stack(
        [p]
        + [lax.axis_index(axis).astype(jnp.int32) for axis in (MEM, "core", GRP)]
    )

    def block(side, batch):
        columns = jnp.stack([side, 2 + side])
        return projected(columns, batch, inject_rows[0], flat, basis, phantom)

    def exchange(x):
        return lax.all_to_all(x, ALIKE, 0, 0, tiled=True)

    size = lax.axis_size(ALIKE)
    came_0 = swapped(block(1 - p, 0), RING)
    (parts,) = by_columns(join_kernel, "join", (*block(p, 0), *came_0), [(size, 16)])
    came_1 = swapped(block(1 - p, 1), RING)
    (both,) = by_columns(
        middle_kernel, "middle", (exchange(parts), *block(p, 1), *came_1), [(size, 2, 16)]
    )
    copies, *own_0 = by_columns(
        turn_kernel, "turn", (exchange(both),), [(size, 16), (size, 8), (size, 8)]
    )
    far_0 = swapped(own_0, RING)
    own_1 = by_columns(part_kernel, "part", (exchange(copies),), [(size, 8)] * 2)
    far_1 = swapped(own_1, RING)
    refs_t = refs.T
    members = lax.axis_size(MEM)
    powers_0, rounded_0, sent = scores_of(
        at, own_0, far_0, prior_blocks[0, :1], refs_t, None, members
    )
    powers_1, rounded_1, sent = scores_of(
        at, own_1, far_1, prior_blocks[0, 1:], refs_t, sent, members
    )
    stats = lax.all_to_all(sent, MEM, 0, 0, tiled=True)
    keep, send = totals_of(
        at, stats, sent, (powers_0, powers_1), (rounded_0, rounded_1), lax.axis_size(PEERS)
    )
    parts = keep + lax.ppermute(send, "core", [(0, 1), (1, 0)])
    parts = lax.all_to_all(parts, PEERS, 0, 0, tiled=True)
    return final_of(at, parts, refs)


def solution(mesh):
    fine = Mesh(mesh.devices.reshape(4, 2, 2, 4, 2, 4), GRP + MEM)
    placed = (
        P(GRP, None, None, MEM),
        P(GRP, MEM),
        P(GRP, None, None),
        P(GRP, None, None),
        P(MEM, None),
        P(None, MEM),
    )
    return jax.shard_map(
        shards, mesh=fine, in_specs=placed, out_specs=P(GRP, MEM), check_vma=False
    )
```

time: 228 us -> 232 us (1.018)
  blocking collectives: 148 us -> 78.9 us
  starting transfers between devices: 23 us -> 88.6 us
  Pallas kernels: 17.9 us -> 29.2 us
  local copies, waits for them, and re-layouts: 7.79 us -> 1.24 us
    all_to_all x2 -> x1, blocking collectives: 108 us -> 42.5 us  [exchange(): return lax.all_to_all(x, ALIKE, 0, 0, tiled=True)]
    ppermute x4 -> x8, starting transfers between devices: 17.3 us -> 53.6 us  [swapped(): lax.ppermute(x, axis, p)]
    all_to_all x0 -> x2, starting transfers between devices: none -> 28.5 us  [exchange(): return lax.all_to_all(x, ALIKE, 0, 0, tiled=True)]
    pallas_call x4 -> x8, Pallas kernels: 6.19 us -> 15.7 us  [the longest x4 10.4 us: projected(): pl.pallas_call(functools.partial(project_kernel, batch), grid_spec=pltpu....]
    all_to_all x0 -> x2, waiting for transfers between devices: none -> 3.27 us  [exchange(): return lax.all_to_all(x, ALIKE, 0, 0, tiled=True)]
    ppermute x4 -> x8, waiting for transfers between devices: 27.9 us -> 26 us  [swapped(): lax.ppermute(x, axis, p)]
    pallas_call x1 -> x2, Pallas kernels: 6.42 us -> 8.18 us  [scores_of(): pl.pallas_call(score_kernel, grid_spec=pltpu.PrefetchScalarGridSpec(num_s...]
  transfers between devices with their start and end apart: 5 -> 11, of which waited for: 5 -> 7; matrix products, arithmetic and copies ran while one was open for 1% -> 0% of each run, Pallas kernels for 1% -> 6%
where the time goes in v5:
time: 232 us; the launch traced here: 230 us
  starting transfers between devices  88.6 us (38%)
  blocking collectives  78.9 us (34%)
  waiting for transfers between devices  31.6 us (14%)
  Pallas kernels  29.2 us (13%)
    ppermute x8, starting transfers between devices, swapped(): lax.ppermute(x, axis, p)  53.6 us
    all_to_all x1, blocking collectives, exchange(): return lax.all_to_all(x, ALIKE, 0, 0, tiled=True)  42.5 us
    all_to_all x2, starting transfers between devices, exchange(): return lax.all_to_all(x, ALIKE, 0, 0, tiled=True)  28.5 us
    ppermute x8, waiting for transfers between devices, swapped(): lax.ppermute(x, axis, p)  26 us
    all_to_all x1, blocking collectives, shards(): parts = lax.all_to_all(parts, PEERS, 0, 0, tiled=True)  20.5 us
    all_to_all x1, blocking collectives, shards(): stats = lax.all_to_all(sent, MEM, 0, 0, tiled=True)  16 us
    pallas_call x4, Pallas kernels, projected(): pl.pallas_call(functools.partial(project_kernel, batch), grid_spec=pltpu....  10.4 us
    pallas_call x2, Pallas kernels, scores_of(): pl.pallas_call(score_kernel, grid_spec=pltpu.PrefetchScalarGridSpec(num_s...  8.18 us
  transfers between devices with their start and end apart: 11, of which 7 were waited for; matrix products, arithmetic and copies ran while one was open for 0% of the time, Pallas kernels for 6%

profile of v5, /device:TPU:1, one launch (start us, length us, event | category | flops | bytes accessed | tf_op | source)
XLA Modules:
  0.0 230.1 jit_solution(10036804817060733345)
XLA Ops:
  0.0 0.0 copy-start.2
  0.0 0.1 pad_add_fusion.2.at
  0.1 0.7 copy-done.1
  0.8 2.6 %project.5 = (f32[128,768]{1,0:T(8,128)S(1)}, f32[128,768]{1,0:T(8,128)S(1)}) custom-call(s32[2]{0:T(128)S(1)} %pad_add_fusion.2.at, s32[2,64]{1,0:T(2,128)S(1)} %bitcast.16, bf16[1536,512]{1,0:T(8,128)(2,1)} %bitcast.20, bf16[512,512]{1,0:T(8,128)(2,1)} %basis.7, bf16[1,512]{1,0:T(2,128)(2,1)} %phantom.7), custom_call_target="tpu_custom_call" | custom-call | tf_op jit(solution)/shard_map/project/pallas_call | solution.py:78
  3.4 4.0 %collective-permute-start = (f32[128,768]{1,0:T(8,128)S(1)}, f32[128,768]{1,0:T(8,128)S(1)}, u32[]{:S(2)}, u32[]{:S(2)}) collective-permute-start(f32[128,768]{1,0:T(8,128)S(1)} %get-tuple-element.28), channel_id=1, source_target_pairs={{0,4},{4,0},{8,12},{12,8},{16,20},{20,16},{24,28},{28,24},{1,5},{5... | collective-permute-start | bytes 1179656 | tf_op jit(solution)/shard_map/ppermute | solution.py:339
  7.4 4.9 %collective-permute-start.1 = (f32[128,768]{1,0:T(8,128)S(1)}, f32[128,768]{1,0:T(8,128)S(1)}, u32[]{:S(2)}, u32[]{:S(2)}) collective-permute-start(f32[128,768]{1,0:T(8,128)S(1)} %get-tuple-element.29), channel_id=1, source_target_pairs={{0,28},{4,8},{8,4},{12,16},{16,12},{20,24},{24,20},{28,0},{1,29},{... | collective-permute-start | bytes 1179656 | tf_op jit(solution)/shard_map/ppermute | solution.py:339
  12.3 0.1 pad_add_fusion.1.at
  12.4 0.0 copy-done.2
  12.4 2.6 %project.4 = (f32[128,768]{1,0:T(8,128)S(1)}, f32[128,768]{1,0:T(8,128)S(1)}) custom-call(s32[2]{0:T(128)S(1)} %pad_add_fusion.1.at, s32[2,64]{1,0:T(2,128)S(1)} %bitcast.17, bf16[1536,512]{1,0:T(8,128)(2,1)} %bitcast.21, bf16[512,512]{1,0:T(8,128)(2,1)} %basis.7, bf16[1,512]{1,0:T(2,128)(2,1)} %phantom.7), custom_call_target="tpu_custom_call" | custom-call | tf_op jit(solution)/shard_map/project/pallas_call | solution.py:78
  15.0 0.0 collective-permute-done.came_a
  15.0 4.1 %collective-permute-done.1.came_b = f32[128,768]{1,0:T(8,128)S(1)} collective-permute-done((f32[128,768]{1,0:T(8,128)S(1)}, f32[128,768]{1,0:T(8,128)S(1)}, u32[]{:S(2)}, u32[]{:S(2)}) %collective-permute-start.1) | collective-permute-done | bytes 393248 | tf_op jit(solution)/shard_map/ppermute | solution.py:339
  19.1 1.6 join.1
  20.8 15.5 %all-to-all-start = ((f32[16,16,768]{2,1,0:T(8,128)}), f32[16,16,768]{2,1,0:T(8,128)S(1)}, u32[]{:S(2)}, u32[]{:S(2)}) async-start(f32[16,16,768]{2,1,0:T(8,128)} %join.1), calls=%async_computation | async-start | bytes 1572864 | tf_op jit(solution)/shard_map/all_to_all | solution.py:356
  36.3 2.6 %project.7 = (f32[128,768]{1,0:T(8,128)S(1)}, f32[128,768]{1,0:T(8,128)S(1)}) custom-call(s32[2]{0:T(128)S(1)} %pad_add_fusion.2.at, s32[2,64]{1,0:T(2,128)S(1)} %bitcast.18, bf16[1536,512]{1,0:T(8,128)(2,1)} %bitcast.22, bf16[512,512]{1,0:T(8,128)(2,1)} %basis.7, bf16[1,512]{1,0:T(2,128)(2,1)} %phantom.7), custom_call_target="tpu_custom_call" | custom-call | tf_op jit(solution)/shard_map/project/pallas_call | solution.py:78
  38.9 1.9 collective-permute-start.2
  40.8 5.7 %collective-permute-start.3 = (f32[128,768]{1,0:T(8,128)S(1)}, f32[128,768]{1,0:T(8,128)S(1)}, u32[]{:S(2)}, u32[]{:S(2)}) collective-permute-start(f32[128,768]{1,0:T(8,128)S(1)} %get-tuple-element.33), channel_id=1, source_target_pairs={{0,28},{4,8},{8,4},{12,16},{16,12},{20,24},{24,20},{28,0},{1,29},{... | collective-permute-start | bytes 1179656 | tf_op jit(solution)/shard_map/ppermute | solution.py:339
  46.5 2.6 %project.6 = (f32[128,768]{1,0:T(8,128)S(1)}, f32[128,768]{1,0:T(8,128)S(1)}) custom-call(s32[2]{0:T(128)S(1)} %pad_add_fusion.1.at, s32[2,64]{1,0:T(2,128)S(1)} %bitcast.19, bf16[1536,512]{1,0:T(8,128)(2,1)} %bitcast.23, bf16[512,512]{1,0:T(8,128)(2,1)} %basis.7, bf16[1,512]{1,0:T(2,128)(2,1)} %phantom.7), custom_call_target="tpu_custom_call" | custom-call | tf_op jit(solution)/shard_map/project/pallas_call | solution.py:78
  49.1 11.5 %collective-permute-done.2.came_a = f32[128,768]{1,0:T(8,128)S(1)} collective-permute-done((f32[128,768]{1,0:T(8,128)S(1)}, f32[128,768]{1,0:T(8,128)S(1)}, u32[]{:S(2)}, u32[]{:S(2)}) %collective-permute-start.2) | collective-permute-done | bytes 393248 | tf_op jit(solution)/shard_map/ppermute | solution.py:339
  60.6 4.2 %collective-permute-done.3.came_b = f32[128,768]{1,0:T(8,128)S(1)} collective-permute-done((f32[128,768]{1,0:T(8,128)S(1)}, f32[128,768]{1,0:T(8,128)S(1)}, u32[]{:S(2)}, u32[]{:S(2)}) %collective-permute-start.3) | collective-permute-done | bytes 393248 | tf_op jit(solution)/shard_map/ppermute | solution.py:339
  64.8 0.0 all-to-all-done.parts
  64.8 0.5 middle.1
  65.3 42.5 %all_to_all.25.both = f32[16,2,16,768]{3,2,1,0:T(8,128)S(1)} all-to-all(f32[16,2,16,768]{3,2,1,0:T(8,128)S(1)} %middle.1), channel_id=1, replica_groups=mesh['x'=4,'zl'=2,'core'=2,'yh'=4,'yl'=2,'zh'=4] {'yh','zh'}, dimensions={0} | all-to-all | bytes 3145728 | tf_op jit(solution)/shard_map/all_to_all | solution.py:356
  107.8 1.7 turn.1
  109.4 13.0 %all-to-all-start.2 = ((f32[16,16,768]{2,1,0:T(8,128)}), f32[16,16,768]{2,1,0:T(8,128)S(1)}, u32[]{:S(2)}, u32[]{:S(2)}) async-start(f32[16,16,768]{2,1,0:T(8,128)} %get-tuple-element.34), calls=%async_computation.2 | async-start | bytes 1572864 | tf_op jit(solution)/shard_map/all_to_all | solution.py:356
  122.4 0.0 copy-start.3
  122.5 11.3 %collective-permute-start.6 = (f32[16,8,768]{2,1,0:T(8,128)S(1)}, f32[16,8,768]{2,1,0:T(8,128)}, u32[]{:S(2)}, u32[]{:S(2)}) collective-permute-start(f32[16,8,768]{2,1,0:T(8,128)S(1)} %get-tuple-element.37.own_a), channel_id=1, source_target_pairs={{0,4},{4,0},{8,12},{12,8},{16,20},{20,16},{24,28},{28,24},{1,5},{5... | collective-permute-start | bytes 1179656 | tf_op jit(solution)/shard_map/ppermute | solution.py:339
  133.7 4.2 %collective-permute-start.7 = (f32[16,8,768]{2,1,0:T(8,128)S(1)}, f32[16,8,768]{2,1,0:T(8,128)}, u32[]{:S(2)}, u32[]{:S(2)}) collective-permute-start(f32[16,8,768]{2,1,0:T(8,128)S(1)} %get-tuple-element.38.own_b), channel_id=1, source_target_pairs={{0,28},{4,8},{8,4},{12,16},{16,12},{20,24},{24,20},{28,0},{1,29},{... | collective-permute-start | bytes 1179656 | tf_op jit(solution)/shard_map/ppermute | solution.py:339
  137.9 3.3 %all-to-all-done.2.own = f32[16,16,768]{2,1,0:T(8,128)S(1)} async-done(((f32[16,16,768]{2,1,0:T(8,128)}), f32[16,16,768]{2,1,0:T(8,128)S(1)}, u32[]{:S(2)}, u32[]{:S(2)}) %all-to-all-start.2) | async-done | bytes 786464 | tf_op jit(solution)/shard_map/all_to_all | solution.py:356
  141.2 1.5 part.1
  142.7 19.7 %collective-permute-start.4 = (f32[16,8,768]{2,1,0:T(8,128)S(1)}, f32[16,8,768]{2,1,0:T(8,128)}, u32[]{:S(2)}, u32[]{:S(2)}) collective-permute-start(f32[16,8,768]{2,1,0:T(8,128)S(1)} %get-tuple-element.35.own_a), channel_id=1, source_target_pairs={{0,4},{4,0},{8,12},{12,8},{16,20},{20,16},{24,28},{28,24},{1,5},{5... | collective-permute-start | bytes 1179656 | tf_op jit(solution)/shard_map/ppermute | solution.py:339
  162.4 1.9 collective-permute-start.5
  164.3 0.0 copy-done
  164.3 0.5 copy.7
  164.9 0.1 pad_add_fusion.at
  165.0 0.0 copy-done.3
  165.0 0.0 collective-permute-done.6.came_a
  165.0 0.0 collective-permute-done.7.came_b
  165.0 4.0 %scores.2 = (f32[1024,768]{1,0:T(8,128)S(1)}, bf16[512,768]{1,0:T(8,128)(2,1)S(1)}, f32[32,12,128]{2,1,0:T(8,128)S(1)}) custom-call(s32[4]{0:T(128)S(1)} %pad_add_fusion.at, f32[16,8,768]{2,1,0:T(8,128)S(1)} %get-tuple-element.37.own_a, f32[16,8,768]{2,1,0:T(8,128)S(1)} %get-tuple-element.38.own_b, f32[16,8,768]{2,1,0:T(8,128)} %collective-permute-done.6.came_a, ...), custom_call_target="tpu_custom_call" | custom-call | tf_op jit(solution)/shard_map/scores/pallas_call | solution.py:209
  169.0 2.0 collective-permute-done.4.came_a
  171.1 4.2 %collective-permute-done.5.came_b = f32[16,8,768]{2,1,0:T(8,128)} collective-permute-done((f32[16,8,768]{2,1,0:T(8,128)}, f32[16,8,768]{2,1,0:T(8,128)}, u32[]{:S(2)}, u32[]{:S(2)}) %collective-permute-start.5) | collective-permute-done | bytes 393248 | tf_op jit(solution)/shard_map/ppermute | solution.py:339
  175.2 4.2 %scores.3 = (f32[1024,768]{1,0:T(8,128)S(1)}, bf16[512,768]{1,0:T(8,128)(2,1)S(1)}, f32[32,24,128]{2,1,0:T(8,128)S(1)}) custom-call(s32[4]{0:T(128)S(1)} %pad_add_fusion.at, f32[16,8,768]{2,1,0:T(8,128)S(1)} %get-tuple-element.35.own_a, f32[16,8,768]{2,1,0:T(8,128)} %get-tuple-element.36.own_b, f32[16,8,768]{2,1,0:T(8,128)} %collective-permute-done.4.came_a, ...), custom_call_target="tpu_custom_call" | custom-call | tf_op jit(solution)/shard_map/scores/pallas_call | solution.py:209
  179.4 16.0 %all_to_all.26.stats = f32[32,24,128]{2,1,0:T(8,128)S(1)} all-to-all(f32[32,24,128]{2,1,0:T(8,128)S(1)} %get-tuple-element.40.own), channel_id=1, replica_groups=mesh['x'=4,'zl'=2,'core'=2,'yh'=4,'yl'=2,'zh'=4] {'yh','yl','zh'}, dimensions={0} | all-to-all | bytes 786432 | tf_op jit(solution)/shard_map/all_to_all | solution.py:379
  195.4 4.1 %totals.1 = (f32[8,264,128]{2,1,0:T(8,128)S(1)}, f32[8,264,128]{2,1,0:T(8,128)S(1)}) custom-call(s32[4]{0:T(128)S(1)} %pad_add_fusion.at, f32[32,24,128]{2,1,0:T(8,128)S(1)} %all_to_all.26.stats, f32[32,24,128]{2,1,0:T(8,128)S(1)} %get-tuple-element.40.own, f32[1024,768]{1,0:T(8,128)S(1)} %get-tuple-element.41.powers_0, ...), custom_call_target="tpu_custom_call" | custom-call | tf_op jit(solution)/shard_map/totals/pallas_call | solution.py:283
  199.5 6.5 %collective-permute-start.8 = (f32[8,264,128]{2,1,0:T(8,128)S(1)}, f32[8,264,128]{2,1,0:T(8,128)S(1)}, u32[]{:S(2)}, u32[]{:S(2)}) collective-permute-start(f32[8,264,128]{2,1,0:T(8,128)S(1)} %get-tuple-element.46), channel_id=1, source_target_pairs={{0,32},{32,0},{1,33},{33,1},{2,34},{34,2},{3,35},{35,3},{4,36},{36... | collective-permute-start | bytes 3244040 | tf_op jit(solution)/shard_map/ppermute | solution.py:383
  205.9 2.3 %collective-permute-done.8 = f32[8,264,128]{2,1,0:T(8,128)S(1)} collective-permute-done((f32[8,264,128]{2,1,0:T(8,128)S(1)}, f32[8,264,128]{2,1,0:T(8,128)S(1)}, u32[]{:S(2)}, u32[]{:S(2)}) %collective-permute-start.8) | collective-permute-done | bytes 1081376 | tf_op jit(solution)/shard_map/ppermute | solution.py:383
  208.3 0.1 add.30
  208.4 20.5 %all_to_all.27.parts = f32[8,264,128]{2,1,0:T(8,128)S(1)} all-to-all(f32[8,264,128]{2,1,0:T(8,128)S(1)} %add.30), channel_id=1, replica_groups=mesh['x'=4,'zl'=2,'core'=2,'yh'=4,'yl'=2,'zh'=4] {'x','zl'}, dimensions={0} | all-to-all | bytes 2162688 | tf_op jit(solution)/shard_map/all_to_all | solution.py:384
  228.9 1.3 final.1
  (4 shorter events, 0.0 us)
Async XLA Ops:
  0.0 12.4 %copy-start.2 = (s32[1,2,64]{2,1,0:T(2,128)S(1)}, s32[1,2,64]{2,1,0:T(2,128)}, u32[]{:S(2)}) copy-start(s32[1,2,64]{2,1,0:T(2,128)} %param.8) | copy-start | bytes 1540
  0.1 0.7 copy-start.1
  3.4 11.6 %collective-permute-start = (f32[128,768]{1,0:T(8,128)S(1)}, f32[128,768]{1,0:T(8,128)S(1)}, u32[]{:S(2)}, u32[]{:S(2)}) collective-permute-start(f32[128,768]{1,0:T(8,128)S(1)} %get-tuple-element.28), channel_id=1, source_target_pairs={{0,4},{4,0},{8,12},{12,8},{16,20},{20,16},{24,28},{28,24},{1,5},{5... | collective-permute-start | bytes 1179656 | tf_op jit(solution)/shard_map/ppermute | solution.py:339
  7.4 11.7 %collective-permute-start.1 = (f32[128,768]{1,0:T(8,128)S(1)}, f32[128,768]{1,0:T(8,128)S(1)}, u32[]{:S(2)}, u32[]{:S(2)}) collective-permute-start(f32[128,768]{1,0:T(8,128)S(1)} %get-tuple-element.29), channel_id=1, source_target_pairs={{0,28},{4,8},{8,4},{12,16},{16,12},{20,24},{24,20},{28,0},{1,29},{... | collective-permute-start | bytes 1179656 | tf_op jit(solution)/shard_map/ppermute | solution.py:339
  20.8 44.0 %all-to-all-start = ((f32[16,16,768]{2,1,0:T(8,128)}), f32[16,16,768]{2,1,0:T(8,128)S(1)}, u32[]{:S(2)}, u32[]{:S(2)}) async-start(f32[16,16,768]{2,1,0:T(8,128)} %join.1), calls=%async_computation | async-start | bytes 1572864 | tf_op jit(solution)/shard_map/all_to_all | solution.py:356
  38.9 21.7 %collective-permute-start.2 = (f32[128,768]{1,0:T(8,128)S(1)}, f32[128,768]{1,0:T(8,128)S(1)}, u32[]{:S(2)}, u32[]{:S(2)}) collective-permute-start(f32[128,768]{1,0:T(8,128)S(1)} %get-tuple-element.32), channel_id=1, source_target_pairs={{0,4},{4,0},{8,12},{12,8},{16,20},{20,16},{24,28},{28,24},{1,5},{5... | collective-permute-start | bytes 1179656 | tf_op jit(solution)/shard_map/ppermute | solution.py:339
  40.8 23.9 %collective-permute-start.3 = (f32[128,768]{1,0:T(8,128)S(1)}, f32[128,768]{1,0:T(8,128)S(1)}, u32[]{:S(2)}, u32[]{:S(2)}) collective-permute-start(f32[128,768]{1,0:T(8,128)S(1)} %get-tuple-element.33), channel_id=1, source_target_pairs={{0,28},{4,8},{8,4},{12,16},{16,12},{20,24},{24,20},{28,0},{1,29},{... | collective-permute-start | bytes 1179656 | tf_op jit(solution)/shard_map/ppermute | solution.py:339
  109.4 54.9 %copy-start = (bf16[512,1024]{1,0:T(8,128)(2,1)S(1)}, bf16[512,1024]{1,0:T(8,128)(2,1)}, u32[]{:S(2)}) copy-start(bf16[512,1024]{1,0:T(8,128)(2,1)} %refs.1) | copy-start | bytes 3145732
  109.4 31.8 %all-to-all-start.2 = ((f32[16,16,768]{2,1,0:T(8,128)}), f32[16,16,768]{2,1,0:T(8,128)S(1)}, u32[]{:S(2)}, u32[]{:S(2)}) async-start(f32[16,16,768]{2,1,0:T(8,128)} %get-tuple-element.34), calls=%async_computation.2 | async-start | bytes 1572864 | tf_op jit(solution)/shard_map/all_to_all | solution.py:356
  122.4 42.5 %copy-start.3 = (s32[1,2,768]{2,1,0:T(2,128)S(1)}, s32[1,2,768]{2,1,0:T(2,128)}, u32[]{:S(2)}) copy-start(s32[1,2,768]{2,1,0:T(2,128)} %param.9) | copy-start | bytes 18436
  122.5 42.5 %collective-permute-start.6 = (f32[16,8,768]{2,1,0:T(8,128)S(1)}, f32[16,8,768]{2,1,0:T(8,128)}, u32[]{:S(2)}, u32[]{:S(2)}) collective-permute-start(f32[16,8,768]{2,1,0:T(8,128)S(1)} %get-tuple-element.37.own_a), channel_id=1, source_target_pairs={{0,4},{4,0},{8,12},{12,8},{16,20},{20,16},{24,28},{28,24},{1,5},{5... | collective-permute-start | bytes 1179656 | tf_op jit(solution)/shard_map/ppermute | solution.py:339
  133.7 31.3 %collective-permute-start.7 = (f32[16,8,768]{2,1,0:T(8,128)S(1)}, f32[16,8,768]{2,1,0:T(8,128)}, u32[]{:S(2)}, u32[]{:S(2)}) collective-permute-start(f32[16,8,768]{2,1,0:T(8,128)S(1)} %get-tuple-element.38.own_b), channel_id=1, source_target_pairs={{0,28},{4,8},{8,4},{12,16},{16,12},{20,24},{24,20},{28,0},{1,29},{... | collective-permute-start | bytes 1179656 | tf_op jit(solution)/shard_map/ppermute | solution.py:339
  142.7 28.4 %collective-permute-start.4 = (f32[16,8,768]{2,1,0:T(8,128)S(1)}, f32[16,8,768]{2,1,0:T(8,128)}, u32[]{:S(2)}, u32[]{:S(2)}) collective-permute-start(f32[16,8,768]{2,1,0:T(8,128)S(1)} %get-tuple-element.35.own_a), channel_id=1, source_target_pairs={{0,4},{4,0},{8,12},{12,8},{16,20},{20,16},{24,28},{28,24},{1,5},{5... | collective-permute-start | bytes 1179656 | tf_op jit(solution)/shard_map/ppermute | solution.py:339
  162.4 12.9 %collective-permute-start.5 = (f32[16,8,768]{2,1,0:T(8,128)}, f32[16,8,768]{2,1,0:T(8,128)}, u32[]{:S(2)}, u32[]{:S(2)}) collective-permute-start(f32[16,8,768]{2,1,0:T(8,128)} %get-tuple-element.36.own_b), channel_id=1, source_target_pairs={{0,28},{4,8},{8,4},{12,16},{16,12},{20,24},{24,20},{28,0},{1,29},{... | collective-permute-start | bytes 1179656 | tf_op jit(solution)/shard_map/ppermute | solution.py:339
  199.5 8.8 %collective-permute-start.8 = (f32[8,264,128]{2,1,0:T(8,128)S(1)}, f32[8,264,128]{2,1,0:T(8,128)S(1)}, u32[]{:S(2)}, u32[]{:S(2)}) collective-permute-start(f32[8,264,128]{2,1,0:T(8,128)S(1)} %get-tuple-element.46), channel_id=1, source_target_pairs={{0,32},{32,0},{1,33},{33,1},{2,34},{34,2},{3,35},{35,3},{4,36},{36... | collective-permute-start | bytes 3244040 | tf_op jit(solution)/shard_map/ppermute | solution.py:383

commit v6 on v3

v6 whole, which is shorter than its diff:
```python
import jax
import jax.numpy as jnp
from jax import lax
from jax.experimental import pallas as pl
from jax.experimental.pallas import tpu as pltpu
from jax.sharding import Mesh, PartitionSpec as P

OBLOCK = 256
PRIOR_INCREMENT = 3.0
GRP = ("x", "zl", "core")
RING = ("yh", "yl")
TALL = ("zhh", "zhl")
MEM = RING + TALL
ALIKE = ("yh", "zhh")
PEERS = ("x", "zl")
LANES = 128
BIG = pltpu.CompilerParams(vmem_limit_bytes=16 << 20)
SMALL = pltpu.CompilerParams(vmem_limit_bytes=8 << 20)
LAST = (((1,), (1,)), ((), ()))


def project_kernel(at, inject, images, basis, phantom, *rest):
    outs, (pixels_in, columns, ghost, sems) = rest[:-4], rest[-4:]
    which = pixels_in.shape[0]
    width = pixels_in.shape[1]
    count = columns.shape[1]
    first = pl.multiple_of(at[0] * count, count)
    loads = [
        pltpu.make_async_copy(basis.at[:, pl.ds(first, count)], columns, sems.at[which]),
        pltpu.make_async_copy(phantom, ghost, sems.at[which + 1]),
    ] + [
        pltpu.make_async_copy(images.at[pl.ds(k * width, width), :], pixels_in.at[k], sems.at[k])
        for k in range(which)
    ]
    for load in loads:
        load.start()
    per_batch = which // inject.shape[0]
    hits = []
    for k in range(which):
        position = (k % per_batch) * width + lax.broadcasted_iota(jnp.int32, (1, width), 1)
        hit = jnp.zeros((1, width), jnp.float32)
        for i in range(inject.shape[1]):
            hit = jnp.where(position == inject[k // per_batch, i], 1.0, hit)
        hits.append(hit)
    loads[0].wait()
    loads[1].wait()
    mine = columns[...].T
    spread = jnp.broadcast_to(ghost[...], (LANES, ghost.shape[1]))
    extra = lax.dot_general(mine, spread, LAST, preferred_element_type=jnp.float32)
    share = count // len(outs)
    for k in range(which):
        loads[2 + k].wait()
        plain = lax.dot_general(mine, pixels_in[k], LAST, preferred_element_type=jnp.float32)
        for c in range(width // LANES):
            cut = slice(c * LANES, (c + 1) * LANES)
            value = plain[:, cut] + extra * hits[k][:, cut]
            for j, out in enumerate(outs):
                out[:, k * width + c * LANES : k * width + (c + 1) * LANES] = value[
                    j * share : (j + 1) * share
                ]


def projected(block, inject, images, basis, phantom, pieces):
    rows, pixels = images.shape
    steps = 2 * inject.shape[0]
    count = basis.shape[1] // 4
    out = jax.ShapeDtypeStruct((count // pieces, rows), jnp.float32)
    images, basis, phantom = (
        pltpu.with_memory_space_constraint(x, pltpu.HBM) for x in (images, basis, phantom)
    )
    found = pl.pallas_call(
        project_kernel,
        grid_spec=pltpu.PrefetchScalarGridSpec(
            num_scalar_prefetch=2,
            grid=(1,),
            in_specs=[pl.BlockSpec(memory_space=pltpu.HBM)] * 3,
            out_specs=[pl.BlockSpec(out.shape, lambda j, at, s: (0, 0))] * pieces,
            scratch_shapes=[
                pltpu.VMEM((steps, rows // steps, pixels), images.dtype),
                pltpu.VMEM((pixels, count), basis.dtype),
                pltpu.VMEM((1, pixels), phantom.dtype),
                pltpu.SemaphoreType.DMA((steps + 2,)),
            ],
        ),
        out_shape=[out] * pieces,
        compiler_params=SMALL,
        name="project",
    )(block, inject, images, basis, phantom)
    return tuple(found)


def whole(kernel, name, operands, shapes, at=None, scratch=(), params=SMALL):
    lead = [] if at is None else [at]
    return pl.pallas_call(
        kernel,
        in_specs=[pl.BlockSpec(memory_space=pltpu.SMEM)] * len(lead)
        + [pl.BlockSpec(memory_space=pltpu.VMEM)] * len(operands),
        out_specs=[pl.BlockSpec(memory_space=pltpu.VMEM)] * len(shapes),
        out_shape=[jax.ShapeDtypeStruct(shape, dtype) for shape, dtype in shapes],
        scratch_shapes=list(scratch),
        compiler_params=params,
        name=name,
    )(*lead, *operands)


def relay_kernel(here_a, here_b, came_a, came_b, low, high):
    members = low.shape[0]
    for side, out in enumerate((low, high)):
        for q in range(members):
            cut = slice((side * members + q) * 8, (side * members + q + 1) * 8)
            out[q, :8, :] = here_a[cut, :] + came_a[cut, :]
            out[q, 8:, :] = here_b[cut, :] + came_b[cut, :]


def relayed(here, came):
    count, rows = here[0].shape
    shape = ((count // 16, 16, rows), jnp.float32)
    return whole(relay_kernel, "relay", (*here, *came), [shape, shape])


def join_kernel(here_a, here_b, came_a, came_b, low, high, out):
    members = low.shape[0]
    for side, other in enumerate((low, high)):
        for q in range(members):
            m = side * members + q
            cut = slice(m * 8, (m + 1) * 8)
            out[m, :8, :] = here_a[cut, :] + came_a[cut, :] + other[q, :8, :]
            out[m, 8:, :] = here_b[cut, :] + came_b[cut, :] + other[q, 8:, :]


def joined(here, came, others):
    count, rows = here[0].shape
    shape = ((count // 8, 16, rows), jnp.float32)
    return whole(join_kernel, "join", (*here, *came, *others), [shape])[0]


def spread_kernel(parts, out):
    width = 256

    def column(j, carry):
        cut = pl.ds(pl.multiple_of(j * width, width), width)
        total = parts[0, :, cut]
        for k in range(1, parts.shape[0]):
            total = total + parts[k, :, cut]
        for k in range(out.shape[0]):
            out[k, :, cut] = total
        return carry

    lax.fori_loop(0, parts.shape[2] // width, column, 0)


def summed_copies(parts):
    return whole(spread_kernel, "spread", (parts,), [(parts.shape, jnp.float32)])[0]


def peel_kernel(low, high, out_a, out_b):
    middle = low.shape[0]
    for offset, source in ((0, low), (middle, high)):
        out_a[offset : offset + middle] = source[:, :8, :]
        out_b[offset : offset + middle] = source[:, 8:, :]


def peeled(low, high):
    members, _, rows = low.shape
    shape = ((2 * members, 8, rows), jnp.float32)
    return whole(peel_kernel, "peel", (low, high), [shape, shape])


def score_kernel(
    at, own, low, high, near_a, near_b, far_a, far_b, prior, refs_t, powers, rounded, stats
):
    width = 256
    orient, eigen = refs_t.shape
    lines = stats.shape[1] // 2
    half = eigen // 8
    quarter = half // 2

    def column(step, carry):
        cut = pl.ds(pl.multiple_of(step * width, width), width)

        def put(which, offset, block):
            count = block.shape[0] * block.shape[1]
            place = pl.multiple_of(at[which] * 2 * half + offset, quarter)
            rounded[pl.ds(place, count), cut] = block.reshape(count, width).astype(jnp.bfloat16)

        put(0, 0, far_a[:, :, cut])
        put(0, half, far_b[:, :, cut])
        put(1, 0, near_a[:, :, cut])
        put(1, half, near_b[:, :, cut])
        for offset, source in ((0, low), (quarter, high)):
            put(2, offset, source[:, :8, cut])
            put(2, half + offset, source[:, 8:, cut])
        put(3, 0, own[:, :8, cut])
        put(3, half, own[:, 8:, cut])
        scores = jnp.dot(refs_t[...], rounded[:, cut], preferred_element_type=jnp.float32)
        block = prior[:, cut] - at[4] * (orient // OBLOCK)
        parts = [
            scores[k * OBLOCK : (k + 1) * OBLOCK] + jnp.where(block == k, PRIOR_INCREMENT, 0.0)
            for k in range(orient // OBLOCK)
        ]
        tops = [jnp.max(part, axis=0, keepdims=True) for part in parts]
        top = tops[0]
        for other in tops[1:]:
            top = jnp.maximum(top, other)
        total = jnp.zeros_like(top)
        for k, part in enumerate(parts):
            power = jnp.exp(part - top)
            powers[k * OBLOCK : (k + 1) * OBLOCK, cut] = power
            total = total + jnp.sum(power, axis=0, keepdims=True)
        for h in range(width // LANES):
            line = step * (width // LANES) + h
            side = slice(h * LANES, (h + 1) * LANES)
            shape = (stats.shape[0], 1, LANES)
            stats[:, pl.ds(line, 1), :] = jnp.broadcast_to(top[None, :, side], shape)
            stats[:, pl.ds(lines + line, 1), :] = jnp.broadcast_to(total[None, :, side], shape)
        return carry

    lax.fori_loop(0, powers.shape[1] // width, column, 0)


def scores_of(at, held, prior, refs_t, members):
    rows = prior.shape[1]
    orient, eigen = refs_t.shape
    shapes = [
        ((orient, rows), jnp.float32),
        ((eigen, rows), jnp.bfloat16),
        ((members, 2 * rows // LANES, LANES), jnp.float32),
    ]
    return whole(score_kernel, "scores", (*held, prior, refs_t), shapes, at=at, params=BIG)


def total_kernel(at, stats, own, powers, rounded, keep, send, factor):
    width = 256
    eigen, rows = rounded.shape
    peers = keep.shape[0]
    share = eigen // (2 * peers)
    lines = rows // LANES
    body = keep.shape[1] - keep.shape[1] % share
    tops = stats[:, :lines, :]
    top = jnp.max(tops, axis=0)
    total = jnp.sum(stats[:, lines:, :] * jnp.exp(tops - top[None]), axis=0)
    scale = jnp.exp(own[0, :lines, :] - top) / total
    for k in range(lines):
        factor[:, k * LANES : (k + 1) * LANES] = scale[k : k + 1, :]
    first = at[5] == 0
    ones = jnp.ones((16, rows), jnp.bfloat16)

    def orients(step, carry):
        block = powers[pl.ds(pl.multiple_of(step * width, width), width), :]
        weights = (block * factor[...]).astype(jnp.bfloat16)
        totals = lax.dot_general(rounded[...], weights, LAST, preferred_element_type=jnp.float32)
        masses = lax.dot_general(ones, weights, LAST, preferred_element_type=jnp.float32)
        for h in range(width // LANES):
            column = step * (width // LANES) + h
            cut = slice(h * LANES, (h + 1) * LANES)
            place = pl.ds(pl.multiple_of(column * share, share), share)
            for q in range(peers):
                even = totals[2 * q * share : (2 * q + 1) * share, cut]
                odd = totals[(2 * q + 1) * share : (2 * q + 2) * share, cut]
                keep[q, place, :] = jnp.where(first, even, odd)
                send[q, place, :] = jnp.where(first, odd, even)
            mass = jnp.broadcast_to(masses[None, 0:1, cut], (peers, 1, LANES))
            keep[:, pl.ds(body + column, 1), :] = mass
            send[:, pl.ds(body + column, 1), :] = mass
        return carry

    lax.fori_loop(0, powers.shape[0] // width, orients, 0)


def totals_of(at, stats, sent, powers, rounded, peers):
    eigen, rows = rounded.shape
    orient = powers.shape[0]
    deep = (eigen // (2 * peers) + 1) * (orient // LANES)
    shape = ((peers, deep, LANES), jnp.float32)
    return whole(
        total_kernel,
        "totals",
        (stats, sent, powers, rounded),
        [shape, shape],
        at=at,
        scratch=[pltpu.VMEM((1, rows), jnp.float32)],
        params=BIG,
    )


def final_kernel(at, parts, refs, out):
    share, orient = out.shape
    both = parts[0]
    for d in range(1, parts.shape[0]):
        both = both + parts[d]
    body = share * (orient // LANES)
    for k in range(orient // LANES):
        cut = slice(k * LANES, (k + 1) * LANES)
        above = both[k * share : (k + 1) * share] + refs[:, cut].astype(jnp.float32)
        out[:, cut] = above / (both[body + k : body + k + 1] + 1.0)


def final_of(at, parts, refs):
    eigen, orient = refs.shape
    share = eigen // (2 * parts.shape[0])
    return pl.pallas_call(
        final_kernel,
        grid_spec=pltpu.PrefetchScalarGridSpec(
            num_scalar_prefetch=1,
            grid=(1,),
            in_specs=[
                pl.BlockSpec(parts.shape, lambda j, at: (0, 0, 0)),
                pl.BlockSpec((share, orient), lambda j, at: (at[6], 0)),
            ],
            out_specs=pl.BlockSpec((share, orient), lambda j, at: (0, 0)),
        ),
        out_shape=jax.ShapeDtypeStruct((share, orient), jnp.float32),
        compiler_params=SMALL,
        name="final",
    )(at, parts, refs)


def swapped(pair, axis):
    size = lax.axis_size(axis)
    with_a = [(i, i ^ 1) for i in range(size)]
    with_b = [(i, (i + (1 if i % 2 else -1)) % size) for i in range(size)]
    return tuple(lax.ppermute(x, axis, p) for x, p in zip(pair, (with_a, with_b)))


def shards(images, phantom, inject_rows, prior_blocks, basis, refs):
    rows = images.shape[1] * images.shape[2]
    flat = images[0].reshape(rows, basis.shape[0])
    p, q = lax.axis_index("yl"), lax.axis_index("zhl")
    at = jnp.stack(
        [
            (1 - p) * 2 + 1 - q,
            (1 - p) * 2 + q,
            p * 2 + 1 - q,
            p * 2 + q,
            lax.axis_index(MEM),
            lax.axis_index("core"),
            lax.axis_index(GRP),
        ]
    ).astype(jnp.int32)
    blocks = [
        projected(at[k : k + 1], inject_rows[0], flat, basis, phantom, 2) for k in range(4)
    ]

    through = swapped(blocks[0], RING)
    came = swapped(blocks[1], RING)
    others = swapped(relayed(blocks[2], through), TALL)
    parts = joined(blocks[3], came, others)
    parts = lax.all_to_all(parts, ALIKE, 0, 0, tiled=True)
    own = lax.all_to_all(summed_copies(parts), ALIKE, 0, 0, tiled=True)
    middle = own.shape[0] // 2
    low, high = swapped((own[:middle], own[middle:]), TALL)
    near = swapped((own[:, :8], own[:, 8:]), RING)
    far = swapped(peeled(low, high), RING)
    powers, rounded, sent = scores_of(
        at,
        (own, low, high, *near, *far),
        prior_blocks[0].reshape(1, rows),
        refs.T,
        lax.axis_size(MEM),
    )
    stats = lax.all_to_all(sent, MEM, 0, 0, tiled=True)
    keep, send = totals_of(at, stats, sent, powers, rounded, lax.axis_size(PEERS))
    parts = keep + lax.ppermute(send, "core", [(0, 1), (1, 0)])
    parts = lax.all_to_all(parts, PEERS, 0, 0, tiled=True)
    return final_of(at, parts, refs)


def solution(mesh):
    fine = Mesh(mesh.devices.reshape(4, 2, 2, 4, 2, 2, 2), GRP + MEM)
    placed = (
        P(GRP, None, None, MEM),
        P(GRP, MEM),
        P(GRP, None, None),
        P(GRP, None, None),
        P(MEM, None),
        P(None, MEM),
    )
    return jax.shard_map(
        shards, mesh=fine, in_specs=placed, out_specs=P(GRP, MEM), check_vma=False
    )
```

time: 218 us -> 216 us (level)
  local copies, waits for them, and re-layouts: 6.46 us -> 3.41 us
    pallas_call x4, Pallas kernels: 7.8 us -> 11.7 us  [projected(): pl.pallas_call(project_kernel, grid_spec=pltpu.PrefetchScalarGridSpec(num...]
    unnamed x24 -> x14, local copies, waits for them, and re-layouts: 5.39 us -> 2.32 us
    pallas_call x6, Pallas kernels: 13.3 us -> 10.8 us  [whole(): pl.pallas_call(kernel, in_specs=[pl.BlockSpec(memory_space=pltpu.SMEM)] *...]
  transfers between devices with their start and end apart: 13 -> 13, of which waited for: 7 -> 7; matrix products, arithmetic and copies ran while one was open for 1% -> 1% of each run, Pallas kernels for 4% -> 5%
where the time goes in v6:
time: 216 us; the launch traced here: 215 us
  blocking collectives  109 us (50%)
  starting transfers between devices  50.5 us (23%)
  waiting for transfers between devices  28 us (13%)
  Pallas kernels  23.8 us (11%)
  local copies, waits for them, and re-layouts  3.41 us (2%)
    ppermute x12, starting transfers between devices, swapped(): lax.ppermute(x, axis, p)  44.8 us
    all_to_all x1, blocking collectives, shards(): parts = lax.all_to_all(parts, ALIKE, 0, 0, tiled=True)  40.3 us
    all_to_all x1, blocking collectives, shards(): own = lax.all_to_all(summed_copies(parts), ALIKE, 0, 0, tiled=True)  28.1 us
    ppermute x12, waiting for transfers between devices, swapped(): lax.ppermute(x, axis, p)  25.7 us
    all_to_all x1, blocking collectives, shards(): parts = lax.all_to_all(parts, PEERS, 0, 0, tiled=True)  20.8 us
    all_to_all x1, blocking collectives, shards(): stats = lax.all_to_all(sent, MEM, 0, 0, tiled=True)  19.4 us
    pallas_call x4, Pallas kernels, projected(): pl.pallas_call(project_kernel, grid_spec=pltpu.PrefetchScalarGridSpec(num...  11.7 us
    pallas_call x6, Pallas kernels, whole(): pl.pallas_call(kernel, in_specs=[pl.BlockSpec(memory_space=pltpu.SMEM)] *...  10.8 us
  transfers between devices with their start and end apart: 13, of which 7 were waited for; matrix products, arithmetic and copies ran while one was open for 1% of the time, Pallas kernels for 5%

profile of v6, /device:TPU:1, one launch (start us, length us, event | category | flops | bytes accessed | tf_op | source)
XLA Modules:
  0.0 214.7 jit_solution(9958672685097720031)
XLA Ops:
  0.0 0.7 copy-done.3
  0.8 2.9 %project.7 = (f32[64,1536]{1,0:T(8,128)S(1)}, f32[64,1536]{1,0:T(8,128)S(1)}) custom-call(s32[1]{0:T(128)} %bitcast.at, s32[2,64]{1,0:T(2,128)S(1)} %bitcast.14, bf16[1536,512]{1,0:T(8,128)(2,1)} %bitcast.18, bf16[512,512]{1,0:T(8,128)(2,1)} %basis.7, bf16[1,512]{1,0:T(2,128)(2,1)} %phantom.7), custom_call_target="tpu_custom_call" | custom-call | tf_op jit(solution)/shard_map/project/pallas_call | solution.py:71
  3.7 4.0 %collective-permute-start.2 = (f32[64,1536]{1,0:T(8,128)S(1)}, f32[64,1536]{1,0:T(8,128)S(1)}, u32[]{:S(2)}, u32[]{:S(2)}) collective-permute-start(f32[64,1536]{1,0:T(8,128)S(1)} %get-tuple-element.28), channel_id=1, source_target_pairs={{0,4},{4,0},{8,12},{12,8},{16,20},{20,16},{24,28},{28,24},{1,5},{5... | collective-permute-start | bytes 1179656 | tf_op jit(solution)/shard_map/ppermute | solution.py:322
  7.7 4.9 %collective-permute-start.3 = (f32[64,1536]{1,0:T(8,128)S(1)}, f32[64,1536]{1,0:T(8,128)S(1)}, u32[]{:S(2)}, u32[]{:S(2)}) collective-permute-start(f32[64,1536]{1,0:T(8,128)S(1)} %get-tuple-element.29), channel_id=1, source_target_pairs={{0,28},{4,8},{8,4},{12,16},{16,12},{20,24},{24,20},{28,0},{1,29},{... | collective-permute-start | bytes 1179656 | tf_op jit(solution)/shard_map/ppermute | solution.py:322
  12.6 2.9 %project.5 = (f32[64,1536]{1,0:T(8,128)S(1)}, f32[64,1536]{1,0:T(8,128)S(1)}) custom-call(s32[1]{0:T(128)} %bitcast.1.at, s32[2,64]{1,0:T(2,128)S(1)} %bitcast.15, bf16[1536,512]{1,0:T(8,128)(2,1)} %bitcast.19, bf16[512,512]{1,0:T(8,128)(2,1)} %basis.7, bf16[1,512]{1,0:T(2,128)(2,1)} %phantom.7), custom_call_target="tpu_custom_call" | custom-call | tf_op jit(solution)/shard_map/project/pallas_call | solution.py:71
  15.5 1.9 collective-permute-start
  17.5 4.0 %collective-permute-start.1 = (f32[64,1536]{1,0:T(8,128)S(1)}, f32[64,1536]{1,0:T(8,128)S(1)}, u32[]{:S(2)}, u32[]{:S(2)}) collective-permute-start(f32[64,1536]{1,0:T(8,128)S(1)} %get-tuple-element.25), channel_id=1, source_target_pairs={{0,28},{4,8},{8,4},{12,16},{16,12},{20,24},{24,20},{28,0},{1,29},{... | collective-permute-start | bytes 1179656 | tf_op jit(solution)/shard_map/ppermute | solution.py:322
  21.5 2.9 %project.6 = (f32[64,1536]{1,0:T(8,128)S(1)}, f32[64,1536]{1,0:T(8,128)S(1)}) custom-call(s32[1]{0:T(128)} %bitcast.2.at, s32[2,64]{1,0:T(2,128)S(1)} %bitcast.16, bf16[1536,512]{1,0:T(8,128)(2,1)} %bitcast.20, bf16[512,512]{1,0:T(8,128)(2,1)} %basis.7, bf16[1,512]{1,0:T(2,128)(2,1)} %phantom.7), custom_call_target="tpu_custom_call" | custom-call | tf_op jit(solution)/shard_map/project/pallas_call | solution.py:71
  24.4 0.0 collective-permute-done.3.came_b
  24.4 0.1 relay.1
  24.6 5.8 %collective-permute-start.4 = (f32[4,16,1536]{2,1,0:T(8,128)S(1)}, f32[4,16,1536]{2,1,0:T(8,128)S(1)}, u32[]{:S(2)}, u32[]{:S(2)}) collective-permute-start(f32[4,16,1536]{2,1,0:T(8,128)S(1)} %get-tuple-element.30), channel_id=1, source_target_pairs={{0,1},{1,0},{2,3},{3,2},{4,5},{5,4},{6,7},{7,6},{8,9},{9,8},{10,11... | collective-permute-start | bytes 1179656 | tf_op jit(solution)/shard_map/ppermute | solution.py:322
  30.4 7.0 %collective-permute-start.5 = (f32[4,16,1536]{2,1,0:T(8,128)S(1)}, f32[4,16,1536]{2,1,0:T(8,128)S(1)}, u32[]{:S(2)}, u32[]{:S(2)}) collective-permute-start(f32[4,16,1536]{2,1,0:T(8,128)S(1)} %get-tuple-element.31), channel_id=1, source_target_pairs={{0,3},{1,2},{2,1},{3,0},{4,7},{5,6},{6,5},{7,4},{8,11},{9,10},{10,... | collective-permute-start | bytes 1179656 | tf_op jit(solution)/shard_map/ppermute | solution.py:322
  37.4 2.9 %project.4 = (f32[64,1536]{1,0:T(8,128)S(1)}, f32[64,1536]{1,0:T(8,128)S(1)}) custom-call(s32[1]{0:T(128)} %bitcast.3.at, s32[2,64]{1,0:T(2,128)S(1)} %bitcast.17, bf16[1536,512]{1,0:T(8,128)(2,1)} %bitcast.21, bf16[512,512]{1,0:T(8,128)(2,1)} %basis.7, bf16[1,512]{1,0:T(2,128)(2,1)} %phantom.7), custom_call_target="tpu_custom_call" | custom-call | tf_op jit(solution)/shard_map/project/pallas_call | solution.py:71
  40.3 0.0 collective-permute-done.came_a
  40.3 0.0 collective-permute-done.1.came_b
  40.4 6.2 %collective-permute-done.4.low = f32[4,16,1536]{2,1,0:T(8,128)S(1)} collective-permute-done((f32[4,16,1536]{2,1,0:T(8,128)S(1)}, f32[4,16,1536]{2,1,0:T(8,128)S(1)}, u32[]{:S(2)}, u32[]{:S(2)}) %collective-permute-start.4) | collective-permute-done | bytes 393248 | tf_op jit(solution)/shard_map/ppermute | solution.py:322
  46.5 0.3 collective-permute-done.5.high
  46.9 0.1 join.1
  47.0 40.3 %all_to_all.20.parts = f32[8,16,1536]{2,1,0:T(8,128)S(1)} all-to-all(f32[8,16,1536]{2,1,0:T(8,128)S(1)} %join.1), channel_id=1, replica_groups=mesh['x'=4,'zl'=2,'core'=2,'yh'=4,'yl'=2,'zhh'=2,'zhl'=2] {'yh','zhh'}, dimensions={0} | all-to-all | bytes 1572864 | tf_op jit(solution)/shard_map/all_to_all | solution.py:348
  87.3 0.1 spread.1
  87.4 28.1 %all_to_all.21.own = f32[8,16,1536]{2,1,0:T(8,128)S(1)} all-to-all(f32[8,16,1536]{2,1,0:T(8,128)S(1)} %spread.1), channel_id=1, replica_groups=mesh['x'=4,'zl'=2,'core'=2,'yh'=4,'yl'=2,'zhh'=2,'zhl'=2] {'yh','zhh'}, dimensions={0} | all-to-all | bytes 1572864 | tf_op jit(solution)/shard_map/all_to_all | solution.py:349
  115.5 0.1 fusion.1
  115.5 1.9 collective-permute-start.7
  117.5 0.0 copy-start.5
  117.5 0.0 copy-start
  117.5 5.0 %collective-permute-start.6 = (f32[4,16,1536]{2,1,0:T(8,128)S(1)}, f32[4,16,1536]{2,1,0:T(8,128)S(1)}, u32[]{:S(2)}, u32[]{:S(2)}) collective-permute-start(f32[4,16,1536]{2,1,0:T(8,128)S(1)} %get-tuple-element.42), channel_id=1, source_target_pairs={{0,1},{1,0},{2,3},{3,2},{4,5},{5,4},{6,7},{7,6},{8,9},{9,8},{10,11... | collective-permute-start | bytes 1179656 | tf_op jit(solution)/shard_map/ppermute | solution.py:322
  122.5 1.0 fusion
  123.4 1.9 collective-permute-start.9
  125.3 2.3 %collective-permute-start.8 = (f32[8,8,1536]{2,1,0:T(8,128)}, f32[8,8,1536]{2,1,0:T(8,128)}, u32[]{:S(2)}, u32[]{:S(2)}) collective-permute-start(f32[8,8,1536]{2,1,0:T(8,128)} %get-tuple-element.40), channel_id=1, source_target_pairs={{0,4},{4,0},{8,12},{12,8},{16,20},{20,16},{24,28},{28,24},{1,5},{5... | collective-permute-start | bytes 1179656 | tf_op jit(solution)/shard_map/ppermute | solution.py:322
  127.6 9.0 %collective-permute-done.7.high = f32[4,16,1536]{2,1,0:T(8,128)S(1)} collective-permute-done((f32[4,16,1536]{2,1,0:T(8,128)S(1)}, f32[4,16,1536]{2,1,0:T(8,128)S(1)}, u32[]{:S(2)}, u32[]{:S(2)}) %collective-permute-start.7) | collective-permute-done | bytes 393248 | tf_op jit(solution)/shard_map/ppermute | solution.py:322
  136.6 1.3 collective-permute-done.6.low
  137.9 1.0 peel.1
  138.9 1.9 collective-permute-start.10
  140.8 4.1 %collective-permute-start.11 = (f32[8,8,1536]{2,1,0:T(8,128)}, f32[8,8,1536]{2,1,0:T(8,128)}, u32[]{:S(2)}, u32[]{:S(2)}) collective-permute-start(f32[8,8,1536]{2,1,0:T(8,128)} %get-tuple-element.33), channel_id=1, source_target_pairs={{0,28},{4,8},{8,4},{12,16},{16,12},{20,24},{24,20},{28,0},{1,29},{... | collective-permute-start | bytes 1179656 | tf_op jit(solution)/shard_map/ppermute | solution.py:322
  145.0 0.5 copy.7
  145.5 0.1 stack.31.at
  145.6 0.0 collective-permute-done.9.near_b
  145.6 5.8 %collective-permute-done.10.far_a = f32[8,8,1536]{2,1,0:T(8,128)} collective-permute-done((f32[8,8,1536]{2,1,0:T(8,128)}, f32[8,8,1536]{2,1,0:T(8,128)}, u32[]{:S(2)}, u32[]{:S(2)}) %collective-permute-start.10) | collective-permute-done | bytes 393248 | tf_op jit(solution)/shard_map/ppermute | solution.py:322
  151.4 3.1 %collective-permute-done.11.far_b = f32[8,8,1536]{2,1,0:T(8,128)} collective-permute-done((f32[8,8,1536]{2,1,0:T(8,128)}, f32[8,8,1536]{2,1,0:T(8,128)}, u32[]{:S(2)}, u32[]{:S(2)}) %collective-permute-start.11) | collective-permute-done | bytes 393248 | tf_op jit(solution)/shard_map/ppermute | solution.py:322
  154.5 1.0 copy-done.2
  155.5 5.5 %scores.1 = (f32[1024,1536]{1,0:T(8,128)S(1)}, bf16[512,1536]{1,0:T(8,128)(2,1)S(1)}, f32[32,24,128]{2,1,0:T(8,128)S(1)}) custom-call(s32[7]{0:T(128)S(1)} %stack.31.at, f32[8,16,1536]{2,1,0:T(8,128)S(1)} %all_to_all.21.own, f32[4,16,1536]{2,1,0:T(8,128)S(1)} %copy-done.2, f32[4,16,1536]{2,1,0:T(8,128)S(1)} %collective-permute-done.7.high, ...), custom_call_target="tpu_custom_call" | custom-call | tf_op jit(solution)/shard_map/scores/pallas_call | solution.py:94
  161.1 19.4 %all_to_all.22.stats = f32[32,24,128]{2,1,0:T(8,128)S(1)} all-to-all(f32[32,24,128]{2,1,0:T(8,128)S(1)} %get-tuple-element.34.own), channel_id=1, replica_groups=mesh['x'=4,'zl'=2,'core'=2,'yh'=4,'yl'=2,'zhh'=2,'zhl'=2] {'yh','yl','zh..., dimensions={0} | all-to-all | bytes 786432 | tf_op jit(solution)/shard_map/all_to_all | solution.py:361
  180.5 4.0 %totals.1 = (f32[8,264,128]{2,1,0:T(8,128)S(1)}, f32[8,264,128]{2,1,0:T(8,128)S(1)}) custom-call(s32[7]{0:T(128)S(1)} %stack.31.at, f32[32,24,128]{2,1,0:T(8,128)S(1)} %all_to_all.22.stats, f32[32,24,128]{2,1,0:T(8,128)S(1)} %get-tuple-element.34.own, f32[1024,1536]{1,0:T(8,128)S(1)} %get-tuple-element.35.powers, bf16[512,1536]{1,0:T(8,128)(2,1)S(1)} %get-tuple-element.36.rounded), custom_call_target="tpu_custom_call" | custom-call | tf_op jit(solution)/shard_map/totals/pallas_call | solution.py:94
  184.5 5.7 %collective-permute-start.12 = (f32[8,264,128]{2,1,0:T(8,128)S(1)}, f32[8,264,128]{2,1,0:T(8,128)S(1)}, u32[]{:S(2)}, u32[]{:S(2)}) collective-permute-start(f32[8,264,128]{2,1,0:T(8,128)S(1)} %get-tuple-element.38), channel_id=1, source_target_pairs={{0,32},{32,0},{1,33},{33,1},{2,34},{34,2},{3,35},{35,3},{4,36},{36... | collective-permute-start | bytes 3244040 | tf_op jit(solution)/shard_map/ppermute | solution.py:363
  190.2 2.3 %collective-permute-done.12 = f32[8,264,128]{2,1,0:T(8,128)S(1)} collective-permute-done((f32[8,264,128]{2,1,0:T(8,128)S(1)}, f32[8,264,128]{2,1,0:T(8,128)S(1)}, u32[]{:S(2)}, u32[]{:S(2)}) %collective-permute-start.12) | collective-permute-done | bytes 1081376 | tf_op jit(solution)/shard_map/ppermute | solution.py:363
  192.5 0.1 add.39
  192.7 20.8 %all_to_all.23.parts = f32[8,264,128]{2,1,0:T(8,128)S(1)} all-to-all(f32[8,264,128]{2,1,0:T(8,128)S(1)} %add.39), channel_id=1, replica_groups=mesh['x'=4,'zl'=2,'core'=2,'yh'=4,'yl'=2,'zhh'=2,'zhl'=2] {'x','zl'}, dimensions={0} | all-to-all | bytes 2162688 | tf_op jit(solution)/shard_map/all_to_all | solution.py:364
  213.5 1.3 final.1
  (11 shorter events, 0.0 us)
Async XLA Ops:
  0.0 12.6 %copy-start.4 = (s32[1,2,64]{2,1,0:T(2,128)S(1)}, s32[1,2,64]{2,1,0:T(2,128)}, u32[]{:S(2)}) copy-start(s32[1,2,64]{2,1,0:T(2,128)} %param.8) | copy-start | bytes 1540
  0.0 0.8 copy-start.3
  3.7 20.8 %collective-permute-start.2 = (f32[64,1536]{1,0:T(8,128)S(1)}, f32[64,1536]{1,0:T(8,128)S(1)}, u32[]{:S(2)}, u32[]{:S(2)}) collective-permute-start(f32[64,1536]{1,0:T(8,128)S(1)} %get-tuple-element.28), channel_id=1, source_target_pairs={{0,4},{4,0},{8,12},{12,8},{16,20},{20,16},{24,28},{28,24},{1,5},{5... | collective-permute-start | bytes 1179656 | tf_op jit(solution)/shard_map/ppermute | solution.py:322
  7.7 16.7 %collective-permute-start.3 = (f32[64,1536]{1,0:T(8,128)S(1)}, f32[64,1536]{1,0:T(8,128)S(1)}, u32[]{:S(2)}, u32[]{:S(2)}) collective-permute-start(f32[64,1536]{1,0:T(8,128)S(1)} %get-tuple-element.29), channel_id=1, source_target_pairs={{0,28},{4,8},{8,4},{12,16},{16,12},{20,24},{24,20},{28,0},{1,29},{... | collective-permute-start | bytes 1179656 | tf_op jit(solution)/shard_map/ppermute | solution.py:322
  15.5 24.8 %collective-permute-start = (f32[64,1536]{1,0:T(8,128)S(1)}, f32[64,1536]{1,0:T(8,128)S(1)}, u32[]{:S(2)}, u32[]{:S(2)}) collective-permute-start(f32[64,1536]{1,0:T(8,128)S(1)} %get-tuple-element.24), channel_id=1, source_target_pairs={{0,4},{4,0},{8,12},{12,8},{16,20},{20,16},{24,28},{28,24},{1,5},{5... | collective-permute-start | bytes 1179656 | tf_op jit(solution)/shard_map/ppermute | solution.py:322
  17.5 22.9 %collective-permute-start.1 = (f32[64,1536]{1,0:T(8,128)S(1)}, f32[64,1536]{1,0:T(8,128)S(1)}, u32[]{:S(2)}, u32[]{:S(2)}) collective-permute-start(f32[64,1536]{1,0:T(8,128)S(1)} %get-tuple-element.25), channel_id=1, source_target_pairs={{0,28},{4,8},{8,4},{12,16},{16,12},{20,24},{24,20},{28,0},{1,29},{... | collective-permute-start | bytes 1179656 | tf_op jit(solution)/shard_map/ppermute | solution.py:322
  24.6 22.0 %collective-permute-start.4 = (f32[4,16,1536]{2,1,0:T(8,128)S(1)}, f32[4,16,1536]{2,1,0:T(8,128)S(1)}, u32[]{:S(2)}, u32[]{:S(2)}) collective-permute-start(f32[4,16,1536]{2,1,0:T(8,128)S(1)} %get-tuple-element.30), channel_id=1, source_target_pairs={{0,1},{1,0},{2,3},{3,2},{4,5},{5,4},{6,7},{7,6},{8,9},{9,8},{10,11... | collective-permute-start | bytes 1179656 | tf_op jit(solution)/shard_map/ppermute | solution.py:322
  30.4 16.5 %collective-permute-start.5 = (f32[4,16,1536]{2,1,0:T(8,128)S(1)}, f32[4,16,1536]{2,1,0:T(8,128)S(1)}, u32[]{:S(2)}, u32[]{:S(2)}) collective-permute-start(f32[4,16,1536]{2,1,0:T(8,128)S(1)} %get-tuple-element.31), channel_id=1, source_target_pairs={{0,3},{1,2},{2,1},{3,0},{4,7},{5,6},{6,5},{7,4},{8,11},{9,10},{10,... | collective-permute-start | bytes 1179656 | tf_op jit(solution)/shard_map/ppermute | solution.py:322
  115.5 21.1 %collective-permute-start.7 = (f32[4,16,1536]{2,1,0:T(8,128)S(1)}, f32[4,16,1536]{2,1,0:T(8,128)S(1)}, u32[]{:S(2)}, u32[]{:S(2)}) collective-permute-start(f32[4,16,1536]{2,1,0:T(8,128)S(1)} %get-tuple-element.41), channel_id=1, source_target_pairs={{0,3},{1,2},{2,1},{3,0},{4,7},{5,6},{6,5},{7,4},{8,11},{9,10},{10,... | collective-permute-start | bytes 1179656 | tf_op jit(solution)/shard_map/ppermute | solution.py:322
  117.5 27.5 %copy-start.5 = (s32[1,2,768]{2,1,0:T(2,128)S(1)}, s32[1,2,768]{2,1,0:T(2,128)}, u32[]{:S(2)}) copy-start(s32[1,2,768]{2,1,0:T(2,128)} %param.9) | copy-start | bytes 18436
  117.5 27.5 %copy-start = (bf16[512,1024]{1,0:T(8,128)(2,1)S(1)}, bf16[512,1024]{1,0:T(8,128)(2,1)}, u32[]{:S(2)}) copy-start(bf16[512,1024]{1,0:T(8,128)(2,1)} %refs.1) | copy-start | bytes 3145732
  117.5 20.4 %collective-permute-start.6 = (f32[4,16,1536]{2,1,0:T(8,128)S(1)}, f32[4,16,1536]{2,1,0:T(8,128)S(1)}, u32[]{:S(2)}, u32[]{:S(2)}) collective-permute-start(f32[4,16,1536]{2,1,0:T(8,128)S(1)} %get-tuple-element.42), channel_id=1, source_target_pairs={{0,1},{1,0},{2,3},{3,2},{4,5},{5,4},{6,7},{7,6},{8,9},{9,8},{10,11... | collective-permute-start | bytes 1179656 | tf_op jit(solution)/shard_map/ppermute | solution.py:322
  123.4 22.2 %collective-permute-start.9 = (f32[8,8,1536]{2,1,0:T(8,128)}, f32[8,8,1536]{2,1,0:T(8,128)}, u32[]{:S(2)}, u32[]{:S(2)}) collective-permute-start(f32[8,8,1536]{2,1,0:T(8,128)} %get-tuple-element.39), channel_id=1, source_target_pairs={{0,28},{4,8},{8,4},{12,16},{16,12},{20,24},{24,20},{28,0},{1,29},{... | collective-permute-start | bytes 1179656 | tf_op jit(solution)/shard_map/ppermute | solution.py:322
  125.3 20.3 %collective-permute-start.8 = (f32[8,8,1536]{2,1,0:T(8,128)}, f32[8,8,1536]{2,1,0:T(8,128)}, u32[]{:S(2)}, u32[]{:S(2)}) collective-permute-start(f32[8,8,1536]{2,1,0:T(8,128)} %get-tuple-element.40), channel_id=1, source_target_pairs={{0,4},{4,0},{8,12},{12,8},{16,20},{20,16},{24,28},{28,24},{1,5},{5... | collective-permute-start | bytes 1179656 | tf_op jit(solution)/shard_map/ppermute | solution.py:322
  137.9 7.0 %copy-start.1 = (f32[4,16,1536]{2,1,0:T(8,128)}, f32[4,16,1536]{2,1,0:T(8,128)S(1)}, u32[]{:S(2)}) copy-start(f32[4,16,1536]{2,1,0:T(8,128)S(1)} %collective-permute-done.6.low) | copy-start | bytes 1179652
  138.9 12.5 %collective-permute-start.10 = (f32[8,8,1536]{2,1,0:T(8,128)}, f32[8,8,1536]{2,1,0:T(8,128)}, u32[]{:S(2)}, u32[]{:S(2)}) collective-permute-start(f32[8,8,1536]{2,1,0:T(8,128)} %get-tuple-element.32), channel_id=1, source_target_pairs={{0,4},{4,0},{8,12},{12,8},{16,20},{20,16},{24,28},{28,24},{1,5},{5... | collective-permute-start | bytes 1179656 | tf_op jit(solution)/shard_map/ppermute | solution.py:322
  140.8 13.7 %collective-permute-start.11 = (f32[8,8,1536]{2,1,0:T(8,128)}, f32[8,8,1536]{2,1,0:T(8,128)}, u32[]{:S(2)}, u32[]{:S(2)}) collective-permute-start(f32[8,8,1536]{2,1,0:T(8,128)} %get-tuple-element.33), channel_id=1, source_target_pairs={{0,28},{4,8},{8,4},{12,16},{16,12},{20,24},{24,20},{28,0},{1,29},{... | collective-permute-start | bytes 1179656 | tf_op jit(solution)/shard_map/ppermute | solution.py:322
  154.5 1.0 copy-start.2
  184.5 8.1 %collective-permute-start.12 = (f32[8,264,128]{2,1,0:T(8,128)S(1)}, f32[8,264,128]{2,1,0:T(8,128)S(1)}, u32[]{:S(2)}, u32[]{:S(2)}) collective-permute-start(f32[8,264,128]{2,1,0:T(8,128)S(1)} %get-tuple-element.38), channel_id=1, source_target_pairs={{0,32},{32,0},{1,33},{33,1},{2,34},{34,2},{3,35},{35,3},{4,36},{36... | collective-permute-start | bytes 3244040 | tf_op jit(solution)/shard_map/ppermute | solution.py:363

commit v7 on v6

--- a/solution.py
+++ b/solution.py
@@ -1,3 +1,5 @@
+import functools
+
 import jax
 import jax.numpy as jnp
 from jax import lax
@@ -166,25 +168,22 @@
     return whole(peel_kernel, "peel", (low, high), [shape, shape])
 
 
-def score_kernel(
-    at, own, low, high, near_a, near_b, far_a, far_b, prior, refs_t, powers, rounded, stats
-):
+def put_block(at, rounded, cut, which, offset, block):
+    count = block.shape[0] * block.shape[1]
+    place = at[which] * (rounded.shape[0] // 4) + offset
+    place = pl.multiple_of(place, rounded.shape[0] // 16)
+    rounded[pl.ds(place, count), cut] = block.reshape(count, -1).astype(jnp.bfloat16)
+
+
+def stage_kernel(at, own, low, high, near_a, near_b, staged):
     width = 256
-    orient, eigen = refs_t.shape
-    lines = stats.shape[1] // 2
-    half = eigen // 8
+    half = staged.shape[0] // 8
     quarter = half // 2
 
     def column(step, carry):
         cut = pl.ds(pl.multiple_of(step * width, width), width)
-
-        def put(which, offset, block):
-            count = block.shape[0] * block.shape[1]
-            place = pl.multiple_of(at[which] * 2 * half + offset, quarter)
-            rounded[pl.ds(place, count), cut] = block.reshape(count, width).astype(jnp.bfloat16)
-
-        put(0, 0, far_a[:, :, cut])
-        put(0, half, far_b[:, :, cut])
+        put = functools.partial(put_block, at, staged, cut)
+        put(0, 0, jnp.zeros((16, 8, width), jnp.float32))
         put(1, 0, near_a[:, :, cut])
         put(1, half, near_b[:, :, cut])
         for offset, source in ((0, low), (quarter, high)):
@@ -192,6 +191,27 @@
             put(2, half + offset, source[:, 8:, cut])
         put(3, 0, own[:, :8, cut])
         put(3, half, own[:, 8:, cut])
+        return carry
+
+    lax.fori_loop(0, staged.shape[1] // width, column, 0)
+
+
+def staged_of(at, held):
+    members, high, rows = held[0].shape
+    shape = ((members * high * 4, rows), jnp.bfloat16)
+    return whole(stage_kernel, "stage", held, [shape], at=at)[0]
+
+
+def score_kernel(at, staged, far_a, far_b, prior, refs_t, powers, rounded, stats):
+    width = 256
+    orient, eigen = refs_t.shape
+    lines = stats.shape[1] // 2
+
+    def column(step, carry):
+        cut = pl.ds(pl.multiple_of(step * width, width), width)
+        rounded[:, cut] = staged[:, cut]
+        put_block(at, rounded, cut, 0, 0, far_a[:, :, cut])
+        put_block(at, rounded, cut, 0, eigen // 8, far_b[:, :, cut])
         scores = jnp.dot(refs_t[...], rounded[:, cut], preferred_element_type=jnp.float32)
         block = prior[:, cut] - at[4] * (orient // OBLOCK)
         parts = [
@@ -337,14 +357,16 @@
             lax.axis_index(GRP),
         ]
     ).astype(jnp.int32)
-    blocks = [
-        projected(at[k : k + 1], inject_rows[0], flat, basis, phantom, 2) for k in range(4)
-    ]
-
-    through = swapped(blocks[0], RING)
-    came = swapped(blocks[1], RING)
-    others = swapped(relayed(blocks[2], through), TALL)
-    parts = joined(blocks[3], came, others)
+    def block(which):
+        return projected(which, inject_rows[0], flat, basis, phantom, 2)
+
+    through = swapped(block(at[0:1]), RING)
+    turned = relayed(block(at[2:3]), through)
+    kept = block(at[3:4])
+    low, high, after = lax.optimization_barrier((*turned, at[1:2]))
+    others = swapped((low, high), TALL)
+    came = swapped(block(after), RING)
+    parts = joined(kept, came, others)
     parts = lax.all_to_all(parts, ALIKE, 0, 0, tiled=True)
     own = lax.all_to_all(summed_copies(parts), ALIKE, 0, 0, tiled=True)
     middle = own.shape[0] // 2
@@ -353,7 +375,7 @@
     far = swapped(peeled(low, high), RING)
     powers, rounded, sent = scores_of(
         at,
-        (own, low, high, *near, *far),
+        (staged_of(at, (own, low, high, *near)), *far),
         prior_blocks[0].reshape(1, rows),
         refs.T,
         lax.axis_size(MEM),

time: 216 us -> 214 us (level)
  blocking collectives: 109 us -> 102 us
  starting transfers between devices: 50.5 us -> 54.2 us
    all_to_all x1, blocking collectives: 40.3 us -> 35 us  [shards(): parts = lax.all_to_all(parts, ALIKE, 0, 0, tiled=True)]
    ppermute x12, starting transfers between devices: 44.8 us -> 47.8 us  [swapped(): lax.ppermute(x, axis, p)]
    pallas_call x6 -> x7, Pallas kernels: 10.8 us -> 12 us  [whole(): pl.pallas_call(kernel, in_specs=[pl.BlockSpec(memory_space=pltpu.SMEM)] *...]
  transfers between devices with their start and end apart: 13 -> 13, of which waited for: 7 -> 8; matrix products, arithmetic and copies ran while one was open for 1% -> 1% of each run, Pallas kernels for 5% -> 5%
where the time goes in v7:
time: 214 us; the launch traced here: 212 us
  blocking collectives  102 us (48%)
  starting transfers between devices  54.2 us (25%)
  waiting for transfers between devices  26.6 us (12%)
  Pallas kernels  24.9 us (12%)
  local copies, waits for them, and re-layouts  3.43 us (2%)
    ppermute x12, starting transfers between devices, swapped(): lax.ppermute(x, axis, p)  47.8 us
    all_to_all x1, blocking collectives, shards(): parts = lax.all_to_all(parts, ALIKE, 0, 0, tiled=True)  35 us
    all_to_all x1, blocking collectives, shards(): own = lax.all_to_all(summed_copies(parts), ALIKE, 0, 0, tiled=True)  29 us
    ppermute x12, waiting for transfers between devices, swapped(): lax.ppermute(x, axis, p)  24.3 us
    all_to_all x1, blocking collectives, shards(): parts = lax.all_to_all(parts, PEERS, 0, 0, tiled=True)  19.8 us
    all_to_all x1, blocking collectives, shards(): stats = lax.all_to_all(sent, MEM, 0, 0, tiled=True)  18.5 us
    pallas_call x7, Pallas kernels, whole(): pl.pallas_call(kernel, in_specs=[pl.BlockSpec(memory_space=pltpu.SMEM)] *...  12 us
    pallas_call x4, Pallas kernels, projected(): pl.pallas_call(project_kernel, grid_spec=pltpu.PrefetchScalarGridSpec(num...  11.7 us
  transfers between devices with their start and end apart: 13, of which 8 were waited for; matrix products, arithmetic and copies ran while one was open for 1% of the time, Pallas kernels for 5%

profile of v7, /device:TPU:1, one launch (start us, length us, event | category | flops | bytes accessed | tf_op | source)
XLA Modules:
  0.0 211.9 jit_solution(3354893735179798821)
XLA Ops:
  0.0 0.7 copy-done.3
  0.8 2.9 %project.6 = (f32[64,1536]{1,0:T(8,128)S(1)}, f32[64,1536]{1,0:T(8,128)S(1)}) custom-call(s32[1]{0:T(128)} %bitcast.at, s32[2,64]{1,0:T(2,128)S(1)} %bitcast.14, bf16[1536,512]{1,0:T(8,128)(2,1)} %bitcast.18, bf16[512,512]{1,0:T(8,128)(2,1)} %basis.7, bf16[1,512]{1,0:T(2,128)(2,1)} %phantom.7), custom_call_target="tpu_custom_call" | custom-call | tf_op jit(solution)/shard_map/project/pallas_call | solution.py:73
  3.7 4.0 %collective-permute-start = (f32[64,1536]{1,0:T(8,128)S(1)}, f32[64,1536]{1,0:T(8,128)S(1)}, u32[]{:S(2)}, u32[]{:S(2)}) collective-permute-start(f32[64,1536]{1,0:T(8,128)S(1)} %get-tuple-element.29), channel_id=1, source_target_pairs={{0,4},{4,0},{8,12},{12,8},{16,20},{20,16},{24,28},{28,24},{1,5},{5... | collective-permute-start | bytes 1179656 | tf_op jit(solution)/shard_map/ppermute | solution.py:342
  7.7 4.9 %collective-permute-start.1 = (f32[64,1536]{1,0:T(8,128)S(1)}, f32[64,1536]{1,0:T(8,128)S(1)}, u32[]{:S(2)}, u32[]{:S(2)}) collective-permute-start(f32[64,1536]{1,0:T(8,128)S(1)} %get-tuple-element.30), channel_id=1, source_target_pairs={{0,28},{4,8},{8,4},{12,16},{16,12},{20,24},{24,20},{28,0},{1,29},{... | collective-permute-start | bytes 1179656 | tf_op jit(solution)/shard_map/ppermute | solution.py:342
  12.6 2.9 %project.5 = (f32[64,1536]{1,0:T(8,128)S(1)}, f32[64,1536]{1,0:T(8,128)S(1)}) custom-call(s32[1]{0:T(128)} %bitcast.2.at, s32[2,64]{1,0:T(2,128)S(1)} %bitcast.15, bf16[1536,512]{1,0:T(8,128)(2,1)} %bitcast.19, bf16[512,512]{1,0:T(8,128)(2,1)} %basis.7, bf16[1,512]{1,0:T(2,128)(2,1)} %phantom.7), custom_call_target="tpu_custom_call" | custom-call | tf_op jit(solution)/shard_map/project/pallas_call | solution.py:73
  15.5 0.0 collective-permute-done.came_a
  15.5 3.9 %collective-permute-done.1.came_b = f32[64,1536]{1,0:T(8,128)S(1)} collective-permute-done((f32[64,1536]{1,0:T(8,128)S(1)}, f32[64,1536]{1,0:T(8,128)S(1)}, u32[]{:S(2)}, u32[]{:S(2)}) %collective-permute-start.1) | collective-permute-done | bytes 393248 | tf_op jit(solution)/shard_map/ppermute | solution.py:342
  19.5 0.1 relay.1
  19.6 7.5 %collective-permute-start.4 = (f32[4,16,1536]{2,1,0:T(8,128)S(1)}, f32[4,16,1536]{2,1,0:T(8,128)S(1)}, u32[]{:S(2)}, u32[]{:S(2)}) collective-permute-start(f32[4,16,1536]{2,1,0:T(8,128)S(1)} %get-tuple-element.36), channel_id=1, source_target_pairs={{0,1},{1,0},{2,3},{3,2},{4,5},{5,4},{6,7},{7,6},{8,9},{9,8},{10,11... | collective-permute-start | bytes 1179656 | tf_op jit(solution)/shard_map/ppermute | solution.py:342
  27.0 7.0 %collective-permute-start.5 = (f32[4,16,1536]{2,1,0:T(8,128)S(1)}, f32[4,16,1536]{2,1,0:T(8,128)S(1)}, u32[]{:S(2)}, u32[]{:S(2)}) collective-permute-start(f32[4,16,1536]{2,1,0:T(8,128)S(1)} %get-tuple-element.37), channel_id=1, source_target_pairs={{0,3},{1,2},{2,1},{3,0},{4,7},{5,6},{6,5},{7,4},{8,11},{9,10},{10,... | collective-permute-start | bytes 1179656 | tf_op jit(solution)/shard_map/ppermute | solution.py:342
  34.0 2.9 %project.7 = (f32[64,1536]{1,0:T(8,128)S(1)}, f32[64,1536]{1,0:T(8,128)S(1)}) custom-call(s32[1]{0:T(128)} %bitcast.1.at, s32[2,64]{1,0:T(2,128)S(1)} %bitcast.16, bf16[1536,512]{1,0:T(8,128)(2,1)} %bitcast.20, bf16[512,512]{1,0:T(8,128)(2,1)} %basis.7, bf16[1,512]{1,0:T(2,128)(2,1)} %phantom.7), custom_call_target="tpu_custom_call" | custom-call | tf_op jit(solution)/shard_map/project/pallas_call | solution.py:73
  37.0 1.9 collective-permute-start.2
  38.9 4.2 %collective-permute-start.3 = (f32[64,1536]{1,0:T(8,128)S(1)}, f32[64,1536]{1,0:T(8,128)S(1)}, u32[]{:S(2)}, u32[]{:S(2)}) collective-permute-start(f32[64,1536]{1,0:T(8,128)S(1)} %get-tuple-element.35), channel_id=1, source_target_pairs={{0,28},{4,8},{8,4},{12,16},{16,12},{20,24},{24,20},{28,0},{1,29},{... | collective-permute-start | bytes 1179656 | tf_op jit(solution)/shard_map/ppermute | solution.py:342
  43.2 2.9 %project.4 = (f32[64,1536]{1,0:T(8,128)S(1)}, f32[64,1536]{1,0:T(8,128)S(1)}) custom-call(s32[1]{0:T(128)} %bitcast.3.at, s32[2,64]{1,0:T(2,128)S(1)} %bitcast.17, bf16[1536,512]{1,0:T(8,128)(2,1)} %bitcast.21, bf16[512,512]{1,0:T(8,128)(2,1)} %basis.7, bf16[1,512]{1,0:T(2,128)(2,1)} %phantom.7), custom_call_target="tpu_custom_call" | custom-call | tf_op jit(solution)/shard_map/project/pallas_call | solution.py:73
  46.1 0.0 collective-permute-done.4.low
  46.1 1.3 collective-permute-done.2.came_a
  47.4 3.1 %collective-permute-done.3.came_b = f32[64,1536]{1,0:T(8,128)S(1)} collective-permute-done((f32[64,1536]{1,0:T(8,128)S(1)}, f32[64,1536]{1,0:T(8,128)S(1)}, u32[]{:S(2)}, u32[]{:S(2)}) %collective-permute-start.3) | collective-permute-done | bytes 393248 | tf_op jit(solution)/shard_map/ppermute | solution.py:342
  50.5 0.1 join.1
  50.6 35.0 %all_to_all.20.parts = f32[8,16,1536]{2,1,0:T(8,128)S(1)} all-to-all(f32[8,16,1536]{2,1,0:T(8,128)S(1)} %join.1), channel_id=1, replica_groups=mesh['x'=4,'zl'=2,'core'=2,'yh'=4,'yl'=2,'zhh'=2,'zhl'=2] {'yh','zhh'}, dimensions={0} | all-to-all | bytes 1572864 | tf_op jit(solution)/shard_map/all_to_all | solution.py:370
  85.6 0.1 spread.1
  85.8 29.0 %all_to_all.21.own = f32[8,16,1536]{2,1,0:T(8,128)S(1)} all-to-all(f32[8,16,1536]{2,1,0:T(8,128)S(1)} %spread.1), channel_id=1, replica_groups=mesh['x'=4,'zl'=2,'core'=2,'yh'=4,'yl'=2,'zhh'=2,'zhl'=2] {'yh','zhh'}, dimensions={0} | all-to-all | bytes 1572864 | tf_op jit(solution)/shard_map/all_to_all | solution.py:371
  114.7 0.1 fusion.1
  114.8 1.9 collective-permute-start.7
  116.7 0.0 copy-start.5
  116.7 0.0 copy-start
  116.7 3.1 %collective-permute-start.6 = (f32[4,16,1536]{2,1,0:T(8,128)S(1)}, f32[4,16,1536]{2,1,0:T(8,128)S(1)}, u32[]{:S(2)}, u32[]{:S(2)}) collective-permute-start(f32[4,16,1536]{2,1,0:T(8,128)S(1)} %get-tuple-element.48), channel_id=1, source_target_pairs={{0,1},{1,0},{2,3},{3,2},{4,5},{5,4},{6,7},{7,6},{8,9},{9,8},{10,11... | collective-permute-start | bytes 1179656 | tf_op jit(solution)/shard_map/ppermute | solution.py:342
  119.9 1.0 fusion
  120.9 1.9 collective-permute-start.9
  122.8 5.1 %collective-permute-start.8 = (f32[8,8,1536]{2,1,0:T(8,128)}, f32[8,8,1536]{2,1,0:T(8,128)}, u32[]{:S(2)}, u32[]{:S(2)}) collective-permute-start(f32[8,8,1536]{2,1,0:T(8,128)} %get-tuple-element.46), channel_id=1, source_target_pairs={{0,4},{4,0},{8,12},{12,8},{16,20},{20,16},{24,28},{28,24},{1,5},{5... | collective-permute-start | bytes 1179656 | tf_op jit(solution)/shard_map/ppermute | solution.py:342
  127.9 4.9 %collective-permute-done.7.high = f32[4,16,1536]{2,1,0:T(8,128)S(1)} collective-permute-done((f32[4,16,1536]{2,1,0:T(8,128)S(1)}, f32[4,16,1536]{2,1,0:T(8,128)S(1)}, u32[]{:S(2)}, u32[]{:S(2)}) %collective-permute-start.7) | collective-permute-done | bytes 393248 | tf_op jit(solution)/shard_map/ppermute | solution.py:342
  132.8 5.7 %collective-permute-done.6.low = f32[4,16,1536]{2,1,0:T(8,128)S(1)} collective-permute-done((f32[4,16,1536]{2,1,0:T(8,128)S(1)}, f32[4,16,1536]{2,1,0:T(8,128)S(1)}, u32[]{:S(2)}, u32[]{:S(2)}) %collective-permute-start.6) | collective-permute-done | bytes 393248 | tf_op jit(solution)/shard_map/ppermute | solution.py:342
  138.5 1.0 peel.1
  139.5 1.9 collective-permute-start.10
  141.4 4.3 %collective-permute-start.11 = (f32[8,8,1536]{2,1,0:T(8,128)}, f32[8,8,1536]{2,1,0:T(8,128)}, u32[]{:S(2)}, u32[]{:S(2)}) collective-permute-start(f32[8,8,1536]{2,1,0:T(8,128)} %get-tuple-element.39), channel_id=1, source_target_pairs={{0,28},{4,8},{8,4},{12,16},{16,12},{20,24},{24,20},{28,0},{1,29},{... | collective-permute-start | bytes 1179656 | tf_op jit(solution)/shard_map/ppermute | solution.py:342
  145.7 0.5 copy.7
  146.3 0.1 stack.31.at
  146.4 1.0 copy-done.2
  147.4 1.4 stage.1.staged
  148.8 2.3 %collective-permute-done.10.far_a = f32[8,8,1536]{2,1,0:T(8,128)} collective-permute-done((f32[8,8,1536]{2,1,0:T(8,128)}, f32[8,8,1536]{2,1,0:T(8,128)}, u32[]{:S(2)}, u32[]{:S(2)}) %collective-permute-start.10) | collective-permute-done | bytes 393248 | tf_op jit(solution)/shard_map/ppermute | solution.py:342
  151.1 3.1 %collective-permute-done.11.far_b = f32[8,8,1536]{2,1,0:T(8,128)} collective-permute-done((f32[8,8,1536]{2,1,0:T(8,128)}, f32[8,8,1536]{2,1,0:T(8,128)}, u32[]{:S(2)}, u32[]{:S(2)}) %collective-permute-start.11) | collective-permute-done | bytes 393248 | tf_op jit(solution)/shard_map/ppermute | solution.py:342
  154.3 5.2 %scores.1 = (f32[1024,1536]{1,0:T(8,128)S(1)}, bf16[512,1536]{1,0:T(8,128)(2,1)S(1)}, f32[32,24,128]{2,1,0:T(8,128)S(1)}) custom-call(s32[7]{0:T(128)S(1)} %stack.31.at, bf16[512,1536]{1,0:T(8,128)(2,1)S(1)} %stage.1.staged, f32[8,8,1536]{2,1,0:T(8,128)} %collective-permute-done.10.far_a, f32[8,8,1536]{2,1,0:T(8,128)} %collective-permute-done.11.far_b, ...), custom_call_target="tpu_custom_call" | custom-call | tf_op jit(solution)/shard_map/scores/pallas_call | solution.py:96
  159.5 18.5 %all_to_all.22.stats = f32[32,24,128]{2,1,0:T(8,128)S(1)} all-to-all(f32[32,24,128]{2,1,0:T(8,128)S(1)} %get-tuple-element.40.own), channel_id=1, replica_groups=mesh['x'=4,'zl'=2,'core'=2,'yh'=4,'yl'=2,'zhh'=2,'zhl'=2] {'yh','yl','zh..., dimensions={0} | all-to-all | bytes 786432 | tf_op jit(solution)/shard_map/all_to_all | solution.py:383
  178.0 4.0 %totals.1 = (f32[8,264,128]{2,1,0:T(8,128)S(1)}, f32[8,264,128]{2,1,0:T(8,128)S(1)}) custom-call(s32[7]{0:T(128)S(1)} %stack.31.at, f32[32,24,128]{2,1,0:T(8,128)S(1)} %all_to_all.22.stats, f32[32,24,128]{2,1,0:T(8,128)S(1)} %get-tuple-element.40.own, f32[1024,1536]{1,0:T(8,128)S(1)} %get-tuple-element.41.powers, bf16[512,1536]{1,0:T(8,128)(2,1)S(1)} %get-tuple-element.42.rounded), custom_call_target="tpu_custom_call" | custom-call | tf_op jit(solution)/shard_map/totals/pallas_call | solution.py:96
  182.0 6.4 %collective-permute-start.12 = (f32[8,264,128]{2,1,0:T(8,128)S(1)}, f32[8,264,128]{2,1,0:T(8,128)S(1)}, u32[]{:S(2)}, u32[]{:S(2)}) collective-permute-start(f32[8,264,128]{2,1,0:T(8,128)S(1)} %get-tuple-element.44), channel_id=1, source_target_pairs={{0,32},{32,0},{1,33},{33,1},{2,34},{34,2},{3,35},{35,3},{4,36},{36... | collective-permute-start | bytes 3244040 | tf_op jit(solution)/shard_map/ppermute | solution.py:385
  188.4 2.3 %collective-permute-done.12 = f32[8,264,128]{2,1,0:T(8,128)S(1)} collective-permute-done((f32[8,264,128]{2,1,0:T(8,128)S(1)}, f32[8,264,128]{2,1,0:T(8,128)S(1)}, u32[]{:S(2)}, u32[]{:S(2)}) %collective-permute-start.12) | collective-permute-done | bytes 1081376 | tf_op jit(solution)/shard_map/ppermute | solution.py:385
  190.7 0.1 add.39
  190.8 19.8 %all_to_all.23.parts = f32[8,264,128]{2,1,0:T(8,128)S(1)} all-to-all(f32[8,264,128]{2,1,0:T(8,128)S(1)} %add.39), channel_id=1, replica_groups=mesh['x'=4,'zl'=2,'core'=2,'yh'=4,'yl'=2,'zhh'=2,'zhl'=2] {'x','zl'}, dimensions={0} | all-to-all | bytes 2162688 | tf_op jit(solution)/shard_map/all_to_all | solution.py:386
  210.6 1.3 final.1
  (12 shorter events, 0.0 us)
Async XLA Ops:
  0.0 12.6 %copy-start.4 = (s32[1,2,64]{2,1,0:T(2,128)S(1)}, s32[1,2,64]{2,1,0:T(2,128)}, u32[]{:S(2)}) copy-start(s32[1,2,64]{2,1,0:T(2,128)} %param.8) | copy-start | bytes 1540
  0.0 0.8 copy-start.3
  3.7 11.9 %collective-permute-start = (f32[64,1536]{1,0:T(8,128)S(1)}, f32[64,1536]{1,0:T(8,128)S(1)}, u32[]{:S(2)}, u32[]{:S(2)}) collective-permute-start(f32[64,1536]{1,0:T(8,128)S(1)} %get-tuple-element.29), channel_id=1, source_target_pairs={{0,4},{4,0},{8,12},{12,8},{16,20},{20,16},{24,28},{28,24},{1,5},{5... | collective-permute-start | bytes 1179656 | tf_op jit(solution)/shard_map/ppermute | solution.py:342
  7.7 11.7 %collective-permute-start.1 = (f32[64,1536]{1,0:T(8,128)S(1)}, f32[64,1536]{1,0:T(8,128)S(1)}, u32[]{:S(2)}, u32[]{:S(2)}) collective-permute-start(f32[64,1536]{1,0:T(8,128)S(1)} %get-tuple-element.30), channel_id=1, source_target_pairs={{0,28},{4,8},{8,4},{12,16},{16,12},{20,24},{24,20},{28,0},{1,29},{... | collective-permute-start | bytes 1179656 | tf_op jit(solution)/shard_map/ppermute | solution.py:342
  19.6 26.5 %collective-permute-start.4 = (f32[4,16,1536]{2,1,0:T(8,128)S(1)}, f32[4,16,1536]{2,1,0:T(8,128)S(1)}, u32[]{:S(2)}, u32[]{:S(2)}) collective-permute-start(f32[4,16,1536]{2,1,0:T(8,128)S(1)} %get-tuple-element.36), channel_id=1, source_target_pairs={{0,1},{1,0},{2,3},{3,2},{4,5},{5,4},{6,7},{7,6},{8,9},{9,8},{10,11... | collective-permute-start | bytes 1179656 | tf_op jit(solution)/shard_map/ppermute | solution.py:342
  27.0 19.1 %collective-permute-start.5 = (f32[4,16,1536]{2,1,0:T(8,128)S(1)}, f32[4,16,1536]{2,1,0:T(8,128)S(1)}, u32[]{:S(2)}, u32[]{:S(2)}) collective-permute-start(f32[4,16,1536]{2,1,0:T(8,128)S(1)} %get-tuple-element.37), channel_id=1, source_target_pairs={{0,3},{1,2},{2,1},{3,0},{4,7},{5,6},{6,5},{7,4},{8,11},{9,10},{10,... | collective-permute-start | bytes 1179656 | tf_op jit(solution)/shard_map/ppermute | solution.py:342
  37.0 10.4 %collective-permute-start.2 = (f32[64,1536]{1,0:T(8,128)S(1)}, f32[64,1536]{1,0:T(8,128)S(1)}, u32[]{:S(2)}, u32[]{:S(2)}) collective-permute-start(f32[64,1536]{1,0:T(8,128)S(1)} %get-tuple-element.34), channel_id=1, source_target_pairs={{0,4},{4,0},{8,12},{12,8},{16,20},{20,16},{24,28},{28,24},{1,5},{5... | collective-permute-start | bytes 1179656 | tf_op jit(solution)/shard_map/ppermute | solution.py:342
  38.9 11.6 %collective-permute-start.3 = (f32[64,1536]{1,0:T(8,128)S(1)}, f32[64,1536]{1,0:T(8,128)S(1)}, u32[]{:S(2)}, u32[]{:S(2)}) collective-permute-start(f32[64,1536]{1,0:T(8,128)S(1)} %get-tuple-element.35), channel_id=1, source_target_pairs={{0,28},{4,8},{8,4},{12,16},{16,12},{20,24},{24,20},{28,0},{1,29},{... | collective-permute-start | bytes 1179656 | tf_op jit(solution)/shard_map/ppermute | solution.py:342
  114.8 18.0 %collective-permute-start.7 = (f32[4,16,1536]{2,1,0:T(8,128)S(1)}, f32[4,16,1536]{2,1,0:T(8,128)S(1)}, u32[]{:S(2)}, u32[]{:S(2)}) collective-permute-start(f32[4,16,1536]{2,1,0:T(8,128)S(1)} %get-tuple-element.47), channel_id=1, source_target_pairs={{0,3},{1,2},{2,1},{3,0},{4,7},{5,6},{6,5},{7,4},{8,11},{9,10},{10,... | collective-permute-start | bytes 1179656 | tf_op jit(solution)/shard_map/ppermute | solution.py:342
  116.7 29.0 %copy-start.5 = (s32[1,2,768]{2,1,0:T(2,128)S(1)}, s32[1,2,768]{2,1,0:T(2,128)}, u32[]{:S(2)}) copy-start(s32[1,2,768]{2,1,0:T(2,128)} %param.9) | copy-start | bytes 18436
  116.7 29.0 %copy-start = (bf16[512,1024]{1,0:T(8,128)(2,1)S(1)}, bf16[512,1024]{1,0:T(8,128)(2,1)}, u32[]{:S(2)}) copy-start(bf16[512,1024]{1,0:T(8,128)(2,1)} %refs.1) | copy-start | bytes 3145732
  116.7 21.7 %collective-permute-start.6 = (f32[4,16,1536]{2,1,0:T(8,128)S(1)}, f32[4,16,1536]{2,1,0:T(8,128)S(1)}, u32[]{:S(2)}, u32[]{:S(2)}) collective-permute-start(f32[4,16,1536]{2,1,0:T(8,128)S(1)} %get-tuple-element.48), channel_id=1, source_target_pairs={{0,1},{1,0},{2,3},{3,2},{4,5},{5,4},{6,7},{7,6},{8,9},{9,8},{10,11... | collective-permute-start | bytes 1179656 | tf_op jit(solution)/shard_map/ppermute | solution.py:342
  120.9 25.5 %collective-permute-start.9 = (f32[8,8,1536]{2,1,0:T(8,128)}, f32[8,8,1536]{2,1,0:T(8,128)}, u32[]{:S(2)}, u32[]{:S(2)}) collective-permute-start(f32[8,8,1536]{2,1,0:T(8,128)} %get-tuple-element.45), channel_id=1, source_target_pairs={{0,28},{4,8},{8,4},{12,16},{16,12},{20,24},{24,20},{28,0},{1,29},{... | collective-permute-start | bytes 1179656 | tf_op jit(solution)/shard_map/ppermute | solution.py:342
  122.8 23.6 %collective-permute-start.8 = (f32[8,8,1536]{2,1,0:T(8,128)}, f32[8,8,1536]{2,1,0:T(8,128)}, u32[]{:S(2)}, u32[]{:S(2)}) collective-permute-start(f32[8,8,1536]{2,1,0:T(8,128)} %get-tuple-element.46), channel_id=1, source_target_pairs={{0,4},{4,0},{8,12},{12,8},{16,20},{20,16},{24,28},{28,24},{1,5},{5... | collective-permute-start | bytes 1179656 | tf_op jit(solution)/shard_map/ppermute | solution.py:342
  138.5 7.2 %copy-start.1 = (f32[4,16,1536]{2,1,0:T(8,128)}, f32[4,16,1536]{2,1,0:T(8,128)S(1)}, u32[]{:S(2)}) copy-start(f32[4,16,1536]{2,1,0:T(8,128)S(1)} %collective-permute-done.6.low) | copy-start | bytes 1179652
  139.5 11.7 %collective-permute-start.10 = (f32[8,8,1536]{2,1,0:T(8,128)}, f32[8,8,1536]{2,1,0:T(8,128)}, u32[]{:S(2)}, u32[]{:S(2)}) collective-permute-start(f32[8,8,1536]{2,1,0:T(8,128)} %get-tuple-element.38), channel_id=1, source_target_pairs={{0,4},{4,0},{8,12},{12,8},{16,20},{20,16},{24,28},{28,24},{1,5},{5... | collective-permute-start | bytes 1179656 | tf_op jit(solution)/shard_map/ppermute | solution.py:342
  141.4 12.9 %collective-permute-start.11 = (f32[8,8,1536]{2,1,0:T(8,128)}, f32[8,8,1536]{2,1,0:T(8,128)}, u32[]{:S(2)}, u32[]{:S(2)}) collective-permute-start(f32[8,8,1536]{2,1,0:T(8,128)} %get-tuple-element.39), channel_id=1, source_target_pairs={{0,28},{4,8},{8,4},{12,16},{16,12},{20,24},{24,20},{28,0},{1,29},{... | collective-permute-start | bytes 1179656 | tf_op jit(solution)/shard_map/ppermute | solution.py:342
  146.4 1.0 copy-start.2
  182.0 8.7 %collective-permute-start.12 = (f32[8,264,128]{2,1,0:T(8,128)S(1)}, f32[8,264,128]{2,1,0:T(8,128)S(1)}, u32[]{:S(2)}, u32[]{:S(2)}) collective-permute-start(f32[8,264,128]{2,1,0:T(8,128)S(1)} %get-tuple-element.44), channel_id=1, source_target_pairs={{0,32},{32,0},{1,33},{33,1},{2,34},{34,2},{3,35},{35,3},{4,36},{36... | collective-permute-start | bytes 3244040 | tf_op jit(solution)/shard_map/ppermute | solution.py:385

commit v8 on v7

--- a/solution.py
+++ b/solution.py
@@ -215,16 +215,16 @@
         scores = jnp.dot(refs_t[...], rounded[:, cut], preferred_element_type=jnp.float32)
         block = prior[:, cut] - at[4] * (orient // OBLOCK)
         parts = [
-            scores[k * OBLOCK : (k + 1) * OBLOCK] + jnp.where(block == k, PRIOR_INCREMENT, 0.0)
+            (scores[k * OBLOCK : (k + 1) * OBLOCK], jnp.where(block == k, PRIOR_INCREMENT, 0.0))
             for k in range(orient // OBLOCK)
         ]
-        tops = [jnp.max(part, axis=0, keepdims=True) for part in parts]
+        tops = [jnp.max(part, axis=0, keepdims=True) + bonus for part, bonus in parts]
         top = tops[0]
         for other in tops[1:]:
             top = jnp.maximum(top, other)
         total = jnp.zeros_like(top)
-        for k, part in enumerate(parts):
-            power = jnp.exp(part - top)
+        for k, (part, bonus) in enumerate(parts):
+            power = jnp.exp(part - (top - bonus))
             powers[k * OBLOCK : (k + 1) * OBLOCK, cut] = power
             total = total + jnp.sum(power, axis=0, keepdims=True)
         for h in range(width // LANES):
@@ -249,58 +249,56 @@
     return whole(score_kernel, "scores", (*held, prior, refs_t), shapes, at=at, params=BIG)
 
 
-def total_kernel(at, stats, own, powers, rounded, keep, send, factor):
+def total_kernel(other, at, stats, own, powers, rounded, out, factor, mine):
     width = 256
     eigen, rows = rounded.shape
-    peers = keep.shape[0]
+    peers = out.shape[0]
     share = eigen // (2 * peers)
     lines = rows // LANES
-    body = keep.shape[1] - keep.shape[1] % share
+    body = out.shape[1] - out.shape[1] % share
     tops = stats[:, :lines, :]
     top = jnp.max(tops, axis=0)
     total = jnp.sum(stats[:, lines:, :] * jnp.exp(tops - top[None]), axis=0)
     scale = jnp.exp(own[0, :lines, :] - top) / total
     for k in range(lines):
         factor[:, k * LANES : (k + 1) * LANES] = scale[k : k + 1, :]
-    first = at[5] == 0
+    core = 1 - at[5] if other else at[5]
+    for q in range(peers):
+        place = pl.multiple_of((2 * q + core) * share, share)
+        mine[q * share : (q + 1) * share, :] = rounded[pl.ds(place, share), :]
     ones = jnp.ones((16, rows), jnp.bfloat16)
 
     def orients(step, carry):
         block = powers[pl.ds(pl.multiple_of(step * width, width), width), :]
         weights = (block * factor[...]).astype(jnp.bfloat16)
-        totals = lax.dot_general(rounded[...], weights, LAST, preferred_element_type=jnp.float32)
+        totals = lax.dot_general(mine[...], weights, LAST, preferred_element_type=jnp.float32)
         masses = lax.dot_general(ones, weights, LAST, preferred_element_type=jnp.float32)
         for h in range(width // LANES):
             column = step * (width // LANES) + h
             cut = slice(h * LANES, (h + 1) * LANES)
             place = pl.ds(pl.multiple_of(column * share, share), share)
             for q in range(peers):
-                even = totals[2 * q * share : (2 * q + 1) * share, cut]
-                odd = totals[(2 * q + 1) * share : (2 * q + 2) * share, cut]
-                keep[q, place, :] = jnp.where(first, even, odd)
-                send[q, place, :] = jnp.where(first, odd, even)
+                out[q, place, :] = totals[q * share : (q + 1) * share, cut]
             mass = jnp.broadcast_to(masses[None, 0:1, cut], (peers, 1, LANES))
-            keep[:, pl.ds(body + column, 1), :] = mass
-            send[:, pl.ds(body + column, 1), :] = mass
+            out[:, pl.ds(body + column, 1), :] = mass
         return carry
 
     lax.fori_loop(0, powers.shape[0] // width, orients, 0)
 
 
-def totals_of(at, stats, sent, powers, rounded, peers):
+def totals_of(other, at, stats, sent, powers, rounded, peers):
     eigen, rows = rounded.shape
     orient = powers.shape[0]
     deep = (eigen // (2 * peers) + 1) * (orient // LANES)
-    shape = ((peers, deep, LANES), jnp.float32)
     return whole(
-        total_kernel,
+        functools.partial(total_kernel, other),
         "totals",
         (stats, sent, powers, rounded),
-        [shape, shape],
+        [((peers, deep, LANES), jnp.float32)],
         at=at,
-        scratch=[pltpu.VMEM((1, rows), jnp.float32)],
+        scratch=[pltpu.VMEM((1, rows), jnp.float32), pltpu.VMEM((eigen // 2, rows), jnp.bfloat16)],
         params=BIG,
-    )
+    )[0]
 
 
 def final_kernel(at, parts, refs, out):
@@ -381,8 +379,9 @@
         lax.axis_size(MEM),
     )
     stats = lax.all_to_all(sent, MEM, 0, 0, tiled=True)
-    keep, send = totals_of(at, stats, sent, powers, rounded, lax.axis_size(PEERS))
-    parts = keep + lax.ppermute(send, "core", [(0, 1), (1, 0)])
+    sums = (stats, sent, powers, rounded, lax.axis_size(PEERS))
+    came = lax.ppermute(totals_of(True, at, *sums), "core", [(0, 1), (1, 0)])
+    parts = totals_of(False, at, *sums) + came
     parts = lax.all_to_all(parts, PEERS, 0, 0, tiled=True)
     return final_of(at, parts, refs)
 

time: 214 us -> 214 us (level)
  waiting for transfers between devices: 26.6 us -> 24.3 us
  Pallas kernels: 24.9 us -> 27.1 us
    ppermute x1, waiting for transfers between devices: 2.31 us -> 0.01 us  [shards(): came = lax.ppermute(totals_of(True, at, *sums), 'core', [(0, 1), (1, 0)])]
    pallas_call x7 -> x8, Pallas kernels: 12 us -> 14.1 us  [whole(): pl.pallas_call(kernel, in_specs=[pl.BlockSpec(memory_space=pltpu.SMEM)] *...]
  transfers between devices with their start and end apart: 13 -> 13, of which waited for: 8 -> 7; matrix products, arithmetic and copies ran while one was open for 1% -> 1% of each run, Pallas kernels for 5% -> 7%
where the time goes in v8:
time: 214 us; the launch traced here: 212 us
  blocking collectives  103 us (48%)
  starting transfers between devices  54.2 us (25%)
  Pallas kernels  27.1 us (13%)
  waiting for transfers between devices  24.3 us (11%)
  local copies, waits for them, and re-layouts  3.44 us (2%)
    ppermute x12, starting transfers between devices, swapped(): lax.ppermute(x, axis, p)  47.8 us
    all_to_all x1, blocking collectives, shards(): parts = lax.all_to_all(parts, ALIKE, 0, 0, tiled=True)  35 us
    all_to_all x1, blocking collectives, shards(): own = lax.all_to_all(summed_copies(parts), ALIKE, 0, 0, tiled=True)  29 us
    ppermute x12, waiting for transfers between devices, swapped(): lax.ppermute(x, axis, p)  24.3 us
    all_to_all x1, blocking collectives, shards(): parts = lax.all_to_all(parts, PEERS, 0, 0, tiled=True)  20.1 us
    all_to_all x1, blocking collectives, shards(): stats = lax.all_to_all(sent, MEM, 0, 0, tiled=True)  18.5 us
    pallas_call x8, Pallas kernels, whole(): pl.pallas_call(kernel, in_specs=[pl.BlockSpec(memory_space=pltpu.SMEM)] *...  14.1 us
    pallas_call x4, Pallas kernels, projected(): pl.pallas_call(project_kernel, grid_spec=pltpu.PrefetchScalarGridSpec(num...  11.7 us
  transfers between devices with their start and end apart: 13, of which 7 were waited for; matrix products, arithmetic and copies ran while one was open for 1% of the time, Pallas kernels for 7%

profile of v8, /device:TPU:1, one launch (start us, length us, event | category | flops | bytes accessed | tf_op | source)
XLA Modules:
  0.0 212.0 jit_solution(5459570918537037109)
XLA Ops:
  0.0 0.7 copy-done.3
  0.8 2.9 %project.6 = (f32[64,1536]{1,0:T(8,128)S(1)}, f32[64,1536]{1,0:T(8,128)S(1)}) custom-call(s32[1]{0:T(128)} %bitcast.at, s32[2,64]{1,0:T(2,128)S(1)} %bitcast.14, bf16[1536,512]{1,0:T(8,128)(2,1)} %bitcast.18, bf16[512,512]{1,0:T(8,128)(2,1)} %basis.7, bf16[1,512]{1,0:T(2,128)(2,1)} %phantom.7), custom_call_target="tpu_custom_call" | custom-call | tf_op jit(solution)/shard_map/project/pallas_call | solution.py:73
  3.7 4.0 %collective-permute-start = (f32[64,1536]{1,0:T(8,128)S(1)}, f32[64,1536]{1,0:T(8,128)S(1)}, u32[]{:S(2)}, u32[]{:S(2)}) collective-permute-start(f32[64,1536]{1,0:T(8,128)S(1)} %get-tuple-element.27), channel_id=1, source_target_pairs={{0,4},{4,0},{8,12},{12,8},{16,20},{20,16},{24,28},{28,24},{1,5},{5... | collective-permute-start | bytes 1179656 | tf_op jit(solution)/shard_map/ppermute | solution.py:340
  7.7 4.9 %collective-permute-start.1 = (f32[64,1536]{1,0:T(8,128)S(1)}, f32[64,1536]{1,0:T(8,128)S(1)}, u32[]{:S(2)}, u32[]{:S(2)}) collective-permute-start(f32[64,1536]{1,0:T(8,128)S(1)} %get-tuple-element.28), channel_id=1, source_target_pairs={{0,28},{4,8},{8,4},{12,16},{16,12},{20,24},{24,20},{28,0},{1,29},{... | collective-permute-start | bytes 1179656 | tf_op jit(solution)/shard_map/ppermute | solution.py:340
  12.6 2.9 %project.5 = (f32[64,1536]{1,0:T(8,128)S(1)}, f32[64,1536]{1,0:T(8,128)S(1)}) custom-call(s32[1]{0:T(128)} %bitcast.2.at, s32[2,64]{1,0:T(2,128)S(1)} %bitcast.15, bf16[1536,512]{1,0:T(8,128)(2,1)} %bitcast.19, bf16[512,512]{1,0:T(8,128)(2,1)} %basis.7, bf16[1,512]{1,0:T(2,128)(2,1)} %phantom.7), custom_call_target="tpu_custom_call" | custom-call | tf_op jit(solution)/shard_map/project/pallas_call | solution.py:73
  15.5 0.0 collective-permute-done.came_a
  15.5 3.9 %collective-permute-done.1.came_b = f32[64,1536]{1,0:T(8,128)S(1)} collective-permute-done((f32[64,1536]{1,0:T(8,128)S(1)}, f32[64,1536]{1,0:T(8,128)S(1)}, u32[]{:S(2)}, u32[]{:S(2)}) %collective-permute-start.1) | collective-permute-done | bytes 393248 | tf_op jit(solution)/shard_map/ppermute | solution.py:340
  19.5 0.1 relay.1
  19.6 7.5 %collective-permute-start.4 = (f32[4,16,1536]{2,1,0:T(8,128)S(1)}, f32[4,16,1536]{2,1,0:T(8,128)S(1)}, u32[]{:S(2)}, u32[]{:S(2)}) collective-permute-start(f32[4,16,1536]{2,1,0:T(8,128)S(1)} %get-tuple-element.34), channel_id=1, source_target_pairs={{0,1},{1,0},{2,3},{3,2},{4,5},{5,4},{6,7},{7,6},{8,9},{9,8},{10,11... | collective-permute-start | bytes 1179656 | tf_op jit(solution)/shard_map/ppermute | solution.py:340
  27.0 7.0 %collective-permute-start.5 = (f32[4,16,1536]{2,1,0:T(8,128)S(1)}, f32[4,16,1536]{2,1,0:T(8,128)S(1)}, u32[]{:S(2)}, u32[]{:S(2)}) collective-permute-start(f32[4,16,1536]{2,1,0:T(8,128)S(1)} %get-tuple-element.35), channel_id=1, source_target_pairs={{0,3},{1,2},{2,1},{3,0},{4,7},{5,6},{6,5},{7,4},{8,11},{9,10},{10,... | collective-permute-start | bytes 1179656 | tf_op jit(solution)/shard_map/ppermute | solution.py:340
  34.0 2.9 %project.7 = (f32[64,1536]{1,0:T(8,128)S(1)}, f32[64,1536]{1,0:T(8,128)S(1)}) custom-call(s32[1]{0:T(128)} %bitcast.1.at, s32[2,64]{1,0:T(2,128)S(1)} %bitcast.16, bf16[1536,512]{1,0:T(8,128)(2,1)} %bitcast.20, bf16[512,512]{1,0:T(8,128)(2,1)} %basis.7, bf16[1,512]{1,0:T(2,128)(2,1)} %phantom.7), custom_call_target="tpu_custom_call" | custom-call | tf_op jit(solution)/shard_map/project/pallas_call | solution.py:73
  37.0 1.9 collective-permute-start.2
  38.9 4.2 %collective-permute-start.3 = (f32[64,1536]{1,0:T(8,128)S(1)}, f32[64,1536]{1,0:T(8,128)S(1)}, u32[]{:S(2)}, u32[]{:S(2)}) collective-permute-start(f32[64,1536]{1,0:T(8,128)S(1)} %get-tuple-element.33), channel_id=1, source_target_pairs={{0,28},{4,8},{8,4},{12,16},{16,12},{20,24},{24,20},{28,0},{1,29},{... | collective-permute-start | bytes 1179656 | tf_op jit(solution)/shard_map/ppermute | solution.py:340
  43.2 2.9 %project.4 = (f32[64,1536]{1,0:T(8,128)S(1)}, f32[64,1536]{1,0:T(8,128)S(1)}) custom-call(s32[1]{0:T(128)} %bitcast.3.at, s32[2,64]{1,0:T(2,128)S(1)} %bitcast.17, bf16[1536,512]{1,0:T(8,128)(2,1)} %bitcast.21, bf16[512,512]{1,0:T(8,128)(2,1)} %basis.7, bf16[1,512]{1,0:T(2,128)(2,1)} %phantom.7), custom_call_target="tpu_custom_call" | custom-call | tf_op jit(solution)/shard_map/project/pallas_call | solution.py:73
  46.1 0.0 collective-permute-done.4.low
  46.1 1.3 collective-permute-done.2.came_a
  47.4 3.1 %collective-permute-done.3.came_b = f32[64,1536]{1,0:T(8,128)S(1)} collective-permute-done((f32[64,1536]{1,0:T(8,128)S(1)}, f32[64,1536]{1,0:T(8,128)S(1)}, u32[]{:S(2)}, u32[]{:S(2)}) %collective-permute-start.3) | collective-permute-done | bytes 393248 | tf_op jit(solution)/shard_map/ppermute | solution.py:340
  50.5 0.1 join.1
  50.6 35.0 %all_to_all.20.parts = f32[8,16,1536]{2,1,0:T(8,128)S(1)} all-to-all(f32[8,16,1536]{2,1,0:T(8,128)S(1)} %join.1), channel_id=1, replica_groups=mesh['x'=4,'zl'=2,'core'=2,'yh'=4,'yl'=2,'zhh'=2,'zhl'=2] {'yh','zhh'}, dimensions={0} | all-to-all | bytes 1572864 | tf_op jit(solution)/shard_map/all_to_all | solution.py:368
  85.6 0.1 spread.1
  85.8 29.0 %all_to_all.21.own = f32[8,16,1536]{2,1,0:T(8,128)S(1)} all-to-all(f32[8,16,1536]{2,1,0:T(8,128)S(1)} %spread.1), channel_id=1, replica_groups=mesh['x'=4,'zl'=2,'core'=2,'yh'=4,'yl'=2,'zhh'=2,'zhl'=2] {'yh','zhh'}, dimensions={0} | all-to-all | bytes 1572864 | tf_op jit(solution)/shard_map/all_to_all | solution.py:369
  114.7 0.1 fusion.1
  114.8 1.9 collective-permute-start.7
  116.7 0.0 copy-start.5
  116.7 0.0 copy-start
  116.7 3.1 %collective-permute-start.6 = (f32[4,16,1536]{2,1,0:T(8,128)S(1)}, f32[4,16,1536]{2,1,0:T(8,128)S(1)}, u32[]{:S(2)}, u32[]{:S(2)}) collective-permute-start(f32[4,16,1536]{2,1,0:T(8,128)S(1)} %get-tuple-element.44), channel_id=1, source_target_pairs={{0,1},{1,0},{2,3},{3,2},{4,5},{5,4},{6,7},{7,6},{8,9},{9,8},{10,11... | collective-permute-start | bytes 1179656 | tf_op jit(solution)/shard_map/ppermute | solution.py:340
  119.9 1.0 fusion
  120.9 1.9 collective-permute-start.9
  122.8 5.1 %collective-permute-start.8 = (f32[8,8,1536]{2,1,0:T(8,128)}, f32[8,8,1536]{2,1,0:T(8,128)}, u32[]{:S(2)}, u32[]{:S(2)}) collective-permute-start(f32[8,8,1536]{2,1,0:T(8,128)} %get-tuple-element.42), channel_id=1, source_target_pairs={{0,4},{4,0},{8,12},{12,8},{16,20},{20,16},{24,28},{28,24},{1,5},{5... | collective-permute-start | bytes 1179656 | tf_op jit(solution)/shard_map/ppermute | solution.py:340
  127.9 4.9 %collective-permute-done.7.high = f32[4,16,1536]{2,1,0:T(8,128)S(1)} collective-permute-done((f32[4,16,1536]{2,1,0:T(8,128)S(1)}, f32[4,16,1536]{2,1,0:T(8,128)S(1)}, u32[]{:S(2)}, u32[]{:S(2)}) %collective-permute-start.7) | collective-permute-done | bytes 393248 | tf_op jit(solution)/shard_map/ppermute | solution.py:340
  132.8 5.7 %collective-permute-done.6.low = f32[4,16,1536]{2,1,0:T(8,128)S(1)} collective-permute-done((f32[4,16,1536]{2,1,0:T(8,128)S(1)}, f32[4,16,1536]{2,1,0:T(8,128)S(1)}, u32[]{:S(2)}, u32[]{:S(2)}) %collective-permute-start.6) | collective-permute-done | bytes 393248 | tf_op jit(solution)/shard_map/ppermute | solution.py:340
  138.5 1.0 peel.1
  139.4 1.9 collective-permute-start.10
  141.4 4.3 %collective-permute-start.11 = (f32[8,8,1536]{2,1,0:T(8,128)}, f32[8,8,1536]{2,1,0:T(8,128)}, u32[]{:S(2)}, u32[]{:S(2)}) collective-permute-start(f32[8,8,1536]{2,1,0:T(8,128)} %get-tuple-element.37), channel_id=1, source_target_pairs={{0,28},{4,8},{8,4},{12,16},{16,12},{20,24},{24,20},{28,0},{1,29},{... | collective-permute-start | bytes 1179656 | tf_op jit(solution)/shard_map/ppermute | solution.py:340
  145.7 0.5 copy.7
  146.3 0.1 stack.31.at
  146.4 1.0 copy-done.2
  147.4 1.4 stage.1.staged
  148.8 2.3 %collective-permute-done.10.far_a = f32[8,8,1536]{2,1,0:T(8,128)} collective-permute-done((f32[8,8,1536]{2,1,0:T(8,128)}, f32[8,8,1536]{2,1,0:T(8,128)}, u32[]{:S(2)}, u32[]{:S(2)}) %collective-permute-start.10) | collective-permute-done | bytes 393248 | tf_op jit(solution)/shard_map/ppermute | solution.py:340
  151.1 3.1 %collective-permute-done.11.far_b = f32[8,8,1536]{2,1,0:T(8,128)} collective-permute-done((f32[8,8,1536]{2,1,0:T(8,128)}, f32[8,8,1536]{2,1,0:T(8,128)}, u32[]{:S(2)}, u32[]{:S(2)}) %collective-permute-start.11) | collective-permute-done | bytes 393248 | tf_op jit(solution)/shard_map/ppermute | solution.py:340
  154.3 5.2 %scores.1 = (f32[1024,1536]{1,0:T(8,128)S(1)}, bf16[512,1536]{1,0:T(8,128)(2,1)S(1)}, f32[32,24,128]{2,1,0:T(8,128)S(1)}) custom-call(s32[7]{0:T(128)S(1)} %stack.31.at, bf16[512,1536]{1,0:T(8,128)(2,1)S(1)} %stage.1.staged, f32[8,8,1536]{2,1,0:T(8,128)} %collective-permute-done.10.far_a, f32[8,8,1536]{2,1,0:T(8,128)} %collective-permute-done.11.far_b, ...), custom_call_target="tpu_custom_call" | custom-call | tf_op jit(solution)/shard_map/scores/pallas_call | solution.py:96
  159.5 18.5 %all_to_all.22.stats = f32[32,24,128]{2,1,0:T(8,128)S(1)} all-to-all(f32[32,24,128]{2,1,0:T(8,128)S(1)} %get-tuple-element.38.own), channel_id=1, replica_groups=mesh['x'=4,'zl'=2,'core'=2,'yh'=4,'yl'=2,'zhh'=2,'zhl'=2] {'yh','yl','zh..., dimensions={0} | all-to-all | bytes 786432 | tf_op jit(solution)/shard_map/all_to_all | solution.py:381
  178.0 3.1 %totals.3 = f32[8,264,128]{2,1,0:T(8,128)S(1)} custom-call(s32[7]{0:T(128)S(1)} %stack.31.at, f32[32,24,128]{2,1,0:T(8,128)S(1)} %all_to_all.22.stats, f32[32,24,128]{2,1,0:T(8,128)S(1)} %get-tuple-element.38.own, f32[1024,1536]{1,0:T(8,128)S(1)} %get-tuple-element.39.powers, bf16[512,1536]{1,0:T(8,128)(2,1)S(1)} %get-tuple-element.40.rounded), custom_call_target="tpu_custom_call" | custom-call | tf_op jit(solution)/shard_map/totals/pallas_call | solution.py:96
  181.1 6.3 %collective-permute-start.12 = (f32[8,264,128]{2,1,0:T(8,128)S(1)}, f32[8,264,128]{2,1,0:T(8,128)S(1)}, u32[]{:S(2)}, u32[]{:S(2)}) collective-permute-start(f32[8,264,128]{2,1,0:T(8,128)S(1)} %totals.3), channel_id=1, source_target_pairs={{0,32},{32,0},{1,33},{33,1},{2,34},{34,2},{3,35},{35,3},{4,36},{36... | collective-permute-start | bytes 3244040 | tf_op jit(solution)/shard_map/ppermute | solution.py:383
  187.5 3.1 %totals.2 = f32[8,264,128]{2,1,0:T(8,128)S(1)} custom-call(s32[7]{0:T(128)S(1)} %stack.31.at, f32[32,24,128]{2,1,0:T(8,128)S(1)} %all_to_all.22.stats, f32[32,24,128]{2,1,0:T(8,128)S(1)} %get-tuple-element.38.own, f32[1024,1536]{1,0:T(8,128)S(1)} %get-tuple-element.39.powers, bf16[512,1536]{1,0:T(8,128)(2,1)S(1)} %get-tuple-element.40.rounded), custom_call_target="tpu_custom_call" | custom-call | tf_op jit(solution)/shard_map/totals/pallas_call | solution.py:96
  190.6 0.1 add.39
  190.7 20.1 %all_to_all.23.parts = f32[8,264,128]{2,1,0:T(8,128)S(1)} all-to-all(f32[8,264,128]{2,1,0:T(8,128)S(1)} %add.39), channel_id=1, replica_groups=mesh['x'=4,'zl'=2,'core'=2,'yh'=4,'yl'=2,'zhh'=2,'zhl'=2] {'x','zl'}, dimensions={0} | all-to-all | bytes 2162688 | tf_op jit(solution)/shard_map/all_to_all | solution.py:385
  210.8 1.3 final.1
  (13 shorter events, 0.0 us)
Async XLA Ops:
  0.0 12.6 %copy-start.4 = (s32[1,2,64]{2,1,0:T(2,128)S(1)}, s32[1,2,64]{2,1,0:T(2,128)}, u32[]{:S(2)}) copy-start(s32[1,2,64]{2,1,0:T(2,128)} %param.8) | copy-start | bytes 1540
  0.0 0.8 copy-start.3
  3.7 11.9 %collective-permute-start = (f32[64,1536]{1,0:T(8,128)S(1)}, f32[64,1536]{1,0:T(8,128)S(1)}, u32[]{:S(2)}, u32[]{:S(2)}) collective-permute-start(f32[64,1536]{1,0:T(8,128)S(1)} %get-tuple-element.27), channel_id=1, source_target_pairs={{0,4},{4,0},{8,12},{12,8},{16,20},{20,16},{24,28},{28,24},{1,5},{5... | collective-permute-start | bytes 1179656 | tf_op jit(solution)/shard_map/ppermute | solution.py:340
  7.7 11.7 %collective-permute-start.1 = (f32[64,1536]{1,0:T(8,128)S(1)}, f32[64,1536]{1,0:T(8,128)S(1)}, u32[]{:S(2)}, u32[]{:S(2)}) collective-permute-start(f32[64,1536]{1,0:T(8,128)S(1)} %get-tuple-element.28), channel_id=1, source_target_pairs={{0,28},{4,8},{8,4},{12,16},{16,12},{20,24},{24,20},{28,0},{1,29},{... | collective-permute-start | bytes 1179656 | tf_op jit(solution)/shard_map/ppermute | solution.py:340
  19.6 26.5 %collective-permute-start.4 = (f32[4,16,1536]{2,1,0:T(8,128)S(1)}, f32[4,16,1536]{2,1,0:T(8,128)S(1)}, u32[]{:S(2)}, u32[]{:S(2)}) collective-permute-start(f32[4,16,1536]{2,1,0:T(8,128)S(1)} %get-tuple-element.34), channel_id=1, source_target_pairs={{0,1},{1,0},{2,3},{3,2},{4,5},{5,4},{6,7},{7,6},{8,9},{9,8},{10,11... | collective-permute-start | bytes 1179656 | tf_op jit(solution)/shard_map/ppermute | solution.py:340
  27.0 19.1 %collective-permute-start.5 = (f32[4,16,1536]{2,1,0:T(8,128)S(1)}, f32[4,16,1536]{2,1,0:T(8,128)S(1)}, u32[]{:S(2)}, u32[]{:S(2)}) collective-permute-start(f32[4,16,1536]{2,1,0:T(8,128)S(1)} %get-tuple-element.35), channel_id=1, source_target_pairs={{0,3},{1,2},{2,1},{3,0},{4,7},{5,6},{6,5},{7,4},{8,11},{9,10},{10,... | collective-permute-start | bytes 1179656 | tf_op jit(solution)/shard_map/ppermute | solution.py:340
  37.0 10.4 %collective-permute-start.2 = (f32[64,1536]{1,0:T(8,128)S(1)}, f32[64,1536]{1,0:T(8,128)S(1)}, u32[]{:S(2)}, u32[]{:S(2)}) collective-permute-start(f32[64,1536]{1,0:T(8,128)S(1)} %get-tuple-element.32), channel_id=1, source_target_pairs={{0,4},{4,0},{8,12},{12,8},{16,20},{20,16},{24,28},{28,24},{1,5},{5... | collective-permute-start | bytes 1179656 | tf_op jit(solution)/shard_map/ppermute | solution.py:340
  38.9 11.6 %collective-permute-start.3 = (f32[64,1536]{1,0:T(8,128)S(1)}, f32[64,1536]{1,0:T(8,128)S(1)}, u32[]{:S(2)}, u32[]{:S(2)}) collective-permute-start(f32[64,1536]{1,0:T(8,128)S(1)} %get-tuple-element.33), channel_id=1, source_target_pairs={{0,28},{4,8},{8,4},{12,16},{16,12},{20,24},{24,20},{28,0},{1,29},{... | collective-permute-start | bytes 1179656 | tf_op jit(solution)/shard_map/ppermute | solution.py:340
  114.8 18.0 %collective-permute-start.7 = (f32[4,16,1536]{2,1,0:T(8,128)S(1)}, f32[4,16,1536]{2,1,0:T(8,128)S(1)}, u32[]{:S(2)}, u32[]{:S(2)}) collective-permute-start(f32[4,16,1536]{2,1,0:T(8,128)S(1)} %get-tuple-element.43), channel_id=1, source_target_pairs={{0,3},{1,2},{2,1},{3,0},{4,7},{5,6},{6,5},{7,4},{8,11},{9,10},{10,... | collective-permute-start | bytes 1179656 | tf_op jit(solution)/shard_map/ppermute | solution.py:340
  116.7 29.0 %copy-start.5 = (s32[1,2,768]{2,1,0:T(2,128)S(1)}, s32[1,2,768]{2,1,0:T(2,128)}, u32[]{:S(2)}) copy-start(s32[1,2,768]{2,1,0:T(2,128)} %param.9) | copy-start | bytes 18436
  116.7 29.0 %copy-start = (bf16[512,1024]{1,0:T(8,128)(2,1)S(1)}, bf16[512,1024]{1,0:T(8,128)(2,1)}, u32[]{:S(2)}) copy-start(bf16[512,1024]{1,0:T(8,128)(2,1)} %refs.1) | copy-start | bytes 3145732
  116.7 21.7 %collective-permute-start.6 = (f32[4,16,1536]{2,1,0:T(8,128)S(1)}, f32[4,16,1536]{2,1,0:T(8,128)S(1)}, u32[]{:S(2)}, u32[]{:S(2)}) collective-permute-start(f32[4,16,1536]{2,1,0:T(8,128)S(1)} %get-tuple-element.44), channel_id=1, source_target_pairs={{0,1},{1,0},{2,3},{3,2},{4,5},{5,4},{6,7},{7,6},{8,9},{9,8},{10,11... | collective-permute-start | bytes 1179656 | tf_op jit(solution)/shard_map/ppermute | solution.py:340
  120.9 25.5 %collective-permute-start.9 = (f32[8,8,1536]{2,1,0:T(8,128)}, f32[8,8,1536]{2,1,0:T(8,128)}, u32[]{:S(2)}, u32[]{:S(2)}) collective-permute-start(f32[8,8,1536]{2,1,0:T(8,128)} %get-tuple-element.41), channel_id=1, source_target_pairs={{0,28},{4,8},{8,4},{12,16},{16,12},{20,24},{24,20},{28,0},{1,29},{... | collective-permute-start | bytes 1179656 | tf_op jit(solution)/shard_map/ppermute | solution.py:340
  122.8 23.6 %collective-permute-start.8 = (f32[8,8,1536]{2,1,0:T(8,128)}, f32[8,8,1536]{2,1,0:T(8,128)}, u32[]{:S(2)}, u32[]{:S(2)}) collective-permute-start(f32[8,8,1536]{2,1,0:T(8,128)} %get-tuple-element.42), channel_id=1, source_target_pairs={{0,4},{4,0},{8,12},{12,8},{16,20},{20,16},{24,28},{28,24},{1,5},{5... | collective-permute-start | bytes 1179656 | tf_op jit(solution)/shard_map/ppermute | solution.py:340
  138.5 7.2 %copy-start.1 = (f32[4,16,1536]{2,1,0:T(8,128)}, f32[4,16,1536]{2,1,0:T(8,128)S(1)}, u32[]{:S(2)}) copy-start(f32[4,16,1536]{2,1,0:T(8,128)S(1)} %collective-permute-done.6.low) | copy-start | bytes 1179652
  139.4 11.7 %collective-permute-start.10 = (f32[8,8,1536]{2,1,0:T(8,128)}, f32[8,8,1536]{2,1,0:T(8,128)}, u32[]{:S(2)}, u32[]{:S(2)}) collective-permute-start(f32[8,8,1536]{2,1,0:T(8,128)} %get-tuple-element.36), channel_id=1, source_target_pairs={{0,4},{4,0},{8,12},{12,8},{16,20},{20,16},{24,28},{28,24},{1,5},{5... | collective-permute-start | bytes 1179656 | tf_op jit(solution)/shard_map/ppermute | solution.py:340
  141.4 12.9 %collective-permute-start.11 = (f32[8,8,1536]{2,1,0:T(8,128)}, f32[8,8,1536]{2,1,0:T(8,128)}, u32[]{:S(2)}, u32[]{:S(2)}) collective-permute-start(f32[8,8,1536]{2,1,0:T(8,128)} %get-tuple-element.37), channel_id=1, source_target_pairs={{0,28},{4,8},{8,4},{12,16},{16,12},{20,24},{24,20},{28,0},{1,29},{... | collective-permute-start | bytes 1179656 | tf_op jit(solution)/shard_map/ppermute | solution.py:340
  146.4 1.0 copy-start.2
  181.1 9.4 %collective-permute-start.12 = (f32[8,264,128]{2,1,0:T(8,128)S(1)}, f32[8,264,128]{2,1,0:T(8,128)S(1)}, u32[]{:S(2)}, u32[]{:S(2)}) collective-permute-start(f32[8,264,128]{2,1,0:T(8,128)S(1)} %totals.3), channel_id=1, source_target_pairs={{0,32},{32,0},{1,33},{33,1},{2,34},{34,2},{3,35},{35,3},{4,36},{36... | collective-permute-start | bytes 3244040 | tf_op jit(solution)/shard_map/ppermute | solution.py:383

commit v9 on v8

--- a/solution.py
+++ b/solution.py
@@ -13,8 +13,9 @@
 RING = ("yh", "yl")
 TALL = ("zhh", "zhl")
 MEM = RING + TALL
-ALIKE = ("yh", "zhh")
-PEERS = ("x", "zl")
+ALIKE = ("zhh", "yh")
+EVERY = ("zhl", "zhh", "yl", "yh")
+PEERS = ("zl", "x")
 LANES = 128
 BIG = pltpu.CompilerParams(vmem_limit_bytes=16 << 20)
 SMALL = pltpu.CompilerParams(vmem_limit_bytes=8 << 20)
@@ -249,7 +250,7 @@
     return whole(score_kernel, "scores", (*held, prior, refs_t), shapes, at=at, params=BIG)
 
 
-def total_kernel(other, at, stats, own, powers, rounded, out, factor, mine):
+def total_kernel(other, outer, at, stats, own, powers, rounded, out, factor, mine):
     width = 256
     eigen, rows = rounded.shape
     peers = out.shape[0]
@@ -264,7 +265,8 @@
         factor[:, k * LANES : (k + 1) * LANES] = scale[k : k + 1, :]
     core = 1 - at[5] if other else at[5]
     for q in range(peers):
-        place = pl.multiple_of((2 * q + core) * share, share)
+        owner = q % (peers // outer) * outer + q // (peers // outer)
+        place = pl.multiple_of((2 * owner + core) * share, share)
         mine[q * share : (q + 1) * share, :] = rounded[pl.ds(place, share), :]
     ones = jnp.ones((16, rows), jnp.bfloat16)
 
@@ -291,7 +293,7 @@
     orient = powers.shape[0]
     deep = (eigen // (2 * peers) + 1) * (orient // LANES)
     return whole(
-        functools.partial(total_kernel, other),
+        functools.partial(total_kernel, other, lax.axis_size(PEERS[0])),
         "totals",
         (stats, sent, powers, rounded),
         [((peers, deep, LANES), jnp.float32)],
@@ -378,7 +380,7 @@
         refs.T,
         lax.axis_size(MEM),
     )
-    stats = lax.all_to_all(sent, MEM, 0, 0, tiled=True)
+    stats = lax.all_to_all(sent, EVERY, 0, 0, tiled=True)
     sums = (stats, sent, powers, rounded, lax.axis_size(PEERS))
     came = lax.ppermute(totals_of(True, at, *sums), "core", [(0, 1), (1, 0)])
     parts = totals_of(False, at, *sums) + came

time: 214 us -> 215 us (level)
  starting transfers between devices: 54.2 us -> 48.2 us
  waiting for transfers between devices: 24.3 us -> 29.8 us
    ppermute x12, waiting for transfers between devices: 24.3 us -> 29.7 us  [swapped(): lax.ppermute(x, axis, p)]
    ppermute x12, starting transfers between devices: 47.8 us -> 42.9 us  [swapped(): lax.ppermute(x, axis, p)]
where the time goes in v9:
time: 215 us; the launch traced here: 214 us
  blocking collectives  105 us (49%)
  starting transfers between devices  48.2 us (22%)
  waiting for transfers between devices  29.8 us (14%)
  Pallas kernels  27.1 us (13%)
  local copies, waits for them, and re-layouts  3.44 us (2%)
    ppermute x12, starting transfers between devices, swapped(): lax.ppermute(x, axis, p)  42.9 us
    all_to_all x1, blocking collectives, shards(): parts = lax.all_to_all(parts, ALIKE, 0, 0, tiled=True)  35.1 us
    all_to_all x1, blocking collectives, shards(): own = lax.all_to_all(summed_copies(parts), ALIKE, 0, 0, tiled=True)  30.4 us
    ppermute x12, waiting for transfers between devices, swapped(): lax.ppermute(x, axis, p)  29.7 us
    all_to_all x1, blocking collectives, shards(): stats = lax.all_to_all(sent, EVERY, 0, 0, tiled=True)  20.3 us
    all_to_all x1, blocking collectives, shards(): parts = lax.all_to_all(parts, PEERS, 0, 0, tiled=True)  19.4 us
    pallas_call x8, Pallas kernels, whole(): pl.pallas_call(kernel, in_specs=[pl.BlockSpec(memory_space=pltpu.SMEM)] *...  14.1 us
    pallas_call x4, Pallas kernels, projected(): pl.pallas_call(project_kernel, grid_spec=pltpu.PrefetchScalarGridSpec(num...  11.7 us
  transfers between devices with their start and end apart: 13, of which 7 were waited for; matrix products, arithmetic and copies ran while one was open for 1% of the time, Pallas kernels for 7%

profile of v9, /device:TPU:1, one launch (start us, length us, event | category | flops | bytes accessed | tf_op | source)
XLA Modules:
  0.0 213.9 jit_solution(5194961195935748423)
XLA Ops:
  0.0 0.7 copy-done.3
  0.8 2.9 %project.6 = (f32[64,1536]{1,0:T(8,128)S(1)}, f32[64,1536]{1,0:T(8,128)S(1)}) custom-call(s32[1]{0:T(128)} %bitcast.at, s32[2,64]{1,0:T(2,128)S(1)} %bitcast.14, bf16[1536,512]{1,0:T(8,128)(2,1)} %bitcast.18, bf16[512,512]{1,0:T(8,128)(2,1)} %basis.7, bf16[1,512]{1,0:T(2,128)(2,1)} %phantom.7), custom_call_target="tpu_custom_call" | custom-call | tf_op jit(solution)/shard_map/project/pallas_call | solution.py:74
  3.7 4.0 %collective-permute-start = (f32[64,1536]{1,0:T(8,128)S(1)}, f32[64,1536]{1,0:T(8,128)S(1)}, u32[]{:S(2)}, u32[]{:S(2)}) collective-permute-start(f32[64,1536]{1,0:T(8,128)S(1)} %get-tuple-element.27), channel_id=1, source_target_pairs={{0,4},{4,0},{8,12},{12,8},{16,20},{20,16},{24,28},{28,24},{1,5},{5... | collective-permute-start | bytes 1179656 | tf_op jit(solution)/shard_map/ppermute | solution.py:342
  7.7 4.9 %collective-permute-start.1 = (f32[64,1536]{1,0:T(8,128)S(1)}, f32[64,1536]{1,0:T(8,128)S(1)}, u32[]{:S(2)}, u32[]{:S(2)}) collective-permute-start(f32[64,1536]{1,0:T(8,128)S(1)} %get-tuple-element.28), channel_id=1, source_target_pairs={{0,28},{4,8},{8,4},{12,16},{16,12},{20,24},{24,20},{28,0},{1,29},{... | collective-permute-start | bytes 1179656 | tf_op jit(solution)/shard_map/ppermute | solution.py:342
  12.6 2.9 %project.5 = (f32[64,1536]{1,0:T(8,128)S(1)}, f32[64,1536]{1,0:T(8,128)S(1)}) custom-call(s32[1]{0:T(128)} %bitcast.2.at, s32[2,64]{1,0:T(2,128)S(1)} %bitcast.15, bf16[1536,512]{1,0:T(8,128)(2,1)} %bitcast.19, bf16[512,512]{1,0:T(8,128)(2,1)} %basis.7, bf16[1,512]{1,0:T(2,128)(2,1)} %phantom.7), custom_call_target="tpu_custom_call" | custom-call | tf_op jit(solution)/shard_map/project/pallas_call | solution.py:74
  15.5 0.0 collective-permute-done.came_a
  15.5 3.9 %collective-permute-done.1.came_b = f32[64,1536]{1,0:T(8,128)S(1)} collective-permute-done((f32[64,1536]{1,0:T(8,128)S(1)}, f32[64,1536]{1,0:T(8,128)S(1)}, u32[]{:S(2)}, u32[]{:S(2)}) %collective-permute-start.1) | collective-permute-done | bytes 393248 | tf_op jit(solution)/shard_map/ppermute | solution.py:342
  19.5 0.1 relay.1
  19.6 7.5 %collective-permute-start.4 = (f32[4,16,1536]{2,1,0:T(8,128)S(1)}, f32[4,16,1536]{2,1,0:T(8,128)S(1)}, u32[]{:S(2)}, u32[]{:S(2)}) collective-permute-start(f32[4,16,1536]{2,1,0:T(8,128)S(1)} %get-tuple-element.34), channel_id=1, source_target_pairs={{0,1},{1,0},{2,3},{3,2},{4,5},{5,4},{6,7},{7,6},{8,9},{9,8},{10,11... | collective-permute-start | bytes 1179656 | tf_op jit(solution)/shard_map/ppermute | solution.py:342
  27.0 7.0 %collective-permute-start.5 = (f32[4,16,1536]{2,1,0:T(8,128)S(1)}, f32[4,16,1536]{2,1,0:T(8,128)S(1)}, u32[]{:S(2)}, u32[]{:S(2)}) collective-permute-start(f32[4,16,1536]{2,1,0:T(8,128)S(1)} %get-tuple-element.35), channel_id=1, source_target_pairs={{0,3},{1,2},{2,1},{3,0},{4,7},{5,6},{6,5},{7,4},{8,11},{9,10},{10,... | collective-permute-start | bytes 1179656 | tf_op jit(solution)/shard_map/ppermute | solution.py:342
  34.0 2.9 %project.7 = (f32[64,1536]{1,0:T(8,128)S(1)}, f32[64,1536]{1,0:T(8,128)S(1)}) custom-call(s32[1]{0:T(128)} %bitcast.1.at, s32[2,64]{1,0:T(2,128)S(1)} %bitcast.16, bf16[1536,512]{1,0:T(8,128)(2,1)} %bitcast.20, bf16[512,512]{1,0:T(8,128)(2,1)} %basis.7, bf16[1,512]{1,0:T(2,128)(2,1)} %phantom.7), custom_call_target="tpu_custom_call" | custom-call | tf_op jit(solution)/shard_map/project/pallas_call | solution.py:74
  37.0 1.9 collective-permute-start.2
  38.9 4.2 %collective-permute-start.3 = (f32[64,1536]{1,0:T(8,128)S(1)}, f32[64,1536]{1,0:T(8,128)S(1)}, u32[]{:S(2)}, u32[]{:S(2)}) collective-permute-start(f32[64,1536]{1,0:T(8,128)S(1)} %get-tuple-element.33), channel_id=1, source_target_pairs={{0,28},{4,8},{8,4},{12,16},{16,12},{20,24},{24,20},{28,0},{1,29},{... | collective-permute-start | bytes 1179656 | tf_op jit(solution)/shard_map/ppermute | solution.py:342
  43.2 2.9 %project.4 = (f32[64,1536]{1,0:T(8,128)S(1)}, f32[64,1536]{1,0:T(8,128)S(1)}) custom-call(s32[1]{0:T(128)} %bitcast.3.at, s32[2,64]{1,0:T(2,128)S(1)} %bitcast.17, bf16[1536,512]{1,0:T(8,128)(2,1)} %bitcast.21, bf16[512,512]{1,0:T(8,128)(2,1)} %basis.7, bf16[1,512]{1,0:T(2,128)(2,1)} %phantom.7), custom_call_target="tpu_custom_call" | custom-call | tf_op jit(solution)/shard_map/project/pallas_call | solution.py:74
  46.1 0.0 collective-permute-done.4.low
  46.1 1.3 collective-permute-done.2.came_a
  47.4 3.1 %collective-permute-done.3.came_b = f32[64,1536]{1,0:T(8,128)S(1)} collective-permute-done((f32[64,1536]{1,0:T(8,128)S(1)}, f32[64,1536]{1,0:T(8,128)S(1)}, u32[]{:S(2)}, u32[]{:S(2)}) %collective-permute-start.3) | collective-permute-done | bytes 393248 | tf_op jit(solution)/shard_map/ppermute | solution.py:342
  50.5 0.1 join.1
  50.6 35.1 %all_to_all.20.parts = f32[8,16,1536]{2,1,0:T(8,128)S(1)} all-to-all(f32[8,16,1536]{2,1,0:T(8,128)S(1)} %join.1), channel_id=1, replica_groups=mesh['x'=4,'zl'=2,'core'=2,'yh'=4,'yl'=2,'zhh'=2,'zhl'=2] {'zhh','yh'}, dimensions={0} | all-to-all | bytes 1572864 | tf_op jit(solution)/shard_map/all_to_all | solution.py:370
  85.7 0.1 spread.1
  85.9 30.4 %all_to_all.21.own = f32[8,16,1536]{2,1,0:T(8,128)S(1)} all-to-all(f32[8,16,1536]{2,1,0:T(8,128)S(1)} %spread.1), channel_id=1, replica_groups=mesh['x'=4,'zl'=2,'core'=2,'yh'=4,'yl'=2,'zhh'=2,'zhl'=2] {'zhh','yh'}, dimensions={0} | all-to-all | bytes 1572864 | tf_op jit(solution)/shard_map/all_to_all | solution.py:371
  116.2 0.1 fusion.1
  116.3 1.9 collective-permute-start.7
  118.2 0.0 copy-start.5
  118.2 0.0 copy-start
  118.2 2.4 %collective-permute-start.6 = (f32[4,16,1536]{2,1,0:T(8,128)S(1)}, f32[4,16,1536]{2,1,0:T(8,128)S(1)}, u32[]{:S(2)}, u32[]{:S(2)}) collective-permute-start(f32[4,16,1536]{2,1,0:T(8,128)S(1)} %get-tuple-element.44), channel_id=1, source_target_pairs={{0,1},{1,0},{2,3},{3,2},{4,5},{5,4},{6,7},{7,6},{8,9},{9,8},{10,11... | collective-permute-start | bytes 1179656 | tf_op jit(solution)/shard_map/ppermute | solution.py:342
  120.7 1.0 fusion
  121.7 1.9 collective-permute-start.9
  123.6 3.2 %collective-permute-start.8 = (f32[8,8,1536]{2,1,0:T(8,128)}, f32[8,8,1536]{2,1,0:T(8,128)}, u32[]{:S(2)}, u32[]{:S(2)}) collective-permute-start(f32[8,8,1536]{2,1,0:T(8,128)} %get-tuple-element.42), channel_id=1, source_target_pairs={{0,4},{4,0},{8,12},{12,8},{16,20},{20,16},{24,28},{28,24},{1,5},{5... | collective-permute-start | bytes 1179656 | tf_op jit(solution)/shard_map/ppermute | solution.py:342
  126.8 11.4 %collective-permute-done.7.high = f32[4,16,1536]{2,1,0:T(8,128)S(1)} collective-permute-done((f32[4,16,1536]{2,1,0:T(8,128)S(1)}, f32[4,16,1536]{2,1,0:T(8,128)S(1)}, u32[]{:S(2)}, u32[]{:S(2)}) %collective-permute-start.7) | collective-permute-done | bytes 393248 | tf_op jit(solution)/shard_map/ppermute | solution.py:342
  138.2 1.5 collective-permute-done.6.low
  139.7 1.0 peel.1
  140.7 1.9 collective-permute-start.10
  142.6 1.9 collective-permute-start.11
  144.6 0.5 copy.7
  145.2 0.1 stack.31.at
  145.3 1.0 copy-done.2
  146.3 1.4 stage.1.staged
  147.7 5.4 %collective-permute-done.10.far_a = f32[8,8,1536]{2,1,0:T(8,128)} collective-permute-done((f32[8,8,1536]{2,1,0:T(8,128)}, f32[8,8,1536]{2,1,0:T(8,128)}, u32[]{:S(2)}, u32[]{:S(2)}) %collective-permute-start.10) | collective-permute-done | bytes 393248 | tf_op jit(solution)/shard_map/ppermute | solution.py:342
  153.1 3.1 %collective-permute-done.11.far_b = f32[8,8,1536]{2,1,0:T(8,128)} collective-permute-done((f32[8,8,1536]{2,1,0:T(8,128)}, f32[8,8,1536]{2,1,0:T(8,128)}, u32[]{:S(2)}, u32[]{:S(2)}) %collective-permute-start.11) | collective-permute-done | bytes 393248 | tf_op jit(solution)/shard_map/ppermute | solution.py:342
  156.2 5.2 %scores.1 = (f32[1024,1536]{1,0:T(8,128)S(1)}, bf16[512,1536]{1,0:T(8,128)(2,1)S(1)}, f32[32,24,128]{2,1,0:T(8,128)S(1)}) custom-call(s32[7]{0:T(128)S(1)} %stack.31.at, bf16[512,1536]{1,0:T(8,128)(2,1)S(1)} %stage.1.staged, f32[8,8,1536]{2,1,0:T(8,128)} %collective-permute-done.10.far_a, f32[8,8,1536]{2,1,0:T(8,128)} %collective-permute-done.11.far_b, ...), custom_call_target="tpu_custom_call" | custom-call | tf_op jit(solution)/shard_map/scores/pallas_call | solution.py:97
  161.5 20.3 %all_to_all.22.stats = f32[32,24,128]{2,1,0:T(8,128)S(1)} all-to-all(f32[32,24,128]{2,1,0:T(8,128)S(1)} %get-tuple-element.38.own), channel_id=1, replica_groups=mesh['x'=4,'zl'=2,'core'=2,'yh'=4,'yl'=2,'zhh'=2,'zhl'=2] {'zhl','zhh','..., dimensions={0} | all-to-all | bytes 786432 | tf_op jit(solution)/shard_map/all_to_all | solution.py:383
  181.7 3.1 %totals.3 = f32[8,264,128]{2,1,0:T(8,128)S(1)} custom-call(s32[7]{0:T(128)S(1)} %stack.31.at, f32[32,24,128]{2,1,0:T(8,128)S(1)} %all_to_all.22.stats, f32[32,24,128]{2,1,0:T(8,128)S(1)} %get-tuple-element.38.own, f32[1024,1536]{1,0:T(8,128)S(1)} %get-tuple-element.39.powers, bf16[512,1536]{1,0:T(8,128)(2,1)S(1)} %get-tuple-element.40.rounded), custom_call_target="tpu_custom_call" | custom-call | tf_op jit(solution)/shard_map/totals/pallas_call | solution.py:97
  184.8 5.3 %collective-permute-start.12 = (f32[8,264,128]{2,1,0:T(8,128)S(1)}, f32[8,264,128]{2,1,0:T(8,128)S(1)}, u32[]{:S(2)}, u32[]{:S(2)}) collective-permute-start(f32[8,264,128]{2,1,0:T(8,128)S(1)} %totals.3), channel_id=1, source_target_pairs={{0,32},{32,0},{1,33},{33,1},{2,34},{34,2},{3,35},{35,3},{4,36},{36... | collective-permute-start | bytes 3244040 | tf_op jit(solution)/shard_map/ppermute | solution.py:385
  190.1 3.1 %totals.2 = f32[8,264,128]{2,1,0:T(8,128)S(1)} custom-call(s32[7]{0:T(128)S(1)} %stack.31.at, f32[32,24,128]{2,1,0:T(8,128)S(1)} %all_to_all.22.stats, f32[32,24,128]{2,1,0:T(8,128)S(1)} %get-tuple-element.38.own, f32[1024,1536]{1,0:T(8,128)S(1)} %get-tuple-element.39.powers, bf16[512,1536]{1,0:T(8,128)(2,1)S(1)} %get-tuple-element.40.rounded), custom_call_target="tpu_custom_call" | custom-call | tf_op jit(solution)/shard_map/totals/pallas_call | solution.py:97
  193.2 0.1 add.39
  193.3 19.4 %all_to_all.23.parts = f32[8,264,128]{2,1,0:T(8,128)S(1)} all-to-all(f32[8,264,128]{2,1,0:T(8,128)S(1)} %add.39), channel_id=1, replica_groups=mesh['x'=4,'zl'=2,'core'=2,'yh'=4,'yl'=2,'zhh'=2,'zhl'=2] {'zl','x'}, dimensions={0} | all-to-all | bytes 2162688 | tf_op jit(solution)/shard_map/all_to_all | solution.py:387
  212.7 1.3 final.1
  (13 shorter events, 0.0 us)
Async XLA Ops:
  0.0 12.6 %copy-start.4 = (s32[1,2,64]{2,1,0:T(2,128)S(1)}, s32[1,2,64]{2,1,0:T(2,128)}, u32[]{:S(2)}) copy-start(s32[1,2,64]{2,1,0:T(2,128)} %param.8) | copy-start | bytes 1540
  0.0 0.8 copy-start.3
  3.7 11.9 %collective-permute-start = (f32[64,1536]{1,0:T(8,128)S(1)}, f32[64,1536]{1,0:T(8,128)S(1)}, u32[]{:S(2)}, u32[]{:S(2)}) collective-permute-start(f32[64,1536]{1,0:T(8,128)S(1)} %get-tuple-element.27), channel_id=1, source_target_pairs={{0,4},{4,0},{8,12},{12,8},{16,20},{20,16},{24,28},{28,24},{1,5},{5... | collective-permute-start | bytes 1179656 | tf_op jit(solution)/shard_map/ppermute | solution.py:342
  7.7 11.7 %collective-permute-start.1 = (f32[64,1536]{1,0:T(8,128)S(1)}, f32[64,1536]{1,0:T(8,128)S(1)}, u32[]{:S(2)}, u32[]{:S(2)}) collective-permute-start(f32[64,1536]{1,0:T(8,128)S(1)} %get-tuple-element.28), channel_id=1, source_target_pairs={{0,28},{4,8},{8,4},{12,16},{16,12},{20,24},{24,20},{28,0},{1,29},{... | collective-permute-start | bytes 1179656 | tf_op jit(solution)/shard_map/ppermute | solution.py:342
  19.6 26.5 %collective-permute-start.4 = (f32[4,16,1536]{2,1,0:T(8,128)S(1)}, f32[4,16,1536]{2,1,0:T(8,128)S(1)}, u32[]{:S(2)}, u32[]{:S(2)}) collective-permute-start(f32[4,16,1536]{2,1,0:T(8,128)S(1)} %get-tuple-element.34), channel_id=1, source_target_pairs={{0,1},{1,0},{2,3},{3,2},{4,5},{5,4},{6,7},{7,6},{8,9},{9,8},{10,11... | collective-permute-start | bytes 1179656 | tf_op jit(solution)/shard_map/ppermute | solution.py:342
  27.0 19.1 %collective-permute-start.5 = (f32[4,16,1536]{2,1,0:T(8,128)S(1)}, f32[4,16,1536]{2,1,0:T(8,128)S(1)}, u32[]{:S(2)}, u32[]{:S(2)}) collective-permute-start(f32[4,16,1536]{2,1,0:T(8,128)S(1)} %get-tuple-element.35), channel_id=1, source_target_pairs={{0,3},{1,2},{2,1},{3,0},{4,7},{5,6},{6,5},{7,4},{8,11},{9,10},{10,... | collective-permute-start | bytes 1179656 | tf_op jit(solution)/shard_map/ppermute | solution.py:342
  37.0 10.4 %collective-permute-start.2 = (f32[64,1536]{1,0:T(8,128)S(1)}, f32[64,1536]{1,0:T(8,128)S(1)}, u32[]{:S(2)}, u32[]{:S(2)}) collective-permute-start(f32[64,1536]{1,0:T(8,128)S(1)} %get-tuple-element.32), channel_id=1, source_target_pairs={{0,4},{4,0},{8,12},{12,8},{16,20},{20,16},{24,28},{28,24},{1,5},{5... | collective-permute-start | bytes 1179656 | tf_op jit(solution)/shard_map/ppermute | solution.py:342
  38.9 11.6 %collective-permute-start.3 = (f32[64,1536]{1,0:T(8,128)S(1)}, f32[64,1536]{1,0:T(8,128)S(1)}, u32[]{:S(2)}, u32[]{:S(2)}) collective-permute-start(f32[64,1536]{1,0:T(8,128)S(1)} %get-tuple-element.33), channel_id=1, source_target_pairs={{0,28},{4,8},{8,4},{12,16},{16,12},{20,24},{24,20},{28,0},{1,29},{... | collective-permute-start | bytes 1179656 | tf_op jit(solution)/shard_map/ppermute | solution.py:342
  116.3 22.0 %collective-permute-start.7 = (f32[4,16,1536]{2,1,0:T(8,128)S(1)}, f32[4,16,1536]{2,1,0:T(8,128)S(1)}, u32[]{:S(2)}, u32[]{:S(2)}) collective-permute-start(f32[4,16,1536]{2,1,0:T(8,128)S(1)} %get-tuple-element.43), channel_id=1, source_target_pairs={{0,3},{1,2},{2,1},{3,0},{4,7},{5,6},{6,5},{7,4},{8,11},{9,10},{10,... | collective-permute-start | bytes 1179656 | tf_op jit(solution)/shard_map/ppermute | solution.py:342
  118.2 26.4 %copy-start.5 = (s32[1,2,768]{2,1,0:T(2,128)S(1)}, s32[1,2,768]{2,1,0:T(2,128)}, u32[]{:S(2)}) copy-start(s32[1,2,768]{2,1,0:T(2,128)} %param.9) | copy-start | bytes 18436
  118.2 26.4 %copy-start = (bf16[512,1024]{1,0:T(8,128)(2,1)S(1)}, bf16[512,1024]{1,0:T(8,128)(2,1)}, u32[]{:S(2)}) copy-start(bf16[512,1024]{1,0:T(8,128)(2,1)} %refs.1) | copy-start | bytes 3145732
  118.2 21.5 %collective-permute-start.6 = (f32[4,16,1536]{2,1,0:T(8,128)S(1)}, f32[4,16,1536]{2,1,0:T(8,128)S(1)}, u32[]{:S(2)}, u32[]{:S(2)}) collective-permute-start(f32[4,16,1536]{2,1,0:T(8,128)S(1)} %get-tuple-element.44), channel_id=1, source_target_pairs={{0,1},{1,0},{2,3},{3,2},{4,5},{5,4},{6,7},{7,6},{8,9},{9,8},{10,11... | collective-permute-start | bytes 1179656 | tf_op jit(solution)/shard_map/ppermute | solution.py:342
  121.7 23.6 %collective-permute-start.9 = (f32[8,8,1536]{2,1,0:T(8,128)}, f32[8,8,1536]{2,1,0:T(8,128)}, u32[]{:S(2)}, u32[]{:S(2)}) collective-permute-start(f32[8,8,1536]{2,1,0:T(8,128)} %get-tuple-element.41), channel_id=1, source_target_pairs={{0,28},{4,8},{8,4},{12,16},{16,12},{20,24},{24,20},{28,0},{1,29},{... | collective-permute-start | bytes 1179656 | tf_op jit(solution)/shard_map/ppermute | solution.py:342
  123.6 21.7 %collective-permute-start.8 = (f32[8,8,1536]{2,1,0:T(8,128)}, f32[8,8,1536]{2,1,0:T(8,128)}, u32[]{:S(2)}, u32[]{:S(2)}) collective-permute-start(f32[8,8,1536]{2,1,0:T(8,128)} %get-tuple-element.42), channel_id=1, source_target_pairs={{0,4},{4,0},{8,12},{12,8},{16,20},{20,16},{24,28},{28,24},{1,5},{5... | collective-permute-start | bytes 1179656 | tf_op jit(solution)/shard_map/ppermute | solution.py:342
  139.7 4.9 %copy-start.1 = (f32[4,16,1536]{2,1,0:T(8,128)}, f32[4,16,1536]{2,1,0:T(8,128)S(1)}, u32[]{:S(2)}) copy-start(f32[4,16,1536]{2,1,0:T(8,128)S(1)} %collective-permute-done.6.low) | copy-start | bytes 1179652
  140.7 12.4 %collective-permute-start.10 = (f32[8,8,1536]{2,1,0:T(8,128)}, f32[8,8,1536]{2,1,0:T(8,128)}, u32[]{:S(2)}, u32[]{:S(2)}) collective-permute-start(f32[8,8,1536]{2,1,0:T(8,128)} %get-tuple-element.36), channel_id=1, source_target_pairs={{0,4},{4,0},{8,12},{12,8},{16,20},{20,16},{24,28},{28,24},{1,5},{5... | collective-permute-start | bytes 1179656 | tf_op jit(solution)/shard_map/ppermute | solution.py:342
  142.6 13.6 %collective-permute-start.11 = (f32[8,8,1536]{2,1,0:T(8,128)}, f32[8,8,1536]{2,1,0:T(8,128)}, u32[]{:S(2)}, u32[]{:S(2)}) collective-permute-start(f32[8,8,1536]{2,1,0:T(8,128)} %get-tuple-element.37), channel_id=1, source_target_pairs={{0,28},{4,8},{8,4},{12,16},{16,12},{20,24},{24,20},{28,0},{1,29},{... | collective-permute-start | bytes 1179656 | tf_op jit(solution)/shard_map/ppermute | solution.py:342
  145.3 1.0 copy-start.2
  184.8 8.4 %collective-permute-start.12 = (f32[8,264,128]{2,1,0:T(8,128)S(1)}, f32[8,264,128]{2,1,0:T(8,128)S(1)}, u32[]{:S(2)}, u32[]{:S(2)}) collective-permute-start(f32[8,264,128]{2,1,0:T(8,128)S(1)} %totals.3), channel_id=1, source_target_pairs={{0,32},{32,0},{1,33},{33,1},{2,34},{34,2},{3,35},{35,3},{4,36},{36... | collective-permute-start | bytes 3244040 | tf_op jit(solution)/shard_map/ppermute | solution.py:385

commit v10 on v9

--- a/solution.py
+++ b/solution.py
@@ -13,7 +13,7 @@
 RING = ("yh", "yl")
 TALL = ("zhh", "zhl")
 MEM = RING + TALL
-ALIKE = ("zhh", "yh")
+ALIKE = ("yh", "zhh")
 EVERY = ("zhl", "zhh", "yl", "yh")
 PEERS = ("zl", "x")
 LANES = 128
@@ -68,8 +68,8 @@
     steps = 2 * inject.shape[0]
     count = basis.shape[1] // 4
     out = jax.ShapeDtypeStruct((count // pieces, rows), jnp.float32)
-    images, basis, phantom = (
-        pltpu.with_memory_space_constraint(x, pltpu.HBM) for x in (images, basis, phantom)
+    inject, images, basis, phantom = (
+        pltpu.with_memory_space_constraint(x, pltpu.HBM) for x in (inject, images, basis, phantom)
     )
     found = pl.pallas_call(
         project_kernel,

time: 215 us -> 214 us (level)
  waiting for transfers between devices: 29.8 us -> 23.9 us
  starting transfers between devices: 48.2 us -> 52.6 us
    ppermute x12, waiting for transfers between devices: 29.7 us -> 23.9 us  [swapped(): lax.ppermute(x, axis, p)]
    ppermute x12, starting transfers between devices: 42.9 us -> 47.5 us  [swapped(): lax.ppermute(x, axis, p)]
where the time goes in v10:
time: 214 us; the launch traced here: 213 us
  blocking collectives  106 us (50%)
  starting transfers between devices  52.6 us (25%)
  Pallas kernels  27.6 us (13%)
  waiting for transfers between devices  23.9 us (11%)
  local copies, waits for them, and re-layouts  2.69 us (1%)
    ppermute x12, starting transfers between devices, swapped(): lax.ppermute(x, axis, p)  47.5 us
    all_to_all x1, blocking collectives, shards(): parts = lax.all_to_all(parts, ALIKE, 0, 0, tiled=True)  34.9 us
    all_to_all x1, blocking collectives, shards(): own = lax.all_to_all(summed_copies(parts), ALIKE, 0, 0, tiled=True)  29 us
    ppermute x12, waiting for transfers between devices, swapped(): lax.ppermute(x, axis, p)  23.9 us
    all_to_all x1, blocking collectives, shards(): stats = lax.all_to_all(sent, EVERY, 0, 0, tiled=True)  22.1 us
    all_to_all x1, blocking collectives, shards(): parts = lax.all_to_all(parts, PEERS, 0, 0, tiled=True)  19.7 us
    pallas_call x8, Pallas kernels, whole(): pl.pallas_call(kernel, in_specs=[pl.BlockSpec(memory_space=pltpu.SMEM)] *...  14.1 us
    pallas_call x4, Pallas kernels, projected(): pl.pallas_call(project_kernel, grid_spec=pltpu.PrefetchScalarGridSpec(num...  12.2 us
  transfers between devices with their start and end apart: 13, of which 7 were waited for; matrix products, arithmetic and copies ran while one was open for 1% of the time, Pallas kernels for 7%

profile of v10, /device:TPU:1, one launch (start us, length us, event | category | flops | bytes accessed | tf_op | source)
XLA Modules:
  0.0 213.0 jit_solution(1089717676878408017)
XLA Ops:
  0.0 3.0 %project.6 = (f32[64,1536]{1,0:T(8,128)S(1)}, f32[64,1536]{1,0:T(8,128)S(1)}) custom-call(s32[1]{0:T(128)} %bitcast.at, s32[2,64]{1,0:T(2,128)} %bitcast.18, bf16[1536,512]{1,0:T(8,128)(2,1)} %bitcast.14, bf16[512,512]{1,0:T(8,128)(2,1)} %basis.7, bf16[1,512]{1,0:T(2,128)(2,1)} %phantom.7), custom_call_target="tpu_custom_call" | custom-call | tf_op jit(solution)/shard_map/project/pallas_call | solution.py:74
  3.1 4.0 %collective-permute-start = (f32[64,1536]{1,0:T(8,128)S(1)}, f32[64,1536]{1,0:T(8,128)S(1)}, u32[]{:S(2)}, u32[]{:S(2)}) collective-permute-start(f32[64,1536]{1,0:T(8,128)S(1)} %get-tuple-element.27), channel_id=1, source_target_pairs={{0,4},{4,0},{8,12},{12,8},{16,20},{20,16},{24,28},{28,24},{1,5},{5... | collective-permute-start | bytes 1179656 | tf_op jit(solution)/shard_map/ppermute | solution.py:342
  7.1 4.9 %collective-permute-start.1 = (f32[64,1536]{1,0:T(8,128)S(1)}, f32[64,1536]{1,0:T(8,128)S(1)}, u32[]{:S(2)}, u32[]{:S(2)}) collective-permute-start(f32[64,1536]{1,0:T(8,128)S(1)} %get-tuple-element.28), channel_id=1, source_target_pairs={{0,28},{4,8},{8,4},{12,16},{16,12},{20,24},{24,20},{28,0},{1,29},{... | collective-permute-start | bytes 1179656 | tf_op jit(solution)/shard_map/ppermute | solution.py:342
  12.0 3.1 %project.5 = (f32[64,1536]{1,0:T(8,128)S(1)}, f32[64,1536]{1,0:T(8,128)S(1)}) custom-call(s32[1]{0:T(128)} %bitcast.2.at, s32[2,64]{1,0:T(2,128)} %bitcast.19, bf16[1536,512]{1,0:T(8,128)(2,1)} %bitcast.15, bf16[512,512]{1,0:T(8,128)(2,1)} %basis.7, bf16[1,512]{1,0:T(2,128)(2,1)} %phantom.7), custom_call_target="tpu_custom_call" | custom-call | tf_op jit(solution)/shard_map/project/pallas_call | solution.py:74
  15.1 3.8 %collective-permute-done.1.came_b = f32[64,1536]{1,0:T(8,128)S(1)} collective-permute-done((f32[64,1536]{1,0:T(8,128)S(1)}, f32[64,1536]{1,0:T(8,128)S(1)}, u32[]{:S(2)}, u32[]{:S(2)}) %collective-permute-start.1) | collective-permute-done | bytes 393248 | tf_op jit(solution)/shard_map/ppermute | solution.py:342
  18.8 0.1 relay.1
  18.9 7.5 %collective-permute-start.4 = (f32[4,16,1536]{2,1,0:T(8,128)S(1)}, f32[4,16,1536]{2,1,0:T(8,128)S(1)}, u32[]{:S(2)}, u32[]{:S(2)}) collective-permute-start(f32[4,16,1536]{2,1,0:T(8,128)S(1)} %get-tuple-element.34), channel_id=1, source_target_pairs={{0,1},{1,0},{2,3},{3,2},{4,5},{5,4},{6,7},{7,6},{8,9},{9,8},{10,11... | collective-permute-start | bytes 1179656 | tf_op jit(solution)/shard_map/ppermute | solution.py:342
  26.4 7.0 %collective-permute-start.5 = (f32[4,16,1536]{2,1,0:T(8,128)S(1)}, f32[4,16,1536]{2,1,0:T(8,128)S(1)}, u32[]{:S(2)}, u32[]{:S(2)}) collective-permute-start(f32[4,16,1536]{2,1,0:T(8,128)S(1)} %get-tuple-element.35), channel_id=1, source_target_pairs={{0,3},{1,2},{2,1},{3,0},{4,7},{5,6},{6,5},{7,4},{8,11},{9,10},{10,... | collective-permute-start | bytes 1179656 | tf_op jit(solution)/shard_map/ppermute | solution.py:342
  33.4 3.1 %project.7 = (f32[64,1536]{1,0:T(8,128)S(1)}, f32[64,1536]{1,0:T(8,128)S(1)}) custom-call(s32[1]{0:T(128)} %bitcast.1.at, s32[2,64]{1,0:T(2,128)} %bitcast.20, bf16[1536,512]{1,0:T(8,128)(2,1)} %bitcast.16, bf16[512,512]{1,0:T(8,128)(2,1)} %basis.7, bf16[1,512]{1,0:T(2,128)(2,1)} %phantom.7), custom_call_target="tpu_custom_call" | custom-call | tf_op jit(solution)/shard_map/project/pallas_call | solution.py:74
  36.5 1.9 collective-permute-start.2
  38.4 4.2 %collective-permute-start.3 = (f32[64,1536]{1,0:T(8,128)S(1)}, f32[64,1536]{1,0:T(8,128)S(1)}, u32[]{:S(2)}, u32[]{:S(2)}) collective-permute-start(f32[64,1536]{1,0:T(8,128)S(1)} %get-tuple-element.33), channel_id=1, source_target_pairs={{0,28},{4,8},{8,4},{12,16},{16,12},{20,24},{24,20},{28,0},{1,29},{... | collective-permute-start | bytes 1179656 | tf_op jit(solution)/shard_map/ppermute | solution.py:342
  42.7 3.1 %project.4 = (f32[64,1536]{1,0:T(8,128)S(1)}, f32[64,1536]{1,0:T(8,128)S(1)}) custom-call(s32[1]{0:T(128)} %bitcast.3.at, s32[2,64]{1,0:T(2,128)} %bitcast.21, bf16[1536,512]{1,0:T(8,128)(2,1)} %bitcast.17, bf16[512,512]{1,0:T(8,128)(2,1)} %basis.7, bf16[1,512]{1,0:T(2,128)(2,1)} %phantom.7), custom_call_target="tpu_custom_call" | custom-call | tf_op jit(solution)/shard_map/project/pallas_call | solution.py:74
  45.7 0.0 collective-permute-done.5.high
  45.8 1.1 collective-permute-done.2.came_a
  46.9 3.1 %collective-permute-done.3.came_b = f32[64,1536]{1,0:T(8,128)S(1)} collective-permute-done((f32[64,1536]{1,0:T(8,128)S(1)}, f32[64,1536]{1,0:T(8,128)S(1)}, u32[]{:S(2)}, u32[]{:S(2)}) %collective-permute-start.3) | collective-permute-done | bytes 393248 | tf_op jit(solution)/shard_map/ppermute | solution.py:342
  50.0 0.1 join.1
  50.1 34.9 %all_to_all.20.parts = f32[8,16,1536]{2,1,0:T(8,128)S(1)} all-to-all(f32[8,16,1536]{2,1,0:T(8,128)S(1)} %join.1), channel_id=1, replica_groups=mesh['x'=4,'zl'=2,'core'=2,'yh'=4,'yl'=2,'zhh'=2,'zhl'=2] {'yh','zhh'}, dimensions={0} | all-to-all | bytes 1572864 | tf_op jit(solution)/shard_map/all_to_all | solution.py:370
  85.1 0.1 spread.1
  85.2 29.0 %all_to_all.21.own = f32[8,16,1536]{2,1,0:T(8,128)S(1)} all-to-all(f32[8,16,1536]{2,1,0:T(8,128)S(1)} %spread.1), channel_id=1, replica_groups=mesh['x'=4,'zl'=2,'core'=2,'yh'=4,'yl'=2,'zhh'=2,'zhl'=2] {'yh','zhh'}, dimensions={0} | all-to-all | bytes 1572864 | tf_op jit(solution)/shard_map/all_to_all | solution.py:371
  114.2 0.1 fusion.1
  114.3 1.9 collective-permute-start.7
  116.2 0.0 copy-start.3
  116.2 0.0 copy-start
  116.2 3.0 %collective-permute-start.6 = (f32[4,16,1536]{2,1,0:T(8,128)S(1)}, f32[4,16,1536]{2,1,0:T(8,128)S(1)}, u32[]{:S(2)}, u32[]{:S(2)}) collective-permute-start(f32[4,16,1536]{2,1,0:T(8,128)S(1)} %get-tuple-element.44), channel_id=1, source_target_pairs={{0,1},{1,0},{2,3},{3,2},{4,5},{5,4},{6,7},{7,6},{8,9},{9,8},{10,11... | collective-permute-start | bytes 1179656 | tf_op jit(solution)/shard_map/ppermute | solution.py:342
  119.3 1.0 fusion
  120.3 1.9 collective-permute-start.9
  122.2 5.2 %collective-permute-start.8 = (f32[8,8,1536]{2,1,0:T(8,128)}, f32[8,8,1536]{2,1,0:T(8,128)}, u32[]{:S(2)}, u32[]{:S(2)}) collective-permute-start(f32[8,8,1536]{2,1,0:T(8,128)} %get-tuple-element.42), channel_id=1, source_target_pairs={{0,4},{4,0},{8,12},{12,8},{16,20},{20,16},{24,28},{28,24},{1,5},{5... | collective-permute-start | bytes 1179656 | tf_op jit(solution)/shard_map/ppermute | solution.py:342
  127.4 5.5 %collective-permute-done.7.high = f32[4,16,1536]{2,1,0:T(8,128)S(1)} collective-permute-done((f32[4,16,1536]{2,1,0:T(8,128)S(1)}, f32[4,16,1536]{2,1,0:T(8,128)S(1)}, u32[]{:S(2)}, u32[]{:S(2)}) %collective-permute-start.7) | collective-permute-done | bytes 393248 | tf_op jit(solution)/shard_map/ppermute | solution.py:342
  133.0 4.7 %collective-permute-done.6.low = f32[4,16,1536]{2,1,0:T(8,128)S(1)} collective-permute-done((f32[4,16,1536]{2,1,0:T(8,128)S(1)}, f32[4,16,1536]{2,1,0:T(8,128)S(1)}, u32[]{:S(2)}, u32[]{:S(2)}) %collective-permute-start.6) | collective-permute-done | bytes 393248 | tf_op jit(solution)/shard_map/ppermute | solution.py:342
  137.7 1.0 peel.1
  138.7 1.9 collective-permute-start.10
  140.6 3.9 %collective-permute-start.11 = (f32[8,8,1536]{2,1,0:T(8,128)}, f32[8,8,1536]{2,1,0:T(8,128)}, u32[]{:S(2)}, u32[]{:S(2)}) collective-permute-start(f32[8,8,1536]{2,1,0:T(8,128)} %get-tuple-element.37), channel_id=1, source_target_pairs={{0,28},{4,8},{8,4},{12,16},{16,12},{20,24},{24,20},{28,0},{1,29},{... | collective-permute-start | bytes 1179656 | tf_op jit(solution)/shard_map/ppermute | solution.py:342
  144.6 0.5 copy.7
  145.2 0.1 stack.31.at
  145.3 0.0 collective-permute-done.8.near_a
  145.3 1.0 copy-done.2
  146.3 1.4 stage.1.staged
  147.7 2.4 %collective-permute-done.10.far_a = f32[8,8,1536]{2,1,0:T(8,128)} collective-permute-done((f32[8,8,1536]{2,1,0:T(8,128)}, f32[8,8,1536]{2,1,0:T(8,128)}, u32[]{:S(2)}, u32[]{:S(2)}) %collective-permute-start.10) | collective-permute-done | bytes 393248 | tf_op jit(solution)/shard_map/ppermute | solution.py:342
  150.1 3.1 %collective-permute-done.11.far_b = f32[8,8,1536]{2,1,0:T(8,128)} collective-permute-done((f32[8,8,1536]{2,1,0:T(8,128)}, f32[8,8,1536]{2,1,0:T(8,128)}, u32[]{:S(2)}, u32[]{:S(2)}) %collective-permute-start.11) | collective-permute-done | bytes 393248 | tf_op jit(solution)/shard_map/ppermute | solution.py:342
  153.2 5.2 %scores.1 = (f32[1024,1536]{1,0:T(8,128)S(1)}, bf16[512,1536]{1,0:T(8,128)(2,1)S(1)}, f32[32,24,128]{2,1,0:T(8,128)S(1)}) custom-call(s32[7]{0:T(128)S(1)} %stack.31.at, bf16[512,1536]{1,0:T(8,128)(2,1)S(1)} %stage.1.staged, f32[8,8,1536]{2,1,0:T(8,128)} %collective-permute-done.10.far_a, f32[8,8,1536]{2,1,0:T(8,128)} %collective-permute-done.11.far_b, ...), custom_call_target="tpu_custom_call" | custom-call | tf_op jit(solution)/shard_map/scores/pallas_call | solution.py:97
  158.5 22.1 %all_to_all.22.stats = f32[32,24,128]{2,1,0:T(8,128)S(1)} all-to-all(f32[32,24,128]{2,1,0:T(8,128)S(1)} %get-tuple-element.38.own), channel_id=1, replica_groups=mesh['x'=4,'zl'=2,'core'=2,'yh'=4,'yl'=2,'zhh'=2,'zhl'=2] {'zhl','zhh','..., dimensions={0} | all-to-all | bytes 786432 | tf_op jit(solution)/shard_map/all_to_all | solution.py:383
  180.6 3.1 %totals.3 = f32[8,264,128]{2,1,0:T(8,128)S(1)} custom-call(s32[7]{0:T(128)S(1)} %stack.31.at, f32[32,24,128]{2,1,0:T(8,128)S(1)} %all_to_all.22.stats, f32[32,24,128]{2,1,0:T(8,128)S(1)} %get-tuple-element.38.own, f32[1024,1536]{1,0:T(8,128)S(1)} %get-tuple-element.39.powers, bf16[512,1536]{1,0:T(8,128)(2,1)S(1)} %get-tuple-element.40.rounded), custom_call_target="tpu_custom_call" | custom-call | tf_op jit(solution)/shard_map/totals/pallas_call | solution.py:97
  183.6 5.1 %collective-permute-start.12 = (f32[8,264,128]{2,1,0:T(8,128)S(1)}, f32[8,264,128]{2,1,0:T(8,128)S(1)}, u32[]{:S(2)}, u32[]{:S(2)}) collective-permute-start(f32[8,264,128]{2,1,0:T(8,128)S(1)} %totals.3), channel_id=1, source_target_pairs={{0,32},{32,0},{1,33},{33,1},{2,34},{34,2},{3,35},{35,3},{4,36},{36... | collective-permute-start | bytes 3244040 | tf_op jit(solution)/shard_map/ppermute | solution.py:385
  188.8 3.1 %totals.2 = f32[8,264,128]{2,1,0:T(8,128)S(1)} custom-call(s32[7]{0:T(128)S(1)} %stack.31.at, f32[32,24,128]{2,1,0:T(8,128)S(1)} %all_to_all.22.stats, f32[32,24,128]{2,1,0:T(8,128)S(1)} %get-tuple-element.38.own, f32[1024,1536]{1,0:T(8,128)S(1)} %get-tuple-element.39.powers, bf16[512,1536]{1,0:T(8,128)(2,1)S(1)} %get-tuple-element.40.rounded), custom_call_target="tpu_custom_call" | custom-call | tf_op jit(solution)/shard_map/totals/pallas_call | solution.py:97
  191.9 0.0 collective-permute-done.12
  191.9 0.1 add.39
  192.0 19.7 %all_to_all.23.parts = f32[8,264,128]{2,1,0:T(8,128)S(1)} all-to-all(f32[8,264,128]{2,1,0:T(8,128)S(1)} %add.39), channel_id=1, replica_groups=mesh['x'=4,'zl'=2,'core'=2,'yh'=4,'yl'=2,'zhh'=2,'zhl'=2] {'zl','x'}, dimensions={0} | all-to-all | bytes 2162688 | tf_op jit(solution)/shard_map/all_to_all | solution.py:387
  211.7 1.3 final.1
  (9 shorter events, 0.0 us)
Async XLA Ops:
  3.1 12.0 %collective-permute-start = (f32[64,1536]{1,0:T(8,128)S(1)}, f32[64,1536]{1,0:T(8,128)S(1)}, u32[]{:S(2)}, u32[]{:S(2)}) collective-permute-start(f32[64,1536]{1,0:T(8,128)S(1)} %get-tuple-element.27), channel_id=1, source_target_pairs={{0,4},{4,0},{8,12},{12,8},{16,20},{20,16},{24,28},{28,24},{1,5},{5... | collective-permute-start | bytes 1179656 | tf_op jit(solution)/shard_map/ppermute | solution.py:342
  7.1 11.7 %collective-permute-start.1 = (f32[64,1536]{1,0:T(8,128)S(1)}, f32[64,1536]{1,0:T(8,128)S(1)}, u32[]{:S(2)}, u32[]{:S(2)}) collective-permute-start(f32[64,1536]{1,0:T(8,128)S(1)} %get-tuple-element.28), channel_id=1, source_target_pairs={{0,28},{4,8},{8,4},{12,16},{16,12},{20,24},{24,20},{28,0},{1,29},{... | collective-permute-start | bytes 1179656 | tf_op jit(solution)/shard_map/ppermute | solution.py:342
  18.9 26.8 %collective-permute-start.4 = (f32[4,16,1536]{2,1,0:T(8,128)S(1)}, f32[4,16,1536]{2,1,0:T(8,128)S(1)}, u32[]{:S(2)}, u32[]{:S(2)}) collective-permute-start(f32[4,16,1536]{2,1,0:T(8,128)S(1)} %get-tuple-element.34), channel_id=1, source_target_pairs={{0,1},{1,0},{2,3},{3,2},{4,5},{5,4},{6,7},{7,6},{8,9},{9,8},{10,11... | collective-permute-start | bytes 1179656 | tf_op jit(solution)/shard_map/ppermute | solution.py:342
  26.4 19.4 %collective-permute-start.5 = (f32[4,16,1536]{2,1,0:T(8,128)S(1)}, f32[4,16,1536]{2,1,0:T(8,128)S(1)}, u32[]{:S(2)}, u32[]{:S(2)}) collective-permute-start(f32[4,16,1536]{2,1,0:T(8,128)S(1)} %get-tuple-element.35), channel_id=1, source_target_pairs={{0,3},{1,2},{2,1},{3,0},{4,7},{5,6},{6,5},{7,4},{8,11},{9,10},{10,... | collective-permute-start | bytes 1179656 | tf_op jit(solution)/shard_map/ppermute | solution.py:342
  36.5 10.4 %collective-permute-start.2 = (f32[64,1536]{1,0:T(8,128)S(1)}, f32[64,1536]{1,0:T(8,128)S(1)}, u32[]{:S(2)}, u32[]{:S(2)}) collective-permute-start(f32[64,1536]{1,0:T(8,128)S(1)} %get-tuple-element.32), channel_id=1, source_target_pairs={{0,4},{4,0},{8,12},{12,8},{16,20},{20,16},{24,28},{28,24},{1,5},{5... | collective-permute-start | bytes 1179656 | tf_op jit(solution)/shard_map/ppermute | solution.py:342
  38.4 11.6 %collective-permute-start.3 = (f32[64,1536]{1,0:T(8,128)S(1)}, f32[64,1536]{1,0:T(8,128)S(1)}, u32[]{:S(2)}, u32[]{:S(2)}) collective-permute-start(f32[64,1536]{1,0:T(8,128)S(1)} %get-tuple-element.33), channel_id=1, source_target_pairs={{0,28},{4,8},{8,4},{12,16},{16,12},{20,24},{24,20},{28,0},{1,29},{... | collective-permute-start | bytes 1179656 | tf_op jit(solution)/shard_map/ppermute | solution.py:342
  114.3 18.7 %collective-permute-start.7 = (f32[4,16,1536]{2,1,0:T(8,128)S(1)}, f32[4,16,1536]{2,1,0:T(8,128)S(1)}, u32[]{:S(2)}, u32[]{:S(2)}) collective-permute-start(f32[4,16,1536]{2,1,0:T(8,128)S(1)} %get-tuple-element.43), channel_id=1, source_target_pairs={{0,3},{1,2},{2,1},{3,0},{4,7},{5,6},{6,5},{7,4},{8,11},{9,10},{10,... | collective-permute-start | bytes 1179656 | tf_op jit(solution)/shard_map/ppermute | solution.py:342
  116.2 28.4 %copy-start.3 = (s32[1,2,768]{2,1,0:T(2,128)S(1)}, s32[1,2,768]{2,1,0:T(2,128)}, u32[]{:S(2)}) copy-start(s32[1,2,768]{2,1,0:T(2,128)} %param.9) | copy-start | bytes 18436
  116.2 28.4 %copy-start = (bf16[512,1024]{1,0:T(8,128)(2,1)S(1)}, bf16[512,1024]{1,0:T(8,128)(2,1)}, u32[]{:S(2)}) copy-start(bf16[512,1024]{1,0:T(8,128)(2,1)} %refs.1) | copy-start | bytes 3145732
  116.2 21.5 %collective-permute-start.6 = (f32[4,16,1536]{2,1,0:T(8,128)S(1)}, f32[4,16,1536]{2,1,0:T(8,128)S(1)}, u32[]{:S(2)}, u32[]{:S(2)}) collective-permute-start(f32[4,16,1536]{2,1,0:T(8,128)S(1)} %get-tuple-element.44), channel_id=1, source_target_pairs={{0,1},{1,0},{2,3},{3,2},{4,5},{5,4},{6,7},{7,6},{8,9},{9,8},{10,11... | collective-permute-start | bytes 1179656 | tf_op jit(solution)/shard_map/ppermute | solution.py:342
  120.3 25.0 %collective-permute-start.9 = (f32[8,8,1536]{2,1,0:T(8,128)}, f32[8,8,1536]{2,1,0:T(8,128)}, u32[]{:S(2)}, u32[]{:S(2)}) collective-permute-start(f32[8,8,1536]{2,1,0:T(8,128)} %get-tuple-element.41), channel_id=1, source_target_pairs={{0,28},{4,8},{8,4},{12,16},{16,12},{20,24},{24,20},{28,0},{1,29},{... | collective-permute-start | bytes 1179656 | tf_op jit(solution)/shard_map/ppermute | solution.py:342
  122.2 23.1 %collective-permute-start.8 = (f32[8,8,1536]{2,1,0:T(8,128)}, f32[8,8,1536]{2,1,0:T(8,128)}, u32[]{:S(2)}, u32[]{:S(2)}) collective-permute-start(f32[8,8,1536]{2,1,0:T(8,128)} %get-tuple-element.42), channel_id=1, source_target_pairs={{0,4},{4,0},{8,12},{12,8},{16,20},{20,16},{24,28},{28,24},{1,5},{5... | collective-permute-start | bytes 1179656 | tf_op jit(solution)/shard_map/ppermute | solution.py:342
  137.7 6.9 %copy-start.1 = (f32[4,16,1536]{2,1,0:T(8,128)}, f32[4,16,1536]{2,1,0:T(8,128)S(1)}, u32[]{:S(2)}) copy-start(f32[4,16,1536]{2,1,0:T(8,128)S(1)} %collective-permute-done.6.low) | copy-start | bytes 1179652
  138.7 11.4 %collective-permute-start.10 = (f32[8,8,1536]{2,1,0:T(8,128)}, f32[8,8,1536]{2,1,0:T(8,128)}, u32[]{:S(2)}, u32[]{:S(2)}) collective-permute-start(f32[8,8,1536]{2,1,0:T(8,128)} %get-tuple-element.36), channel_id=1, source_target_pairs={{0,4},{4,0},{8,12},{12,8},{16,20},{20,16},{24,28},{28,24},{1,5},{5... | collective-permute-start | bytes 1179656 | tf_op jit(solution)/shard_map/ppermute | solution.py:342
  140.6 12.6 %collective-permute-start.11 = (f32[8,8,1536]{2,1,0:T(8,128)}, f32[8,8,1536]{2,1,0:T(8,128)}, u32[]{:S(2)}, u32[]{:S(2)}) collective-permute-start(f32[8,8,1536]{2,1,0:T(8,128)} %get-tuple-element.37), channel_id=1, source_target_pairs={{0,28},{4,8},{8,4},{12,16},{16,12},{20,24},{24,20},{28,0},{1,29},{... | collective-permute-start | bytes 1179656 | tf_op jit(solution)/shard_map/ppermute | solution.py:342
  145.3 1.0 copy-start.2
  183.6 8.2 %collective-permute-start.12 = (f32[8,264,128]{2,1,0:T(8,128)S(1)}, f32[8,264,128]{2,1,0:T(8,128)S(1)}, u32[]{:S(2)}, u32[]{:S(2)}) collective-permute-start(f32[8,264,128]{2,1,0:T(8,128)S(1)} %totals.3), channel_id=1, source_target_pairs={{0,32},{32,0},{1,33},{33,1},{2,34},{34,2},{3,35},{35,3},{4,36},{36... | collective-permute-start | bytes 3244040 | tf_op jit(solution)/shard_map/ppermute | solution.py:385

commit v11 on v10

--- a/solution.py
+++ b/solution.py
@@ -226,7 +226,7 @@
         total = jnp.zeros_like(top)
         for k, (part, bonus) in enumerate(parts):
             power = jnp.exp(part - (top - bonus))
-            powers[k * OBLOCK : (k + 1) * OBLOCK, cut] = power
+            powers[k * OBLOCK : (k + 1) * OBLOCK, cut] = power.astype(jnp.bfloat16)
             total = total + jnp.sum(power, axis=0, keepdims=True)
         for h in range(width // LANES):
             line = step * (width // LANES) + h
@@ -243,7 +243,7 @@
     rows = prior.shape[1]
     orient, eigen = refs_t.shape
     shapes = [
-        ((orient, rows), jnp.float32),
+        ((orient, rows), jnp.bfloat16),
         ((eigen, rows), jnp.bfloat16),
         ((members, 2 * rows // LANES, LANES), jnp.float32),
     ]
@@ -272,7 +272,7 @@
 
     def orients(step, carry):
         block = powers[pl.ds(pl.multiple_of(step * width, width), width), :]
-        weights = (block * factor[...]).astype(jnp.bfloat16)
+        weights = (block.astype(jnp.float32) * factor[...]).astype(jnp.bfloat16)
         totals = lax.dot_general(mine[...], weights, LAST, preferred_element_type=jnp.float32)
         masses = lax.dot_general(ones, weights, LAST, preferred_element_type=jnp.float32)
         for h in range(width // LANES):

time: 214 us -> 214 us (level)
  no operation moved by 1% of the time
where the time goes in v11:
time: 214 us; the launch traced here: 213 us
  blocking collectives  106 us (50%)
  starting transfers between devices  52.6 us (25%)
  Pallas kernels  27.7 us (13%)
  waiting for transfers between devices  23.9 us (11%)
  local copies, waits for them, and re-layouts  2.69 us (1%)
    ppermute x12, starting transfers between devices, swapped(): lax.ppermute(x, axis, p)  47.5 us
    all_to_all x1, blocking collectives, shards(): parts = lax.all_to_all(parts, ALIKE, 0, 0, tiled=True)  34.9 us
    all_to_all x1, blocking collectives, shards(): own = lax.all_to_all(summed_copies(parts), ALIKE, 0, 0, tiled=True)  29 us
    ppermute x12, waiting for transfers between devices, swapped(): lax.ppermute(x, axis, p)  23.9 us
    all_to_all x1, blocking collectives, shards(): stats = lax.all_to_all(sent, EVERY, 0, 0, tiled=True)  22.1 us
    all_to_all x1, blocking collectives, shards(): parts = lax.all_to_all(parts, PEERS, 0, 0, tiled=True)  19.8 us
    pallas_call x8, Pallas kernels, whole(): pl.pallas_call(kernel, in_specs=[pl.BlockSpec(memory_space=pltpu.SMEM)] *...  14.2 us
    pallas_call x4, Pallas kernels, projected(): pl.pallas_call(project_kernel, grid_spec=pltpu.PrefetchScalarGridSpec(num...  12.2 us
  transfers between devices with their start and end apart: 13, of which 7 were waited for; matrix products, arithmetic and copies ran while one was open for 1% of the time, Pallas kernels for 7%

profile of v11, /device:TPU:1, one launch (start us, length us, event | category | flops | bytes accessed | tf_op | source)
XLA Modules:
  0.0 213.1 jit_solution(8877461785809957281)
XLA Ops:
  0.0 3.0 %project.6 = (f32[64,1536]{1,0:T(8,128)S(1)}, f32[64,1536]{1,0:T(8,128)S(1)}) custom-call(s32[1]{0:T(128)} %bitcast.at, s32[2,64]{1,0:T(2,128)} %bitcast.18, bf16[1536,512]{1,0:T(8,128)(2,1)} %bitcast.14, bf16[512,512]{1,0:T(8,128)(2,1)} %basis.7, bf16[1,512]{1,0:T(2,128)(2,1)} %phantom.7), custom_call_target="tpu_custom_call" | custom-call | tf_op jit(solution)/shard_map/project/pallas_call | solution.py:74
  3.1 4.0 %collective-permute-start = (f32[64,1536]{1,0:T(8,128)S(1)}, f32[64,1536]{1,0:T(8,128)S(1)}, u32[]{:S(2)}, u32[]{:S(2)}) collective-permute-start(f32[64,1536]{1,0:T(8,128)S(1)} %get-tuple-element.27), channel_id=1, source_target_pairs={{0,4},{4,0},{8,12},{12,8},{16,20},{20,16},{24,28},{28,24},{1,5},{5... | collective-permute-start | bytes 1179656 | tf_op jit(solution)/shard_map/ppermute | solution.py:342
  7.1 4.9 %collective-permute-start.1 = (f32[64,1536]{1,0:T(8,128)S(1)}, f32[64,1536]{1,0:T(8,128)S(1)}, u32[]{:S(2)}, u32[]{:S(2)}) collective-permute-start(f32[64,1536]{1,0:T(8,128)S(1)} %get-tuple-element.28), channel_id=1, source_target_pairs={{0,28},{4,8},{8,4},{12,16},{16,12},{20,24},{24,20},{28,0},{1,29},{... | collective-permute-start | bytes 1179656 | tf_op jit(solution)/shard_map/ppermute | solution.py:342
  12.0 3.1 %project.5 = (f32[64,1536]{1,0:T(8,128)S(1)}, f32[64,1536]{1,0:T(8,128)S(1)}) custom-call(s32[1]{0:T(128)} %bitcast.2.at, s32[2,64]{1,0:T(2,128)} %bitcast.19, bf16[1536,512]{1,0:T(8,128)(2,1)} %bitcast.15, bf16[512,512]{1,0:T(8,128)(2,1)} %basis.7, bf16[1,512]{1,0:T(2,128)(2,1)} %phantom.7), custom_call_target="tpu_custom_call" | custom-call | tf_op jit(solution)/shard_map/project/pallas_call | solution.py:74
  15.0 0.0 collective-permute-done.came_a
  15.1 3.8 %collective-permute-done.1.came_b = f32[64,1536]{1,0:T(8,128)S(1)} collective-permute-done((f32[64,1536]{1,0:T(8,128)S(1)}, f32[64,1536]{1,0:T(8,128)S(1)}, u32[]{:S(2)}, u32[]{:S(2)}) %collective-permute-start.1) | collective-permute-done | bytes 393248 | tf_op jit(solution)/shard_map/ppermute | solution.py:342
  18.8 0.1 relay.1
  18.9 7.5 %collective-permute-start.4 = (f32[4,16,1536]{2,1,0:T(8,128)S(1)}, f32[4,16,1536]{2,1,0:T(8,128)S(1)}, u32[]{:S(2)}, u32[]{:S(2)}) collective-permute-start(f32[4,16,1536]{2,1,0:T(8,128)S(1)} %get-tuple-element.34), channel_id=1, source_target_pairs={{0,1},{1,0},{2,3},{3,2},{4,5},{5,4},{6,7},{7,6},{8,9},{9,8},{10,11... | collective-permute-start | bytes 1179656 | tf_op jit(solution)/shard_map/ppermute | solution.py:342
  26.4 7.0 %collective-permute-start.5 = (f32[4,16,1536]{2,1,0:T(8,128)S(1)}, f32[4,16,1536]{2,1,0:T(8,128)S(1)}, u32[]{:S(2)}, u32[]{:S(2)}) collective-permute-start(f32[4,16,1536]{2,1,0:T(8,128)S(1)} %get-tuple-element.35), channel_id=1, source_target_pairs={{0,3},{1,2},{2,1},{3,0},{4,7},{5,6},{6,5},{7,4},{8,11},{9,10},{10,... | collective-permute-start | bytes 1179656 | tf_op jit(solution)/shard_map/ppermute | solution.py:342
  33.4 3.1 %project.7 = (f32[64,1536]{1,0:T(8,128)S(1)}, f32[64,1536]{1,0:T(8,128)S(1)}) custom-call(s32[1]{0:T(128)} %bitcast.1.at, s32[2,64]{1,0:T(2,128)} %bitcast.20, bf16[1536,512]{1,0:T(8,128)(2,1)} %bitcast.16, bf16[512,512]{1,0:T(8,128)(2,1)} %basis.7, bf16[1,512]{1,0:T(2,128)(2,1)} %phantom.7), custom_call_target="tpu_custom_call" | custom-call | tf_op jit(solution)/shard_map/project/pallas_call | solution.py:74
  36.5 1.9 collective-permute-start.2
  38.4 4.2 %collective-permute-start.3 = (f32[64,1536]{1,0:T(8,128)S(1)}, f32[64,1536]{1,0:T(8,128)S(1)}, u32[]{:S(2)}, u32[]{:S(2)}) collective-permute-start(f32[64,1536]{1,0:T(8,128)S(1)} %get-tuple-element.33), channel_id=1, source_target_pairs={{0,28},{4,8},{8,4},{12,16},{16,12},{20,24},{24,20},{28,0},{1,29},{... | collective-permute-start | bytes 1179656 | tf_op jit(solution)/shard_map/ppermute | solution.py:342
  42.7 3.1 %project.4 = (f32[64,1536]{1,0:T(8,128)S(1)}, f32[64,1536]{1,0:T(8,128)S(1)}) custom-call(s32[1]{0:T(128)} %bitcast.3.at, s32[2,64]{1,0:T(2,128)} %bitcast.21, bf16[1536,512]{1,0:T(8,128)(2,1)} %bitcast.17, bf16[512,512]{1,0:T(8,128)(2,1)} %basis.7, bf16[1,512]{1,0:T(2,128)(2,1)} %phantom.7), custom_call_target="tpu_custom_call" | custom-call | tf_op jit(solution)/shard_map/project/pallas_call | solution.py:74
  45.7 0.0 collective-permute-done.5.high
  45.8 1.1 collective-permute-done.2.came_a
  46.9 3.1 %collective-permute-done.3.came_b = f32[64,1536]{1,0:T(8,128)S(1)} collective-permute-done((f32[64,1536]{1,0:T(8,128)S(1)}, f32[64,1536]{1,0:T(8,128)S(1)}, u32[]{:S(2)}, u32[]{:S(2)}) %collective-permute-start.3) | collective-permute-done | bytes 393248 | tf_op jit(solution)/shard_map/ppermute | solution.py:342
  50.0 0.1 join.1
  50.1 34.9 %all_to_all.20.parts = f32[8,16,1536]{2,1,0:T(8,128)S(1)} all-to-all(f32[8,16,1536]{2,1,0:T(8,128)S(1)} %join.1), channel_id=1, replica_groups=mesh['x'=4,'zl'=2,'core'=2,'yh'=4,'yl'=2,'zhh'=2,'zhl'=2] {'yh','zhh'}, dimensions={0} | all-to-all | bytes 1572864 | tf_op jit(solution)/shard_map/all_to_all | solution.py:370
  85.1 0.1 spread.1
  85.2 29.0 %all_to_all.21.own = f32[8,16,1536]{2,1,0:T(8,128)S(1)} all-to-all(f32[8,16,1536]{2,1,0:T(8,128)S(1)} %spread.1), channel_id=1, replica_groups=mesh['x'=4,'zl'=2,'core'=2,'yh'=4,'yl'=2,'zhh'=2,'zhl'=2] {'yh','zhh'}, dimensions={0} | all-to-all | bytes 1572864 | tf_op jit(solution)/shard_map/all_to_all | solution.py:371
  114.2 0.1 fusion.1
  114.3 1.9 collective-permute-start.7
  116.2 0.0 copy-start.3
  116.2 0.0 copy-start
  116.2 3.0 %collective-permute-start.6 = (f32[4,16,1536]{2,1,0:T(8,128)S(1)}, f32[4,16,1536]{2,1,0:T(8,128)S(1)}, u32[]{:S(2)}, u32[]{:S(2)}) collective-permute-start(f32[4,16,1536]{2,1,0:T(8,128)S(1)} %get-tuple-element.44), channel_id=1, source_target_pairs={{0,1},{1,0},{2,3},{3,2},{4,5},{5,4},{6,7},{7,6},{8,9},{9,8},{10,11... | collective-permute-start | bytes 1179656 | tf_op jit(solution)/shard_map/ppermute | solution.py:342
  119.3 1.0 fusion
  120.3 1.9 collective-permute-start.9
  122.2 5.2 %collective-permute-start.8 = (f32[8,8,1536]{2,1,0:T(8,128)}, f32[8,8,1536]{2,1,0:T(8,128)}, u32[]{:S(2)}, u32[]{:S(2)}) collective-permute-start(f32[8,8,1536]{2,1,0:T(8,128)} %get-tuple-element.42), channel_id=1, source_target_pairs={{0,4},{4,0},{8,12},{12,8},{16,20},{20,16},{24,28},{28,24},{1,5},{5... | collective-permute-start | bytes 1179656 | tf_op jit(solution)/shard_map/ppermute | solution.py:342
  127.4 5.5 %collective-permute-done.7.high = f32[4,16,1536]{2,1,0:T(8,128)S(1)} collective-permute-done((f32[4,16,1536]{2,1,0:T(8,128)S(1)}, f32[4,16,1536]{2,1,0:T(8,128)S(1)}, u32[]{:S(2)}, u32[]{:S(2)}) %collective-permute-start.7) | collective-permute-done | bytes 393248 | tf_op jit(solution)/shard_map/ppermute | solution.py:342
  133.0 4.7 %collective-permute-done.6.low = f32[4,16,1536]{2,1,0:T(8,128)S(1)} collective-permute-done((f32[4,16,1536]{2,1,0:T(8,128)S(1)}, f32[4,16,1536]{2,1,0:T(8,128)S(1)}, u32[]{:S(2)}, u32[]{:S(2)}) %collective-permute-start.6) | collective-permute-done | bytes 393248 | tf_op jit(solution)/shard_map/ppermute | solution.py:342
  137.7 1.0 peel.1
  138.7 1.9 collective-permute-start.10
  140.6 3.9 %collective-permute-start.11 = (f32[8,8,1536]{2,1,0:T(8,128)}, f32[8,8,1536]{2,1,0:T(8,128)}, u32[]{:S(2)}, u32[]{:S(2)}) collective-permute-start(f32[8,8,1536]{2,1,0:T(8,128)} %get-tuple-element.37), channel_id=1, source_target_pairs={{0,28},{4,8},{8,4},{12,16},{16,12},{20,24},{24,20},{28,0},{1,29},{... | collective-permute-start | bytes 1179656 | tf_op jit(solution)/shard_map/ppermute | solution.py:342
  144.6 0.5 copy.7
  145.2 0.1 stack.31.at
  145.3 0.0 collective-permute-done.8.near_a
  145.3 1.0 copy-done.2
  146.3 1.4 stage.1.staged
  147.7 2.4 %collective-permute-done.10.far_a = f32[8,8,1536]{2,1,0:T(8,128)} collective-permute-done((f32[8,8,1536]{2,1,0:T(8,128)}, f32[8,8,1536]{2,1,0:T(8,128)}, u32[]{:S(2)}, u32[]{:S(2)}) %collective-permute-start.10) | collective-permute-done | bytes 393248 | tf_op jit(solution)/shard_map/ppermute | solution.py:342
  150.1 3.1 %collective-permute-done.11.far_b = f32[8,8,1536]{2,1,0:T(8,128)} collective-permute-done((f32[8,8,1536]{2,1,0:T(8,128)}, f32[8,8,1536]{2,1,0:T(8,128)}, u32[]{:S(2)}, u32[]{:S(2)}) %collective-permute-start.11) | collective-permute-done | bytes 393248 | tf_op jit(solution)/shard_map/ppermute | solution.py:342
  153.2 5.3 %scores.1 = (bf16[1024,1536]{1,0:T(8,128)(2,1)S(1)}, bf16[512,1536]{1,0:T(8,128)(2,1)S(1)}, f32[32,24,128]{2,1,0:T(8,128)S(1)}) custom-call(s32[7]{0:T(128)S(1)} %stack.31.at, bf16[512,1536]{1,0:T(8,128)(2,1)S(1)} %stage.1.staged, f32[8,8,1536]{2,1,0:T(8,128)} %collective-permute-done.10.far_a, f32[8,8,1536]{2,1,0:T(8,128)} %collective-permute-done.11.far_b, ...), custom_call_target="tpu_custom_call" | custom-call | tf_op jit(solution)/shard_map/scores/pallas_call | solution.py:97
  158.5 22.1 %all_to_all.22.stats = f32[32,24,128]{2,1,0:T(8,128)S(1)} all-to-all(f32[32,24,128]{2,1,0:T(8,128)S(1)} %get-tuple-element.38.own), channel_id=1, replica_groups=mesh['x'=4,'zl'=2,'core'=2,'yh'=4,'yl'=2,'zhh'=2,'zhl'=2] {'zhl','zhh','..., dimensions={0} | all-to-all | bytes 786432 | tf_op jit(solution)/shard_map/all_to_all | solution.py:383
  180.6 3.1 %totals.3 = f32[8,264,128]{2,1,0:T(8,128)S(1)} custom-call(s32[7]{0:T(128)S(1)} %stack.31.at, f32[32,24,128]{2,1,0:T(8,128)S(1)} %all_to_all.22.stats, f32[32,24,128]{2,1,0:T(8,128)S(1)} %get-tuple-element.38.own, bf16[1024,1536]{1,0:T(8,128)(2,1)S(1)} %get-tuple-element.39.powers, bf16[512,1536]{1,0:T(8,128)(2,1)S(1)} %get-tuple-element.40.rounded), custom_call_target="tpu_custom_call" | custom-call | tf_op jit(solution)/shard_map/totals/pallas_call | solution.py:97
  183.7 5.1 %collective-permute-start.12 = (f32[8,264,128]{2,1,0:T(8,128)S(1)}, f32[8,264,128]{2,1,0:T(8,128)S(1)}, u32[]{:S(2)}, u32[]{:S(2)}) collective-permute-start(f32[8,264,128]{2,1,0:T(8,128)S(1)} %totals.3), channel_id=1, source_target_pairs={{0,32},{32,0},{1,33},{33,1},{2,34},{34,2},{3,35},{35,3},{4,36},{36... | collective-permute-start | bytes 3244040 | tf_op jit(solution)/shard_map/ppermute | solution.py:385
  188.9 3.1 %totals.2 = f32[8,264,128]{2,1,0:T(8,128)S(1)} custom-call(s32[7]{0:T(128)S(1)} %stack.31.at, f32[32,24,128]{2,1,0:T(8,128)S(1)} %all_to_all.22.stats, f32[32,24,128]{2,1,0:T(8,128)S(1)} %get-tuple-element.38.own, bf16[1024,1536]{1,0:T(8,128)(2,1)S(1)} %get-tuple-element.39.powers, bf16[512,1536]{1,0:T(8,128)(2,1)S(1)} %get-tuple-element.40.rounded), custom_call_target="tpu_custom_call" | custom-call | tf_op jit(solution)/shard_map/totals/pallas_call | solution.py:97
  192.0 0.1 add.39
  192.1 19.8 %all_to_all.23.parts = f32[8,264,128]{2,1,0:T(8,128)S(1)} all-to-all(f32[8,264,128]{2,1,0:T(8,128)S(1)} %add.39), channel_id=1, replica_groups=mesh['x'=4,'zl'=2,'core'=2,'yh'=4,'yl'=2,'zhh'=2,'zhl'=2] {'zl','x'}, dimensions={0} | all-to-all | bytes 2162688 | tf_op jit(solution)/shard_map/all_to_all | solution.py:387
  211.9 1.3 final.1
  (9 shorter events, 0.0 us)
Async XLA Ops:
  3.1 12.0 %collective-permute-start = (f32[64,1536]{1,0:T(8,128)S(1)}, f32[64,1536]{1,0:T(8,128)S(1)}, u32[]{:S(2)}, u32[]{:S(2)}) collective-permute-start(f32[64,1536]{1,0:T(8,128)S(1)} %get-tuple-element.27), channel_id=1, source_target_pairs={{0,4},{4,0},{8,12},{12,8},{16,20},{20,16},{24,28},{28,24},{1,5},{5... | collective-permute-start | bytes 1179656 | tf_op jit(solution)/shard_map/ppermute | solution.py:342
  7.1 11.7 %collective-permute-start.1 = (f32[64,1536]{1,0:T(8,128)S(1)}, f32[64,1536]{1,0:T(8,128)S(1)}, u32[]{:S(2)}, u32[]{:S(2)}) collective-permute-start(f32[64,1536]{1,0:T(8,128)S(1)} %get-tuple-element.28), channel_id=1, source_target_pairs={{0,28},{4,8},{8,4},{12,16},{16,12},{20,24},{24,20},{28,0},{1,29},{... | collective-permute-start | bytes 1179656 | tf_op jit(solution)/shard_map/ppermute | solution.py:342
  18.9 26.8 %collective-permute-start.4 = (f32[4,16,1536]{2,1,0:T(8,128)S(1)}, f32[4,16,1536]{2,1,0:T(8,128)S(1)}, u32[]{:S(2)}, u32[]{:S(2)}) collective-permute-start(f32[4,16,1536]{2,1,0:T(8,128)S(1)} %get-tuple-element.34), channel_id=1, source_target_pairs={{0,1},{1,0},{2,3},{3,2},{4,5},{5,4},{6,7},{7,6},{8,9},{9,8},{10,11... | collective-permute-start | bytes 1179656 | tf_op jit(solution)/shard_map/ppermute | solution.py:342
  26.4 19.4 %collective-permute-start.5 = (f32[4,16,1536]{2,1,0:T(8,128)S(1)}, f32[4,16,1536]{2,1,0:T(8,128)S(1)}, u32[]{:S(2)}, u32[]{:S(2)}) collective-permute-start(f32[4,16,1536]{2,1,0:T(8,128)S(1)} %get-tuple-element.35), channel_id=1, source_target_pairs={{0,3},{1,2},{2,1},{3,0},{4,7},{5,6},{6,5},{7,4},{8,11},{9,10},{10,... | collective-permute-start | bytes 1179656 | tf_op jit(solution)/shard_map/ppermute | solution.py:342
  36.5 10.4 %collective-permute-start.2 = (f32[64,1536]{1,0:T(8,128)S(1)}, f32[64,1536]{1,0:T(8,128)S(1)}, u32[]{:S(2)}, u32[]{:S(2)}) collective-permute-start(f32[64,1536]{1,0:T(8,128)S(1)} %get-tuple-element.32), channel_id=1, source_target_pairs={{0,4},{4,0},{8,12},{12,8},{16,20},{20,16},{24,28},{28,24},{1,5},{5... | collective-permute-start | bytes 1179656 | tf_op jit(solution)/shard_map/ppermute | solution.py:342
  38.4 11.6 %collective-permute-start.3 = (f32[64,1536]{1,0:T(8,128)S(1)}, f32[64,1536]{1,0:T(8,128)S(1)}, u32[]{:S(2)}, u32[]{:S(2)}) collective-permute-start(f32[64,1536]{1,0:T(8,128)S(1)} %get-tuple-element.33), channel_id=1, source_target_pairs={{0,28},{4,8},{8,4},{12,16},{16,12},{20,24},{24,20},{28,0},{1,29},{... | collective-permute-start | bytes 1179656 | tf_op jit(solution)/shard_map/ppermute | solution.py:342
  114.3 18.7 %collective-permute-start.7 = (f32[4,16,1536]{2,1,0:T(8,128)S(1)}, f32[4,16,1536]{2,1,0:T(8,128)S(1)}, u32[]{:S(2)}, u32[]{:S(2)}) collective-permute-start(f32[4,16,1536]{2,1,0:T(8,128)S(1)} %get-tuple-element.43), channel_id=1, source_target_pairs={{0,3},{1,2},{2,1},{3,0},{4,7},{5,6},{6,5},{7,4},{8,11},{9,10},{10,... | collective-permute-start | bytes 1179656 | tf_op jit(solution)/shard_map/ppermute | solution.py:342
  116.2 28.4 %copy-start.3 = (s32[1,2,768]{2,1,0:T(2,128)S(1)}, s32[1,2,768]{2,1,0:T(2,128)}, u32[]{:S(2)}) copy-start(s32[1,2,768]{2,1,0:T(2,128)} %param.9) | copy-start | bytes 18436
  116.2 28.4 %copy-start = (bf16[512,1024]{1,0:T(8,128)(2,1)S(1)}, bf16[512,1024]{1,0:T(8,128)(2,1)}, u32[]{:S(2)}) copy-start(bf16[512,1024]{1,0:T(8,128)(2,1)} %refs.1) | copy-start | bytes 3145732
  116.2 21.5 %collective-permute-start.6 = (f32[4,16,1536]{2,1,0:T(8,128)S(1)}, f32[4,16,1536]{2,1,0:T(8,128)S(1)}, u32[]{:S(2)}, u32[]{:S(2)}) collective-permute-start(f32[4,16,1536]{2,1,0:T(8,128)S(1)} %get-tuple-element.44), channel_id=1, source_target_pairs={{0,1},{1,0},{2,3},{3,2},{4,5},{5,4},{6,7},{7,6},{8,9},{9,8},{10,11... | collective-permute-start | bytes 1179656 | tf_op jit(solution)/shard_map/ppermute | solution.py:342
  120.3 25.0 %collective-permute-start.9 = (f32[8,8,1536]{2,1,0:T(8,128)}, f32[8,8,1536]{2,1,0:T(8,128)}, u32[]{:S(2)}, u32[]{:S(2)}) collective-permute-start(f32[8,8,1536]{2,1,0:T(8,128)} %get-tuple-element.41), channel_id=1, source_target_pairs={{0,28},{4,8},{8,4},{12,16},{16,12},{20,24},{24,20},{28,0},{1,29},{... | collective-permute-start | bytes 1179656 | tf_op jit(solution)/shard_map/ppermute | solution.py:342
  122.2 23.1 %collective-permute-start.8 = (f32[8,8,1536]{2,1,0:T(8,128)}, f32[8,8,1536]{2,1,0:T(8,128)}, u32[]{:S(2)}, u32[]{:S(2)}) collective-permute-start(f32[8,8,1536]{2,1,0:T(8,128)} %get-tuple-element.42), channel_id=1, source_target_pairs={{0,4},{4,0},{8,12},{12,8},{16,20},{20,16},{24,28},{28,24},{1,5},{5... | collective-permute-start | bytes 1179656 | tf_op jit(solution)/shard_map/ppermute | solution.py:342
  137.7 6.9 %copy-start.1 = (f32[4,16,1536]{2,1,0:T(8,128)}, f32[4,16,1536]{2,1,0:T(8,128)S(1)}, u32[]{:S(2)}) copy-start(f32[4,16,1536]{2,1,0:T(8,128)S(1)} %collective-permute-done.6.low) | copy-start | bytes 1179652
  138.7 11.4 %collective-permute-start.10 = (f32[8,8,1536]{2,1,0:T(8,128)}, f32[8,8,1536]{2,1,0:T(8,128)}, u32[]{:S(2)}, u32[]{:S(2)}) collective-permute-start(f32[8,8,1536]{2,1,0:T(8,128)} %get-tuple-element.36), channel_id=1, source_target_pairs={{0,4},{4,0},{8,12},{12,8},{16,20},{20,16},{24,28},{28,24},{1,5},{5... | collective-permute-start | bytes 1179656 | tf_op jit(solution)/shard_map/ppermute | solution.py:342
  140.6 12.6 %collective-permute-start.11 = (f32[8,8,1536]{2,1,0:T(8,128)}, f32[8,8,1536]{2,1,0:T(8,128)}, u32[]{:S(2)}, u32[]{:S(2)}) collective-permute-start(f32[8,8,1536]{2,1,0:T(8,128)} %get-tuple-element.37), channel_id=1, source_target_pairs={{0,28},{4,8},{8,4},{12,16},{16,12},{20,24},{24,20},{28,0},{1,29},{... | collective-permute-start | bytes 1179656 | tf_op jit(solution)/shard_map/ppermute | solution.py:342
  145.3 1.0 copy-start.2
  183.7 8.2 %collective-permute-start.12 = (f32[8,264,128]{2,1,0:T(8,128)S(1)}, f32[8,264,128]{2,1,0:T(8,128)S(1)}, u32[]{:S(2)}, u32[]{:S(2)}) collective-permute-start(f32[8,264,128]{2,1,0:T(8,128)S(1)} %totals.3), channel_id=1, source_target_pairs={{0,32},{32,0},{1,33},{33,1},{2,34},{34,2},{3,35},{35,3},{4,36},{36... | collective-permute-start | bytes 3244040 | tf_op jit(solution)/shard_map/ppermute | solution.py:385

commit v12 on v10

--- a/solution.py
+++ b/solution.py
@@ -236,7 +236,7 @@
             stats[:, pl.ds(lines + line, 1), :] = jnp.broadcast_to(total[None, :, side], shape)
         return carry
 
-    lax.fori_loop(0, powers.shape[1] // width, column, 0)
+    lax.fori_loop(0, powers.shape[1] // width, column, 0, unroll=2)
 
 
 def scores_of(at, held, prior, refs_t, members):
@@ -285,7 +285,7 @@
             out[:, pl.ds(body + column, 1), :] = mass
         return carry
 
-    lax.fori_loop(0, powers.shape[0] // width, orients, 0)
+    lax.fori_loop(0, powers.shape[0] // width, orients, 0, unroll=2)
 
 
 def totals_of(other, at, stats, sent, powers, rounded, peers):

time: 214 us -> 213 us (level)
  no operation moved by 1% of the time
where the time goes in v12:
time: 213 us; the launch traced here: 212 us
  blocking collectives  106 us (50%)
  starting transfers between devices  52.6 us (25%)
  Pallas kernels  26.2 us (12%)
  waiting for transfers between devices  23.9 us (11%)
  local copies, waits for them, and re-layouts  2.69 us (1%)
    ppermute x12, starting transfers between devices, swapped(): lax.ppermute(x, axis, p)  47.5 us
    all_to_all x1, blocking collectives, shards(): parts = lax.all_to_all(parts, ALIKE, 0, 0, tiled=True)  34.9 us
    all_to_all x1, blocking collectives, shards(): own = lax.all_to_all(summed_copies(parts), ALIKE, 0, 0, tiled=True)  29 us
    ppermute x12, waiting for transfers between devices, swapped(): lax.ppermute(x, axis, p)  23.9 us
    all_to_all x1, blocking collectives, shards(): stats = lax.all_to_all(sent, EVERY, 0, 0, tiled=True)  22.1 us
    all_to_all x1, blocking collectives, shards(): parts = lax.all_to_all(parts, PEERS, 0, 0, tiled=True)  19.8 us
    pallas_call x8, Pallas kernels, whole(): pl.pallas_call(kernel, in_specs=[pl.BlockSpec(memory_space=pltpu.SMEM)] *...  12.8 us
    pallas_call x4, Pallas kernels, projected(): pl.pallas_call(project_kernel, grid_spec=pltpu.PrefetchScalarGridSpec(num...  12.2 us
  transfers between devices with their start and end apart: 13, of which 7 were waited for; matrix products, arithmetic and copies ran while one was open for 1% of the time, Pallas kernels for 7%

profile of v12, /device:TPU:1, one launch (start us, length us, event | category | flops | bytes accessed | tf_op | source)
XLA Modules:
  0.0 211.7 jit_solution(9145389076620138625)
XLA Ops:
  0.0 3.0 %project.6 = (f32[64,1536]{1,0:T(8,128)S(1)}, f32[64,1536]{1,0:T(8,128)S(1)}) custom-call(s32[1]{0:T(128)} %bitcast.at, s32[2,64]{1,0:T(2,128)} %bitcast.18, bf16[1536,512]{1,0:T(8,128)(2,1)} %bitcast.14, bf16[512,512]{1,0:T(8,128)(2,1)} %basis.7, bf16[1,512]{1,0:T(2,128)(2,1)} %phantom.7), custom_call_target="tpu_custom_call" | custom-call | tf_op jit(solution)/shard_map/project/pallas_call | solution.py:74
  3.1 4.0 %collective-permute-start = (f32[64,1536]{1,0:T(8,128)S(1)}, f32[64,1536]{1,0:T(8,128)S(1)}, u32[]{:S(2)}, u32[]{:S(2)}) collective-permute-start(f32[64,1536]{1,0:T(8,128)S(1)} %get-tuple-element.27), channel_id=1, source_target_pairs={{0,4},{4,0},{8,12},{12,8},{16,20},{20,16},{24,28},{28,24},{1,5},{5... | collective-permute-start | bytes 1179656 | tf_op jit(solution)/shard_map/ppermute | solution.py:342
  7.1 4.9 %collective-permute-start.1 = (f32[64,1536]{1,0:T(8,128)S(1)}, f32[64,1536]{1,0:T(8,128)S(1)}, u32[]{:S(2)}, u32[]{:S(2)}) collective-permute-start(f32[64,1536]{1,0:T(8,128)S(1)} %get-tuple-element.28), channel_id=1, source_target_pairs={{0,28},{4,8},{8,4},{12,16},{16,12},{20,24},{24,20},{28,0},{1,29},{... | collective-permute-start | bytes 1179656 | tf_op jit(solution)/shard_map/ppermute | solution.py:342
  12.0 3.1 %project.5 = (f32[64,1536]{1,0:T(8,128)S(1)}, f32[64,1536]{1,0:T(8,128)S(1)}) custom-call(s32[1]{0:T(128)} %bitcast.2.at, s32[2,64]{1,0:T(2,128)} %bitcast.19, bf16[1536,512]{1,0:T(8,128)(2,1)} %bitcast.15, bf16[512,512]{1,0:T(8,128)(2,1)} %basis.7, bf16[1,512]{1,0:T(2,128)(2,1)} %phantom.7), custom_call_target="tpu_custom_call" | custom-call | tf_op jit(solution)/shard_map/project/pallas_call | solution.py:74
  15.1 3.8 %collective-permute-done.1.came_b = f32[64,1536]{1,0:T(8,128)S(1)} collective-permute-done((f32[64,1536]{1,0:T(8,128)S(1)}, f32[64,1536]{1,0:T(8,128)S(1)}, u32[]{:S(2)}, u32[]{:S(2)}) %collective-permute-start.1) | collective-permute-done | bytes 393248 | tf_op jit(solution)/shard_map/ppermute | solution.py:342
  18.8 0.1 relay.1
  18.9 7.5 %collective-permute-start.4 = (f32[4,16,1536]{2,1,0:T(8,128)S(1)}, f32[4,16,1536]{2,1,0:T(8,128)S(1)}, u32[]{:S(2)}, u32[]{:S(2)}) collective-permute-start(f32[4,16,1536]{2,1,0:T(8,128)S(1)} %get-tuple-element.34), channel_id=1, source_target_pairs={{0,1},{1,0},{2,3},{3,2},{4,5},{5,4},{6,7},{7,6},{8,9},{9,8},{10,11... | collective-permute-start | bytes 1179656 | tf_op jit(solution)/shard_map/ppermute | solution.py:342
  26.4 7.0 %collective-permute-start.5 = (f32[4,16,1536]{2,1,0:T(8,128)S(1)}, f32[4,16,1536]{2,1,0:T(8,128)S(1)}, u32[]{:S(2)}, u32[]{:S(2)}) collective-permute-start(f32[4,16,1536]{2,1,0:T(8,128)S(1)} %get-tuple-element.35), channel_id=1, source_target_pairs={{0,3},{1,2},{2,1},{3,0},{4,7},{5,6},{6,5},{7,4},{8,11},{9,10},{10,... | collective-permute-start | bytes 1179656 | tf_op jit(solution)/shard_map/ppermute | solution.py:342
  33.4 3.1 %project.7 = (f32[64,1536]{1,0:T(8,128)S(1)}, f32[64,1536]{1,0:T(8,128)S(1)}) custom-call(s32[1]{0:T(128)} %bitcast.1.at, s32[2,64]{1,0:T(2,128)} %bitcast.20, bf16[1536,512]{1,0:T(8,128)(2,1)} %bitcast.16, bf16[512,512]{1,0:T(8,128)(2,1)} %basis.7, bf16[1,512]{1,0:T(2,128)(2,1)} %phantom.7), custom_call_target="tpu_custom_call" | custom-call | tf_op jit(solution)/shard_map/project/pallas_call | solution.py:74
  36.5 1.9 collective-permute-start.2
  38.4 4.2 %collective-permute-start.3 = (f32[64,1536]{1,0:T(8,128)S(1)}, f32[64,1536]{1,0:T(8,128)S(1)}, u32[]{:S(2)}, u32[]{:S(2)}) collective-permute-start(f32[64,1536]{1,0:T(8,128)S(1)} %get-tuple-element.33), channel_id=1, source_target_pairs={{0,28},{4,8},{8,4},{12,16},{16,12},{20,24},{24,20},{28,0},{1,29},{... | collective-permute-start | bytes 1179656 | tf_op jit(solution)/shard_map/ppermute | solution.py:342
  42.7 3.1 %project.4 = (f32[64,1536]{1,0:T(8,128)S(1)}, f32[64,1536]{1,0:T(8,128)S(1)}) custom-call(s32[1]{0:T(128)} %bitcast.3.at, s32[2,64]{1,0:T(2,128)} %bitcast.21, bf16[1536,512]{1,0:T(8,128)(2,1)} %bitcast.17, bf16[512,512]{1,0:T(8,128)(2,1)} %basis.7, bf16[1,512]{1,0:T(2,128)(2,1)} %phantom.7), custom_call_target="tpu_custom_call" | custom-call | tf_op jit(solution)/shard_map/project/pallas_call | solution.py:74
  45.7 0.0 collective-permute-done.5.high
  45.8 1.1 collective-permute-done.2.came_a
  46.9 3.1 %collective-permute-done.3.came_b = f32[64,1536]{1,0:T(8,128)S(1)} collective-permute-done((f32[64,1536]{1,0:T(8,128)S(1)}, f32[64,1536]{1,0:T(8,128)S(1)}, u32[]{:S(2)}, u32[]{:S(2)}) %collective-permute-start.3) | collective-permute-done | bytes 393248 | tf_op jit(solution)/shard_map/ppermute | solution.py:342
  50.0 0.1 join.1
  50.1 34.9 %all_to_all.20.parts = f32[8,16,1536]{2,1,0:T(8,128)S(1)} all-to-all(f32[8,16,1536]{2,1,0:T(8,128)S(1)} %join.1), channel_id=1, replica_groups=mesh['x'=4,'zl'=2,'core'=2,'yh'=4,'yl'=2,'zhh'=2,'zhl'=2] {'yh','zhh'}, dimensions={0} | all-to-all | bytes 1572864 | tf_op jit(solution)/shard_map/all_to_all | solution.py:370
  85.1 0.1 spread.1
  85.2 29.0 %all_to_all.21.own = f32[8,16,1536]{2,1,0:T(8,128)S(1)} all-to-all(f32[8,16,1536]{2,1,0:T(8,128)S(1)} %spread.1), channel_id=1, replica_groups=mesh['x'=4,'zl'=2,'core'=2,'yh'=4,'yl'=2,'zhh'=2,'zhl'=2] {'yh','zhh'}, dimensions={0} | all-to-all | bytes 1572864 | tf_op jit(solution)/shard_map/all_to_all | solution.py:371
  114.2 0.1 fusion.1
  114.3 1.9 collective-permute-start.7
  116.2 0.0 copy-start.3
  116.2 0.0 copy-start
  116.2 3.0 %collective-permute-start.6 = (f32[4,16,1536]{2,1,0:T(8,128)S(1)}, f32[4,16,1536]{2,1,0:T(8,128)S(1)}, u32[]{:S(2)}, u32[]{:S(2)}) collective-permute-start(f32[4,16,1536]{2,1,0:T(8,128)S(1)} %get-tuple-element.44), channel_id=1, source_target_pairs={{0,1},{1,0},{2,3},{3,2},{4,5},{5,4},{6,7},{7,6},{8,9},{9,8},{10,11... | collective-permute-start | bytes 1179656 | tf_op jit(solution)/shard_map/ppermute | solution.py:342
  119.3 1.0 fusion
  120.3 1.9 collective-permute-start.9
  122.2 5.2 %collective-permute-start.8 = (f32[8,8,1536]{2,1,0:T(8,128)}, f32[8,8,1536]{2,1,0:T(8,128)}, u32[]{:S(2)}, u32[]{:S(2)}) collective-permute-start(f32[8,8,1536]{2,1,0:T(8,128)} %get-tuple-element.42), channel_id=1, source_target_pairs={{0,4},{4,0},{8,12},{12,8},{16,20},{20,16},{24,28},{28,24},{1,5},{5... | collective-permute-start | bytes 1179656 | tf_op jit(solution)/shard_map/ppermute | solution.py:342
  127.4 5.5 %collective-permute-done.7.high = f32[4,16,1536]{2,1,0:T(8,128)S(1)} collective-permute-done((f32[4,16,1536]{2,1,0:T(8,128)S(1)}, f32[4,16,1536]{2,1,0:T(8,128)S(1)}, u32[]{:S(2)}, u32[]{:S(2)}) %collective-permute-start.7) | collective-permute-done | bytes 393248 | tf_op jit(solution)/shard_map/ppermute | solution.py:342
  133.0 4.7 %collective-permute-done.6.low = f32[4,16,1536]{2,1,0:T(8,128)S(1)} collective-permute-done((f32[4,16,1536]{2,1,0:T(8,128)S(1)}, f32[4,16,1536]{2,1,0:T(8,128)S(1)}, u32[]{:S(2)}, u32[]{:S(2)}) %collective-permute-start.6) | collective-permute-done | bytes 393248 | tf_op jit(solution)/shard_map/ppermute | solution.py:342
  137.7 1.0 peel.1
  138.7 1.9 collective-permute-start.10
  140.6 3.9 %collective-permute-start.11 = (f32[8,8,1536]{2,1,0:T(8,128)}, f32[8,8,1536]{2,1,0:T(8,128)}, u32[]{:S(2)}, u32[]{:S(2)}) collective-permute-start(f32[8,8,1536]{2,1,0:T(8,128)} %get-tuple-element.37), channel_id=1, source_target_pairs={{0,28},{4,8},{8,4},{12,16},{16,12},{20,24},{24,20},{28,0},{1,29},{... | collective-permute-start | bytes 1179656 | tf_op jit(solution)/shard_map/ppermute | solution.py:342
  144.6 0.5 copy.7
  145.2 0.1 stack.31.at
  145.3 0.0 collective-permute-done.8.near_a
  145.3 1.0 copy-done.2
  146.3 1.4 stage.1.staged
  147.7 2.4 %collective-permute-done.10.far_a = f32[8,8,1536]{2,1,0:T(8,128)} collective-permute-done((f32[8,8,1536]{2,1,0:T(8,128)}, f32[8,8,1536]{2,1,0:T(8,128)}, u32[]{:S(2)}, u32[]{:S(2)}) %collective-permute-start.10) | collective-permute-done | bytes 393248 | tf_op jit(solution)/shard_map/ppermute | solution.py:342
  150.1 3.1 %collective-permute-done.11.far_b = f32[8,8,1536]{2,1,0:T(8,128)} collective-permute-done((f32[8,8,1536]{2,1,0:T(8,128)}, f32[8,8,1536]{2,1,0:T(8,128)}, u32[]{:S(2)}, u32[]{:S(2)}) %collective-permute-start.11) | collective-permute-done | bytes 393248 | tf_op jit(solution)/shard_map/ppermute | solution.py:342
  153.2 4.7 %scores.1 = (f32[1024,1536]{1,0:T(8,128)S(1)}, bf16[512,1536]{1,0:T(8,128)(2,1)S(1)}, f32[32,24,128]{2,1,0:T(8,128)S(1)}) custom-call(s32[7]{0:T(128)S(1)} %stack.31.at, bf16[512,1536]{1,0:T(8,128)(2,1)S(1)} %stage.1.staged, f32[8,8,1536]{2,1,0:T(8,128)} %collective-permute-done.10.far_a, f32[8,8,1536]{2,1,0:T(8,128)} %collective-permute-done.11.far_b, ...), custom_call_target="tpu_custom_call" | custom-call | tf_op jit(solution)/shard_map/scores/pallas_call | solution.py:97
  157.9 22.1 %all_to_all.22.stats = f32[32,24,128]{2,1,0:T(8,128)S(1)} all-to-all(f32[32,24,128]{2,1,0:T(8,128)S(1)} %get-tuple-element.38.own), channel_id=1, replica_groups=mesh['x'=4,'zl'=2,'core'=2,'yh'=4,'yl'=2,'zhh'=2,'zhl'=2] {'zhl','zhh','..., dimensions={0} | all-to-all | bytes 786432 | tf_op jit(solution)/shard_map/all_to_all | solution.py:383
  180.0 2.7 %totals.3 = f32[8,264,128]{2,1,0:T(8,128)S(1)} custom-call(s32[7]{0:T(128)S(1)} %stack.31.at, f32[32,24,128]{2,1,0:T(8,128)S(1)} %all_to_all.22.stats, f32[32,24,128]{2,1,0:T(8,128)S(1)} %get-tuple-element.38.own, f32[1024,1536]{1,0:T(8,128)S(1)} %get-tuple-element.39.powers, bf16[512,1536]{1,0:T(8,128)(2,1)S(1)} %get-tuple-element.40.rounded), custom_call_target="tpu_custom_call" | custom-call | tf_op jit(solution)/shard_map/totals/pallas_call | solution.py:97
  182.7 5.1 %collective-permute-start.12 = (f32[8,264,128]{2,1,0:T(8,128)S(1)}, f32[8,264,128]{2,1,0:T(8,128)S(1)}, u32[]{:S(2)}, u32[]{:S(2)}) collective-permute-start(f32[8,264,128]{2,1,0:T(8,128)S(1)} %totals.3), channel_id=1, source_target_pairs={{0,32},{32,0},{1,33},{33,1},{2,34},{34,2},{3,35},{35,3},{4,36},{36... | collective-permute-start | bytes 3244040 | tf_op jit(solution)/shard_map/ppermute | solution.py:385
  187.9 2.7 %totals.2 = f32[8,264,128]{2,1,0:T(8,128)S(1)} custom-call(s32[7]{0:T(128)S(1)} %stack.31.at, f32[32,24,128]{2,1,0:T(8,128)S(1)} %all_to_all.22.stats, f32[32,24,128]{2,1,0:T(8,128)S(1)} %get-tuple-element.38.own, f32[1024,1536]{1,0:T(8,128)S(1)} %get-tuple-element.39.powers, bf16[512,1536]{1,0:T(8,128)(2,1)S(1)} %get-tuple-element.40.rounded), custom_call_target="tpu_custom_call" | custom-call | tf_op jit(solution)/shard_map/totals/pallas_call | solution.py:97
  190.6 0.0 collective-permute-done.12
  190.6 0.1 add.39
  190.7 19.8 %all_to_all.23.parts = f32[8,264,128]{2,1,0:T(8,128)S(1)} all-to-all(f32[8,264,128]{2,1,0:T(8,128)S(1)} %add.39), channel_id=1, replica_groups=mesh['x'=4,'zl'=2,'core'=2,'yh'=4,'yl'=2,'zhh'=2,'zhl'=2] {'zl','x'}, dimensions={0} | all-to-all | bytes 2162688 | tf_op jit(solution)/shard_map/all_to_all | solution.py:387
  210.5 1.3 final.1
  (9 shorter events, 0.0 us)
Async XLA Ops:
  3.1 12.0 %collective-permute-start = (f32[64,1536]{1,0:T(8,128)S(1)}, f32[64,1536]{1,0:T(8,128)S(1)}, u32[]{:S(2)}, u32[]{:S(2)}) collective-permute-start(f32[64,1536]{1,0:T(8,128)S(1)} %get-tuple-element.27), channel_id=1, source_target_pairs={{0,4},{4,0},{8,12},{12,8},{16,20},{20,16},{24,28},{28,24},{1,5},{5... | collective-permute-start | bytes 1179656 | tf_op jit(solution)/shard_map/ppermute | solution.py:342
  7.1 11.7 %collective-permute-start.1 = (f32[64,1536]{1,0:T(8,128)S(1)}, f32[64,1536]{1,0:T(8,128)S(1)}, u32[]{:S(2)}, u32[]{:S(2)}) collective-permute-start(f32[64,1536]{1,0:T(8,128)S(1)} %get-tuple-element.28), channel_id=1, source_target_pairs={{0,28},{4,8},{8,4},{12,16},{16,12},{20,24},{24,20},{28,0},{1,29},{... | collective-permute-start | bytes 1179656 | tf_op jit(solution)/shard_map/ppermute | solution.py:342
  18.9 26.8 %collective-permute-start.4 = (f32[4,16,1536]{2,1,0:T(8,128)S(1)}, f32[4,16,1536]{2,1,0:T(8,128)S(1)}, u32[]{:S(2)}, u32[]{:S(2)}) collective-permute-start(f32[4,16,1536]{2,1,0:T(8,128)S(1)} %get-tuple-element.34), channel_id=1, source_target_pairs={{0,1},{1,0},{2,3},{3,2},{4,5},{5,4},{6,7},{7,6},{8,9},{9,8},{10,11... | collective-permute-start | bytes 1179656 | tf_op jit(solution)/shard_map/ppermute | solution.py:342
  26.4 19.4 %collective-permute-start.5 = (f32[4,16,1536]{2,1,0:T(8,128)S(1)}, f32[4,16,1536]{2,1,0:T(8,128)S(1)}, u32[]{:S(2)}, u32[]{:S(2)}) collective-permute-start(f32[4,16,1536]{2,1,0:T(8,128)S(1)} %get-tuple-element.35), channel_id=1, source_target_pairs={{0,3},{1,2},{2,1},{3,0},{4,7},{5,6},{6,5},{7,4},{8,11},{9,10},{10,... | collective-permute-start | bytes 1179656 | tf_op jit(solution)/shard_map/ppermute | solution.py:342
  36.5 10.4 %collective-permute-start.2 = (f32[64,1536]{1,0:T(8,128)S(1)}, f32[64,1536]{1,0:T(8,128)S(1)}, u32[]{:S(2)}, u32[]{:S(2)}) collective-permute-start(f32[64,1536]{1,0:T(8,128)S(1)} %get-tuple-element.32), channel_id=1, source_target_pairs={{0,4},{4,0},{8,12},{12,8},{16,20},{20,16},{24,28},{28,24},{1,5},{5... | collective-permute-start | bytes 1179656 | tf_op jit(solution)/shard_map/ppermute | solution.py:342
  38.4 11.6 %collective-permute-start.3 = (f32[64,1536]{1,0:T(8,128)S(1)}, f32[64,1536]{1,0:T(8,128)S(1)}, u32[]{:S(2)}, u32[]{:S(2)}) collective-permute-start(f32[64,1536]{1,0:T(8,128)S(1)} %get-tuple-element.33), channel_id=1, source_target_pairs={{0,28},{4,8},{8,4},{12,16},{16,12},{20,24},{24,20},{28,0},{1,29},{... | collective-permute-start | bytes 1179656 | tf_op jit(solution)/shard_map/ppermute | solution.py:342
  114.3 18.7 %collective-permute-start.7 = (f32[4,16,1536]{2,1,0:T(8,128)S(1)}, f32[4,16,1536]{2,1,0:T(8,128)S(1)}, u32[]{:S(2)}, u32[]{:S(2)}) collective-permute-start(f32[4,16,1536]{2,1,0:T(8,128)S(1)} %get-tuple-element.43), channel_id=1, source_target_pairs={{0,3},{1,2},{2,1},{3,0},{4,7},{5,6},{6,5},{7,4},{8,11},{9,10},{10,... | collective-permute-start | bytes 1179656 | tf_op jit(solution)/shard_map/ppermute | solution.py:342
  116.2 28.4 %copy-start.3 = (s32[1,2,768]{2,1,0:T(2,128)S(1)}, s32[1,2,768]{2,1,0:T(2,128)}, u32[]{:S(2)}) copy-start(s32[1,2,768]{2,1,0:T(2,128)} %param.9) | copy-start | bytes 18436
  116.2 28.4 %copy-start = (bf16[512,1024]{1,0:T(8,128)(2,1)S(1)}, bf16[512,1024]{1,0:T(8,128)(2,1)}, u32[]{:S(2)}) copy-start(bf16[512,1024]{1,0:T(8,128)(2,1)} %refs.1) | copy-start | bytes 3145732
  116.2 21.5 %collective-permute-start.6 = (f32[4,16,1536]{2,1,0:T(8,128)S(1)}, f32[4,16,1536]{2,1,0:T(8,128)S(1)}, u32[]{:S(2)}, u32[]{:S(2)}) collective-permute-start(f32[4,16,1536]{2,1,0:T(8,128)S(1)} %get-tuple-element.44), channel_id=1, source_target_pairs={{0,1},{1,0},{2,3},{3,2},{4,5},{5,4},{6,7},{7,6},{8,9},{9,8},{10,11... | collective-permute-start | bytes 1179656 | tf_op jit(solution)/shard_map/ppermute | solution.py:342
  120.3 25.0 %collective-permute-start.9 = (f32[8,8,1536]{2,1,0:T(8,128)}, f32[8,8,1536]{2,1,0:T(8,128)}, u32[]{:S(2)}, u32[]{:S(2)}) collective-permute-start(f32[8,8,1536]{2,1,0:T(8,128)} %get-tuple-element.41), channel_id=1, source_target_pairs={{0,28},{4,8},{8,4},{12,16},{16,12},{20,24},{24,20},{28,0},{1,29},{... | collective-permute-start | bytes 1179656 | tf_op jit(solution)/shard_map/ppermute | solution.py:342
  122.2 23.1 %collective-permute-start.8 = (f32[8,8,1536]{2,1,0:T(8,128)}, f32[8,8,1536]{2,1,0:T(8,128)}, u32[]{:S(2)}, u32[]{:S(2)}) collective-permute-start(f32[8,8,1536]{2,1,0:T(8,128)} %get-tuple-element.42), channel_id=1, source_target_pairs={{0,4},{4,0},{8,12},{12,8},{16,20},{20,16},{24,28},{28,24},{1,5},{5... | collective-permute-start | bytes 1179656 | tf_op jit(solution)/shard_map/ppermute | solution.py:342
  137.7 6.9 %copy-start.1 = (f32[4,16,1536]{2,1,0:T(8,128)}, f32[4,16,1536]{2,1,0:T(8,128)S(1)}, u32[]{:S(2)}) copy-start(f32[4,16,1536]{2,1,0:T(8,128)S(1)} %collective-permute-done.6.low) | copy-start | bytes 1179652
  138.7 11.4 %collective-permute-start.10 = (f32[8,8,1536]{2,1,0:T(8,128)}, f32[8,8,1536]{2,1,0:T(8,128)}, u32[]{:S(2)}, u32[]{:S(2)}) collective-permute-start(f32[8,8,1536]{2,1,0:T(8,128)} %get-tuple-element.36), channel_id=1, source_target_pairs={{0,4},{4,0},{8,12},{12,8},{16,20},{20,16},{24,28},{28,24},{1,5},{5... | collective-permute-start | bytes 1179656 | tf_op jit(solution)/shard_map/ppermute | solution.py:342
  140.6 12.6 %collective-permute-start.11 = (f32[8,8,1536]{2,1,0:T(8,128)}, f32[8,8,1536]{2,1,0:T(8,128)}, u32[]{:S(2)}, u32[]{:S(2)}) collective-permute-start(f32[8,8,1536]{2,1,0:T(8,128)} %get-tuple-element.37), channel_id=1, source_target_pairs={{0,28},{4,8},{8,4},{12,16},{16,12},{20,24},{24,20},{28,0},{1,29},{... | collective-permute-start | bytes 1179656 | tf_op jit(solution)/shard_map/ppermute | solution.py:342
  145.3 1.0 copy-start.2
  182.7 7.8 %collective-permute-start.12 = (f32[8,264,128]{2,1,0:T(8,128)S(1)}, f32[8,264,128]{2,1,0:T(8,128)S(1)}, u32[]{:S(2)}, u32[]{:S(2)}) collective-permute-start(f32[8,264,128]{2,1,0:T(8,128)S(1)} %totals.3), channel_id=1, source_target_pairs={{0,32},{32,0},{1,33},{33,1},{2,34},{34,2},{3,35},{35,3},{4,36},{36... | collective-permute-start | bytes 3244040 | tf_op jit(solution)/shard_map/ppermute | solution.py:385

commit v13 on v12

--- a/solution.py
+++ b/solution.py
@@ -236,7 +236,7 @@
             stats[:, pl.ds(lines + line, 1), :] = jnp.broadcast_to(total[None, :, side], shape)
         return carry
 
-    lax.fori_loop(0, powers.shape[1] // width, column, 0, unroll=2)
+    lax.fori_loop(0, powers.shape[1] // width, column, 0, unroll=True)
 
 
 def scores_of(at, held, prior, refs_t, members):
@@ -285,7 +285,7 @@
             out[:, pl.ds(body + column, 1), :] = mass
         return carry
 
-    lax.fori_loop(0, powers.shape[0] // width, orients, 0, unroll=2)
+    lax.fori_loop(0, powers.shape[0] // width, orients, 0, unroll=True)
 
 
 def totals_of(other, at, stats, sent, powers, rounded, peers):

time: 213 us -> 212 us (level)
  no operation moved by 1% of the time
where the time goes in v13:
time: 212 us; the launch traced here: 210 us
  blocking collectives  106 us (50%)
  starting transfers between devices  52.6 us (25%)
  Pallas kernels  25.1 us (12%)
  waiting for transfers between devices  23.9 us (11%)
  local copies, waits for them, and re-layouts  2.69 us (1%)
    ppermute x12, starting transfers between devices, swapped(): lax.ppermute(x, axis, p)  47.5 us
    all_to_all x1, blocking collectives, shards(): parts = lax.all_to_all(parts, ALIKE, 0, 0, tiled=True)  34.9 us
    all_to_all x1, blocking collectives, shards(): own = lax.all_to_all(summed_copies(parts), ALIKE, 0, 0, tiled=True)  29 us
    ppermute x12, waiting for transfers between devices, swapped(): lax.ppermute(x, axis, p)  23.9 us
    all_to_all x1, blocking collectives, shards(): stats = lax.all_to_all(sent, EVERY, 0, 0, tiled=True)  22.1 us
    all_to_all x1, blocking collectives, shards(): parts = lax.all_to_all(parts, PEERS, 0, 0, tiled=True)  19.6 us
    pallas_call x4, Pallas kernels, projected(): pl.pallas_call(project_kernel, grid_spec=pltpu.PrefetchScalarGridSpec(num...  12.2 us
    pallas_call x8, Pallas kernels, whole(): pl.pallas_call(kernel, in_specs=[pl.BlockSpec(memory_space=pltpu.SMEM)] *...  11.6 us
  transfers between devices with their start and end apart: 13, of which 7 were waited for; matrix products, arithmetic and copies ran while one was open for 1% of the time, Pallas kernels for 7%

profile of v13, /device:TPU:1, one launch (start us, length us, event | category | flops | bytes accessed | tf_op | source)
XLA Modules:
  0.0 210.4 jit_solution(11581043936448614465)
XLA Ops:
  0.0 3.0 %project.6 = (f32[64,1536]{1,0:T(8,128)S(1)}, f32[64,1536]{1,0:T(8,128)S(1)}) custom-call(s32[1]{0:T(128)} %bitcast.at, s32[2,64]{1,0:T(2,128)} %bitcast.18, bf16[1536,512]{1,0:T(8,128)(2,1)} %bitcast.14, bf16[512,512]{1,0:T(8,128)(2,1)} %basis.7, bf16[1,512]{1,0:T(2,128)(2,1)} %phantom.7), custom_call_target="tpu_custom_call" | custom-call | tf_op jit(solution)/shard_map/project/pallas_call | solution.py:74
  3.1 4.0 %collective-permute-start = (f32[64,1536]{1,0:T(8,128)S(1)}, f32[64,1536]{1,0:T(8,128)S(1)}, u32[]{:S(2)}, u32[]{:S(2)}) collective-permute-start(f32[64,1536]{1,0:T(8,128)S(1)} %get-tuple-element.27), channel_id=1, source_target_pairs={{0,4},{4,0},{8,12},{12,8},{16,20},{20,16},{24,28},{28,24},{1,5},{5... | collective-permute-start | bytes 1179656 | tf_op jit(solution)/shard_map/ppermute | solution.py:342
  7.1 4.9 %collective-permute-start.1 = (f32[64,1536]{1,0:T(8,128)S(1)}, f32[64,1536]{1,0:T(8,128)S(1)}, u32[]{:S(2)}, u32[]{:S(2)}) collective-permute-start(f32[64,1536]{1,0:T(8,128)S(1)} %get-tuple-element.28), channel_id=1, source_target_pairs={{0,28},{4,8},{8,4},{12,16},{16,12},{20,24},{24,20},{28,0},{1,29},{... | collective-permute-start | bytes 1179656 | tf_op jit(solution)/shard_map/ppermute | solution.py:342
  12.0 3.1 %project.5 = (f32[64,1536]{1,0:T(8,128)S(1)}, f32[64,1536]{1,0:T(8,128)S(1)}) custom-call(s32[1]{0:T(128)} %bitcast.2.at, s32[2,64]{1,0:T(2,128)} %bitcast.19, bf16[1536,512]{1,0:T(8,128)(2,1)} %bitcast.15, bf16[512,512]{1,0:T(8,128)(2,1)} %basis.7, bf16[1,512]{1,0:T(2,128)(2,1)} %phantom.7), custom_call_target="tpu_custom_call" | custom-call | tf_op jit(solution)/shard_map/project/pallas_call | solution.py:74
  15.0 0.0 collective-permute-done.came_a
  15.1 3.8 %collective-permute-done.1.came_b = f32[64,1536]{1,0:T(8,128)S(1)} collective-permute-done((f32[64,1536]{1,0:T(8,128)S(1)}, f32[64,1536]{1,0:T(8,128)S(1)}, u32[]{:S(2)}, u32[]{:S(2)}) %collective-permute-start.1) | collective-permute-done | bytes 393248 | tf_op jit(solution)/shard_map/ppermute | solution.py:342
  18.8 0.1 relay.1
  18.9 7.5 %collective-permute-start.4 = (f32[4,16,1536]{2,1,0:T(8,128)S(1)}, f32[4,16,1536]{2,1,0:T(8,128)S(1)}, u32[]{:S(2)}, u32[]{:S(2)}) collective-permute-start(f32[4,16,1536]{2,1,0:T(8,128)S(1)} %get-tuple-element.34), channel_id=1, source_target_pairs={{0,1},{1,0},{2,3},{3,2},{4,5},{5,4},{6,7},{7,6},{8,9},{9,8},{10,11... | collective-permute-start | bytes 1179656 | tf_op jit(solution)/shard_map/ppermute | solution.py:342
  26.4 7.0 %collective-permute-start.5 = (f32[4,16,1536]{2,1,0:T(8,128)S(1)}, f32[4,16,1536]{2,1,0:T(8,128)S(1)}, u32[]{:S(2)}, u32[]{:S(2)}) collective-permute-start(f32[4,16,1536]{2,1,0:T(8,128)S(1)} %get-tuple-element.35), channel_id=1, source_target_pairs={{0,3},{1,2},{2,1},{3,0},{4,7},{5,6},{6,5},{7,4},{8,11},{9,10},{10,... | collective-permute-start | bytes 1179656 | tf_op jit(solution)/shard_map/ppermute | solution.py:342
  33.4 3.1 %project.7 = (f32[64,1536]{1,0:T(8,128)S(1)}, f32[64,1536]{1,0:T(8,128)S(1)}) custom-call(s32[1]{0:T(128)} %bitcast.1.at, s32[2,64]{1,0:T(2,128)} %bitcast.20, bf16[1536,512]{1,0:T(8,128)(2,1)} %bitcast.16, bf16[512,512]{1,0:T(8,128)(2,1)} %basis.7, bf16[1,512]{1,0:T(2,128)(2,1)} %phantom.7), custom_call_target="tpu_custom_call" | custom-call | tf_op jit(solution)/shard_map/project/pallas_call | solution.py:74
  36.5 1.9 collective-permute-start.2
  38.4 4.2 %collective-permute-start.3 = (f32[64,1536]{1,0:T(8,128)S(1)}, f32[64,1536]{1,0:T(8,128)S(1)}, u32[]{:S(2)}, u32[]{:S(2)}) collective-permute-start(f32[64,1536]{1,0:T(8,128)S(1)} %get-tuple-element.33), channel_id=1, source_target_pairs={{0,28},{4,8},{8,4},{12,16},{16,12},{20,24},{24,20},{28,0},{1,29},{... | collective-permute-start | bytes 1179656 | tf_op jit(solution)/shard_map/ppermute | solution.py:342
  42.7 3.1 %project.4 = (f32[64,1536]{1,0:T(8,128)S(1)}, f32[64,1536]{1,0:T(8,128)S(1)}) custom-call(s32[1]{0:T(128)} %bitcast.3.at, s32[2,64]{1,0:T(2,128)} %bitcast.21, bf16[1536,512]{1,0:T(8,128)(2,1)} %bitcast.17, bf16[512,512]{1,0:T(8,128)(2,1)} %basis.7, bf16[1,512]{1,0:T(2,128)(2,1)} %phantom.7), custom_call_target="tpu_custom_call" | custom-call | tf_op jit(solution)/shard_map/project/pallas_call | solution.py:74
  45.7 0.0 collective-permute-done.5.high
  45.8 1.1 collective-permute-done.2.came_a
  46.9 3.1 %collective-permute-done.3.came_b = f32[64,1536]{1,0:T(8,128)S(1)} collective-permute-done((f32[64,1536]{1,0:T(8,128)S(1)}, f32[64,1536]{1,0:T(8,128)S(1)}, u32[]{:S(2)}, u32[]{:S(2)}) %collective-permute-start.3) | collective-permute-done | bytes 393248 | tf_op jit(solution)/shard_map/ppermute | solution.py:342
  50.0 0.1 join.1
  50.1 34.9 %all_to_all.20.parts = f32[8,16,1536]{2,1,0:T(8,128)S(1)} all-to-all(f32[8,16,1536]{2,1,0:T(8,128)S(1)} %join.1), channel_id=1, replica_groups=mesh['x'=4,'zl'=2,'core'=2,'yh'=4,'yl'=2,'zhh'=2,'zhl'=2] {'yh','zhh'}, dimensions={0} | all-to-all | bytes 1572864 | tf_op jit(solution)/shard_map/all_to_all | solution.py:370
  85.1 0.1 spread.1
  85.2 29.0 %all_to_all.21.own = f32[8,16,1536]{2,1,0:T(8,128)S(1)} all-to-all(f32[8,16,1536]{2,1,0:T(8,128)S(1)} %spread.1), channel_id=1, replica_groups=mesh['x'=4,'zl'=2,'core'=2,'yh'=4,'yl'=2,'zhh'=2,'zhl'=2] {'yh','zhh'}, dimensions={0} | all-to-all | bytes 1572864 | tf_op jit(solution)/shard_map/all_to_all | solution.py:371
  114.2 0.1 fusion.1
  114.3 1.9 collective-permute-start.7
  116.2 0.0 copy-start.3
  116.2 0.0 copy-start
  116.2 3.0 %collective-permute-start.6 = (f32[4,16,1536]{2,1,0:T(8,128)S(1)}, f32[4,16,1536]{2,1,0:T(8,128)S(1)}, u32[]{:S(2)}, u32[]{:S(2)}) collective-permute-start(f32[4,16,1536]{2,1,0:T(8,128)S(1)} %get-tuple-element.44), channel_id=1, source_target_pairs={{0,1},{1,0},{2,3},{3,2},{4,5},{5,4},{6,7},{7,6},{8,9},{9,8},{10,11... | collective-permute-start | bytes 1179656 | tf_op jit(solution)/shard_map/ppermute | solution.py:342
  119.3 1.0 fusion
  120.3 1.9 collective-permute-start.9
  122.2 5.2 %collective-permute-start.8 = (f32[8,8,1536]{2,1,0:T(8,128)}, f32[8,8,1536]{2,1,0:T(8,128)}, u32[]{:S(2)}, u32[]{:S(2)}) collective-permute-start(f32[8,8,1536]{2,1,0:T(8,128)} %get-tuple-element.42), channel_id=1, source_target_pairs={{0,4},{4,0},{8,12},{12,8},{16,20},{20,16},{24,28},{28,24},{1,5},{5... | collective-permute-start | bytes 1179656 | tf_op jit(solution)/shard_map/ppermute | solution.py:342
  127.4 5.5 %collective-permute-done.7.high = f32[4,16,1536]{2,1,0:T(8,128)S(1)} collective-permute-done((f32[4,16,1536]{2,1,0:T(8,128)S(1)}, f32[4,16,1536]{2,1,0:T(8,128)S(1)}, u32[]{:S(2)}, u32[]{:S(2)}) %collective-permute-start.7) | collective-permute-done | bytes 393248 | tf_op jit(solution)/shard_map/ppermute | solution.py:342
  133.0 4.7 %collective-permute-done.6.low = f32[4,16,1536]{2,1,0:T(8,128)S(1)} collective-permute-done((f32[4,16,1536]{2,1,0:T(8,128)S(1)}, f32[4,16,1536]{2,1,0:T(8,128)S(1)}, u32[]{:S(2)}, u32[]{:S(2)}) %collective-permute-start.6) | collective-permute-done | bytes 393248 | tf_op jit(solution)/shard_map/ppermute | solution.py:342
  137.7 1.0 peel.1
  138.7 1.9 collective-permute-start.10
  140.6 3.9 %collective-permute-start.11 = (f32[8,8,1536]{2,1,0:T(8,128)}, f32[8,8,1536]{2,1,0:T(8,128)}, u32[]{:S(2)}, u32[]{:S(2)}) collective-permute-start(f32[8,8,1536]{2,1,0:T(8,128)} %get-tuple-element.37), channel_id=1, source_target_pairs={{0,28},{4,8},{8,4},{12,16},{16,12},{20,24},{24,20},{28,0},{1,29},{... | collective-permute-start | bytes 1179656 | tf_op jit(solution)/shard_map/ppermute | solution.py:342
  144.6 0.5 copy.7
  145.2 0.1 stack.31.at
  145.3 0.0 collective-permute-done.8.near_a
  145.3 1.0 copy-done.2
  146.3 1.4 stage.1.staged
  147.7 2.4 %collective-permute-done.10.far_a = f32[8,8,1536]{2,1,0:T(8,128)} collective-permute-done((f32[8,8,1536]{2,1,0:T(8,128)}, f32[8,8,1536]{2,1,0:T(8,128)}, u32[]{:S(2)}, u32[]{:S(2)}) %collective-permute-start.10) | collective-permute-done | bytes 393248 | tf_op jit(solution)/shard_map/ppermute | solution.py:342
  150.1 3.1 %collective-permute-done.11.far_b = f32[8,8,1536]{2,1,0:T(8,128)} collective-permute-done((f32[8,8,1536]{2,1,0:T(8,128)}, f32[8,8,1536]{2,1,0:T(8,128)}, u32[]{:S(2)}, u32[]{:S(2)}) %collective-permute-start.11) | collective-permute-done | bytes 393248 | tf_op jit(solution)/shard_map/ppermute | solution.py:342
  153.2 4.1 %scores.1 = (f32[1024,1536]{1,0:T(8,128)S(1)}, bf16[512,1536]{1,0:T(8,128)(2,1)S(1)}, f32[32,24,128]{2,1,0:T(8,128)S(1)}) custom-call(s32[7]{0:T(128)S(1)} %stack.31.at, bf16[512,1536]{1,0:T(8,128)(2,1)S(1)} %stage.1.staged, f32[8,8,1536]{2,1,0:T(8,128)} %collective-permute-done.10.far_a, f32[8,8,1536]{2,1,0:T(8,128)} %collective-permute-done.11.far_b, ...), custom_call_target="tpu_custom_call" | custom-call | tf_op jit(solution)/shard_map/scores/pallas_call | solution.py:97
  157.3 22.1 %all_to_all.22.stats = f32[32,24,128]{2,1,0:T(8,128)S(1)} all-to-all(f32[32,24,128]{2,1,0:T(8,128)S(1)} %get-tuple-element.38.own), channel_id=1, replica_groups=mesh['x'=4,'zl'=2,'core'=2,'yh'=4,'yl'=2,'zhh'=2,'zhl'=2] {'zhl','zhh','..., dimensions={0} | all-to-all | bytes 786432 | tf_op jit(solution)/shard_map/all_to_all | solution.py:383
  179.4 2.4 %totals.3 = f32[8,264,128]{2,1,0:T(8,128)S(1)} custom-call(s32[7]{0:T(128)S(1)} %stack.31.at, f32[32,24,128]{2,1,0:T(8,128)S(1)} %all_to_all.22.stats, f32[32,24,128]{2,1,0:T(8,128)S(1)} %get-tuple-element.38.own, f32[1024,1536]{1,0:T(8,128)S(1)} %get-tuple-element.39.powers, bf16[512,1536]{1,0:T(8,128)(2,1)S(1)} %get-tuple-element.40.rounded), custom_call_target="tpu_custom_call" | custom-call | tf_op jit(solution)/shard_map/totals/pallas_call | solution.py:97
  181.8 5.1 %collective-permute-start.12 = (f32[8,264,128]{2,1,0:T(8,128)S(1)}, f32[8,264,128]{2,1,0:T(8,128)S(1)}, u32[]{:S(2)}, u32[]{:S(2)}) collective-permute-start(f32[8,264,128]{2,1,0:T(8,128)S(1)} %totals.3), channel_id=1, source_target_pairs={{0,32},{32,0},{1,33},{33,1},{2,34},{34,2},{3,35},{35,3},{4,36},{36... | collective-permute-start | bytes 3244040 | tf_op jit(solution)/shard_map/ppermute | solution.py:385
  186.9 2.4 %totals.2 = f32[8,264,128]{2,1,0:T(8,128)S(1)} custom-call(s32[7]{0:T(128)S(1)} %stack.31.at, f32[32,24,128]{2,1,0:T(8,128)S(1)} %all_to_all.22.stats, f32[32,24,128]{2,1,0:T(8,128)S(1)} %get-tuple-element.38.own, f32[1024,1536]{1,0:T(8,128)S(1)} %get-tuple-element.39.powers, bf16[512,1536]{1,0:T(8,128)(2,1)S(1)} %get-tuple-element.40.rounded), custom_call_target="tpu_custom_call" | custom-call | tf_op jit(solution)/shard_map/totals/pallas_call | solution.py:97
  189.4 0.1 add.39
  189.5 19.6 %all_to_all.23.parts = f32[8,264,128]{2,1,0:T(8,128)S(1)} all-to-all(f32[8,264,128]{2,1,0:T(8,128)S(1)} %add.39), channel_id=1, replica_groups=mesh['x'=4,'zl'=2,'core'=2,'yh'=4,'yl'=2,'zhh'=2,'zhl'=2] {'zl','x'}, dimensions={0} | all-to-all | bytes 2162688 | tf_op jit(solution)/shard_map/all_to_all | solution.py:387
  209.1 1.3 final.1
  (9 shorter events, 0.0 us)
Async XLA Ops:
  3.1 12.0 %collective-permute-start = (f32[64,1536]{1,0:T(8,128)S(1)}, f32[64,1536]{1,0:T(8,128)S(1)}, u32[]{:S(2)}, u32[]{:S(2)}) collective-permute-start(f32[64,1536]{1,0:T(8,128)S(1)} %get-tuple-element.27), channel_id=1, source_target_pairs={{0,4},{4,0},{8,12},{12,8},{16,20},{20,16},{24,28},{28,24},{1,5},{5... | collective-permute-start | bytes 1179656 | tf_op jit(solution)/shard_map/ppermute | solution.py:342
  7.1 11.7 %collective-permute-start.1 = (f32[64,1536]{1,0:T(8,128)S(1)}, f32[64,1536]{1,0:T(8,128)S(1)}, u32[]{:S(2)}, u32[]{:S(2)}) collective-permute-start(f32[64,1536]{1,0:T(8,128)S(1)} %get-tuple-element.28), channel_id=1, source_target_pairs={{0,28},{4,8},{8,4},{12,16},{16,12},{20,24},{24,20},{28,0},{1,29},{... | collective-permute-start | bytes 1179656 | tf_op jit(solution)/shard_map/ppermute | solution.py:342
  18.9 26.8 %collective-permute-start.4 = (f32[4,16,1536]{2,1,0:T(8,128)S(1)}, f32[4,16,1536]{2,1,0:T(8,128)S(1)}, u32[]{:S(2)}, u32[]{:S(2)}) collective-permute-start(f32[4,16,1536]{2,1,0:T(8,128)S(1)} %get-tuple-element.34), channel_id=1, source_target_pairs={{0,1},{1,0},{2,3},{3,2},{4,5},{5,4},{6,7},{7,6},{8,9},{9,8},{10,11... | collective-permute-start | bytes 1179656 | tf_op jit(solution)/shard_map/ppermute | solution.py:342
  26.4 19.4 %collective-permute-start.5 = (f32[4,16,1536]{2,1,0:T(8,128)S(1)}, f32[4,16,1536]{2,1,0:T(8,128)S(1)}, u32[]{:S(2)}, u32[]{:S(2)}) collective-permute-start(f32[4,16,1536]{2,1,0:T(8,128)S(1)} %get-tuple-element.35), channel_id=1, source_target_pairs={{0,3},{1,2},{2,1},{3,0},{4,7},{5,6},{6,5},{7,4},{8,11},{9,10},{10,... | collective-permute-start | bytes 1179656 | tf_op jit(solution)/shard_map/ppermute | solution.py:342
  36.5 10.4 %collective-permute-start.2 = (f32[64,1536]{1,0:T(8,128)S(1)}, f32[64,1536]{1,0:T(8,128)S(1)}, u32[]{:S(2)}, u32[]{:S(2)}) collective-permute-start(f32[64,1536]{1,0:T(8,128)S(1)} %get-tuple-element.32), channel_id=1, source_target_pairs={{0,4},{4,0},{8,12},{12,8},{16,20},{20,16},{24,28},{28,24},{1,5},{5... | collective-permute-start | bytes 1179656 | tf_op jit(solution)/shard_map/ppermute | solution.py:342
  38.4 11.6 %collective-permute-start.3 = (f32[64,1536]{1,0:T(8,128)S(1)}, f32[64,1536]{1,0:T(8,128)S(1)}, u32[]{:S(2)}, u32[]{:S(2)}) collective-permute-start(f32[64,1536]{1,0:T(8,128)S(1)} %get-tuple-element.33), channel_id=1, source_target_pairs={{0,28},{4,8},{8,4},{12,16},{16,12},{20,24},{24,20},{28,0},{1,29},{... | collective-permute-start | bytes 1179656 | tf_op jit(solution)/shard_map/ppermute | solution.py:342
  114.3 18.7 %collective-permute-start.7 = (f32[4,16,1536]{2,1,0:T(8,128)S(1)}, f32[4,16,1536]{2,1,0:T(8,128)S(1)}, u32[]{:S(2)}, u32[]{:S(2)}) collective-permute-start(f32[4,16,1536]{2,1,0:T(8,128)S(1)} %get-tuple-element.43), channel_id=1, source_target_pairs={{0,3},{1,2},{2,1},{3,0},{4,7},{5,6},{6,5},{7,4},{8,11},{9,10},{10,... | collective-permute-start | bytes 1179656 | tf_op jit(solution)/shard_map/ppermute | solution.py:342
  116.2 28.4 %copy-start.3 = (s32[1,2,768]{2,1,0:T(2,128)S(1)}, s32[1,2,768]{2,1,0:T(2,128)}, u32[]{:S(2)}) copy-start(s32[1,2,768]{2,1,0:T(2,128)} %param.9) | copy-start | bytes 18436
  116.2 28.4 %copy-start = (bf16[512,1024]{1,0:T(8,128)(2,1)S(1)}, bf16[512,1024]{1,0:T(8,128)(2,1)}, u32[]{:S(2)}) copy-start(bf16[512,1024]{1,0:T(8,128)(2,1)} %refs.1) | copy-start | bytes 3145732
  116.2 21.5 %collective-permute-start.6 = (f32[4,16,1536]{2,1,0:T(8,128)S(1)}, f32[4,16,1536]{2,1,0:T(8,128)S(1)}, u32[]{:S(2)}, u32[]{:S(2)}) collective-permute-start(f32[4,16,1536]{2,1,0:T(8,128)S(1)} %get-tuple-element.44), channel_id=1, source_target_pairs={{0,1},{1,0},{2,3},{3,2},{4,5},{5,4},{6,7},{7,6},{8,9},{9,8},{10,11... | collective-permute-start | bytes 1179656 | tf_op jit(solution)/shard_map/ppermute | solution.py:342
  120.3 25.0 %collective-permute-start.9 = (f32[8,8,1536]{2,1,0:T(8,128)}, f32[8,8,1536]{2,1,0:T(8,128)}, u32[]{:S(2)}, u32[]{:S(2)}) collective-permute-start(f32[8,8,1536]{2,1,0:T(8,128)} %get-tuple-element.41), channel_id=1, source_target_pairs={{0,28},{4,8},{8,4},{12,16},{16,12},{20,24},{24,20},{28,0},{1,29},{... | collective-permute-start | bytes 1179656 | tf_op jit(solution)/shard_map/ppermute | solution.py:342
  122.2 23.1 %collective-permute-start.8 = (f32[8,8,1536]{2,1,0:T(8,128)}, f32[8,8,1536]{2,1,0:T(8,128)}, u32[]{:S(2)}, u32[]{:S(2)}) collective-permute-start(f32[8,8,1536]{2,1,0:T(8,128)} %get-tuple-element.42), channel_id=1, source_target_pairs={{0,4},{4,0},{8,12},{12,8},{16,20},{20,16},{24,28},{28,24},{1,5},{5... | collective-permute-start | bytes 1179656 | tf_op jit(solution)/shard_map/ppermute | solution.py:342
  137.7 6.9 %copy-start.1 = (f32[4,16,1536]{2,1,0:T(8,128)}, f32[4,16,1536]{2,1,0:T(8,128)S(1)}, u32[]{:S(2)}) copy-start(f32[4,16,1536]{2,1,0:T(8,128)S(1)} %collective-permute-done.6.low) | copy-start | bytes 1179652
  138.7 11.4 %collective-permute-start.10 = (f32[8,8,1536]{2,1,0:T(8,128)}, f32[8,8,1536]{2,1,0:T(8,128)}, u32[]{:S(2)}, u32[]{:S(2)}) collective-permute-start(f32[8,8,1536]{2,1,0:T(8,128)} %get-tuple-element.36), channel_id=1, source_target_pairs={{0,4},{4,0},{8,12},{12,8},{16,20},{20,16},{24,28},{28,24},{1,5},{5... | collective-permute-start | bytes 1179656 | tf_op jit(solution)/shard_map/ppermute | solution.py:342
  140.6 12.6 %collective-permute-start.11 = (f32[8,8,1536]{2,1,0:T(8,128)}, f32[8,8,1536]{2,1,0:T(8,128)}, u32[]{:S(2)}, u32[]{:S(2)}) collective-permute-start(f32[8,8,1536]{2,1,0:T(8,128)} %get-tuple-element.37), channel_id=1, source_target_pairs={{0,28},{4,8},{8,4},{12,16},{16,12},{20,24},{24,20},{28,0},{1,29},{... | collective-permute-start | bytes 1179656 | tf_op jit(solution)/shard_map/ppermute | solution.py:342
  145.3 1.0 copy-start.2
  181.8 7.5 %collective-permute-start.12 = (f32[8,264,128]{2,1,0:T(8,128)S(1)}, f32[8,264,128]{2,1,0:T(8,128)S(1)}, u32[]{:S(2)}, u32[]{:S(2)}) collective-permute-start(f32[8,264,128]{2,1,0:T(8,128)S(1)} %totals.3), channel_id=1, source_target_pairs={{0,32},{32,0},{1,33},{33,1},{2,34},{34,2},{3,35},{35,3},{4,36},{36... | collective-permute-start | bytes 3244040 | tf_op jit(solution)/shard_map/ppermute | solution.py:385

commit v14 on v13

--- a/solution.py
+++ b/solution.py
@@ -149,7 +149,7 @@
             out[k, :, cut] = total
         return carry
 
-    lax.fori_loop(0, parts.shape[2] // width, column, 0)
+    lax.fori_loop(0, parts.shape[2] // width, column, 0, unroll=True)
 
 
 def summed_copies(parts):
@@ -194,7 +194,7 @@
         put(3, half, own[:, 8:, cut])
         return carry
 
-    lax.fori_loop(0, staged.shape[1] // width, column, 0)
+    lax.fori_loop(0, staged.shape[1] // width, column, 0, unroll=True)
 
 
 def staged_of(at, held):

time: 212 us -> 212 us (level)
  no operation moved by 1% of the time
where the time goes in v14:
time: 212 us; the launch traced here: 210 us
  blocking collectives  106 us (50%)
  starting transfers between devices  52.6 us (25%)
  Pallas kernels  24.9 us (12%)
  waiting for transfers between devices  24 us (11%)
  local copies, waits for them, and re-layouts  2.69 us (1%)
    ppermute x12, starting transfers between devices, swapped(): lax.ppermute(x, axis, p)  47.5 us
    all_to_all x1, blocking collectives, shards(): parts = lax.all_to_all(parts, ALIKE, 0, 0, tiled=True)  34.9 us
    all_to_all x1, blocking collectives, shards(): own = lax.all_to_all(summed_copies(parts), ALIKE, 0, 0, tiled=True)  29 us
    ppermute x12, waiting for transfers between devices, swapped(): lax.ppermute(x, axis, p)  24 us
    all_to_all x1, blocking collectives, shards(): stats = lax.all_to_all(sent, EVERY, 0, 0, tiled=True)  22.1 us
    all_to_all x1, blocking collectives, shards(): parts = lax.all_to_all(parts, PEERS, 0, 0, tiled=True)  19.6 us
    pallas_call x4, Pallas kernels, projected(): pl.pallas_call(project_kernel, grid_spec=pltpu.PrefetchScalarGridSpec(num...  12.2 us
    pallas_call x8, Pallas kernels, whole(): pl.pallas_call(kernel, in_specs=[pl.BlockSpec(memory_space=pltpu.SMEM)] *...  11.4 us
  transfers between devices with their start and end apart: 13, of which 7 were waited for; matrix products, arithmetic and copies ran while one was open for 1% of the time, Pallas kernels for 7%

profile of v14, /device:TPU:1, one launch (start us, length us, event | category | flops | bytes accessed | tf_op | source)
XLA Modules:
  0.0 210.4 jit_solution(4055780322671258009)
XLA Ops:
  0.0 3.0 %project.6 = (f32[64,1536]{1,0:T(8,128)S(1)}, f32[64,1536]{1,0:T(8,128)S(1)}) custom-call(s32[1]{0:T(128)} %bitcast.at, s32[2,64]{1,0:T(2,128)} %bitcast.18, bf16[1536,512]{1,0:T(8,128)(2,1)} %bitcast.14, bf16[512,512]{1,0:T(8,128)(2,1)} %basis.7, bf16[1,512]{1,0:T(2,128)(2,1)} %phantom.7), custom_call_target="tpu_custom_call" | custom-call | tf_op jit(solution)/shard_map/project/pallas_call | solution.py:74
  3.1 4.0 %collective-permute-start = (f32[64,1536]{1,0:T(8,128)S(1)}, f32[64,1536]{1,0:T(8,128)S(1)}, u32[]{:S(2)}, u32[]{:S(2)}) collective-permute-start(f32[64,1536]{1,0:T(8,128)S(1)} %get-tuple-element.27), channel_id=1, source_target_pairs={{0,4},{4,0},{8,12},{12,8},{16,20},{20,16},{24,28},{28,24},{1,5},{5... | collective-permute-start | bytes 1179656 | tf_op jit(solution)/shard_map/ppermute | solution.py:342
  7.1 4.9 %collective-permute-start.1 = (f32[64,1536]{1,0:T(8,128)S(1)}, f32[64,1536]{1,0:T(8,128)S(1)}, u32[]{:S(2)}, u32[]{:S(2)}) collective-permute-start(f32[64,1536]{1,0:T(8,128)S(1)} %get-tuple-element.28), channel_id=1, source_target_pairs={{0,28},{4,8},{8,4},{12,16},{16,12},{20,24},{24,20},{28,0},{1,29},{... | collective-permute-start | bytes 1179656 | tf_op jit(solution)/shard_map/ppermute | solution.py:342
  12.0 3.1 %project.5 = (f32[64,1536]{1,0:T(8,128)S(1)}, f32[64,1536]{1,0:T(8,128)S(1)}) custom-call(s32[1]{0:T(128)} %bitcast.2.at, s32[2,64]{1,0:T(2,128)} %bitcast.19, bf16[1536,512]{1,0:T(8,128)(2,1)} %bitcast.15, bf16[512,512]{1,0:T(8,128)(2,1)} %basis.7, bf16[1,512]{1,0:T(2,128)(2,1)} %phantom.7), custom_call_target="tpu_custom_call" | custom-call | tf_op jit(solution)/shard_map/project/pallas_call | solution.py:74
  15.0 0.0 collective-permute-done.came_a
  15.1 3.8 %collective-permute-done.1.came_b = f32[64,1536]{1,0:T(8,128)S(1)} collective-permute-done((f32[64,1536]{1,0:T(8,128)S(1)}, f32[64,1536]{1,0:T(8,128)S(1)}, u32[]{:S(2)}, u32[]{:S(2)}) %collective-permute-start.1) | collective-permute-done | bytes 393248 | tf_op jit(solution)/shard_map/ppermute | solution.py:342
  18.8 0.1 relay.1
  18.9 7.5 %collective-permute-start.4 = (f32[4,16,1536]{2,1,0:T(8,128)S(1)}, f32[4,16,1536]{2,1,0:T(8,128)S(1)}, u32[]{:S(2)}, u32[]{:S(2)}) collective-permute-start(f32[4,16,1536]{2,1,0:T(8,128)S(1)} %get-tuple-element.34), channel_id=1, source_target_pairs={{0,1},{1,0},{2,3},{3,2},{4,5},{5,4},{6,7},{7,6},{8,9},{9,8},{10,11... | collective-permute-start | bytes 1179656 | tf_op jit(solution)/shard_map/ppermute | solution.py:342
  26.4 7.0 %collective-permute-start.5 = (f32[4,16,1536]{2,1,0:T(8,128)S(1)}, f32[4,16,1536]{2,1,0:T(8,128)S(1)}, u32[]{:S(2)}, u32[]{:S(2)}) collective-permute-start(f32[4,16,1536]{2,1,0:T(8,128)S(1)} %get-tuple-element.35), channel_id=1, source_target_pairs={{0,3},{1,2},{2,1},{3,0},{4,7},{5,6},{6,5},{7,4},{8,11},{9,10},{10,... | collective-permute-start | bytes 1179656 | tf_op jit(solution)/shard_map/ppermute | solution.py:342
  33.4 3.1 %project.7 = (f32[64,1536]{1,0:T(8,128)S(1)}, f32[64,1536]{1,0:T(8,128)S(1)}) custom-call(s32[1]{0:T(128)} %bitcast.1.at, s32[2,64]{1,0:T(2,128)} %bitcast.20, bf16[1536,512]{1,0:T(8,128)(2,1)} %bitcast.16, bf16[512,512]{1,0:T(8,128)(2,1)} %basis.7, bf16[1,512]{1,0:T(2,128)(2,1)} %phantom.7), custom_call_target="tpu_custom_call" | custom-call | tf_op jit(solution)/shard_map/project/pallas_call | solution.py:74
  36.5 1.9 collective-permute-start.2
  38.4 4.2 %collective-permute-start.3 = (f32[64,1536]{1,0:T(8,128)S(1)}, f32[64,1536]{1,0:T(8,128)S(1)}, u32[]{:S(2)}, u32[]{:S(2)}) collective-permute-start(f32[64,1536]{1,0:T(8,128)S(1)} %get-tuple-element.33), channel_id=1, source_target_pairs={{0,28},{4,8},{8,4},{12,16},{16,12},{20,24},{24,20},{28,0},{1,29},{... | collective-permute-start | bytes 1179656 | tf_op jit(solution)/shard_map/ppermute | solution.py:342
  42.7 3.1 %project.4 = (f32[64,1536]{1,0:T(8,128)S(1)}, f32[64,1536]{1,0:T(8,128)S(1)}) custom-call(s32[1]{0:T(128)} %bitcast.3.at, s32[2,64]{1,0:T(2,128)} %bitcast.21, bf16[1536,512]{1,0:T(8,128)(2,1)} %bitcast.17, bf16[512,512]{1,0:T(8,128)(2,1)} %basis.7, bf16[1,512]{1,0:T(2,128)(2,1)} %phantom.7), custom_call_target="tpu_custom_call" | custom-call | tf_op jit(solution)/shard_map/project/pallas_call | solution.py:74
  45.7 0.0 collective-permute-done.4.low
  45.8 1.1 collective-permute-done.2.came_a
  46.9 3.1 %collective-permute-done.3.came_b = f32[64,1536]{1,0:T(8,128)S(1)} collective-permute-done((f32[64,1536]{1,0:T(8,128)S(1)}, f32[64,1536]{1,0:T(8,128)S(1)}, u32[]{:S(2)}, u32[]{:S(2)}) %collective-permute-start.3) | collective-permute-done | bytes 393248 | tf_op jit(solution)/shard_map/ppermute | solution.py:342
  50.0 0.1 join.1
  50.1 34.9 %all_to_all.20.parts = f32[8,16,1536]{2,1,0:T(8,128)S(1)} all-to-all(f32[8,16,1536]{2,1,0:T(8,128)S(1)} %join.1), channel_id=1, replica_groups=mesh['x'=4,'zl'=2,'core'=2,'yh'=4,'yl'=2,'zhh'=2,'zhl'=2] {'yh','zhh'}, dimensions={0} | all-to-all | bytes 1572864 | tf_op jit(solution)/shard_map/all_to_all | solution.py:370
  85.1 0.1 spread.1
  85.2 29.0 %all_to_all.21.own = f32[8,16,1536]{2,1,0:T(8,128)S(1)} all-to-all(f32[8,16,1536]{2,1,0:T(8,128)S(1)} %spread.1), channel_id=1, replica_groups=mesh['x'=4,'zl'=2,'core'=2,'yh'=4,'yl'=2,'zhh'=2,'zhl'=2] {'yh','zhh'}, dimensions={0} | all-to-all | bytes 1572864 | tf_op jit(solution)/shard_map/all_to_all | solution.py:371
  114.2 0.1 fusion.1
  114.2 1.9 collective-permute-start.7
  116.2 0.0 copy-start.3
  116.2 0.0 copy-start
  116.2 3.0 %collective-permute-start.6 = (f32[4,16,1536]{2,1,0:T(8,128)S(1)}, f32[4,16,1536]{2,1,0:T(8,128)S(1)}, u32[]{:S(2)}, u32[]{:S(2)}) collective-permute-start(f32[4,16,1536]{2,1,0:T(8,128)S(1)} %get-tuple-element.44), channel_id=1, source_target_pairs={{0,1},{1,0},{2,3},{3,2},{4,5},{5,4},{6,7},{7,6},{8,9},{9,8},{10,11... | collective-permute-start | bytes 1179656 | tf_op jit(solution)/shard_map/ppermute | solution.py:342
  119.2 1.0 fusion
  120.2 1.9 collective-permute-start.9
  122.1 5.2 %collective-permute-start.8 = (f32[8,8,1536]{2,1,0:T(8,128)}, f32[8,8,1536]{2,1,0:T(8,128)}, u32[]{:S(2)}, u32[]{:S(2)}) collective-permute-start(f32[8,8,1536]{2,1,0:T(8,128)} %get-tuple-element.42), channel_id=1, source_target_pairs={{0,4},{4,0},{8,12},{12,8},{16,20},{20,16},{24,28},{28,24},{1,5},{5... | collective-permute-start | bytes 1179656 | tf_op jit(solution)/shard_map/ppermute | solution.py:342
  127.4 5.5 %collective-permute-done.7.high = f32[4,16,1536]{2,1,0:T(8,128)S(1)} collective-permute-done((f32[4,16,1536]{2,1,0:T(8,128)S(1)}, f32[4,16,1536]{2,1,0:T(8,128)S(1)}, u32[]{:S(2)}, u32[]{:S(2)}) %collective-permute-start.7) | collective-permute-done | bytes 393248 | tf_op jit(solution)/shard_map/ppermute | solution.py:342
  132.9 4.7 %collective-permute-done.6.low = f32[4,16,1536]{2,1,0:T(8,128)S(1)} collective-permute-done((f32[4,16,1536]{2,1,0:T(8,128)S(1)}, f32[4,16,1536]{2,1,0:T(8,128)S(1)}, u32[]{:S(2)}, u32[]{:S(2)}) %collective-permute-start.6) | collective-permute-done | bytes 393248 | tf_op jit(solution)/shard_map/ppermute | solution.py:342
  137.7 1.0 peel.1
  138.7 1.9 collective-permute-start.10
  140.6 3.9 %collective-permute-start.11 = (f32[8,8,1536]{2,1,0:T(8,128)}, f32[8,8,1536]{2,1,0:T(8,128)}, u32[]{:S(2)}, u32[]{:S(2)}) collective-permute-start(f32[8,8,1536]{2,1,0:T(8,128)} %get-tuple-element.37), channel_id=1, source_target_pairs={{0,28},{4,8},{8,4},{12,16},{16,12},{20,24},{24,20},{28,0},{1,29},{... | collective-permute-start | bytes 1179656 | tf_op jit(solution)/shard_map/ppermute | solution.py:342
  144.6 0.5 copy.7
  145.1 0.1 stack.31.at
  145.2 0.0 collective-permute-done.9.near_b
  145.2 1.0 copy-done.2
  146.2 1.3 stage.1.staged
  147.5 2.5 %collective-permute-done.10.far_a = f32[8,8,1536]{2,1,0:T(8,128)} collective-permute-done((f32[8,8,1536]{2,1,0:T(8,128)}, f32[8,8,1536]{2,1,0:T(8,128)}, u32[]{:S(2)}, u32[]{:S(2)}) %collective-permute-start.10) | collective-permute-done | bytes 393248 | tf_op jit(solution)/shard_map/ppermute | solution.py:342
  150.1 3.1 %collective-permute-done.11.far_b = f32[8,8,1536]{2,1,0:T(8,128)} collective-permute-done((f32[8,8,1536]{2,1,0:T(8,128)}, f32[8,8,1536]{2,1,0:T(8,128)}, u32[]{:S(2)}, u32[]{:S(2)}) %collective-permute-start.11) | collective-permute-done | bytes 393248 | tf_op jit(solution)/shard_map/ppermute | solution.py:342
  153.2 4.1 %scores.1 = (f32[1024,1536]{1,0:T(8,128)S(1)}, bf16[512,1536]{1,0:T(8,128)(2,1)S(1)}, f32[32,24,128]{2,1,0:T(8,128)S(1)}) custom-call(s32[7]{0:T(128)S(1)} %stack.31.at, bf16[512,1536]{1,0:T(8,128)(2,1)S(1)} %stage.1.staged, f32[8,8,1536]{2,1,0:T(8,128)} %collective-permute-done.10.far_a, f32[8,8,1536]{2,1,0:T(8,128)} %collective-permute-done.11.far_b, ...), custom_call_target="tpu_custom_call" | custom-call | tf_op jit(solution)/shard_map/scores/pallas_call | solution.py:97
  157.3 22.1 %all_to_all.22.stats = f32[32,24,128]{2,1,0:T(8,128)S(1)} all-to-all(f32[32,24,128]{2,1,0:T(8,128)S(1)} %get-tuple-element.38.own), channel_id=1, replica_groups=mesh['x'=4,'zl'=2,'core'=2,'yh'=4,'yl'=2,'zhh'=2,'zhl'=2] {'zhl','zhh','..., dimensions={0} | all-to-all | bytes 786432 | tf_op jit(solution)/shard_map/all_to_all | solution.py:383
  179.4 2.4 %totals.3 = f32[8,264,128]{2,1,0:T(8,128)S(1)} custom-call(s32[7]{0:T(128)S(1)} %stack.31.at, f32[32,24,128]{2,1,0:T(8,128)S(1)} %all_to_all.22.stats, f32[32,24,128]{2,1,0:T(8,128)S(1)} %get-tuple-element.38.own, f32[1024,1536]{1,0:T(8,128)S(1)} %get-tuple-element.39.powers, bf16[512,1536]{1,0:T(8,128)(2,1)S(1)} %get-tuple-element.40.rounded), custom_call_target="tpu_custom_call" | custom-call | tf_op jit(solution)/shard_map/totals/pallas_call | solution.py:97
  181.8 5.1 %collective-permute-start.12 = (f32[8,264,128]{2,1,0:T(8,128)S(1)}, f32[8,264,128]{2,1,0:T(8,128)S(1)}, u32[]{:S(2)}, u32[]{:S(2)}) collective-permute-start(f32[8,264,128]{2,1,0:T(8,128)S(1)} %totals.3), channel_id=1, source_target_pairs={{0,32},{32,0},{1,33},{33,1},{2,34},{34,2},{3,35},{35,3},{4,36},{36... | collective-permute-start | bytes 3244040 | tf_op jit(solution)/shard_map/ppermute | solution.py:385
  186.9 2.4 %totals.2 = f32[8,264,128]{2,1,0:T(8,128)S(1)} custom-call(s32[7]{0:T(128)S(1)} %stack.31.at, f32[32,24,128]{2,1,0:T(8,128)S(1)} %all_to_all.22.stats, f32[32,24,128]{2,1,0:T(8,128)S(1)} %get-tuple-element.38.own, f32[1024,1536]{1,0:T(8,128)S(1)} %get-tuple-element.39.powers, bf16[512,1536]{1,0:T(8,128)(2,1)S(1)} %get-tuple-element.40.rounded), custom_call_target="tpu_custom_call" | custom-call | tf_op jit(solution)/shard_map/totals/pallas_call | solution.py:97
  189.3 0.1 add.39
  189.5 19.6 %all_to_all.23.parts = f32[8,264,128]{2,1,0:T(8,128)S(1)} all-to-all(f32[8,264,128]{2,1,0:T(8,128)S(1)} %add.39), channel_id=1, replica_groups=mesh['x'=4,'zl'=2,'core'=2,'yh'=4,'yl'=2,'zhh'=2,'zhl'=2] {'zl','x'}, dimensions={0} | all-to-all | bytes 2162688 | tf_op jit(solution)/shard_map/all_to_all | solution.py:387
  209.1 1.3 final.1
  (9 shorter events, 0.0 us)
Async XLA Ops:
  3.1 12.0 %collective-permute-start = (f32[64,1536]{1,0:T(8,128)S(1)}, f32[64,1536]{1,0:T(8,128)S(1)}, u32[]{:S(2)}, u32[]{:S(2)}) collective-permute-start(f32[64,1536]{1,0:T(8,128)S(1)} %get-tuple-element.27), channel_id=1, source_target_pairs={{0,4},{4,0},{8,12},{12,8},{16,20},{20,16},{24,28},{28,24},{1,5},{5... | collective-permute-start | bytes 1179656 | tf_op jit(solution)/shard_map/ppermute | solution.py:342
  7.1 11.7 %collective-permute-start.1 = (f32[64,1536]{1,0:T(8,128)S(1)}, f32[64,1536]{1,0:T(8,128)S(1)}, u32[]{:S(2)}, u32[]{:S(2)}) collective-permute-start(f32[64,1536]{1,0:T(8,128)S(1)} %get-tuple-element.28), channel_id=1, source_target_pairs={{0,28},{4,8},{8,4},{12,16},{16,12},{20,24},{24,20},{28,0},{1,29},{... | collective-permute-start | bytes 1179656 | tf_op jit(solution)/shard_map/ppermute | solution.py:342
  18.9 26.8 %collective-permute-start.4 = (f32[4,16,1536]{2,1,0:T(8,128)S(1)}, f32[4,16,1536]{2,1,0:T(8,128)S(1)}, u32[]{:S(2)}, u32[]{:S(2)}) collective-permute-start(f32[4,16,1536]{2,1,0:T(8,128)S(1)} %get-tuple-element.34), channel_id=1, source_target_pairs={{0,1},{1,0},{2,3},{3,2},{4,5},{5,4},{6,7},{7,6},{8,9},{9,8},{10,11... | collective-permute-start | bytes 1179656 | tf_op jit(solution)/shard_map/ppermute | solution.py:342
  26.4 19.4 %collective-permute-start.5 = (f32[4,16,1536]{2,1,0:T(8,128)S(1)}, f32[4,16,1536]{2,1,0:T(8,128)S(1)}, u32[]{:S(2)}, u32[]{:S(2)}) collective-permute-start(f32[4,16,1536]{2,1,0:T(8,128)S(1)} %get-tuple-element.35), channel_id=1, source_target_pairs={{0,3},{1,2},{2,1},{3,0},{4,7},{5,6},{6,5},{7,4},{8,11},{9,10},{10,... | collective-permute-start | bytes 1179656 | tf_op jit(solution)/shard_map/ppermute | solution.py:342
  36.5 10.4 %collective-permute-start.2 = (f32[64,1536]{1,0:T(8,128)S(1)}, f32[64,1536]{1,0:T(8,128)S(1)}, u32[]{:S(2)}, u32[]{:S(2)}) collective-permute-start(f32[64,1536]{1,0:T(8,128)S(1)} %get-tuple-element.32), channel_id=1, source_target_pairs={{0,4},{4,0},{8,12},{12,8},{16,20},{20,16},{24,28},{28,24},{1,5},{5... | collective-permute-start | bytes 1179656 | tf_op jit(solution)/shard_map/ppermute | solution.py:342
  38.4 11.6 %collective-permute-start.3 = (f32[64,1536]{1,0:T(8,128)S(1)}, f32[64,1536]{1,0:T(8,128)S(1)}, u32[]{:S(2)}, u32[]{:S(2)}) collective-permute-start(f32[64,1536]{1,0:T(8,128)S(1)} %get-tuple-element.33), channel_id=1, source_target_pairs={{0,28},{4,8},{8,4},{12,16},{16,12},{20,24},{24,20},{28,0},{1,29},{... | collective-permute-start | bytes 1179656 | tf_op jit(solution)/shard_map/ppermute | solution.py:342
  114.2 18.7 %collective-permute-start.7 = (f32[4,16,1536]{2,1,0:T(8,128)S(1)}, f32[4,16,1536]{2,1,0:T(8,128)S(1)}, u32[]{:S(2)}, u32[]{:S(2)}) collective-permute-start(f32[4,16,1536]{2,1,0:T(8,128)S(1)} %get-tuple-element.43), channel_id=1, source_target_pairs={{0,3},{1,2},{2,1},{3,0},{4,7},{5,6},{6,5},{7,4},{8,11},{9,10},{10,... | collective-permute-start | bytes 1179656 | tf_op jit(solution)/shard_map/ppermute | solution.py:342
  116.2 28.4 %copy-start.3 = (s32[1,2,768]{2,1,0:T(2,128)S(1)}, s32[1,2,768]{2,1,0:T(2,128)}, u32[]{:S(2)}) copy-start(s32[1,2,768]{2,1,0:T(2,128)} %param.9) | copy-start | bytes 18436
  116.2 28.4 %copy-start = (bf16[512,1024]{1,0:T(8,128)(2,1)S(1)}, bf16[512,1024]{1,0:T(8,128)(2,1)}, u32[]{:S(2)}) copy-start(bf16[512,1024]{1,0:T(8,128)(2,1)} %refs.1) | copy-start | bytes 3145732
  116.2 21.5 %collective-permute-start.6 = (f32[4,16,1536]{2,1,0:T(8,128)S(1)}, f32[4,16,1536]{2,1,0:T(8,128)S(1)}, u32[]{:S(2)}, u32[]{:S(2)}) collective-permute-start(f32[4,16,1536]{2,1,0:T(8,128)S(1)} %get-tuple-element.44), channel_id=1, source_target_pairs={{0,1},{1,0},{2,3},{3,2},{4,5},{5,4},{6,7},{7,6},{8,9},{9,8},{10,11... | collective-permute-start | bytes 1179656 | tf_op jit(solution)/shard_map/ppermute | solution.py:342
  120.2 25.0 %collective-permute-start.9 = (f32[8,8,1536]{2,1,0:T(8,128)}, f32[8,8,1536]{2,1,0:T(8,128)}, u32[]{:S(2)}, u32[]{:S(2)}) collective-permute-start(f32[8,8,1536]{2,1,0:T(8,128)} %get-tuple-element.41), channel_id=1, source_target_pairs={{0,28},{4,8},{8,4},{12,16},{16,12},{20,24},{24,20},{28,0},{1,29},{... | collective-permute-start | bytes 1179656 | tf_op jit(solution)/shard_map/ppermute | solution.py:342
  122.1 23.1 %collective-permute-start.8 = (f32[8,8,1536]{2,1,0:T(8,128)}, f32[8,8,1536]{2,1,0:T(8,128)}, u32[]{:S(2)}, u32[]{:S(2)}) collective-permute-start(f32[8,8,1536]{2,1,0:T(8,128)} %get-tuple-element.42), channel_id=1, source_target_pairs={{0,4},{4,0},{8,12},{12,8},{16,20},{20,16},{24,28},{28,24},{1,5},{5... | collective-permute-start | bytes 1179656 | tf_op jit(solution)/shard_map/ppermute | solution.py:342
  137.7 6.9 %copy-start.1 = (f32[4,16,1536]{2,1,0:T(8,128)}, f32[4,16,1536]{2,1,0:T(8,128)S(1)}, u32[]{:S(2)}) copy-start(f32[4,16,1536]{2,1,0:T(8,128)S(1)} %collective-permute-done.6.low) | copy-start | bytes 1179652
  138.7 11.4 %collective-permute-start.10 = (f32[8,8,1536]{2,1,0:T(8,128)}, f32[8,8,1536]{2,1,0:T(8,128)}, u32[]{:S(2)}, u32[]{:S(2)}) collective-permute-start(f32[8,8,1536]{2,1,0:T(8,128)} %get-tuple-element.36), channel_id=1, source_target_pairs={{0,4},{4,0},{8,12},{12,8},{16,20},{20,16},{24,28},{28,24},{1,5},{5... | collective-permute-start | bytes 1179656 | tf_op jit(solution)/shard_map/ppermute | solution.py:342
  140.6 12.6 %collective-permute-start.11 = (f32[8,8,1536]{2,1,0:T(8,128)}, f32[8,8,1536]{2,1,0:T(8,128)}, u32[]{:S(2)}, u32[]{:S(2)}) collective-permute-start(f32[8,8,1536]{2,1,0:T(8,128)} %get-tuple-element.37), channel_id=1, source_target_pairs={{0,28},{4,8},{8,4},{12,16},{16,12},{20,24},{24,20},{28,0},{1,29},{... | collective-permute-start | bytes 1179656 | tf_op jit(solution)/shard_map/ppermute | solution.py:342
  145.2 1.0 copy-start.2
  181.8 7.5 %collective-permute-start.12 = (f32[8,264,128]{2,1,0:T(8,128)S(1)}, f32[8,264,128]{2,1,0:T(8,128)S(1)}, u32[]{:S(2)}, u32[]{:S(2)}) collective-permute-start(f32[8,264,128]{2,1,0:T(8,128)S(1)} %totals.3), channel_id=1, source_target_pairs={{0,32},{32,0},{1,33},{33,1},{2,34},{34,2},{3,35},{35,3},{4,36},{36... | collective-permute-start | bytes 3244040 | tf_op jit(solution)/shard_map/ppermute | solution.py:385
